TPU v7x, 128 devices: a whole 4x4x4 slice. The times are simulated.
128 devices in a mesh: fsdp: 4 (over z), sp: 32 (over x, y, core).
Axes of the slice: x: 4, y: 4, z: 4, core: 2. Of those that a mesh axis runs over, the one named last changes fastest.
Arguments:
- tokens: bfloat16 [4, 20480, 1536], P('fsdp', 'sp'), may hold values from -6 to 6
- mod_scale: float32 [4, 1536], P('fsdp'), may hold values from 0.25 to 3
- mod_shift: float32 [4, 1536], P('fsdp'), may hold values from -3 to 3
- w_qkv: bfloat16 [1536, 4608], P(None, 'fsdp'), may hold values from -0.15625 to 0.15625
- w_out: bfloat16 [1536, 1536], P('fsdp'), may hold values from -0.15625 to 0.15625
- neighbors: int32 [4, 160, 6], P('fsdp', 'sp'), may hold values from 0 to 19, as said below
- counts: int32 [4, 8], P('fsdp'), may hold values from 1921 to 2560, as said below
Outputs:
- attn_out: bfloat16 [4, 20480, 1536], P('fsdp', 'sp')
Inputs may be any that keep to these rules, and one draw needn't show every extreme that they name: `neighbors`: each list holds 6 different tiles of the same frame, the tile itself first, the others at most one tile row and two tile columns away from it. `counts`: padding lies in the last row of tiles only; in every clip some frame is full.
All inputs are finite; a program needn't handle non-finite values.
Results may differ from a plain program's by a relative error of at most 0.006.
The roundings to bfloat16 on the way count: a program that leaves them out, or rounds other values in their place, can miss the bound.
Values may be sent and summed in bfloat16 or wider, within the bound.
A program may use at most 192 MiB of HBM per device.

v0:
```python
import math

import jax
import jax.numpy as jnp
from jax import lax
from jax.experimental import pallas as pl
from jax.experimental.pallas import tpu as pltpu
from jax.sharding import Mesh
from jax.sharding import PartitionSpec as P

HEADS = 12
HD = 128
TILE = 128
TGW = 5
NBR = 6
PIECES = 4


def passed_along(block, axis, distance):
    devices = range(lax.axis_size(axis))
    route = [(i - distance, i) for i in devices if i - distance in devices]
    return lax.ppermute(block, axis, route)


def layer_norm(tokens, mod_scale, mod_shift):
    values_f32 = tokens.astype(jnp.float32)
    center = jnp.mean(values_f32, axis=-1, keepdims=True)
    spread = jnp.mean((values_f32 - center) ** 2, axis=-1, keepdims=True)
    normal = (values_f32 - center) / jnp.sqrt(spread + 1e-06)
    return (normal * (1.0 + mod_scale) + mod_shift).astype(jnp.bfloat16)


def spatial_kernel(list_ref, scalar_ref, q_ref, k_ref, v_ref, o_ref):
    scaling = 1.0 / math.sqrt(HD)
    first_tile = scalar_ref[0]
    count_here = scalar_ref[1]
    local_tiles = q_ref.shape[0] // TILE
    for t in range(local_tiles):
        query = q_ref[t * TILE : (t + 1) * TILE, :]
        parts = []
        row_max = None
        for n in range(NBR):
            tile_id = list_ref[t * NBR + n]
            start = pl.multiple_of((tile_id - first_tile) * TILE, TILE)
            key = k_ref[pl.ds(start, TILE), :]
            scores = (
                lax.dot_general(
                    query, key, (((1,), (1,)), ((), ())), preferred_element_type=jnp.float32
                )
                * scaling
            )
            key_pos = tile_id * TILE + lax.broadcasted_iota(jnp.int32, scores.shape, 1)
            live = key_pos < count_here
            scores = jnp.where(live, scores, -1e30)
            part_max = jnp.max(scores, axis=-1, keepdims=True)
            row_max = part_max if row_max is None else jnp.maximum(row_max, part_max)
            parts.append((scores, live, start))
        denominator = None
        summed = None
        for scores, live, start in parts:
            exp_terms = jnp.where(live, jnp.exp(scores - row_max), 0.0)
            part_sum = jnp.sum(exp_terms, axis=-1, keepdims=True)
            value = v_ref[pl.ds(start, TILE), :]
            part_out = jnp.dot(
                exp_terms.astype(jnp.bfloat16), value, preferred_element_type=jnp.float32
            )
            denominator = part_sum if denominator is None else denominator + part_sum
            summed = part_out if summed is None else summed + part_out
        o_ref[t * TILE : (t + 1) * TILE, :] = (summed / denominator).astype(o_ref.dtype)


def spatial_rows(queries, kv_all, tile_list, first_tile, count_here):
    rows, feat = queries.shape
    buffer_rows = kv_all.shape[0]
    scalars = jnp.stack([first_tile, count_here]).astype(jnp.int32)
    grid_spec = pltpu.PrefetchScalarGridSpec(
        num_scalar_prefetch=2,
        grid=(HEADS,),
        in_specs=[
            pl.BlockSpec((rows, HD), lambda h, lst, sc: (0, h)),
            pl.BlockSpec((buffer_rows, HD), lambda h, lst, sc: (0, h)),
            pl.BlockSpec((buffer_rows, HD), lambda h, lst, sc: (0, HEADS + h)),
        ],
        out_specs=pl.BlockSpec((rows, HD), lambda h, lst, sc: (0, h)),
    )
    flops = 4 * rows * NBR * TILE * feat
    return pl.pallas_call(
        spatial_kernel,
        grid_spec=grid_spec,
        out_shape=jax.ShapeDtypeStruct((rows, feat), jnp.bfloat16),
        cost_estimate=pl.CostEstimate(
            flops=flops,
            transcendentals=rows * NBR * TILE * HEADS,
            bytes_accessed=2 * (rows * feat * 2 + buffer_rows * feat * 2),
        ),
    )(tile_list.reshape(-1).astype(jnp.int32), scalars, queries, kv_all, kv_all)


def temporal_block(query_part, key_part, spatial_part, clip_counts, first_pos):
    n_frames, per_dev = query_part.shape[0], query_part.shape[1]
    scaling = 1.0 / math.sqrt(HD)
    position = first_pos + jnp.arange(per_dev, dtype=jnp.int32)
    live_mask = (position[:, None] < clip_counts[None, :])[:, None, None, :]
    scores = (
        jnp.einsum(
            "fphd,gphd->phfg", query_part, key_part, preferred_element_type=jnp.float32
        )
        * scaling
    )
    scores = jnp.where(live_mask, scores, -1e30)
    row_max = jnp.max(scores, axis=-1, keepdims=True)
    exp_terms = jnp.where(live_mask, jnp.exp(scores - row_max), 0.0)
    denominator = jnp.sum(exp_terms, axis=-1, keepdims=True)
    weights = exp_terms.astype(jnp.bfloat16)
    summed = jnp.einsum(
        "phfg,gphd->fphd", weights, spatial_part, preferred_element_type=jnp.float32
    )
    result = summed / jnp.transpose(denominator, (2, 0, 1, 3))
    return result.astype(jnp.bfloat16)


def local(tokens, mod_scale, mod_shift, w_qkv, w_out, neighbors, counts):
    tok_count = tokens.shape[1]
    feat_count = tokens.shape[2]
    n_frames = lax.axis_size("frame")
    own = tokens[0]
    above = passed_along(own, "piece", 1)
    below = passed_along(own, "piece", -1)
    w_full = lax.all_gather(w_qkv, "fsdp", axis=1, tiled=True)
    w_out_full = lax.all_gather(w_out, "fsdp", axis=0, tiled=True)
    normed_all = layer_norm(
        jnp.concatenate([above, own, below], axis=0), mod_scale[0], mod_shift[0]
    )
    queries = jnp.dot(
        normed_all[tok_count : 2 * tok_count],
        w_full[:, :feat_count],
        preferred_element_type=jnp.float32,
    ).astype(jnp.bfloat16)
    kv_all = jnp.dot(
        normed_all, w_full[:, feat_count:], preferred_element_type=jnp.float32
    ).astype(jnp.bfloat16)
    key_proj = kv_all[tok_count : 2 * tok_count, :feat_count]
    frame_index = lax.axis_index("frame")
    piece_index = lax.axis_index("piece")
    clip_counts = counts[0]
    count_here = lax.dynamic_index_in_dim(clip_counts, frame_index, 0, keepdims=False)
    rows_here = tok_count // (TGW * TILE)
    first_tile = (piece_index * rows_here - 1) * TGW
    spatial = spatial_rows(queries, kv_all, neighbors[0], first_tile, count_here)
    head_shape = (1, tok_count, HEADS, HD)
    query_part = lax.all_to_all(
        queries.reshape(head_shape), "frame", split_axis=1, concat_axis=0, tiled=True
    )
    key_part = lax.all_to_all(
        key_proj.reshape(head_shape), "frame", split_axis=1, concat_axis=0, tiled=True
    )
    spatial_part = lax.all_to_all(
        spatial.reshape(head_shape), "frame", split_axis=1, concat_axis=0, tiled=True
    )
    per_dev = tok_count // n_frames
    first_pos = piece_index * tok_count + frame_index * per_dev
    temporal = temporal_block(query_part, key_part, spatial_part, clip_counts, first_pos)
    returned = lax.all_to_all(temporal, "frame", split_axis=0, concat_axis=1, tiled=True)
    flat_temporal = returned.reshape(tok_count, feat_count)
    projected = jnp.dot(flat_temporal, w_out_full, preferred_element_type=jnp.float32)
    return projected.astype(jnp.bfloat16).reshape(1, tok_count, feat_count)


def solution(mesh):
    n_fsdp = mesh.shape["fsdp"]
    n_sp = mesh.shape["sp"]
    split = Mesh(
        mesh.devices.reshape(n_fsdp, PIECES, n_sp // PIECES), ("fsdp", "piece", "frame")
    )
    seq = ("piece", "frame")
    placed = (
        P("fsdp", seq, None),
        P("fsdp", None),
        P("fsdp", None),
        P(None, "fsdp"),
        P("fsdp", None),
        P("fsdp", seq, None),
        P("fsdp", None),
    )
    return jax.shard_map(
        local, mesh=split, in_specs=placed, out_specs=P("fsdp", seq, None), check_vma=False
    )
```

profile of v0, /device:TPU:1, one launch (start us, length us, event | category | flops | bytes accessed | tf_op | source)
XLA Modules:
  0.0 346.5 jit_solution(10132381843789499409)
XLA Ops:
  7.3 5.2 %collective-permute-start = (bf16[640,1536]{1,0:T(8,128)(2,1)}, bf16[640,1536]{1,0:T(8,128)(2,1)}, u32[]{:S(2)}, u32[]{:S(2)}) collective-permute-start(bf16[640,1536]{1,0:T(8,128)(2,1)} %bitcast.29), channel_id=1, source_target_pairs={{0,8},{8,16},{16,24},{1,9},{9,17},{17,25},{2,10},{10,18},{18,26},{... | collective-permute-start | bytes 5898248 | tf_op jit(solution)/shard_map/ppermute | solution.py:22
  15.2 37.8 %collective-permute-done = bf16[640,1536]{1,0:T(8,128)(2,1)} collective-permute-done((bf16[640,1536]{1,0:T(8,128)(2,1)}, bf16[640,1536]{1,0:T(8,128)(2,1)}, u32[]{:S(2)}, u32[]{:S(2)}) %collective-permute-start) | collective-permute-done | bytes 1966112 | tf_op jit(solution)/shard_map/ppermute | solution.py:22
  53.0 5.0 %collective-permute-done.1 = bf16[640,1536]{1,0:T(8,128)(2,1)} collective-permute-done((bf16[640,1536]{1,0:T(8,128)(2,1)}, bf16[640,1536]{1,0:T(8,128)(2,1)}, u32[]{:S(2)}, u32[]{:S(2)}) %collective-permute-start.1) | collective-permute-done | bytes 1966112 | tf_op jit(solution)/shard_map/ppermute | solution.py:22
  61.4 4.3 %fusion.3 = f32[1920]{0:T(1024)S(1)} fusion(f32[1920]{0:T(1024)S(1)} %broadcast_multiply_fusion, bf16[640,1536]{1,0:T(8,128)(2,1)} %collective-permute-done.1, bf16[640,1536]{1,0:T(8,128)(2,1)S(1)} %bitcast.32, bf16[640,1536]{1,0:T(8,128)(2,1)} %collective-permute-done), kind=kLoop, calls=%fused_computation.5 | loop fusion | flops 26540160 | bytes 5913600 | tf_op jit(solution)/shard_map/reduce_sum | solution.py:28
  65.7 13.9 %fusion.6 = bf16[1920,1536]{1,0:T(8,128)(2,1)} fusion(f32[1536]{0:T(1024)S(1)} %reduce.2, f32[1536]{0:T(1024)S(1)} %add_reduce_fusion, f32[1920]{0:T(1024)S(1)} %add_sqrt_fusion, f32[1920]{0:T(1024)S(1)} %broadcast_multiply_fusion, bf16[640,1536]{1,0:T(8,128)(2,1)} %collective-permute-done.1, bf16[640,1536]{1,0:T(8,128)(2,1)S(1)} %bitcast.33, ...), kind=kLoop, calls=%fused_computation.8 | loop fusion | flops 32440320 | bytes 11824128 | tf_op jit(solution)/shard_map/convert_element_type | solution.py:30
  79.6 64.7 %all-gather.3.cloned.1.call-done = bf16[1536,4608]{1,0:T(8,128)(2,1)} async-done(((bf16[1536,1152]{1,0:T(8,128)(2,1)}), bf16[1536,4608]{1,0:T(8,128)(2,1)}) %all-gather.3.cloned.1.call-update) | async-done | bytes 14155792 | tf_op jit(solution)/shard_map/all_gather | solution.py:129
  144.2 22.5 %convolution_convert_fusion.k_ref.v_ref = bf16[1920,3072]{1,0:T(8,128)(2,1)S(1)} fusion(bf16[1920,1536]{1,0:T(8,128)(2,1)} %fusion.6, bf16[1536,4608]{1,0:T(8,128)(2,1)} %all-gather.3.cloned.1.call-done), kind=kOutput, calls=%fused_computation.9 | convolution fusion | flops 18125291520 | bytes 27131904 | tf_op jit(solution)/shard_map/dot_general | solution.py:139
  166.8 4.3 %copy-done = bf16[1920,3072]{1,0:T(8,128)(2,1)} copy-done((bf16[1920,3072]{1,0:T(8,128)(2,1)}, bf16[1920,3072]{1,0:T(8,128)(2,1)S(1)}, u32[]{:S(2)}) %copy-start) | copy-done | bytes 11796504
  175.3 5.4 %copy.72 = bf16[1,640,12,128]{3,2,0,1:T(8,128)(2,1)} copy(bf16[1,640,12,128]{1,3,2,0:T(8,128)(2,1)S(1)} %bitcast.35) | data formatting | bytes 3932160 | tf_op jit(solution)/shard_map/reshape | solution.py:155
  180.7 5.0 %all-to-all-start.2 = ((bf16[1,640,12,128]{3,2,0,1:T(8,128)(2,1)}), bf16[1,640,12,128]{3,2,0,1:T(8,128)(2,1)S(1)}, u32[]{:S(2)}, u32[]{:S(2)}) async-start(bf16[1,640,12,128]{3,2,0,1:T(8,128)(2,1)} %copy.72), calls=%async_computation.2 | async-start | bytes 5242880 | tf_op jit(solution)/shard_map/all_to_all | solution.py:154
  186.4 7.4 %fusion.11.q_ref = bf16[640,1536]{1,0:T(8,128)(2,1)} fusion(bf16[1536,4608]{1,0:T(8,128)(2,1)} %all-gather.3.cloned.1.call-done, bf16[1920,1536]{1,0:T(8,128)(2,1)} %fusion.6), kind=kOutput, calls=%fused_computation.16 | convolution fusion | flops 3020881920 | bytes 8650752 | tf_op jit(solution)/shard_map/dot_general | solution.py:134
  193.8 4.0 %copy.68 = bf16[640,1536]{0,1:T(8,128)(2,1)} copy(bf16[640,1536]{1,0:T(8,128)(2,1)} %fusion.11.q_ref) | data formatting | bytes 3932160 | tf_op jit(solution)/shard_map/convert_element_type | solution.py:138
  197.8 4.9 %copy.69 = bf16[1,640,12,128]{3,2,0,1:T(8,128)(2,1)} copy(bf16[1,640,12,128]{1,3,2,0:T(8,128)(2,1)} %bitcast.37) | data formatting | bytes 3932160 | tf_op jit(solution)/shard_map/reshape | solution.py:152
  202.7 14.9 %all-to-all-done.2 = bf16[1,640,12,128]{3,2,0,1:T(8,128)(2,1)S(1)} async-done(((bf16[1,640,12,128]{3,2,0,1:T(8,128)(2,1)}), bf16[1,640,12,128]{3,2,0,1:T(8,128)(2,1)S(1)}, u32[]{:S(2)}, u32[]{:S(2)}) %all-to-all-start.2) | async-done | bytes 1966112 | tf_op jit(solution)/shard_map/all_to_all | solution.py:154
  217.6 5.2 %all-to-all-start.1 = ((bf16[1,640,12,128]{3,2,0,1:T(8,128)(2,1)}), bf16[1,640,12,128]{3,2,0,1:T(8,128)(2,1)}, u32[]{:S(2)}, u32[]{:S(2)}) async-start(bf16[1,640,12,128]{3,2,0,1:T(8,128)(2,1)} %copy.69), calls=%async_computation.1 | async-start | bytes 5242880 | tf_op jit(solution)/shard_map/all_to_all | solution.py:151
  225.4 28.7 %shard_map.73 = bf16[640,1536]{1,0:T(8,128)(2,1)} custom-call(s32[30]{0:T(128)} %reshape_squeeze.3.list_ref, s32[2]{0:T(128)} %pad_add_fusion.scalar_ref, bf16[640,1536]{1,0:T(8,128)(2,1)} %fusion.11.q_ref, bf16[1920,3072]{1,0:T(8,128)(2,1)} %copy-done, bf16[1920,3072]{1,0:T(8,128)(2,1)} %copy-done), custom_call_target="tpu_custom_call" | custom-call | flops 3019898880 | bytes 15728640 | tf_op jit(solution)/shard_map/pallas_call | solution.py:87
  254.0 4.0 %copy.65 = bf16[640,1536]{0,1:T(8,128)(2,1)} copy(bf16[640,1536]{1,0:T(8,128)(2,1)} %shard_map.73) | data formatting | bytes 3932160 | tf_op jit(solution)/shard_map/pallas_call | solution.py:87
  258.0 4.8 %copy.66 = bf16[1,640,12,128]{3,2,0,1:T(8,128)(2,1)} copy(bf16[1,640,12,128]{1,3,2,0:T(8,128)(2,1)} %bitcast.36) | data formatting | bytes 3932160 | tf_op jit(solution)/shard_map/reshape | solution.py:158
  262.8 4.8 %all-to-all-start = ((bf16[1,640,12,128]{3,2,0,1:T(8,128)(2,1)}), bf16[1,640,12,128]{3,2,0,1:T(8,128)(2,1)}, u32[]{:S(2)}, u32[]{:S(2)}) async-start(bf16[1,640,12,128]{3,2,0,1:T(8,128)(2,1)} %copy.66), calls=%async_computation | async-start | bytes 5242880 | tf_op jit(solution)/shard_map/all_to_all | solution.py:157
  267.7 6.0 %fusion.18 = f32[80,12,8,8]{2,3,1,0:T(8,128)} fusion(bf16[8,80,12,128]{3,2,1,0:T(8,128)(2,1)S(1)} %bitcast.34, bf16[8,80,12,128]{3,2,1,0:T(8,128)(2,1)} %bitcast.7), kind=kOutput, calls=%fused_computation.22 | convolution fusion | flops 15728640 | bytes 4177920 | tf_op jit(solution)/shard_map/fphd,gphd->phfg/dot_general | solution.py:105
  278.9 20.8 %all-to-all-done = bf16[1,640,12,128]{3,2,0,1:T(8,128)(2,1)} async-done(((bf16[1,640,12,128]{3,2,0,1:T(8,128)(2,1)}), bf16[1,640,12,128]{3,2,0,1:T(8,128)(2,1)}, u32[]{:S(2)}, u32[]{:S(2)}) %all-to-all-start) | async-done | bytes 1966112 | tf_op jit(solution)/shard_map/all_to_all | solution.py:157
  299.7 3.4 fusion.10
  303.8 28.5 %all_to_all.45 = bf16[8,80,12,128]{3,1,2,0:T(8,128)(2,1)S(1)} all-to-all(bf16[8,80,12,128]{3,1,2,0:T(8,128)(2,1)S(1)} %copy.80), channel_id=1, replica_groups=mesh['fsdp'=4,'piece'=4,'frame'=8] {'frame'}, dimensions={0} | all-to-all | bytes 3932160 | tf_op jit(solution)/shard_map/all_to_all | solution.py:163
  333.0 6.7 %fusion.14 = bf16[1,640,1536]{2,1,0:T(8,128)(2,1)} fusion(bf16[1536,1536]{1,0:T(8,128)(2,1)} %all-gather.5.cloned.1.call-done, bf16[80,8,12,128]{3,2,1,0:T(8,128)(2,1)S(1)} %bitcast.38), kind=kOutput, calls=%fused_computation.18 | convolution fusion | flops 3020881920 | bytes 8650752 | tf_op jit(solution)/shard_map/dot_general | solution.py:165
  (33 shorter events, 20.8 us)
Async XLA Ops:
  6.5 51.5 %copy-start.1 = (bf16[1,640,1536]{2,1,0:T(8,128)(2,1)S(1)}, bf16[1,640,1536]{2,1,0:T(8,128)(2,1)}, u32[]{:S(2)}) copy-start(bf16[1,640,1536]{2,1,0:T(8,128)(2,1)} %param.7) | copy-start | bytes 5898244
  6.5 137.7 %all-gather.3.cloned.1.call-start = ((), (), s32[]{:S(2)}) async-start(), calls=%async_computation.4 | async-start | bytes 17694720 | tf_op jit(solution)/shard_map/all_gather | solution.py:129
  7.3 45.7 %collective-permute-start = (bf16[640,1536]{1,0:T(8,128)(2,1)}, bf16[640,1536]{1,0:T(8,128)(2,1)}, u32[]{:S(2)}, u32[]{:S(2)}) collective-permute-start(bf16[640,1536]{1,0:T(8,128)(2,1)} %bitcast.29), channel_id=1, source_target_pairs={{0,8},{8,16},{16,24},{1,9},{9,17},{17,25},{2,10},{10,18},{18,26},{... | collective-permute-start | bytes 5898248 | tf_op jit(solution)/shard_map/ppermute | solution.py:22
  12.5 45.6 %collective-permute-start.1 = (bf16[640,1536]{1,0:T(8,128)(2,1)}, bf16[640,1536]{1,0:T(8,128)(2,1)}, u32[]{:S(2)}, u32[]{:S(2)}) collective-permute-start(bf16[640,1536]{1,0:T(8,128)(2,1)} %bitcast.30), channel_id=1, source_target_pairs={{8,0},{16,8},{24,16},{9,1},{17,9},{25,17},{10,2},{18,10},{26,18},{... | collective-permute-start | bytes 5898248 | tf_op jit(solution)/shard_map/ppermute | solution.py:22
  166.8 4.3 %copy-start = (bf16[1920,3072]{1,0:T(8,128)(2,1)}, bf16[1920,3072]{1,0:T(8,128)(2,1)S(1)}, u32[]{:S(2)}) copy-start(bf16[1920,3072]{1,0:T(8,128)(2,1)S(1)} %convolution_convert_fusion.k_ref.v_ref) | copy-start | bytes 35389444
  180.7 36.9 %all-to-all-start.2 = ((bf16[1,640,12,128]{3,2,0,1:T(8,128)(2,1)}), bf16[1,640,12,128]{3,2,0,1:T(8,128)(2,1)S(1)}, u32[]{:S(2)}, u32[]{:S(2)}) async-start(bf16[1,640,12,128]{3,2,0,1:T(8,128)(2,1)} %copy.72), calls=%async_computation.2 | async-start | bytes 5242880 | tf_op jit(solution)/shard_map/all_to_all | solution.py:154
  185.7 147.3 %all-gather.5.cloned.1.call-start = ((), (), s32[]{:S(2)}) async-start(), calls=%async_computation.5 | async-start | bytes 5898240 | tf_op jit(solution)/shard_map/all_gather | solution.py:130
  197.8 25.0 %copy-start.2 = (s32[1,5,6]{2,0,1:T(1,128)S(1)}, s32[1,5,6]{2,0,1:T(1,128)}, u32[]{:S(2)}) copy-start(s32[1,5,6]{2,0,1:T(1,128)} %param.12) | copy-start | bytes 364
  197.8 25.6 %copy-start.3 = (s32[1,8]{1,0:T(1,128)S(1)}, s32[1,8]{1,0:T(1,128)}, u32[]{:S(2)}) copy-start(s32[1,8]{1,0:T(1,128)} %param.13) | copy-start | bytes 100
  217.6 45.2 %all-to-all-start.1 = ((bf16[1,640,12,128]{3,2,0,1:T(8,128)(2,1)}), bf16[1,640,12,128]{3,2,0,1:T(8,128)(2,1)}, u32[]{:S(2)}, u32[]{:S(2)}) async-start(bf16[1,640,12,128]{3,2,0,1:T(8,128)(2,1)} %copy.69), calls=%async_computation.1 | async-start | bytes 5242880 | tf_op jit(solution)/shard_map/all_to_all | solution.py:151
  262.8 36.9 %all-to-all-start = ((bf16[1,640,12,128]{3,2,0,1:T(8,128)(2,1)}), bf16[1,640,12,128]{3,2,0,1:T(8,128)(2,1)}, u32[]{:S(2)}, u32[]{:S(2)}) async-start(bf16[1,640,12,128]{3,2,0,1:T(8,128)(2,1)} %copy.66), calls=%async_computation | async-start | bytes 5242880 | tf_op jit(solution)/shard_map/all_to_all | solution.py:157
Sparse Core Ops, SparseCore 0:
  9.0 135.1 all-gather.2
  188.2 53.6 all-gather.4
where the time goes:
time: 348 us; the launch traced here: 347 us
  waiting for transfers between devices  145 us (42%)
  matrix products  46 us (13%)
  local copies, waits for them, and re-layouts  39.1 us (11%)
  Pallas kernels  28.7 us (8%)
  blocking collectives  28.5 us (8%)
  other arithmetic  24.6 us (7%)
  starting transfers between devices  21.4 us (6%)
  between operations  13.5 us (4%)
    all_gather x1, waiting for transfers between devices, local(): w_full = lax.all_gather(w_qkv, 'fsdp', axis=1, tiled=True)  64.7 us
    ppermute x2, waiting for transfers between devices, passed_along(): return lax.ppermute(block, axis, route)  42.8 us
    pallas_call x1, Pallas kernels, spatial_rows(): pl.pallas_call(spatial_kernel, grid_spec=grid_spec, out_shape=jax.ShapeDt...  28.7 us
    all_to_all x1, blocking collectives, local(): lax.all_to_all(temporal, 'frame', split_axis=0, concat_axis=1, tiled=True)  28.5 us
    dot_general x1, matrix products, local(): jnp.dot(normed_all, w_full[:, feat_count:], preferred_element_type=jnp.fl...  22.5 us
    all_to_all x1, waiting for transfers between devices, local(): lax.all_to_all(spatial.reshape(head_shape), 'frame', split_axis=1, concat...  20.8 us
    all_to_all x1, waiting for transfers between devices, local(): lax.all_to_all(key_proj.reshape(head_shape), 'frame', split_axis=1, conca...  14.9 us
    convert_element_type x1, other arithmetic, layer_norm(): return (normal * (1.0 + mod_scale) + mod_shift).astype(jnp.bfloat16)  13.9 us
  transfers between devices with their start and end apart: 7, of which 5 were waited for; matrix products, arithmetic and copies ran while one was open for 19% of the time, Pallas kernels for 8%

commit v1 on v0

--- a/solution.py
+++ b/solution.py
@@ -122,12 +122,19 @@
 def local(tokens, mod_scale, mod_shift, w_qkv, w_out, neighbors, counts):
     tok_count = tokens.shape[1]
     feat_count = tokens.shape[2]
-    n_frames = lax.axis_size("frame")
+    n_frames = lax.axis_size("fy") * lax.axis_size("core")
     own = tokens[0]
     above = passed_along(own, "piece", 1)
     below = passed_along(own, "piece", -1)
-    w_full = lax.all_gather(w_qkv, "fsdp", axis=1, tiled=True)
-    w_out_full = lax.all_gather(w_out, "fsdp", axis=0, tiled=True)
+    core = lax.axis_index("core")
+    half_rows = w_qkv.shape[0] // 2
+    w_half = lax.dynamic_slice_in_dim(w_qkv, core * half_rows, half_rows, axis=0)
+    w_half = lax.all_gather(w_half, "fsdp", axis=1, tiled=True)
+    w_full = lax.all_gather(w_half, "core", axis=0, tiled=True)
+    out_rows = w_out.shape[0] // 2
+    w_out_half = lax.dynamic_slice_in_dim(w_out, core * out_rows, out_rows, axis=0)
+    w_out_half = lax.all_gather(w_out_half, "core", axis=0, tiled=True)
+    w_out_full = lax.all_gather(w_out_half, "fsdp", axis=0, tiled=True)
     normed_all = layer_norm(
         jnp.concatenate([above, own, below], axis=0), mod_scale[0], mod_shift[0]
     )
@@ -140,7 +147,7 @@
         normed_all, w_full[:, feat_count:], preferred_element_type=jnp.float32
     ).astype(jnp.bfloat16)
     key_proj = kv_all[tok_count : 2 * tok_count, :feat_count]
-    frame_index = lax.axis_index("frame")
+    frame_index = lax.axis_index("fy") * lax.axis_size("core") + lax.axis_index("core")
     piece_index = lax.axis_index("piece")
     clip_counts = counts[0]
     count_here = lax.dynamic_index_in_dim(clip_counts, frame_index, 0, keepdims=False)
@@ -148,19 +155,22 @@
     first_tile = (piece_index * rows_here - 1) * TGW
     spatial = spatial_rows(queries, kv_all, neighbors[0], first_tile, count_here)
     head_shape = (1, tok_count, HEADS, HD)
-    query_part = lax.all_to_all(
-        queries.reshape(head_shape), "frame", split_axis=1, concat_axis=0, tiled=True
+    frame_axes = ("fy", "core")
+    qk_part = lax.all_to_all(
+        jnp.stack([queries, key_proj]).reshape((2,) + head_shape),
+        frame_axes,
+        split_axis=2,
+        concat_axis=1,
+        tiled=True,
     )
-    key_part = lax.all_to_all(
-        key_proj.reshape(head_shape), "frame", split_axis=1, concat_axis=0, tiled=True
-    )
+    query_part, key_part = qk_part[0], qk_part[1]
     spatial_part = lax.all_to_all(
-        spatial.reshape(head_shape), "frame", split_axis=1, concat_axis=0, tiled=True
+        spatial.reshape(head_shape), frame_axes, split_axis=1, concat_axis=0, tiled=True
     )
     per_dev = tok_count // n_frames
     first_pos = piece_index * tok_count + frame_index * per_dev
     temporal = temporal_block(query_part, key_part, spatial_part, clip_counts, first_pos)
-    returned = lax.all_to_all(temporal, "frame", split_axis=0, concat_axis=1, tiled=True)
+    returned = lax.all_to_all(temporal, frame_axes, split_axis=0, concat_axis=1, tiled=True)
     flat_temporal = returned.reshape(tok_count, feat_count)
     projected = jnp.dot(flat_temporal, w_out_full, preferred_element_type=jnp.float32)
     return projected.astype(jnp.bfloat16).reshape(1, tok_count, feat_count)
@@ -170,9 +180,10 @@
     n_fsdp = mesh.shape["fsdp"]
     n_sp = mesh.shape["sp"]
     split = Mesh(
-        mesh.devices.reshape(n_fsdp, PIECES, n_sp // PIECES), ("fsdp", "piece", "frame")
+        mesh.devices.reshape(n_fsdp, PIECES, n_sp // PIECES // 2, 2),
+        ("fsdp", "piece", "fy", "core"),
     )
-    seq = ("piece", "frame")
+    seq = ("piece", "fy", "core")
     placed = (
         P("fsdp", seq, None),
         P("fsdp", None),

time: 348 us -> 352 us (1.011)
  local copies, waits for them, and re-layouts: 39.1 us -> 48.1 us
  waiting for transfers between devices: 145 us -> 140 us
  starting transfers between devices: 21.4 us -> 17.3 us
    all_to_all x3 -> x2, waiting for transfers between devices: 35.8 us -> 20.6 us  [the longest x1 14.4 us: local(): lax.all_to_all(spatial.reshape(head_shape), frame_axes, split_axis=1, con...]
    all_gather x2 -> x4, waiting for transfers between devices: 64.7 us -> 75.7 us  [the longest x1 75.7 us: local(): w_half = lax.all_gather(w_half, 'fsdp', axis=1, tiled=True)]
    another operation x0 -> x1, local copies, waits for them, and re-layouts: none -> 10.7 us  [local(): jnp.stack([queries, key_proj]).reshape((2,) + head_shape)]
    reshape x2 -> x0, local copies, waits for them, and re-layouts: 10.3 us -> none  [the longest x1 5.44 us: local(): key_proj.reshape(head_shape)]
    slice x0 -> x1, local copies, waits for them, and re-layouts: none -> 8.5 us  [local(): query_part, key_part = (qk_part[0], qk_part[1])]
    dot_general x1, matrix products: 7.41 us -> 11.7 us  [local(): jnp.dot(normed_all[tok_count:2 * tok_count], w_full[:, :feat_count], pref...]
    another operation x0 -> x1, other arithmetic: none -> 3.81 us  [local(): jnp.stack([queries, key_proj]).reshape((2,) + head_shape)]
    all_to_all x3 -> x2, starting transfers between devices: 14.9 us -> 11.6 us  [the longest x1 6.39 us: local(): lax.all_to_all(jnp.stack([queries, key_proj]).reshape((2,) + head_shape),...]
  transfers between devices with their start and end apart: 7 -> 8, of which waited for: 5 -> 5; matrix products, arithmetic and copies ran while one was open for 19% -> 32% of each run, Pallas kernels for 8% -> 8%
where the time goes in v1:
time: 352 us; the launch traced here: 351 us
  waiting for transfers between devices  140 us (40%)
  matrix products  48.4 us (14%)
  local copies, waits for them, and re-layouts  48.1 us (14%)
  Pallas kernels  28.6 us (8%)
  blocking collectives  28.5 us (8%)
  other arithmetic  26.9 us (8%)
  starting transfers between devices  17.3 us (5%)
  between operations  13.3 us (4%)
    all_gather x1, waiting for transfers between devices, local(): w_half = lax.all_gather(w_half, 'fsdp', axis=1, tiled=True)  75.7 us
    ppermute x2, waiting for transfers between devices, passed_along(): return lax.ppermute(block, axis, route)  43.1 us
    pallas_call x1, Pallas kernels, spatial_rows(): pl.pallas_call(spatial_kernel, grid_spec=grid_spec, out_shape=jax.ShapeDt...  28.6 us
    all_to_all x1, blocking collectives, local(): lax.all_to_all(temporal, frame_axes, split_axis=0, concat_axis=1, tiled=T...  28.5 us
    dot_general x1, matrix products, local(): jnp.dot(normed_all, w_full[:, feat_count:], preferred_element_type=jnp.fl...  22.5 us
    all_to_all x1, waiting for transfers between devices, local(): lax.all_to_all(spatial.reshape(head_shape), frame_axes, split_axis=1, con...  14.4 us
    convert_element_type x1, other arithmetic, layer_norm(): return (normal * (1.0 + mod_scale) + mod_shift).astype(jnp.bfloat16)  13.9 us
    dot_general x1, matrix products, local(): jnp.dot(normed_all[tok_count:2 * tok_count], w_full[:, :feat_count], pref...  11.7 us
  transfers between devices with their start and end apart: 8, of which 5 were waited for; matrix products, arithmetic and copies ran while one was open for 32% of the time, Pallas kernels for 8%

profile of v1, /device:TPU:1, one launch (start us, length us, event | category | flops | bytes accessed | tf_op | source)
XLA Modules:
  0.0 351.1 jit_solution(1279084241644044380)
XLA Ops:
  10.0 75.7 %all-gather.5.cloned.1.call-done = bf16[768,4608]{1,0:T(8,128)(2,1)} async-done(((bf16[768,1152]{1,0:T(8,128)(2,1)}), bf16[768,4608]{1,0:T(8,128)(2,1)}) %all-gather.5.cloned.1.call-update) | async-done | bytes 7077904 | tf_op jit(solution)/shard_map/all_gather | solution.py:132
  85.8 4.4 %collective-permute-start = (bf16[640,1536]{1,0:T(8,128)(2,1)S(1)}, bf16[640,1536]{1,0:T(8,128)(2,1)}, u32[]{:S(2)}, u32[]{:S(2)}) collective-permute-start(bf16[640,1536]{1,0:T(8,128)(2,1)S(1)} %bitcast.29), channel_id=1, source_target_pairs={{0,8},{8,16},{16,24},{1,9},{9,17},{17,25},{2,10},{10,18},{18,26},{... | collective-permute-start | bytes 5898248 | tf_op jit(solution)/shard_map/ppermute | solution.py:22
  92.5 37.9 %collective-permute-done = bf16[640,1536]{1,0:T(8,128)(2,1)} collective-permute-done((bf16[640,1536]{1,0:T(8,128)(2,1)S(1)}, bf16[640,1536]{1,0:T(8,128)(2,1)}, u32[]{:S(2)}, u32[]{:S(2)}) %collective-permute-start) | collective-permute-done | bytes 1966112 | tf_op jit(solution)/shard_map/ppermute | solution.py:22
  130.3 5.2 %collective-permute-done.1 = bf16[640,1536]{1,0:T(8,128)(2,1)} collective-permute-done((bf16[640,1536]{1,0:T(8,128)(2,1)S(1)}, bf16[640,1536]{1,0:T(8,128)(2,1)}, u32[]{:S(2)}, u32[]{:S(2)}) %collective-permute-start.1) | collective-permute-done | bytes 1966112 | tf_op jit(solution)/shard_map/ppermute | solution.py:22
  135.5 3.3 convert_reduce_fusion
  138.8 4.3 %fusion.3 = f32[1920]{0:T(1024)S(1)} fusion(f32[1920]{0:T(1024)S(1)} %broadcast_multiply_fusion, bf16[640,1536]{1,0:T(8,128)(2,1)} %collective-permute-done.1, bf16[640,1536]{1,0:T(8,128)(2,1)S(1)} %bitcast.32, bf16[640,1536]{1,0:T(8,128)(2,1)} %collective-permute-done), kind=kLoop, calls=%fused_computation.5 | loop fusion | flops 26540160 | bytes 5913600 | tf_op jit(solution)/shard_map/reduce_sum | solution.py:28
  143.1 13.9 %fusion.6 = bf16[1920,1536]{1,0:T(8,128)(2,1)} fusion(f32[1536]{0:T(1024)S(1)} %reduce.2, f32[1536]{0:T(1024)S(1)} %add_reduce_fusion, f32[1920]{0:T(1024)S(1)} %add_sqrt_fusion, f32[1920]{0:T(1024)S(1)} %broadcast_multiply_fusion, bf16[640,1536]{1,0:T(8,128)(2,1)} %collective-permute-done.1, bf16[640,1536]{1,0:T(8,128)(2,1)S(1)} %bitcast.33, ...), kind=kLoop, calls=%fused_computation.8 | loop fusion | flops 32440320 | bytes 11824128 | tf_op jit(solution)/shard_map/convert_element_type | solution.py:30
  157.0 22.5 %convolution_convert_fusion.k_ref.v_ref = bf16[1920,3072]{1,0:T(8,128)(2,1)S(1)} fusion(bf16[1920,1536]{1,0:T(8,128)(2,1)} %fusion.6, bf16[1536,4608]{1,0:T(8,128)(2,1)} %all-gather.7.cloned.1.call-done), kind=kOutput, calls=%fused_computation.9 | convolution fusion | flops 18125291520 | bytes 27131904 | tf_op jit(solution)/shard_map/dot_general | solution.py:146
  179.6 11.7 %fusion.11.q_ref = bf16[640,1536]{1,0:T(8,128)(2,1)} fusion(bf16[1536,4608]{1,0:T(8,128)(2,1)} %all-gather.7.cloned.1.call-done, bf16[1920,1536]{1,0:T(8,128)(2,1)} %fusion.6), kind=kOutput, calls=%fused_computation.17 | convolution fusion | flops 3020881920 | bytes 8650752 | tf_op jit(solution)/shard_map/dot_general | solution.py:141
  193.7 4.1 %copy.65 = bf16[640,1536]{0,1:T(8,128)(2,1)} copy(bf16[640,1536]{1,0:T(8,128)(2,1)} %fusion.11.q_ref) | data formatting | bytes 3932160 | tf_op jit(solution)/shard_map/convert_element_type | solution.py:145
  197.8 3.8 %pad_maximum_fusion.1 = bf16[2,1,640,12,128]{2,4,3,1,0:T(8,128)(2,1)} fusion(bf16[1,1,640,12,128]{2,4,3,1,0:T(8,128)(2,1)S(1)} %bitcast.36, bf16[1,1,640,12,128]{2,4,3,1,0:T(8,128)(2,1)} %bitcast.38), kind=kLoop, calls=%fused_computation.14 | loop fusion | flops 1966080 | bytes 7864320 | tf_op jit(solution)/shard_map/stack | solution.py:160
  201.6 10.7 %copy.67 = bf16[2,1,640,12,128]{4,0,3,1,2:T(2,128)(2,1)} copy(bf16[2,1,640,12,128]{2,4,3,1,0:T(8,128)(2,1)} %pad_maximum_fusion.1) | data formatting | bytes 7864320 | tf_op jit(solution)/shard_map/stack | solution.py:160
  212.3 6.4 %all-to-all-start.1 = ((bf16[2,1,640,12,128]{4,0,3,1,2:T(2,128)(2,1)}), bf16[2,1,640,12,128]{4,0,3,1,2:T(2,128)(2,1)}, u32[]{:S(2)}, u32[]{:S(2)}) async-start(bf16[2,1,640,12,128]{4,0,3,1,2:T(2,128)(2,1)} %copy.67), calls=%async_computation.1 | async-start | bytes 7864320 | tf_op jit(solution)/shard_map/all_to_all | solution.py:159
  221.8 28.6 %shard_map.73 = bf16[640,1536]{1,0:T(8,128)(2,1)} custom-call(s32[30]{0:T(128)} %reshape_squeeze.3.list_ref, s32[2]{0:T(128)} %pad_add_fusion.scalar_ref, bf16[640,1536]{1,0:T(8,128)(2,1)} %fusion.11.q_ref, bf16[1920,3072]{1,0:T(8,128)(2,1)} %copy-done.2, bf16[1920,3072]{1,0:T(8,128)(2,1)} %copy-done.2), custom_call_target="tpu_custom_call" | custom-call | flops 3019898880 | bytes 15728640 | tf_op jit(solution)/shard_map/pallas_call | solution.py:87
  253.2 5.5 %copy.63 = bf16[1,640,12,128]{3,2,0,1:T(8,128)(2,1)} copy(bf16[1,640,12,128]{1,3,2,0:T(8,128)(2,1)S(1)} %bitcast.34) | data formatting | bytes 3932160 | tf_op jit(solution)/shard_map/reshape | solution.py:168
  258.7 6.2 %all-to-all-done.1 = bf16[2,1,640,12,128]{4,0,3,1,2:T(2,128)(2,1)} async-done(((bf16[2,1,640,12,128]{4,0,3,1,2:T(2,128)(2,1)}), bf16[2,1,640,12,128]{4,0,3,1,2:T(2,128)(2,1)}, u32[]{:S(2)}, u32[]{:S(2)}) %all-to-all-start.1) | async-done | bytes 3932192 | tf_op jit(solution)/shard_map/all_to_all | solution.py:159
  264.9 5.2 %all-to-all-start = ((bf16[1,640,12,128]{3,2,0,1:T(8,128)(2,1)}), bf16[1,640,12,128]{3,2,0,1:T(8,128)(2,1)}, u32[]{:S(2)}, u32[]{:S(2)}) async-start(bf16[1,640,12,128]{3,2,0,1:T(8,128)(2,1)} %copy.63), calls=%async_computation | async-start | bytes 5242880 | tf_op jit(solution)/shard_map/all_to_all | solution.py:167
  270.0 8.5 %fusion.31 = (bf16[1,1,640,12,128]{4,0,3,1,2:T(2,128)(2,1)S(1)}, bf16[1,1,640,12,128]{4,0,3,1,2:T(2,128)(2,1)S(1)}) fusion(bf16[2,1,640,12,128]{4,0,3,1,2:T(2,128)(2,1)} %all-to-all-done.1), kind=kLoop, calls=%fused_computation.46 | loop fusion | bytes 7864320 | tf_op jit(solution)/shard_map/slice | solution.py:166
  279.5 3.1 fusion.19
  282.6 3.0 copy.72
  287.7 14.4 %all-to-all-done = bf16[1,640,12,128]{3,2,0,1:T(8,128)(2,1)} async-done(((bf16[1,640,12,128]{3,2,0,1:T(8,128)(2,1)}), bf16[1,640,12,128]{3,2,0,1:T(8,128)(2,1)}, u32[]{:S(2)}, u32[]{:S(2)}) %all-to-all-start) | async-done | bytes 1966112 | tf_op jit(solution)/shard_map/all_to_all | solution.py:167
  302.1 3.4 fusion.10
  306.2 28.5 %all_to_all.30 = bf16[8,80,12,128]{3,1,2,0:T(8,128)(2,1)S(1)} all-to-all(bf16[8,80,12,128]{3,1,2,0:T(8,128)(2,1)S(1)} %copy.76), channel_id=1, replica_groups=mesh['fsdp'=4,'piece'=4,'fy'=4,'core'=2] {'fy','core'}, dimensions={0} | all-to-all | bytes 3932160 | tf_op jit(solution)/shard_map/all_to_all | solution.py:173
  336.8 7.8 %fusion.14 = bf16[1,640,1536]{2,1,0:T(8,128)(2,1)} fusion(bf16[1536,1536]{1,0:T(8,128)(2,1)} %all-gather.11.cloned.1.call-done, bf16[80,8,12,128]{3,2,1,0:T(8,128)(2,1)} %bitcast.39), kind=kOutput, calls=%fused_computation.19 | convolution fusion | flops 3020881920 | bytes 8650752 | tf_op jit(solution)/shard_map/dot_general | solution.py:175
  (54 shorter events, 19.9 us)
Async XLA Ops:
  6.5 2.0 copy-start
  6.5 79.2 %all-gather.5.cloned.1.call-start = ((), (), s32[]{:S(2)}) async-start(), calls=%async_computation.3 | async-start | bytes 8847360 | tf_op jit(solution)/shard_map/all_gather | solution.py:132
  9.9 75.9 %copy-start.3 = (bf16[1,640,1536]{2,1,0:T(8,128)(2,1)S(1)}, bf16[1,640,1536]{2,1,0:T(8,128)(2,1)}, u32[]{:S(2)}) copy-start(bf16[1,640,1536]{2,1,0:T(8,128)(2,1)} %param.7) | copy-start | bytes 5898244
  9.9 81.6 %copy-start.5 = (bf16[384,1536]{1,0:T(8,128)(2,1)S(1)}, bf16[384,1536]{1,0:T(8,128)(2,1)}, u32[]{:S(2)}) copy-start(bf16[384,1536]{1,0:T(8,128)(2,1)} %param.11) | copy-start | bytes 3538948
  9.9 147.1 %all-gather.7.cloned.1.call-start = ((), (), s32[]{:S(2)}) async-start(), calls=%async_computation.4 | async-start | bytes 21233664 | tf_op jit(solution)/shard_map/all_gather | solution.py:133
  85.7 6.7 %copy-start.7 = (f32[1,1536]{1,0:T(1,128)S(1)}, f32[1,1536]{1,0:T(1,128)}, u32[]{:S(2)}) copy-start(f32[1,1536]{1,0:T(1,128)} %param.9) | copy-start | bytes 18436
  85.7 6.7 %copy-start.6 = (f32[1,1536]{1,0:T(1,128)S(1)}, f32[1,1536]{1,0:T(1,128)}, u32[]{:S(2)}) copy-start(f32[1,1536]{1,0:T(1,128)} %param.8) | copy-start | bytes 18436
  85.7 133.0 %all-gather.9.cloned.1.call-start = ((), (), s32[]{:S(2)}) async-start(), calls=%async_computation.5 | async-start | bytes 1769472 | tf_op jit(solution)/shard_map/all_gather | solution.py:136
  85.8 44.6 %collective-permute-start = (bf16[640,1536]{1,0:T(8,128)(2,1)S(1)}, bf16[640,1536]{1,0:T(8,128)(2,1)}, u32[]{:S(2)}, u32[]{:S(2)}) collective-permute-start(bf16[640,1536]{1,0:T(8,128)(2,1)S(1)} %bitcast.29), channel_id=1, source_target_pairs={{0,8},{8,16},{16,24},{1,9},{9,17},{17,25},{2,10},{10,18},{18,26},{... | collective-permute-start | bytes 5898248 | tf_op jit(solution)/shard_map/ppermute | solution.py:22
  90.2 45.4 %collective-permute-start.1 = (bf16[640,1536]{1,0:T(8,128)(2,1)S(1)}, bf16[640,1536]{1,0:T(8,128)(2,1)}, u32[]{:S(2)}, u32[]{:S(2)}) collective-permute-start(bf16[640,1536]{1,0:T(8,128)(2,1)S(1)} %bitcast.30), channel_id=1, source_target_pairs={{8,0},{16,8},{24,16},{9,1},{17,9},{25,17},{10,2},{18,10},{26,18},{... | collective-permute-start | bytes 5898248 | tf_op jit(solution)/shard_map/ppermute | solution.py:22
  179.6 11.7 %copy-start.2 = (bf16[1920,3072]{1,0:T(8,128)(2,1)}, bf16[1920,3072]{1,0:T(8,128)(2,1)S(1)}, u32[]{:S(2)}) copy-start(bf16[1920,3072]{1,0:T(8,128)(2,1)S(1)} %convolution_convert_fusion.k_ref.v_ref) | copy-start | bytes 35389444
  193.7 4.1 %copy-start.4 = (bf16[640,1536]{0,1:T(8,128)(2,1)S(1)}, bf16[640,1536]{0,1:T(8,128)(2,1)}, u32[]{:S(2)}) copy-start(bf16[640,1536]{0,1:T(8,128)(2,1)} %copy.66) | copy-start | bytes 5898244
  212.3 7.0 %copy-start.8 = (s32[1,5,6]{2,0,1:T(1,128)S(1)}, s32[1,5,6]{2,0,1:T(1,128)}, u32[]{:S(2)}) copy-start(s32[1,5,6]{2,0,1:T(1,128)} %param.12) | copy-start | bytes 364
  212.3 7.6 %copy-start.9 = (s32[1,8]{1,0:T(1,128)S(1)}, s32[1,8]{1,0:T(1,128)}, u32[]{:S(2)}) copy-start(s32[1,8]{1,0:T(1,128)} %param.13) | copy-start | bytes 100
  212.3 52.5 %all-to-all-start.1 = ((bf16[2,1,640,12,128]{4,0,3,1,2:T(2,128)(2,1)}), bf16[2,1,640,12,128]{4,0,3,1,2:T(2,128)(2,1)}, u32[]{:S(2)}, u32[]{:S(2)}) async-start(bf16[2,1,640,12,128]{4,0,3,1,2:T(2,128)(2,1)} %copy.67), calls=%async_computation.1 | async-start | bytes 7864320 | tf_op jit(solution)/shard_map/all_to_all | solution.py:159
  218.7 118.1 %all-gather.11.cloned.1.call-start = ((), (), s32[]{:S(2)}) async-start(), calls=%async_computation.6 | async-start | bytes 5898240 | tf_op jit(solution)/shard_map/all_gather | solution.py:137
  264.9 37.2 %all-to-all-start = ((bf16[1,640,12,128]{3,2,0,1:T(8,128)(2,1)}), bf16[1,640,12,128]{3,2,0,1:T(8,128)(2,1)}, u32[]{:S(2)}, u32[]{:S(2)}) async-start(bf16[1,640,12,128]{3,2,0,1:T(8,128)(2,1)} %copy.63), calls=%async_computation | async-start | bytes 5242880 | tf_op jit(solution)/shard_map/all_to_all | solution.py:167
  336.8 7.8 %copy-start.1 = (bf16[1536,1152]{1,0:T(8,128)(2,1)S(1)}, bf16[1536,1152]{1,0:T(8,128)(2,1)}, u32[]{:S(2)}) copy-start(bf16[1536,1152]{1,0:T(8,128)(2,1)} %param.10) | copy-start | bytes 10616836
Sparse Core Ops, SparseCore 0:
  10.0 75.6 all-gather.4
  87.4 30.2 all-gather.6
  119.3 13.2 all-gather.8
  220.9 51.7 all-gather.10

commit v2 on v1

--- a/solution.py
+++ b/solution.py
@@ -69,17 +69,17 @@
         o_ref[t * TILE : (t + 1) * TILE, :] = (summed / denominator).astype(o_ref.dtype)
 
 
-def spatial_rows(queries, kv_all, tile_list, first_tile, count_here):
-    rows, feat = queries.shape
-    buffer_rows = kv_all.shape[0]
+def spatial_rows(qkv_all, tile_list, first_tile, count_here):
+    buffer_rows = qkv_all.shape[0]
+    rows, feat = buffer_rows // 3, qkv_all.shape[1] // 3
     scalars = jnp.stack([first_tile, count_here]).astype(jnp.int32)
     grid_spec = pltpu.PrefetchScalarGridSpec(
         num_scalar_prefetch=2,
         grid=(HEADS,),
         in_specs=[
-            pl.BlockSpec((rows, HD), lambda h, lst, sc: (0, h)),
-            pl.BlockSpec((buffer_rows, HD), lambda h, lst, sc: (0, h)),
+            pl.BlockSpec((rows, HD), lambda h, lst, sc: (1, h)),
             pl.BlockSpec((buffer_rows, HD), lambda h, lst, sc: (0, HEADS + h)),
+            pl.BlockSpec((buffer_rows, HD), lambda h, lst, sc: (0, 2 * HEADS + h)),
         ],
         out_specs=pl.BlockSpec((rows, HD), lambda h, lst, sc: (0, h)),
     )
@@ -93,7 +93,80 @@
             transcendentals=rows * NBR * TILE * HEADS,
             bytes_accessed=2 * (rows * feat * 2 + buffer_rows * feat * 2),
         ),
-    )(tile_list.reshape(-1).astype(jnp.int32), scalars, queries, kv_all, kv_all)
+    )(tile_list.reshape(-1).astype(jnp.int32), scalars, qkv_all, qkv_all, qkv_all)
+
+
+MESH_IDS = pl.DeviceIdType.MESH
+
+
+def rim_kernel(tok_ref, rim_ref, send_sem, recv_sem):
+    n_piece = lax.axis_size("piece")
+    piece = lax.axis_index("piece")
+    here = (lax.axis_index("fsdp"), piece, lax.axis_index("fy"), lax.axis_index("core"))
+    up = (here[0], piece - 1, here[2], here[3])
+    down = (here[0], piece + 1, here[2], here[3])
+    has_up = piece > 0
+    has_down = piece < n_piece - 1
+    barrier = pltpu.get_barrier_semaphore()
+
+    @pl.when(has_up)
+    def _():
+        pl.semaphore_signal(barrier, inc=1, device_id=up, device_id_type=MESH_IDS)
+
+    @pl.when(has_down)
+    def _():
+        pl.semaphore_signal(barrier, inc=1, device_id=down, device_id_type=MESH_IDS)
+
+    peers = (piece + n_piece - 1) // n_piece + (2 * n_piece - 2 - piece) // n_piece
+    pl.semaphore_wait(barrier, peers)
+
+    to_down = pltpu.make_async_remote_copy(
+        src_ref=tok_ref,
+        dst_ref=rim_ref.at[0],
+        send_sem=send_sem.at[0],
+        recv_sem=recv_sem.at[0],
+        device_id=down,
+        device_id_type=MESH_IDS,
+    )
+    to_up = pltpu.make_async_remote_copy(
+        src_ref=tok_ref,
+        dst_ref=rim_ref.at[1],
+        send_sem=send_sem.at[1],
+        recv_sem=recv_sem.at[1],
+        device_id=up,
+        device_id_type=MESH_IDS,
+    )
+
+    @pl.when(has_down)
+    def _():
+        to_down.start()
+
+    @pl.when(has_up)
+    def _():
+        to_up.start()
+
+    @pl.when(has_down)
+    def _():
+        to_down.wait_send()
+        to_up.wait_recv()
+
+    @pl.when(has_up)
+    def _():
+        to_up.wait_send()
+        to_down.wait_recv()
+
+
+def exchange_rims(own):
+    rows, feat = own.shape
+    return pl.pallas_call(
+        rim_kernel,
+        out_shape=jax.ShapeDtypeStruct((2, rows, feat), own.dtype),
+        in_specs=[pl.BlockSpec(memory_space=pl.ANY)],
+        out_specs=pl.BlockSpec(memory_space=pl.ANY),
+        scratch_shapes=[pltpu.SemaphoreType.DMA((2,)), pltpu.SemaphoreType.DMA((2,))],
+        compiler_params=pltpu.CompilerParams(collective_id=0, has_side_effects=True),
+        cost_estimate=pl.CostEstimate(flops=0, transcendentals=0, bytes_accessed=80 * rows * feat * 2),
+    )(own)
 
 
 def temporal_block(query_part, key_part, spatial_part, clip_counts, first_pos):
@@ -124,13 +197,15 @@
     feat_count = tokens.shape[2]
     n_frames = lax.axis_size("fy") * lax.axis_size("core")
     own = tokens[0]
-    above = passed_along(own, "piece", 1)
-    below = passed_along(own, "piece", -1)
+    rims = exchange_rims(own)
+    piece_index = lax.axis_index("piece")
+    above = jnp.where(piece_index > 0, rims[0], jnp.zeros_like(own))
+    below = jnp.where(piece_index < lax.axis_size("piece") - 1, rims[1], jnp.zeros_like(own))
     core = lax.axis_index("core")
     half_rows = w_qkv.shape[0] // 2
     w_half = lax.dynamic_slice_in_dim(w_qkv, core * half_rows, half_rows, axis=0)
-    w_half = lax.all_gather(w_half, "fsdp", axis=1, tiled=True)
-    w_full = lax.all_gather(w_half, "core", axis=0, tiled=True)
+    w_pieces = lax.all_gather(w_half, ("fsdp", "core"), axis=0, tiled=False)
+    w_full = w_pieces.reshape(lax.axis_size("fsdp"), w_qkv.shape[0], w_qkv.shape[1])
     out_rows = w_out.shape[0] // 2
     w_out_half = lax.dynamic_slice_in_dim(w_out, core * out_rows, out_rows, axis=0)
     w_out_half = lax.all_gather(w_out_half, "core", axis=0, tiled=True)
@@ -138,22 +213,18 @@
     normed_all = layer_norm(
         jnp.concatenate([above, own, below], axis=0), mod_scale[0], mod_shift[0]
     )
-    queries = jnp.dot(
-        normed_all[tok_count : 2 * tok_count],
-        w_full[:, :feat_count],
-        preferred_element_type=jnp.float32,
-    ).astype(jnp.bfloat16)
-    kv_all = jnp.dot(
-        normed_all, w_full[:, feat_count:], preferred_element_type=jnp.float32
-    ).astype(jnp.bfloat16)
-    key_proj = kv_all[tok_count : 2 * tok_count, :feat_count]
+    qkv_all = jnp.einsum(
+        "tk,jkc->tjc", normed_all, w_full, preferred_element_type=jnp.float32
+    ).astype(jnp.bfloat16).reshape(normed_all.shape[0], 3 * feat_count)
+    queries = qkv_all[tok_count : 2 * tok_count, :feat_count]
+    key_proj = qkv_all[tok_count : 2 * tok_count, feat_count : 2 * feat_count]
     frame_index = lax.axis_index("fy") * lax.axis_size("core") + lax.axis_index("core")
     piece_index = lax.axis_index("piece")
     clip_counts = counts[0]
     count_here = lax.dynamic_index_in_dim(clip_counts, frame_index, 0, keepdims=False)
     rows_here = tok_count // (TGW * TILE)
     first_tile = (piece_index * rows_here - 1) * TGW
-    spatial = spatial_rows(queries, kv_all, neighbors[0], first_tile, count_here)
+    spatial = spatial_rows(qkv_all, neighbors[0], first_tile, count_here)
     head_shape = (1, tok_count, HEADS, HD)
     frame_axes = ("fy", "core")
     qk_part = lax.all_to_all(

time: 352 us -> 316 us (0.90)
  waiting for transfers between devices: 140 us -> 41.6 us
  Pallas kernels: 28.6 us -> 74.6 us
  local copies, waits for them, and re-layouts: 48.1 us -> 78.6 us
  other arithmetic: 26.9 us -> 14.6 us
  starting transfers between devices: 17.3 us -> 9.99 us
  matrix products: 48.4 us -> 53.4 us
    all_gather x2 -> x1, waiting for transfers between devices: 75.7 us -> 20.5 us  [local(): w_pieces = lax.all_gather(w_half, ('fsdp', 'core'), axis=0, tiled=False)]
    pallas_call x0 -> x1, Pallas kernels: none -> 46 us  [exchange_rims(): pl.pallas_call(rim_kernel, out_shape=jax.ShapeDtypeStruct((2, rows, feat)...]
    ppermute x2 -> x0, waiting for transfers between devices: 43.1 us -> none  [passed_along(): return lax.ppermute(block, axis, route)]
    reshape x0 -> x1, local copies, waits for them, and re-layouts: none -> 24.5 us  [local(): qkv_all = jnp.einsum('tk,jkc->tjc', normed_all, w_full, preferred_element...]
    convert_element_type x1 -> x0, other arithmetic: 13.9 us -> none  [layer_norm(): return (normal * (1.0 + mod_scale) + mod_shift).astype(jnp.bfloat16)]
    slice x2 -> x3, local copies, waits for them, and re-layouts: 2.4 us -> 11.3 us  [the longest x2 7.11 us: local(): queries = qkv_all[tok_count:2 * tok_count, :feat_count]]
    ppermute x2 -> x0, starting transfers between devices: 5.69 us -> none  [passed_along(): return lax.ppermute(block, axis, route)]
    dot_general x2 -> x1, matrix products: 34.2 us -> 39.3 us  [local(): jnp.einsum('tk,jkc->tjc', normed_all, w_full, preferred_element_type=jnp....]
  transfers between devices with their start and end apart: 8 -> 5, of which waited for: 5 -> 3; matrix products, arithmetic and copies ran while one was open for 32% -> 43% of each run, Pallas kernels for 8% -> 24%
where the time goes in v2:
time: 316 us; the launch traced here: 315 us
  local copies, waits for them, and re-layouts  78.6 us (25%)
  Pallas kernels  74.6 us (24%)
  matrix products  53.4 us (17%)
  waiting for transfers between devices  41.6 us (13%)
  blocking collectives  28.5 us (9%)
  other arithmetic  14.6 us (5%)
  between operations  13.3 us (4%)
  starting transfers between devices  9.99 us (3%)
    pallas_call x1, Pallas kernels, exchange_rims(): pl.pallas_call(rim_kernel, out_shape=jax.ShapeDtypeStruct((2, rows, feat)...  46 us
    dot_general x1, matrix products, local(): jnp.einsum('tk,jkc->tjc', normed_all, w_full, preferred_element_type=jnp....  39.3 us
    pallas_call x1, Pallas kernels, spatial_rows(): pl.pallas_call(spatial_kernel, grid_spec=grid_spec, out_shape=jax.ShapeDt...  28.7 us
    all_to_all x1, blocking collectives, local(): lax.all_to_all(temporal, frame_axes, split_axis=0, concat_axis=1, tiled=T...  28.5 us
    reshape x1, local copies, waits for them, and re-layouts, local(): qkv_all = jnp.einsum('tk,jkc->tjc', normed_all, w_full, preferred_element...  24.5 us
    all_gather x1, waiting for transfers between devices, local(): w_pieces = lax.all_gather(w_half, ('fsdp', 'core'), axis=0, tiled=False)  20.5 us
    all_to_all x1, waiting for transfers between devices, local(): lax.all_to_all(spatial.reshape(head_shape), frame_axes, split_axis=1, con...  14.3 us
    another operation x1, local copies, waits for them, and re-layouts, local(): jnp.stack([queries, key_proj]).reshape((2,) + head_shape)  10.7 us
  transfers between devices with their start and end apart: 5, of which 3 were waited for; matrix products, arithmetic and copies ran while one was open for 43% of the time, Pallas kernels for 24%

profile of v2, /device:TPU:1, one launch (start us, length us, event | category | flops | bytes accessed | tf_op | source)
XLA Modules:
  0.0 314.7 jit_solution(11096572208756741542)
XLA Ops:
  11.9 46.0 %shard_map.73 = bf16[2,640,1536]{2,1,0:T(8,128)(2,1)} custom-call(bf16[640,1536]{1,0:T(8,128)(2,1)} %bitcast.39), custom_call_target="tpu_custom_call" | custom-call | bytes 157286400 | tf_op jit(solution)/shard_map/pallas_call | solution.py:161
  57.9 2.6 select_bitcast_fusion.1
  61.8 5.4 %fusion.3 = f32[1920]{0:T(1024)S(1)} fusion(f32[1920]{0:T(1024)S(1)} %broadcast_multiply_fusion, bf16[640,1536]{1,0:T(8,128)(2,1)S(1)} %get-tuple-element.10, bf16[640,1536]{1,0:T(8,128)(2,1)S(1)} %bitcast.41, bf16[640,1536]{1,0:T(8,128)(2,1)S(1)} %get-tuple-element.9), kind=kLoop, calls=%fused_computation.6 | loop fusion | flops 26540160 | bytes 5913600 | tf_op jit(solution)/shard_map/reduce_sum | solution.py:28
  67.3 20.5 %all-gather.9.cloned.1.call-done = bf16[6144,1152]{1,0:T(8,128)(2,1)} async-done(((bf16[768,1152]{1,0:T(8,128)(2,1)}), bf16[6144,1152]{1,0:T(8,128)(2,1)}) %all-gather.9.cloned.1.call-update) | async-done | bytes 14155792 | tf_op jit(solution)/shard_map/all_gather | solution.py:207
  87.9 39.3 %convolution_convert_fusion = bf16[1920,4,1152]{0,2,1:T(8,128)(2,1)} fusion(bf16[4,1536,1152]{2,1,0:T(8,128)(2,1)} %bitcast.51, f32[1536]{0:T(1024)S(1)} %reduce.2, f32[1536]{0:T(1024)S(1)} %add_reduce_fusion, f32[1920]{0:T(1024)S(1)} %add_sqrt_fusion, f32[1920]{0:T(1024)S(1)} %broadcast_multiply_fusion, bf16[640,1536]{1,0:T(8,128)(2,1)} %copy-done.4, ...), kind=kOutput, calls=%fused_computation.1 | convolution fusion | flops 27220377600 | bytes 37776384 | tf_op jit(solution)/shard_map/tk,jkc->tjc/dot_general | solution.py:216
  127.2 24.5 %copy.90.q_ref.k_ref.v_ref = bf16[1920,4608]{1,0:T(8,128)(2,1)} copy(bf16[1920,4608]{0,1:T(8,128)(2,1)} %bitcast.38) | data formatting | bytes 35389440 | tf_op jit(solution)/shard_map/reshape | solution.py:218
  151.6 4.3 %fusion.30 = (bf16[640,1536]{1,0:T(8,128)(2,1)}, bf16[640,1536]{1,0:T(8,128)(2,1)}) fusion(bf16[1920,4608]{1,0:T(8,128)(2,1)} %copy.90.q_ref.k_ref.v_ref), kind=kLoop, calls=%fused_computation.48 | loop fusion | bytes 7864320 | tf_op jit(solution)/shard_map/slice | solution.py:219
  156.0 2.8 copy.76
  158.8 4.2 %copy.77 = bf16[640,1536]{0,1:T(8,128)(2,1)} copy(bf16[640,1536]{1,0:T(8,128)(2,1)} %get-tuple-element.6) | data formatting | bytes 3932160 | tf_op jit(solution)/shard_map/slice | solution.py:220
  162.9 3.8 %pad_maximum_fusion.1 = bf16[2,1,640,12,128]{2,4,3,1,0:T(8,128)(2,1)} fusion(bf16[1,1,640,12,128]{2,4,3,1,0:T(8,128)(2,1)} %bitcast.46, bf16[1,1,640,12,128]{2,4,3,1,0:T(8,128)(2,1)S(1)} %bitcast.44), kind=kLoop, calls=%fused_computation.16 | loop fusion | flops 1966080 | bytes 7864320 | tf_op jit(solution)/shard_map/stack | solution.py:231
  166.8 10.7 %copy.78 = bf16[2,1,640,12,128]{4,0,3,1,2:T(2,128)(2,1)} copy(bf16[2,1,640,12,128]{2,4,3,1,0:T(8,128)(2,1)} %pad_maximum_fusion.1) | data formatting | bytes 7864320 | tf_op jit(solution)/shard_map/stack | solution.py:231
  177.5 4.8 %all-to-all-start.1 = ((bf16[2,1,640,12,128]{4,0,3,1,2:T(2,128)(2,1)}), bf16[2,1,640,12,128]{4,0,3,1,2:T(2,128)(2,1)}, u32[]{:S(2)}, u32[]{:S(2)}) async-start(bf16[2,1,640,12,128]{4,0,3,1,2:T(2,128)(2,1)} %copy.78), calls=%async_computation.1 | async-start | bytes 7864320 | tf_op jit(solution)/shard_map/all_to_all | solution.py:230
  185.5 28.7 %shard_map.74 = bf16[640,1536]{1,0:T(8,128)(2,1)} custom-call(s32[30]{0:T(128)} %reshape_squeeze.3.list_ref, s32[2]{0:T(128)} %pad_add_fusion.scalar_ref, bf16[1920,4608]{1,0:T(8,128)(2,1)} %copy.90.q_ref.k_ref.v_ref, bf16[1920,4608]{1,0:T(8,128)(2,1)} %copy.90.q_ref.k_ref.v_ref, bf16[1920,4608]{1,0:T(8,128)(2,1)} %copy.90.q_ref.k_ref.v_ref), custom_call_target="tpu_custom_call" | custom-call | flops 3019898880 | bytes 15728640 | tf_op jit(solution)/shard_map/pallas_call | solution.py:87
  214.2 2.8 copy.73
  217.0 5.4 %copy.74 = bf16[1,640,12,128]{3,2,0,1:T(8,128)(2,1)} copy(bf16[1,640,12,128]{1,3,2,0:T(8,128)(2,1)S(1)} %bitcast.43) | data formatting | bytes 3932160 | tf_op jit(solution)/shard_map/reshape | solution.py:239
  222.4 6.0 %all-to-all-done.1 = bf16[2,1,640,12,128]{4,0,3,1,2:T(2,128)(2,1)} async-done(((bf16[2,1,640,12,128]{4,0,3,1,2:T(2,128)(2,1)}), bf16[2,1,640,12,128]{4,0,3,1,2:T(2,128)(2,1)}, u32[]{:S(2)}, u32[]{:S(2)}) %all-to-all-start.1) | async-done | bytes 3932192 | tf_op jit(solution)/shard_map/all_to_all | solution.py:230
  228.4 5.2 %all-to-all-start = ((bf16[1,640,12,128]{3,2,0,1:T(8,128)(2,1)}), bf16[1,640,12,128]{3,2,0,1:T(8,128)(2,1)}, u32[]{:S(2)}, u32[]{:S(2)}) async-start(bf16[1,640,12,128]{3,2,0,1:T(8,128)(2,1)} %copy.74), calls=%async_computation | async-start | bytes 5242880 | tf_op jit(solution)/shard_map/all_to_all | solution.py:238
  233.6 8.6 %fusion.31 = (bf16[1,1,640,12,128]{4,0,3,1,2:T(2,128)(2,1)S(1)}, bf16[1,1,640,12,128]{4,0,3,1,2:T(2,128)(2,1)S(1)}) fusion(bf16[2,1,640,12,128]{4,0,3,1,2:T(2,128)(2,1)} %all-to-all-done.1), kind=kLoop, calls=%fused_computation.49 | loop fusion | bytes 7864320 | tf_op jit(solution)/shard_map/slice | solution.py:237
  243.1 3.0 fusion.18
  246.2 3.0 copy.83
  251.3 14.3 %all-to-all-done = bf16[1,640,12,128]{3,2,0,1:T(8,128)(2,1)} async-done(((bf16[1,640,12,128]{3,2,0,1:T(8,128)(2,1)}), bf16[1,640,12,128]{3,2,0,1:T(8,128)(2,1)}, u32[]{:S(2)}, u32[]{:S(2)}) %all-to-all-start) | async-done | bytes 1966112 | tf_op jit(solution)/shard_map/all_to_all | solution.py:238
  265.6 3.4 %fusion.13 = bf16[8,80,12,128]{3,0,2,1:T(8,128)(2,1)S(1)} fusion(bf16[80,12,8,8]{3,2,1,0:T(8,128)(2,1)S(1)} %copy.85, bf16[8,80,12,128]{3,2,1,0:T(8,128)(2,1)} %bitcast.9, f32[8,80,12]{0,2,1:T(8,128)S(1)} %copy.86), kind=kOutput, calls=%fused_computation.18 | convolution fusion | flops 17694720 | bytes 4085760 | tf_op jit(solution)/shard_map/phfg,gphd->fphd/dot_general | solution.py:188
  269.8 28.5 %all_to_all.30 = bf16[8,80,12,128]{3,1,2,0:T(8,128)(2,1)S(1)} all-to-all(bf16[8,80,12,128]{3,1,2,0:T(8,128)(2,1)S(1)} %copy.87), channel_id=1, replica_groups=mesh['fsdp'=4,'piece'=4,'fy'=4,'core'=2] {'fy','core'}, dimensions={0} | all-to-all | bytes 3932160 | tf_op jit(solution)/shard_map/all_to_all | solution.py:244
  300.4 7.8 %fusion.14 = bf16[1,640,1536]{2,1,0:T(8,128)(2,1)} fusion(bf16[1536,1536]{1,0:T(8,128)(2,1)} %all-gather.7.cloned.1.call-done, bf16[80,8,12,128]{3,2,1,0:T(8,128)(2,1)} %bitcast.48), kind=kOutput, calls=%fused_computation.20 | convolution fusion | flops 3020881920 | bytes 8650752 | tf_op jit(solution)/shard_map/dot_general | solution.py:246
  (46 shorter events, 15.8 us)
Async XLA Ops:
  6.5 2.0 copy-start
  6.5 81.3 %all-gather.9.cloned.1.call-start = ((), (), s32[]{:S(2)}) async-start(), calls=%async_computation.5 | async-start | bytes 15925248 | tf_op jit(solution)/shard_map/all_gather | solution.py:207
  9.9 172.4 %all-gather.5.cloned.1.call-start = ((), (), s32[]{:S(2)}) async-start(), calls=%async_computation.3 | async-start | bytes 1769472 | tf_op jit(solution)/shard_map/all_gather | solution.py:211
  57.9 2.8 copy-start.2
  60.5 6.7 %copy-start.3 = (bf16[640,1536]{1,0:T(8,128)(2,1)}, bf16[640,1536]{1,0:T(8,128)(2,1)S(1)}, u32[]{:S(2)}) copy-start(bf16[640,1536]{1,0:T(8,128)(2,1)S(1)} %get-tuple-element.9) | copy-start | bytes 5898244
  60.5 6.7 %copy-start.4 = (bf16[640,1536]{1,0:T(8,128)(2,1)}, bf16[640,1536]{1,0:T(8,128)(2,1)S(1)}, u32[]{:S(2)}) copy-start(bf16[640,1536]{1,0:T(8,128)(2,1)S(1)} %get-tuple-element.10) | copy-start | bytes 5898244
  61.8 5.5 %copy-start.5 = (f32[1,1536]{1,0:T(1,128)S(1)}, f32[1,1536]{1,0:T(1,128)}, u32[]{:S(2)}) copy-start(f32[1,1536]{1,0:T(1,128)} %param.8) | copy-start | bytes 18436
  61.8 5.5 %copy-start.6 = (f32[1,1536]{1,0:T(1,128)S(1)}, f32[1,1536]{1,0:T(1,128)}, u32[]{:S(2)}) copy-start(f32[1,1536]{1,0:T(1,128)} %param.9) | copy-start | bytes 18436
  177.5 5.5 %copy-start.7 = (s32[1,5,6]{2,0,1:T(1,128)S(1)}, s32[1,5,6]{2,0,1:T(1,128)}, u32[]{:S(2)}) copy-start(s32[1,5,6]{2,0,1:T(1,128)} %param.12) | copy-start | bytes 364
  177.5 6.1 %copy-start.8 = (s32[1,8]{1,0:T(1,128)S(1)}, s32[1,8]{1,0:T(1,128)}, u32[]{:S(2)}) copy-start(s32[1,8]{1,0:T(1,128)} %param.13) | copy-start | bytes 100
  177.5 50.9 %all-to-all-start.1 = ((bf16[2,1,640,12,128]{4,0,3,1,2:T(2,128)(2,1)}), bf16[2,1,640,12,128]{4,0,3,1,2:T(2,128)(2,1)}, u32[]{:S(2)}, u32[]{:S(2)}) async-start(bf16[2,1,640,12,128]{4,0,3,1,2:T(2,128)(2,1)} %copy.78), calls=%async_computation.1 | async-start | bytes 7864320 | tf_op jit(solution)/shard_map/all_to_all | solution.py:230
  182.3 118.1 %all-gather.7.cloned.1.call-start = ((), (), s32[]{:S(2)}) async-start(), calls=%async_computation.4 | async-start | bytes 5898240 | tf_op jit(solution)/shard_map/all_gather | solution.py:212
  228.4 37.2 %all-to-all-start = ((bf16[1,640,12,128]{3,2,0,1:T(8,128)(2,1)}), bf16[1,640,12,128]{3,2,0,1:T(8,128)(2,1)}, u32[]{:S(2)}, u32[]{:S(2)}) async-start(bf16[1,640,12,128]{3,2,0,1:T(8,128)(2,1)} %copy.74), calls=%async_computation | async-start | bytes 5242880 | tf_op jit(solution)/shard_map/all_to_all | solution.py:238
  300.4 7.8 %copy-start.1 = (bf16[1536,1152]{1,0:T(8,128)(2,1)S(1)}, bf16[1536,1152]{1,0:T(8,128)(2,1)}, u32[]{:S(2)}) copy-start(bf16[1536,1152]{1,0:T(8,128)(2,1)} %param.10) | copy-start | bytes 10616836
Sparse Core Ops, SparseCore 0:
  10.0 77.7 all-gather.8
  89.5 12.2 all-gather.4
  184.8 53.0 all-gather.6

commit v3 on v2

--- a/solution.py
+++ b/solution.py
@@ -70,16 +70,25 @@
 
 
 def spatial_rows(qkv_all, tile_list, first_tile, count_here):
-    buffer_rows = qkv_all.shape[0]
-    rows, feat = buffer_rows // 3, qkv_all.shape[1] // 3
+    buffer_rows = qkv_all.shape[1]
+    rows, feat = buffer_rows // 3, qkv_all.shape[0] * qkv_all.shape[2] // 3
+    per_shard = qkv_all.shape[2] // HD
     scalars = jnp.stack([first_tile, count_here]).astype(jnp.int32)
     grid_spec = pltpu.PrefetchScalarGridSpec(
         num_scalar_prefetch=2,
         grid=(HEADS,),
         in_specs=[
-            pl.BlockSpec((rows, HD), lambda h, lst, sc: (1, h)),
-            pl.BlockSpec((buffer_rows, HD), lambda h, lst, sc: (0, HEADS + h)),
-            pl.BlockSpec((buffer_rows, HD), lambda h, lst, sc: (0, 2 * HEADS + h)),
+            pl.BlockSpec(
+                (None, rows, HD), lambda h, lst, sc: (h // per_shard, 1, h % per_shard)
+            ),
+            pl.BlockSpec(
+                (None, buffer_rows, HD),
+                lambda h, lst, sc: ((HEADS + h) // per_shard, 0, (HEADS + h) % per_shard),
+            ),
+            pl.BlockSpec(
+                (None, buffer_rows, HD),
+                lambda h, lst, sc: ((2 * HEADS + h) // per_shard, 0, (2 * HEADS + h) % per_shard),
+            ),
         ],
         out_specs=pl.BlockSpec((rows, HD), lambda h, lst, sc: (0, h)),
     )
@@ -214,10 +223,15 @@
         jnp.concatenate([above, own, below], axis=0), mod_scale[0], mod_shift[0]
     )
     qkv_all = jnp.einsum(
-        "tk,jkc->tjc", normed_all, w_full, preferred_element_type=jnp.float32
-    ).astype(jnp.bfloat16).reshape(normed_all.shape[0], 3 * feat_count)
-    queries = qkv_all[tok_count : 2 * tok_count, :feat_count]
-    key_proj = qkv_all[tok_count : 2 * tok_count, feat_count : 2 * feat_count]
+        "tk,jkc->jtc", normed_all, w_full, preferred_element_type=jnp.float32
+    ).astype(jnp.bfloat16)
+    qk_own = (
+        qkv_all[:, tok_count : 2 * tok_count]
+        .transpose(1, 0, 2)
+        .reshape(tok_count, 3 * feat_count)[:, : 2 * feat_count]
+    )
+    queries = qk_own[:, :feat_count]
+    key_proj = qk_own[:, feat_count:]
     frame_index = lax.axis_index("fy") * lax.axis_size("core") + lax.axis_index("core")
     piece_index = lax.axis_index("piece")
     clip_counts = counts[0]

time: 316 us -> 297 us (0.940)
  local copies, waits for them, and re-layouts: 78.6 us -> 59.9 us
    reshape x1 -> x0, local copies, waits for them, and re-layouts: 24.5 us -> none  [local(): qkv_all = jnp.einsum('tk,jkc->tjc', normed_all, w_full, preferred_element...]
    transpose x0 -> x2, local copies, waits for them, and re-layouts: none -> 14.5 us  [local(): qk_own = qkv_all[:, tok_count:2 * tok_count].transpose(1, 0, 2).reshape(t...]
    slice x3 -> x1, local copies, waits for them, and re-layouts: 11.3 us -> 2.47 us  [local(): queries = qk_own[:, :feat_count]]
  transfers between devices with their start and end apart: 5 -> 5, of which waited for: 3 -> 3; matrix products, arithmetic and copies ran while one was open for 43% -> 39% of each run, Pallas kernels for 24% -> 25%
where the time goes in v3:
time: 297 us; the launch traced here: 296 us
  Pallas kernels  75.3 us (25%)
  local copies, waits for them, and re-layouts  59.9 us (20%)
  matrix products  54.8 us (18%)
  waiting for transfers between devices  40.8 us (14%)
  blocking collectives  28.5 us (10%)
  between operations  13.3 us (4%)
  other arithmetic  13.1 us (4%)
  starting transfers between devices  10.1 us (3%)
    pallas_call x1, Pallas kernels, exchange_rims(): pl.pallas_call(rim_kernel, out_shape=jax.ShapeDtypeStruct((2, rows, feat)...  46 us
    dot_general x1, matrix products, local(): jnp.einsum('tk,jkc->jtc', normed_all, w_full, preferred_element_type=jnp....  40.7 us
    pallas_call x1, Pallas kernels, spatial_rows(): pl.pallas_call(spatial_kernel, grid_spec=grid_spec, out_shape=jax.ShapeDt...  29.3 us
    all_to_all x1, blocking collectives, local(): lax.all_to_all(temporal, frame_axes, split_axis=0, concat_axis=1, tiled=T...  28.5 us
    all_gather x1, waiting for transfers between devices, local(): w_pieces = lax.all_gather(w_half, ('fsdp', 'core'), axis=0, tiled=False)  20.5 us
    transpose x2, local copies, waits for them, and re-layouts, local(): qk_own = qkv_all[:, tok_count:2 * tok_count].transpose(1, 0, 2).reshape(t...  14.5 us
    all_to_all x1, waiting for transfers between devices, local(): lax.all_to_all(spatial.reshape(head_shape), frame_axes, split_axis=1, con...  14.3 us
    another operation x1, local copies, waits for them, and re-layouts, local(): jnp.stack([queries, key_proj]).reshape((2,) + head_shape)  10.7 us
  transfers between devices with their start and end apart: 5, of which 3 were waited for; matrix products, arithmetic and copies ran while one was open for 39% of the time, Pallas kernels for 25%

profile of v3, /device:TPU:1, one launch (start us, length us, event | category | flops | bytes accessed | tf_op | source)
XLA Modules:
  0.0 295.8 jit_solution(14443932607329373275)
XLA Ops:
  12.0 46.0 %shard_map.73 = bf16[2,640,1536]{2,1,0:T(8,128)(2,1)} custom-call(bf16[640,1536]{1,0:T(8,128)(2,1)} %bitcast.42), custom_call_target="tpu_custom_call" | custom-call | bytes 157286400 | tf_op jit(solution)/shard_map/pallas_call | solution.py:170
  57.9 2.6 select_bitcast_fusion.1
  61.9 5.4 %fusion.4 = f32[1920]{0:T(1024)S(1)} fusion(f32[1920]{0:T(1024)S(1)} %broadcast_multiply_fusion, bf16[640,1536]{1,0:T(8,128)(2,1)S(1)} %get-tuple-element.10, bf16[640,1536]{1,0:T(8,128)(2,1)S(1)} %bitcast.44, bf16[640,1536]{1,0:T(8,128)(2,1)S(1)} %get-tuple-element.9), kind=kLoop, calls=%fused_computation.7 | loop fusion | flops 26540160 | bytes 5913600 | tf_op jit(solution)/shard_map/reduce_sum | solution.py:28
  67.4 20.5 %all-gather.9.cloned.1.call-done = bf16[6144,1152]{1,0:T(8,128)(2,1)} async-done(((bf16[768,1152]{1,0:T(8,128)(2,1)}), bf16[6144,1152]{1,0:T(8,128)(2,1)}) %all-gather.9.cloned.1.call-update) | async-done | bytes 14155792 | tf_op jit(solution)/shard_map/all_gather | solution.py:216
  87.9 40.7 %fusion.1.q_ref.k_ref.v_ref = bf16[4,1920,1152]{2,1,0:T(8,128)(2,1)} fusion(bf16[4,1536,1152]{2,1,0:T(8,128)(2,1)} %bitcast.55, f32[1536]{0:T(1024)S(1)} %reduce.2, f32[1536]{0:T(1024)S(1)} %add_reduce_fusion, f32[1920]{0:T(1024)S(1)} %add_sqrt_fusion, f32[1920]{0:T(1024)S(1)} %broadcast_multiply_fusion, bf16[640,1536]{1,0:T(8,128)(2,1)} %copy-done.4, ...), kind=kOutput, calls=%fused_computation.2 | convolution fusion | flops 27220377600 | bytes 37776384 | tf_op jit(solution)/shard_map/tk,jkc->jtc/dot_general | solution.py:225
  128.6 5.6 %slice_bitcast_fusion = bf16[640,4,1152]{2,0,1:T(8,128)(2,1)} fusion(bf16[4,1920,1152]{2,1,0:T(8,128)(2,1)} %fusion.1.q_ref.k_ref.v_ref), kind=kLoop, calls=%fused_computation.12 | loop fusion | bytes 11796480 | tf_op jit(solution)/shard_map/transpose | solution.py:230
  134.2 8.9 %copy.72 = bf16[640,4,1152]{0,2,1:T(8,128)(2,1)} copy(bf16[640,4,1152]{2,0,1:T(8,128)(2,1)} %slice_bitcast_fusion) | data formatting | bytes 11796480 | tf_op jit(solution)/shard_map/transpose | solution.py:230
  143.1 2.5 fusion.31
  145.6 2.3 pad_maximum_fusion.1
  147.9 10.7 %copy.73 = bf16[2,1,640,12,128]{4,0,3,1,2:T(2,128)(2,1)} copy(bf16[2,1,640,12,128]{2,4,3,1,0:T(8,128)(2,1)} %pad_maximum_fusion.1) | data formatting | bytes 7864320 | tf_op jit(solution)/shard_map/stack | solution.py:245
  158.6 4.8 %all-to-all-start.1 = ((bf16[2,1,640,12,128]{4,0,3,1,2:T(2,128)(2,1)}), bf16[2,1,640,12,128]{4,0,3,1,2:T(2,128)(2,1)}, u32[]{:S(2)}, u32[]{:S(2)}) async-start(bf16[2,1,640,12,128]{4,0,3,1,2:T(2,128)(2,1)} %copy.73), calls=%async_computation.1 | async-start | bytes 7864320 | tf_op jit(solution)/shard_map/all_to_all | solution.py:244
  166.6 29.3 %shard_map.74 = bf16[640,1536]{1,0:T(8,128)(2,1)} custom-call(s32[30]{0:T(128)} %reshape_squeeze.3.list_ref, s32[2]{0:T(128)} %pad_add_fusion.scalar_ref, bf16[4,1920,1152]{2,1,0:T(8,128)(2,1)} %fusion.1.q_ref.k_ref.v_ref, bf16[4,1920,1152]{2,1,0:T(8,128)(2,1)} %fusion.1.q_ref.k_ref.v_ref, bf16[4,1920,1152]{2,1,0:T(8,128)(2,1)} %fusion.1.q_ref.k_ref.v_ref), custom_call_target="tpu_custom_call" | custom-call | flops 3019898880 | bytes 15728640 | tf_op jit(solution)/shard_map/pallas_call | solution.py:96
  196.0 2.8 copy.69
  198.8 5.4 %copy.70 = bf16[1,640,12,128]{3,2,0,1:T(8,128)(2,1)} copy(bf16[1,640,12,128]{1,3,2,0:T(8,128)(2,1)S(1)} %bitcast.47) | data formatting | bytes 3932160 | tf_op jit(solution)/shard_map/reshape | solution.py:253
  204.2 5.3 %all-to-all-done.1 = bf16[2,1,640,12,128]{4,0,3,1,2:T(2,128)(2,1)} async-done(((bf16[2,1,640,12,128]{4,0,3,1,2:T(2,128)(2,1)}), bf16[2,1,640,12,128]{4,0,3,1,2:T(2,128)(2,1)}, u32[]{:S(2)}, u32[]{:S(2)}) %all-to-all-start.1) | async-done | bytes 3932192 | tf_op jit(solution)/shard_map/all_to_all | solution.py:244
  209.5 5.2 %all-to-all-start = ((bf16[1,640,12,128]{3,2,0,1:T(8,128)(2,1)}), bf16[1,640,12,128]{3,2,0,1:T(8,128)(2,1)}, u32[]{:S(2)}, u32[]{:S(2)}) async-start(bf16[1,640,12,128]{3,2,0,1:T(8,128)(2,1)} %copy.70), calls=%async_computation | async-start | bytes 5242880 | tf_op jit(solution)/shard_map/all_to_all | solution.py:252
  214.7 8.6 %fusion.32 = (bf16[1,1,640,12,128]{4,0,3,1,2:T(2,128)(2,1)S(1)}, bf16[1,1,640,12,128]{4,0,3,1,2:T(2,128)(2,1)S(1)}) fusion(bf16[2,1,640,12,128]{4,0,3,1,2:T(2,128)(2,1)} %all-to-all-done.1), kind=kLoop, calls=%fused_computation.51 | loop fusion | bytes 7864320 | tf_op jit(solution)/shard_map/slice | solution.py:251
  224.3 3.0 %fusion.19 = f32[80,12,8,8]{2,3,1,0:T(8,128)} fusion(bf16[8,80,12,128]{3,1,0,2:T(8,128)(2,1)S(1)} %bitcast.49, bf16[8,80,12,128]{3,1,0,2:T(8,128)(2,1)S(1)} %bitcast.48), kind=kOutput, calls=%fused_computation.26 | convolution fusion | flops 15728640 | bytes 4177920 | tf_op jit(solution)/shard_map/fphd,gphd->phfg/dot_general | solution.py:187
  227.3 3.0 %copy.78 = f32[80,12,8,8]{0,3,2,1:T(8,128)S(1)} copy(f32[80,12,8,8]{2,3,1,0:T(8,128)} %fusion.19) | data formatting | bytes 491520 | tf_op jit(solution)/shard_map/fphd,gphd->phfg/dot_general | solution.py:187
  232.4 14.3 %all-to-all-done = bf16[1,640,12,128]{3,2,0,1:T(8,128)(2,1)} async-done(((bf16[1,640,12,128]{3,2,0,1:T(8,128)(2,1)}), bf16[1,640,12,128]{3,2,0,1:T(8,128)(2,1)}, u32[]{:S(2)}, u32[]{:S(2)}) %all-to-all-start) | async-done | bytes 1966112 | tf_op jit(solution)/shard_map/all_to_all | solution.py:252
  246.8 3.4 %fusion.14 = bf16[8,80,12,128]{3,0,2,1:T(8,128)(2,1)S(1)} fusion(bf16[80,12,8,8]{3,2,1,0:T(8,128)(2,1)S(1)} %copy.80, bf16[8,80,12,128]{3,2,1,0:T(8,128)(2,1)} %bitcast.9, f32[8,80,12]{0,2,1:T(8,128)S(1)} %copy.81), kind=kOutput, calls=%fused_computation.20 | convolution fusion | flops 17694720 | bytes 4085760 | tf_op jit(solution)/shard_map/phfg,gphd->fphd/dot_general | solution.py:197
  250.9 28.5 %all_to_all.30 = bf16[8,80,12,128]{3,1,2,0:T(8,128)(2,1)S(1)} all-to-all(bf16[8,80,12,128]{3,1,2,0:T(8,128)(2,1)S(1)} %copy.82), channel_id=1, replica_groups=mesh['fsdp'=4,'piece'=4,'fy'=4,'core'=2] {'fy','core'}, dimensions={0} | all-to-all | bytes 3932160 | tf_op jit(solution)/shard_map/all_to_all | solution.py:258
  279.4 2.1 copy.83
  281.5 7.8 %fusion.15 = bf16[1,640,1536]{2,1,0:T(8,128)(2,1)} fusion(bf16[1536,1536]{1,0:T(8,128)(2,1)} %all-gather.7.cloned.1.call-done, bf16[80,8,12,128]{3,2,1,0:T(8,128)(2,1)} %bitcast.52), kind=kOutput, calls=%fused_computation.22 | convolution fusion | flops 3020881920 | bytes 8650752 | tf_op jit(solution)/shard_map/dot_general | solution.py:260
  (45 shorter events, 13.8 us)
Async XLA Ops:
  6.5 2.0 copy-start
  6.5 81.4 %all-gather.9.cloned.1.call-start = ((), (), s32[]{:S(2)}) async-start(), calls=%async_computation.5 | async-start | bytes 15925248 | tf_op jit(solution)/shard_map/all_gather | solution.py:216
  9.9 153.6 %all-gather.5.cloned.1.call-start = ((), (), s32[]{:S(2)}) async-start(), calls=%async_computation.3 | async-start | bytes 1769472 | tf_op jit(solution)/shard_map/all_gather | solution.py:220
  57.9 2.8 copy-start.2
  60.6 6.7 %copy-start.3 = (bf16[640,1536]{1,0:T(8,128)(2,1)}, bf16[640,1536]{1,0:T(8,128)(2,1)S(1)}, u32[]{:S(2)}) copy-start(bf16[640,1536]{1,0:T(8,128)(2,1)S(1)} %get-tuple-element.9) | copy-start | bytes 5898244
  60.6 6.7 %copy-start.4 = (bf16[640,1536]{1,0:T(8,128)(2,1)}, bf16[640,1536]{1,0:T(8,128)(2,1)S(1)}, u32[]{:S(2)}) copy-start(bf16[640,1536]{1,0:T(8,128)(2,1)S(1)} %get-tuple-element.10) | copy-start | bytes 5898244
  61.8 5.5 %copy-start.5 = (f32[1,1536]{1,0:T(1,128)S(1)}, f32[1,1536]{1,0:T(1,128)}, u32[]{:S(2)}) copy-start(f32[1,1536]{1,0:T(1,128)} %param.8) | copy-start | bytes 18436
  61.8 5.5 %copy-start.6 = (f32[1,1536]{1,0:T(1,128)S(1)}, f32[1,1536]{1,0:T(1,128)}, u32[]{:S(2)}) copy-start(f32[1,1536]{1,0:T(1,128)} %param.9) | copy-start | bytes 18436
  158.6 5.5 %copy-start.7 = (s32[1,5,6]{2,0,1:T(1,128)S(1)}, s32[1,5,6]{2,0,1:T(1,128)}, u32[]{:S(2)}) copy-start(s32[1,5,6]{2,0,1:T(1,128)} %param.12) | copy-start | bytes 364
  158.6 6.1 %copy-start.8 = (s32[1,8]{1,0:T(1,128)S(1)}, s32[1,8]{1,0:T(1,128)}, u32[]{:S(2)}) copy-start(s32[1,8]{1,0:T(1,128)} %param.13) | copy-start | bytes 100
  158.6 50.9 %all-to-all-start.1 = ((bf16[2,1,640,12,128]{4,0,3,1,2:T(2,128)(2,1)}), bf16[2,1,640,12,128]{4,0,3,1,2:T(2,128)(2,1)}, u32[]{:S(2)}, u32[]{:S(2)}) async-start(bf16[2,1,640,12,128]{4,0,3,1,2:T(2,128)(2,1)} %copy.73), calls=%async_computation.1 | async-start | bytes 7864320 | tf_op jit(solution)/shard_map/all_to_all | solution.py:244
  163.4 118.1 %all-gather.7.cloned.1.call-start = ((), (), s32[]{:S(2)}) async-start(), calls=%async_computation.4 | async-start | bytes 5898240 | tf_op jit(solution)/shard_map/all_gather | solution.py:221
  209.5 37.2 %all-to-all-start = ((bf16[1,640,12,128]{3,2,0,1:T(8,128)(2,1)}), bf16[1,640,12,128]{3,2,0,1:T(8,128)(2,1)}, u32[]{:S(2)}, u32[]{:S(2)}) async-start(bf16[1,640,12,128]{3,2,0,1:T(8,128)(2,1)} %copy.70), calls=%async_computation | async-start | bytes 5242880 | tf_op jit(solution)/shard_map/all_to_all | solution.py:252
  281.5 7.8 %copy-start.1 = (bf16[1536,1152]{1,0:T(8,128)(2,1)S(1)}, bf16[1536,1152]{1,0:T(8,128)(2,1)}, u32[]{:S(2)}) copy-start(bf16[1536,1152]{1,0:T(8,128)(2,1)} %param.10) | copy-start | bytes 10616836
Sparse Core Ops, SparseCore 0:
  10.1 77.7 all-gather.8
  89.5 12.2 all-gather.4
  165.9 53.0 all-gather.6

commit v4 on v3

--- a/solution.py
+++ b/solution.py
@@ -69,38 +69,47 @@
         o_ref[t * TILE : (t + 1) * TILE, :] = (summed / denominator).astype(o_ref.dtype)
 
 
-def spatial_rows(qkv_all, tile_list, first_tile, count_here):
+def spatial_rows(qkv_all, tile_list, first_tile, count_here, h0, nh):
     buffer_rows = qkv_all.shape[1]
     rows, feat = buffer_rows // 3, qkv_all.shape[0] * qkv_all.shape[2] // 3
     per_shard = qkv_all.shape[2] // HD
     scalars = jnp.stack([first_tile, count_here]).astype(jnp.int32)
     grid_spec = pltpu.PrefetchScalarGridSpec(
         num_scalar_prefetch=2,
-        grid=(HEADS,),
+        grid=(nh,),
         in_specs=[
             pl.BlockSpec(
-                (None, rows, HD), lambda h, lst, sc: (h // per_shard, 1, h % per_shard)
+                (None, rows, HD),
+                lambda h, lst, sc: ((h0 + h) // per_shard, 1, (h0 + h) % per_shard),
             ),
             pl.BlockSpec(
                 (None, buffer_rows, HD),
-                lambda h, lst, sc: ((HEADS + h) // per_shard, 0, (HEADS + h) % per_shard),
+                lambda h, lst, sc: (
+                    (HEADS + h0 + h) // per_shard,
+                    0,
+                    (HEADS + h0 + h) % per_shard,
+                ),
             ),
             pl.BlockSpec(
                 (None, buffer_rows, HD),
-                lambda h, lst, sc: ((2 * HEADS + h) // per_shard, 0, (2 * HEADS + h) % per_shard),
+                lambda h, lst, sc: (
+                    (2 * HEADS + h0 + h) // per_shard,
+                    0,
+                    (2 * HEADS + h0 + h) % per_shard,
+                ),
             ),
         ],
         out_specs=pl.BlockSpec((rows, HD), lambda h, lst, sc: (0, h)),
     )
-    flops = 4 * rows * NBR * TILE * feat
+    flops = 4 * rows * NBR * TILE * nh * HD
     return pl.pallas_call(
         spatial_kernel,
         grid_spec=grid_spec,
-        out_shape=jax.ShapeDtypeStruct((rows, feat), jnp.bfloat16),
+        out_shape=jax.ShapeDtypeStruct((rows, nh * HD), jnp.bfloat16),
         cost_estimate=pl.CostEstimate(
             flops=flops,
-            transcendentals=rows * NBR * TILE * HEADS,
-            bytes_accessed=2 * (rows * feat * 2 + buffer_rows * feat * 2),
+            transcendentals=rows * NBR * TILE * nh,
+            bytes_accessed=2 * (rows * nh * HD * 2 + buffer_rows * nh * HD * 2),
         ),
     )(tile_list.reshape(-1).astype(jnp.int32), scalars, qkv_all, qkv_all, qkv_all)
 
@@ -225,39 +234,52 @@
     qkv_all = jnp.einsum(
         "tk,jkc->jtc", normed_all, w_full, preferred_element_type=jnp.float32
     ).astype(jnp.bfloat16)
-    qk_own = (
-        qkv_all[:, tok_count : 2 * tok_count]
-        .transpose(1, 0, 2)
-        .reshape(tok_count, 3 * feat_count)[:, : 2 * feat_count]
-    )
-    queries = qk_own[:, :feat_count]
-    key_proj = qk_own[:, feat_count:]
     frame_index = lax.axis_index("fy") * lax.axis_size("core") + lax.axis_index("core")
     piece_index = lax.axis_index("piece")
     clip_counts = counts[0]
     count_here = lax.dynamic_index_in_dim(clip_counts, frame_index, 0, keepdims=False)
     rows_here = tok_count // (TGW * TILE)
     first_tile = (piece_index * rows_here - 1) * TGW
-    spatial = spatial_rows(qkv_all, neighbors[0], first_tile, count_here)
-    head_shape = (1, tok_count, HEADS, HD)
+    per_shard = qkv_all.shape[2] // HD
+    own_rows = qkv_all[:, tok_count : 2 * tok_count]
+
+    def head_columns(block0, nh):
+        pieces = []
+        for b in range(block0, block0 + nh):
+            pieces.append(own_rows[b // per_shard, :, (b % per_shard) * HD : (b % per_shard + 1) * HD])
+        return jnp.concatenate(pieces, axis=1)
+
     frame_axes = ("fy", "core")
-    qk_part = lax.all_to_all(
-        jnp.stack([queries, key_proj]).reshape((2,) + head_shape),
-        frame_axes,
-        split_axis=2,
-        concat_axis=1,
-        tiled=True,
-    )
-    query_part, key_part = qk_part[0], qk_part[1]
-    spatial_part = lax.all_to_all(
-        spatial.reshape(head_shape), frame_axes, split_axis=1, concat_axis=0, tiled=True
-    )
     per_dev = tok_count // n_frames
     first_pos = piece_index * tok_count + frame_index * per_dev
-    temporal = temporal_block(query_part, key_part, spatial_part, clip_counts, first_pos)
-    returned = lax.all_to_all(temporal, frame_axes, split_axis=0, concat_axis=1, tiled=True)
-    flat_temporal = returned.reshape(tok_count, feat_count)
-    projected = jnp.dot(flat_temporal, w_out_full, preferred_element_type=jnp.float32)
+    group = 4
+    projected = None
+    for h0 in range(0, HEADS, group):
+        qk_in = jnp.concatenate(
+            [head_columns(h0, group), head_columns(HEADS + h0, group)], axis=1
+        )
+        qk_part = lax.all_to_all(qk_in, frame_axes, split_axis=0, concat_axis=0, tiled=True)
+        spatial = spatial_rows(qkv_all, neighbors[0], first_tile, count_here, h0, group)
+        spatial_part = lax.all_to_all(spatial, frame_axes, split_axis=0, concat_axis=0, tiled=True)
+        part_shape = (n_frames, per_dev, group, HD)
+        query_part = qk_part[:, : group * HD].reshape(part_shape)
+        key_part = qk_part[:, group * HD :].reshape(part_shape)
+        temporal = temporal_block(
+            query_part, key_part, spatial_part.reshape(part_shape), clip_counts, first_pos
+        )
+        returned = lax.all_to_all(
+            temporal.reshape(tok_count, group * HD),
+            frame_axes,
+            split_axis=0,
+            concat_axis=0,
+            tiled=True,
+        )
+        partial = jnp.dot(
+            returned,
+            w_out_full[h0 * HD : (h0 + group) * HD],
+            preferred_element_type=jnp.float32,
+        )
+        projected = partial if projected is None else projected + partial
     return projected.astype(jnp.bfloat16).reshape(1, tok_count, feat_count)
 
 

time: 297 us -> 347 us (1.17)
  waiting for transfers between devices: 40.8 us -> 77.7 us
  starting transfers between devices: 10.1 us -> 41 us
  blocking collectives: 28.5 us -> 0 us
  matrix products: 54.8 us -> 65.4 us
  Pallas kernels: 75.3 us -> 80.4 us
    all_to_all x2 -> x9, starting transfers between devices: 9.95 us -> 40.9 us  [the longest x3 13.7 us: local(): lax.all_to_all(spatial, frame_axes, split_axis=0, concat_axis=0, tiled=True)]
    all_to_all x1 -> x0, blocking collectives: 28.5 us -> none  [local(): lax.all_to_all(temporal, frame_axes, split_axis=0, concat_axis=1, tiled=T...]
    all_to_all x2 -> x9, waiting for transfers between devices: 19.7 us -> 44.4 us  [the longest x3 15 us: local(): lax.all_to_all(spatial, frame_axes, split_axis=0, concat_axis=0, tiled=True)]
    unnamed x20 -> x65, local copies, waits for them, and re-layouts: 3.14 us -> 19.4 us
    transpose x2 -> x0, local copies, waits for them, and re-layouts: 14.5 us -> none  [local(): qk_own = qkv_all[:, tok_count:2 * tok_count].transpose(1, 0, 2).reshape(t...]
    all_gather x1, waiting for transfers between devices: 20.5 us -> 33.2 us  [local(): w_pieces = lax.all_gather(w_half, ('fsdp', 'core'), axis=0, tiled=False)]
    another operation x1 -> x0, local copies, waits for them, and re-layouts: 10.7 us -> none  [local(): jnp.stack([queries, key_proj]).reshape((2,) + head_shape)]
    dot_general x1 -> x3, matrix products: 7.75 us -> 15.5 us  [local(): jnp.dot(returned, w_out_full[h0 * HD:(h0 + group) * HD], preferred_elemen...]
  transfers between devices with their start and end apart: 5 -> 12, of which waited for: 3 -> 8; matrix products, arithmetic and copies ran while one was open for 39% -> 34% of each run, Pallas kernels for 25% -> 23%
where the time goes in v4:
time: 347 us; the launch traced here: 345 us
  Pallas kernels  80.4 us (23%)
  waiting for transfers between devices  77.7 us (22%)
  matrix products  65.4 us (19%)
  local copies, waits for them, and re-layouts  56.5 us (16%)
  starting transfers between devices  41 us (12%)
  between operations  13.6 us (4%)
  other arithmetic  10.7 us (3%)
    pallas_call x1, Pallas kernels, exchange_rims(): pl.pallas_call(rim_kernel, out_shape=jax.ShapeDtypeStruct((2, rows, feat)...  46 us
    dot_general x1, matrix products, local(): jnp.einsum('tk,jkc->jtc', normed_all, w_full, preferred_element_type=jnp....  40.7 us
    pallas_call x3, Pallas kernels, spatial_rows(): pl.pallas_call(spatial_kernel, grid_spec=grid_spec, out_shape=jax.ShapeDt...  34.5 us
    all_gather x1, waiting for transfers between devices, local(): w_pieces = lax.all_gather(w_half, ('fsdp', 'core'), axis=0, tiled=False)  33.2 us
    unnamed x65, local copies, waits for them, and re-layouts  19.4 us
    dot_general x3, matrix products, local(): jnp.dot(returned, w_out_full[h0 * HD:(h0 + group) * HD], preferred_elemen...  15.5 us
    all_to_all x3, waiting for transfers between devices, local(): lax.all_to_all(spatial, frame_axes, split_axis=0, concat_axis=0, tiled=True)  15 us
    all_to_all x3, waiting for transfers between devices, local(): lax.all_to_all(qk_in, frame_axes, split_axis=0, concat_axis=0, tiled=True)  14.8 us
  transfers between devices with their start and end apart: 12, of which 8 were waited for; matrix products, arithmetic and copies ran while one was open for 34% of the time, Pallas kernels for 23%

profile of v4, /device:TPU:1, one launch (start us, length us, event | category | flops | bytes accessed | tf_op | source)
XLA Modules:
  0.0 345.3 jit_solution(4203625799134531238)
XLA Ops:
  10.2 46.0 %shard_map.73 = bf16[2,640,1536]{2,1,0:T(8,128)(2,1)} custom-call(bf16[640,1536]{1,0:T(8,128)(2,1)} %bitcast.89), custom_call_target="tpu_custom_call" | custom-call | bytes 157286400 | tf_op jit(solution)/shard_map/pallas_call | solution.py:179
  63.2 5.4 %fusion.6 = f32[1920]{0:T(1024)S(1)} fusion(f32[1920]{0:T(1024)S(1)} %broadcast_multiply_fusion, bf16[640,1536]{1,0:T(8,128)(2,1)S(1)} %get-tuple-element.30, bf16[640,1536]{1,0:T(8,128)(2,1)S(1)} %bitcast.91, bf16[640,1536]{1,0:T(8,128)(2,1)S(1)} %get-tuple-element.29), kind=kLoop, calls=%fused_computation.9 | loop fusion | flops 26540160 | bytes 5913600 | tf_op jit(solution)/shard_map/reduce_sum | solution.py:28
  68.6 33.2 %all-gather.9.cloned.1.call-done = bf16[6144,1152]{1,0:T(8,128)(2,1)} async-done(((bf16[768,1152]{1,0:T(8,128)(2,1)}), bf16[6144,1152]{1,0:T(8,128)(2,1)}) %all-gather.9.cloned.1.call-update) | async-done | bytes 14155792 | tf_op jit(solution)/shard_map/all_gather | solution.py:225
  101.8 40.7 %fusion.3.q_ref.k_ref.v_ref = bf16[4,1920,1152]{2,1,0:T(8,128)(2,1)} fusion(bf16[4,1536,1152]{2,1,0:T(8,128)(2,1)} %bitcast.127, f32[1536]{0:T(1024)S(1)} %reduce.2, f32[1536]{0:T(1024)S(1)} %add_reduce_fusion, f32[1920]{0:T(1024)S(1)} %add_sqrt_fusion, f32[1920]{0:T(1024)S(1)} %broadcast_multiply_fusion, bf16[640,1536]{1,0:T(8,128)(2,1)} %copy-done.4, ...), kind=kOutput, calls=%fused_computation.4 | convolution fusion | flops 27220377600 | bytes 37776384 | tf_op jit(solution)/shard_map/tk,jkc->jtc/dot_general | solution.py:234
  142.5 11.5 %shard_map.75 = bf16[640,512]{1,0:T(8,128)(2,1)} custom-call(s32[30]{0:T(128)} %reshape_squeeze.2.list_ref, s32[2]{0:T(128)} %pad_add_fusion.scalar_ref, bf16[4,1920,1152]{2,1,0:T(8,128)(2,1)} %fusion.3.q_ref.k_ref.v_ref, bf16[4,1920,1152]{2,1,0:T(8,128)(2,1)} %fusion.3.q_ref.k_ref.v_ref, bf16[4,1920,1152]{2,1,0:T(8,128)(2,1)} %fusion.3.q_ref.k_ref.v_ref), custom_call_target="tpu_custom_call" | custom-call | flops 1006632960 | bytes 5242880 | tf_op jit(solution)/shard_map/pallas_call | solution.py:105
  154.0 4.5 %all-to-all-start.3 = ((bf16[8,80,512]{2,1,0:T(8,128)(2,1)}), bf16[8,80,512]{2,1,0:T(8,128)(2,1)S(1)}, u32[]{:S(2)}, u32[]{:S(2)}) async-start(bf16[8,80,512]{2,1,0:T(8,128)(2,1)} %bitcast.98), calls=%async_computation.3 | async-start | bytes 1310720 | tf_op jit(solution)/shard_map/all_to_all | solution.py:263
  158.6 11.5 %shard_map.74 = bf16[640,512]{1,0:T(8,128)(2,1)} custom-call(s32[30]{0:T(128)} %reshape_squeeze.2.list_ref, s32[2]{0:T(128)} %pad_add_fusion.scalar_ref, bf16[4,1920,1152]{2,1,0:T(8,128)(2,1)} %fusion.3.q_ref.k_ref.v_ref, bf16[4,1920,1152]{2,1,0:T(8,128)(2,1)} %fusion.3.q_ref.k_ref.v_ref, bf16[4,1920,1152]{2,1,0:T(8,128)(2,1)} %fusion.3.q_ref.k_ref.v_ref), custom_call_target="tpu_custom_call" | custom-call | flops 1006632960 | bytes 5242880 | tf_op jit(solution)/shard_map/pallas_call | solution.py:105
  170.1 11.5 %shard_map.76 = bf16[640,512]{1,0:T(8,128)(2,1)} custom-call(s32[30]{0:T(128)} %reshape_squeeze.2.list_ref, s32[2]{0:T(128)} %pad_add_fusion.scalar_ref, bf16[4,1920,1152]{2,1,0:T(8,128)(2,1)} %fusion.3.q_ref.k_ref.v_ref, bf16[4,1920,1152]{2,1,0:T(8,128)(2,1)} %fusion.3.q_ref.k_ref.v_ref, bf16[4,1920,1152]{2,1,0:T(8,128)(2,1)} %fusion.3.q_ref.k_ref.v_ref), custom_call_target="tpu_custom_call" | custom-call | flops 1006632960 | bytes 5242880 | tf_op jit(solution)/shard_map/pallas_call | solution.py:105
  185.1 4.8 %all-to-all-start = ((bf16[8,80,512]{2,1,0:T(8,128)(2,1)}), bf16[8,80,512]{2,1,0:T(8,128)(2,1)S(1)}, u32[]{:S(2)}, u32[]{:S(2)}) async-start(bf16[8,80,512]{2,1,0:T(8,128)(2,1)} %bitcast.8), calls=%async_computation | async-start | bytes 1310720 | tf_op jit(solution)/shard_map/all_to_all | solution.py:263
  191.1 9.7 %all-to-all-done = bf16[8,80,512]{2,1,0:T(8,128)(2,1)S(1)} async-done(((bf16[8,80,512]{2,1,0:T(8,128)(2,1)}), bf16[8,80,512]{2,1,0:T(8,128)(2,1)S(1)}, u32[]{:S(2)}, u32[]{:S(2)}) %all-to-all-start) | async-done | bytes 655392 | tf_op jit(solution)/shard_map/all_to_all | solution.py:263
  200.8 4.3 %all-to-all-start.6 = ((bf16[8,80,512]{2,1,0:T(8,128)(2,1)}), bf16[8,80,512]{2,1,0:T(8,128)(2,1)S(1)}, u32[]{:S(2)}, u32[]{:S(2)}) async-start(bf16[8,80,512]{2,1,0:T(8,128)(2,1)} %bitcast.39), calls=%async_computation.6 | async-start | bytes 1310720 | tf_op jit(solution)/shard_map/all_to_all | solution.py:263
  210.7 5.3 %all-to-all-done.6 = bf16[8,80,512]{2,1,0:T(8,128)(2,1)S(1)} async-done(((bf16[8,80,512]{2,1,0:T(8,128)(2,1)}), bf16[8,80,512]{2,1,0:T(8,128)(2,1)S(1)}, u32[]{:S(2)}, u32[]{:S(2)}) %all-to-all-start.6) | async-done | bytes 655392 | tf_op jit(solution)/shard_map/all_to_all | solution.py:263
  216.0 4.3 %all-to-all-start.4 = ((bf16[8,80,1024]{2,1,0:T(8,128)(2,1)}), bf16[8,80,1024]{2,1,0:T(8,128)(2,1)S(1)}, u32[]{:S(2)}, u32[]{:S(2)}) async-start(bf16[8,80,1024]{2,1,0:T(8,128)(2,1)} %copy-done.9), calls=%async_computation.4 | async-start | bytes 2621440 | tf_op jit(solution)/shard_map/all_to_all | solution.py:261
  227.9 10.3 %all-to-all-done.4 = bf16[8,80,1024]{2,1,0:T(8,128)(2,1)S(1)} async-done(((bf16[8,80,1024]{2,1,0:T(8,128)(2,1)}), bf16[8,80,1024]{2,1,0:T(8,128)(2,1)S(1)}, u32[]{:S(2)}, u32[]{:S(2)}) %all-to-all-start.4) | async-done | bytes 1310752 | tf_op jit(solution)/shard_map/all_to_all | solution.py:261
  238.3 4.3 %all-to-all-start.1 = ((bf16[8,80,1024]{2,1,0:T(8,128)(2,1)}), bf16[8,80,1024]{2,1,0:T(8,128)(2,1)S(1)}, u32[]{:S(2)}, u32[]{:S(2)}) async-start(bf16[8,80,1024]{2,1,0:T(8,128)(2,1)} %copy-done.8), calls=%async_computation.1 | async-start | bytes 2621440 | tf_op jit(solution)/shard_map/all_to_all | solution.py:261
  262.9 5.0 %all-to-all-start.7 = ((bf16[8,80,1024]{2,1,0:T(8,128)(2,1)}), bf16[8,80,1024]{2,1,0:T(8,128)(2,1)S(1)}, u32[]{:S(2)}, u32[]{:S(2)}) async-start(bf16[8,80,1024]{2,1,0:T(8,128)(2,1)} %constant_dynamic-update-slice_fusion.16), calls=%async_computation.7 | async-start | bytes 2621440 | tf_op jit(solution)/shard_map/all_to_all | solution.py:261
  281.4 4.4 %all-to-all-done.7 = bf16[8,80,1024]{2,1,0:T(8,128)(2,1)S(1)} async-done(((bf16[8,80,1024]{2,1,0:T(8,128)(2,1)}), bf16[8,80,1024]{2,1,0:T(8,128)(2,1)S(1)}, u32[]{:S(2)}, u32[]{:S(2)}) %all-to-all-start.7) | async-done | bytes 1310752 | tf_op jit(solution)/shard_map/all_to_all | solution.py:261
  285.8 4.3 %all-to-all-start.5 = ((bf16[8,80,512]{2,1,0:T(8,128)(2,1)}), bf16[8,80,512]{2,1,0:T(8,128)(2,1)S(1)}, u32[]{:S(2)}, u32[]{:S(2)}) async-start(bf16[8,80,512]{2,1,0:T(8,128)(2,1)} %all_to_all.71), calls=%async_computation.5 | async-start | bytes 1310720 | tf_op jit(solution)/shard_map/all_to_all | solution.py:270
  293.4 7.6 %all-to-all-done.5 = bf16[8,80,512]{2,1,0:T(8,128)(2,1)S(1)} async-done(((bf16[8,80,512]{2,1,0:T(8,128)(2,1)}), bf16[8,80,512]{2,1,0:T(8,128)(2,1)S(1)}, u32[]{:S(2)}, u32[]{:S(2)}) %all-to-all-start.5) | async-done | bytes 655392 | tf_op jit(solution)/shard_map/all_to_all | solution.py:270
  311.2 5.0 %all-to-all-done.2 = bf16[8,80,512]{2,1,0:T(8,128)(2,1)S(1)} async-done(((bf16[8,80,512]{2,1,0:T(8,128)(2,1)}), bf16[8,80,512]{2,1,0:T(8,128)(2,1)S(1)}, u32[]{:S(2)}, u32[]{:S(2)}) %all-to-all-start.2) | async-done | bytes 655392 | tf_op jit(solution)/shard_map/all_to_all | solution.py:270
  316.2 5.0 %all-to-all-start.8 = ((bf16[8,80,512]{2,1,0:T(8,128)(2,1)}), bf16[8,80,512]{2,1,0:T(8,128)(2,1)}, u32[]{:S(2)}, u32[]{:S(2)}) async-start(bf16[8,80,512]{2,1,0:T(8,128)(2,1)} %all_to_all.78), calls=%async_computation.8 | async-start | bytes 1310720 | tf_op jit(solution)/shard_map/all_to_all | solution.py:270
  321.2 4.5 %fusion.18 = f32[640,1536]{1,0:T(8,128)} fusion(bf16[640,512]{1,0:T(8,128)(2,1)S(1)} %bitcast.96, bf16[1536,1536]{1,0:T(8,128)(2,1)} %all-gather.7.cloned.1.call-done), kind=kOutput, calls=%fused_computation.24 | convolution fusion | flops 1006632960 | bytes 6160384 | tf_op jit(solution)/shard_map/dot_general | solution.py:277
  325.7 4.5 %fusion.20 = f32[640,1536]{1,0:T(8,128)} fusion(bf16[640,512]{1,0:T(8,128)(2,1)S(1)} %bitcast.97, bf16[1536,1536]{1,0:T(8,128)(2,1)} %all-gather.7.cloned.1.call-done), kind=kOutput, calls=%fused_computation.26 | convolution fusion | flops 1006632960 | bytes 6160384 | tf_op jit(solution)/shard_map/dot_general | solution.py:277
  332.2 6.5 %fusion.16 = bf16[1,640,1536]{2,1,0:T(8,128)(2,1)} fusion(bf16[640,512]{1,0:T(8,128)(2,1)} %bitcast.53, f32[640,1536]{1,0:T(8,128)} %fusion.20, f32[640,1536]{1,0:T(8,128)} %fusion.18, bf16[1536,1536]{1,0:T(8,128)(2,1)} %all-gather.7.cloned.1.call-done), kind=kOutput, calls=%fused_computation.20 | convolution fusion | flops 1009582080 | bytes 12058624 | tf_op jit(solution)/shard_map/dot_general | solution.py:277
  (132 shorter events, 77.5 us)
Async XLA Ops:
  6.5 62.1 %all-gather.5.cloned.1.call-start = ((), (), s32[]{:S(2)}) async-start(), calls=%async_computation.9 | async-start | bytes 1769472 | tf_op jit(solution)/shard_map/all_gather | solution.py:229
  8.6 93.2 %all-gather.9.cloned.1.call-start = ((), (), s32[]{:S(2)}) async-start(), calls=%async_computation.11 | async-start | bytes 15925248 | tf_op jit(solution)/shard_map/all_gather | solution.py:225
  10.1 311.1 %all-gather.7.cloned.1.call-start = ((), (), s32[]{:S(2)}) async-start(), calls=%async_computation.10 | async-start | bytes 5898240 | tf_op jit(solution)/shard_map/all_gather | solution.py:230
  10.2 46.0 %copy-start.20 = (s32[1,5,6]{2,0,1:T(1,128)S(1)}, s32[1,5,6]{2,0,1:T(1,128)}, u32[]{:S(2)}) copy-start(s32[1,5,6]{2,0,1:T(1,128)} %param.12) | copy-start | bytes 364
  10.2 46.6 %copy-start.19 = (f32[1,1536]{1,0:T(1,128)S(1)}, f32[1,1536]{1,0:T(1,128)}, u32[]{:S(2)}) copy-start(f32[1,1536]{1,0:T(1,128)} %param.9) | copy-start | bytes 18436
  10.2 46.7 %copy-start.21 = (s32[1,8]{1,0:T(1,128)S(1)}, s32[1,8]{1,0:T(1,128)}, u32[]{:S(2)}) copy-start(s32[1,8]{1,0:T(1,128)} %param.13) | copy-start | bytes 100
  10.2 48.5 %copy-start.18 = (f32[1,1536]{1,0:T(1,128)S(1)}, f32[1,1536]{1,0:T(1,128)}, u32[]{:S(2)}) copy-start(f32[1,1536]{1,0:T(1,128)} %param.8) | copy-start | bytes 18436
  154.0 31.0 %all-to-all-start.3 = ((bf16[8,80,512]{2,1,0:T(8,128)(2,1)}), bf16[8,80,512]{2,1,0:T(8,128)(2,1)S(1)}, u32[]{:S(2)}, u32[]{:S(2)}) async-start(bf16[8,80,512]{2,1,0:T(8,128)(2,1)} %bitcast.98), calls=%async_computation.3 | async-start | bytes 1310720 | tf_op jit(solution)/shard_map/all_to_all | solution.py:263
  185.1 15.7 %all-to-all-start = ((bf16[8,80,512]{2,1,0:T(8,128)(2,1)}), bf16[8,80,512]{2,1,0:T(8,128)(2,1)S(1)}, u32[]{:S(2)}, u32[]{:S(2)}) async-start(bf16[8,80,512]{2,1,0:T(8,128)(2,1)} %bitcast.8), calls=%async_computation | async-start | bytes 1310720 | tf_op jit(solution)/shard_map/all_to_all | solution.py:263
  200.8 9.9 %copy-start.5 = (bf16[8,80,512]{2,1,0:T(8,128)(2,1)}, bf16[8,80,512]{2,1,0:T(8,128)(2,1)S(1)}, u32[]{:S(2)}) copy-start(bf16[8,80,512]{2,1,0:T(8,128)(2,1)S(1)} %all-to-all-done) | copy-start | bytes 1966084
  200.8 15.2 %all-to-all-start.6 = ((bf16[8,80,512]{2,1,0:T(8,128)(2,1)}), bf16[8,80,512]{2,1,0:T(8,128)(2,1)S(1)}, u32[]{:S(2)}, u32[]{:S(2)}) async-start(bf16[8,80,512]{2,1,0:T(8,128)(2,1)} %bitcast.39), calls=%async_computation.6 | async-start | bytes 1310720 | tf_op jit(solution)/shard_map/all_to_all | solution.py:263
  216.0 7.0 %copy-start.6 = (bf16[8,80,512]{2,1,0:T(8,128)(2,1)}, bf16[8,80,512]{2,1,0:T(8,128)(2,1)S(1)}, u32[]{:S(2)}) copy-start(bf16[8,80,512]{2,1,0:T(8,128)(2,1)S(1)} %all-to-all-done.6) | copy-start | bytes 1966084
  216.0 22.3 %all-to-all-start.4 = ((bf16[8,80,1024]{2,1,0:T(8,128)(2,1)}), bf16[8,80,1024]{2,1,0:T(8,128)(2,1)S(1)}, u32[]{:S(2)}, u32[]{:S(2)}) async-start(bf16[8,80,1024]{2,1,0:T(8,128)(2,1)} %copy-done.9), calls=%async_computation.4 | async-start | bytes 2621440 | tf_op jit(solution)/shard_map/all_to_all | solution.py:261
  220.4 5.7 %copy-start.12 = (bf16[1,640,128]{2,1,0:T(8,128)(2,1)S(1)}, bf16[1,640,128]{2,1,0:T(8,128)(2,1)}, u32[]{:S(2)}) copy-start(bf16[1,640,128]{2,1,0:T(8,128)(2,1)} %get-tuple-element.22) | copy-start | bytes 491524
  220.4 5.8 %copy-start.11 = (bf16[1,640,128]{2,1,0:T(8,128)(2,1)S(1)}, bf16[1,640,128]{2,1,0:T(8,128)(2,1)}, u32[]{:S(2)}) copy-start(bf16[1,640,128]{2,1,0:T(8,128)(2,1)} %get-tuple-element.21) | copy-start | bytes 491524
  220.4 6.9 %copy-start.10 = (bf16[1,640,128]{2,1,0:T(8,128)(2,1)S(1)}, bf16[1,640,128]{2,1,0:T(8,128)(2,1)}, u32[]{:S(2)}) copy-start(bf16[1,640,128]{2,1,0:T(8,128)(2,1)} %get-tuple-element.12) | copy-start | bytes 491524
  238.3 24.6 %all-to-all-start.1 = ((bf16[8,80,1024]{2,1,0:T(8,128)(2,1)}), bf16[8,80,1024]{2,1,0:T(8,128)(2,1)S(1)}, u32[]{:S(2)}, u32[]{:S(2)}) async-start(bf16[8,80,1024]{2,1,0:T(8,128)(2,1)} %copy-done.8), calls=%async_computation.1 | async-start | bytes 2621440 | tf_op jit(solution)/shard_map/all_to_all | solution.py:261
  262.9 6.9 %copy-start.17 = (bf16[8,80,4,128]{3,2,1,0:T(4,128)(2,1)S(1)}, bf16[8,80,4,128]{3,2,1,0:T(4,128)(2,1)}, u32[]{:S(2)}) copy-start(bf16[8,80,4,128]{3,2,1,0:T(4,128)(2,1)} %reshape.162) | copy-start | bytes 1966084
  262.9 22.9 %all-to-all-start.7 = ((bf16[8,80,1024]{2,1,0:T(8,128)(2,1)}), bf16[8,80,1024]{2,1,0:T(8,128)(2,1)S(1)}, u32[]{:S(2)}, u32[]{:S(2)}) async-start(bf16[8,80,1024]{2,1,0:T(8,128)(2,1)} %constant_dynamic-update-slice_fusion.16), calls=%async_computation.7 | async-start | bytes 2621440 | tf_op jit(solution)/shard_map/all_to_all | solution.py:261
  280.2 9.9 %copy-start.16 = (bf16[8,80,4,128]{3,2,1,0:T(4,128)(2,1)S(1)}, bf16[8,80,4,128]{3,2,1,0:T(4,128)(2,1)}, u32[]{:S(2)}) copy-start(bf16[8,80,4,128]{3,2,1,0:T(4,128)(2,1)} %reshape.159) | copy-start | bytes 1966084
  285.8 15.2 %all-to-all-start.5 = ((bf16[8,80,512]{2,1,0:T(8,128)(2,1)}), bf16[8,80,512]{2,1,0:T(8,128)(2,1)S(1)}, u32[]{:S(2)}, u32[]{:S(2)}) async-start(bf16[8,80,512]{2,1,0:T(8,128)(2,1)} %all_to_all.71), calls=%async_computation.5 | async-start | bytes 1310720 | tf_op jit(solution)/shard_map/all_to_all | solution.py:270
  301.0 15.2 %all-to-all-start.2 = ((bf16[8,80,512]{2,1,0:T(8,128)(2,1)}), bf16[8,80,512]{2,1,0:T(8,128)(2,1)S(1)}, u32[]{:S(2)}, u32[]{:S(2)}) async-start(bf16[8,80,512]{2,1,0:T(8,128)(2,1)} %all_to_all.64), calls=%async_computation.2 | async-start | bytes 1310720 | tf_op jit(solution)/shard_map/all_to_all | solution.py:270
  316.2 16.0 %all-to-all-start.8 = ((bf16[8,80,512]{2,1,0:T(8,128)(2,1)}), bf16[8,80,512]{2,1,0:T(8,128)(2,1)}, u32[]{:S(2)}, u32[]{:S(2)}) async-start(bf16[8,80,512]{2,1,0:T(8,128)(2,1)} %all_to_all.78), calls=%async_computation.8 | async-start | bytes 1310720 | tf_op jit(solution)/shard_map/all_to_all | solution.py:270
  332.2 6.5 %copy-start.1 = (bf16[1536,1152]{1,0:T(8,128)(2,1)S(1)}, bf16[1536,1152]{1,0:T(8,128)(2,1)}, u32[]{:S(2)}) copy-start(bf16[1536,1152]{1,0:T(8,128)(2,1)} %param.10) | copy-start | bytes 10616836
  (10 other events, 27.5 us)
Sparse Core Ops, SparseCore 0:
  9.0 15.5 all-gather.4
  26.3 75.4 all-gather.8
  103.5 52.7 all-gather.6

commit v5 on v3

--- a/solution.py
+++ b/solution.py
@@ -69,25 +69,27 @@
         o_ref[t * TILE : (t + 1) * TILE, :] = (summed / denominator).astype(o_ref.dtype)
 
 
-def spatial_rows(qkv_all, tile_list, first_tile, count_here):
-    buffer_rows = qkv_all.shape[1]
-    rows, feat = buffer_rows // 3, qkv_all.shape[0] * qkv_all.shape[2] // 3
-    per_shard = qkv_all.shape[2] // HD
+def spatial_rows(queries, kv_all, tile_list, first_tile, count_here):
+    buffer_rows = kv_all.shape[1]
+    rows, feat = queries.shape
+    per_shard = kv_all.shape[2] // HD
     scalars = jnp.stack([first_tile, count_here]).astype(jnp.int32)
     grid_spec = pltpu.PrefetchScalarGridSpec(
         num_scalar_prefetch=2,
         grid=(HEADS,),
         in_specs=[
+            pl.BlockSpec((rows, HD), lambda h, lst, sc: (0, h)),
             pl.BlockSpec(
-                (None, rows, HD), lambda h, lst, sc: (h // per_shard, 1, h % per_shard)
+                (None, buffer_rows, HD),
+                lambda h, lst, sc: ((HEADS + h) // per_shard - 1, 0, (HEADS + h) % per_shard),
             ),
             pl.BlockSpec(
                 (None, buffer_rows, HD),
-                lambda h, lst, sc: ((HEADS + h) // per_shard, 0, (HEADS + h) % per_shard),
-            ),
-            pl.BlockSpec(
-                (None, buffer_rows, HD),
-                lambda h, lst, sc: ((2 * HEADS + h) // per_shard, 0, (2 * HEADS + h) % per_shard),
+                lambda h, lst, sc: (
+                    (2 * HEADS + h) // per_shard - 1,
+                    0,
+                    (2 * HEADS + h) % per_shard,
+                ),
             ),
         ],
         out_specs=pl.BlockSpec((rows, HD), lambda h, lst, sc: (0, h)),
@@ -102,7 +104,7 @@
             transcendentals=rows * NBR * TILE * HEADS,
             bytes_accessed=2 * (rows * feat * 2 + buffer_rows * feat * 2),
         ),
-    )(tile_list.reshape(-1).astype(jnp.int32), scalars, qkv_all, qkv_all, qkv_all)
+    )(tile_list.reshape(-1).astype(jnp.int32), scalars, queries, kv_all, kv_all)
 
 
 MESH_IDS = pl.DeviceIdType.MESH
@@ -222,41 +224,50 @@
     normed_all = layer_norm(
         jnp.concatenate([above, own, below], axis=0), mod_scale[0], mod_shift[0]
     )
-    qkv_all = jnp.einsum(
-        "tk,jkc->jtc", normed_all, w_full, preferred_element_type=jnp.float32
+    shard_cols = w_full.shape[2]
+    w_query = jnp.concatenate(
+        [w_full[0], w_full[1, :, : feat_count - shard_cols]], axis=1
+    )
+    queries = jnp.dot(
+        normed_all[tok_count : 2 * tok_count], w_query, preferred_element_type=jnp.float32
     ).astype(jnp.bfloat16)
-    qk_own = (
-        qkv_all[:, tok_count : 2 * tok_count]
-        .transpose(1, 0, 2)
-        .reshape(tok_count, 3 * feat_count)[:, : 2 * feat_count]
-    )
-    queries = qk_own[:, :feat_count]
-    key_proj = qk_own[:, feat_count:]
+    kv_all = jnp.einsum(
+        "tk,jkc->jtc", normed_all, w_full[1:], preferred_element_type=jnp.float32
+    ).astype(jnp.bfloat16)
+    key_cut = feat_count - shard_cols
+    own_kv = kv_all[:, tok_count : 2 * tok_count]
+    key_proj = jnp.concatenate(
+        [own_kv[0, :, key_cut:], own_kv[1, :, : feat_count - shard_cols + key_cut]], axis=1
+    )
     frame_index = lax.axis_index("fy") * lax.axis_size("core") + lax.axis_index("core")
     piece_index = lax.axis_index("piece")
     clip_counts = counts[0]
     count_here = lax.dynamic_index_in_dim(clip_counts, frame_index, 0, keepdims=False)
     rows_here = tok_count // (TGW * TILE)
     first_tile = (piece_index * rows_here - 1) * TGW
-    spatial = spatial_rows(qkv_all, neighbors[0], first_tile, count_here)
-    head_shape = (1, tok_count, HEADS, HD)
+    spatial = spatial_rows(queries, kv_all, neighbors[0], first_tile, count_here)
     frame_axes = ("fy", "core")
     qk_part = lax.all_to_all(
-        jnp.stack([queries, key_proj]).reshape((2,) + head_shape),
+        jnp.concatenate([queries, key_proj], axis=1),
         frame_axes,
-        split_axis=2,
-        concat_axis=1,
+        split_axis=0,
+        concat_axis=0,
         tiled=True,
     )
-    query_part, key_part = qk_part[0], qk_part[1]
-    spatial_part = lax.all_to_all(
-        spatial.reshape(head_shape), frame_axes, split_axis=1, concat_axis=0, tiled=True
-    )
+    spatial_part = lax.all_to_all(spatial, frame_axes, split_axis=0, concat_axis=0, tiled=True)
     per_dev = tok_count // n_frames
     first_pos = piece_index * tok_count + frame_index * per_dev
-    temporal = temporal_block(query_part, key_part, spatial_part, clip_counts, first_pos)
-    returned = lax.all_to_all(temporal, frame_axes, split_axis=0, concat_axis=1, tiled=True)
-    flat_temporal = returned.reshape(tok_count, feat_count)
+    part_shape = (n_frames, per_dev, HEADS, HD)
+    temporal = temporal_block(
+        qk_part[:, :feat_count].reshape(part_shape),
+        qk_part[:, feat_count:].reshape(part_shape),
+        spatial_part.reshape(part_shape),
+        clip_counts,
+        first_pos,
+    )
+    flat_temporal = lax.all_to_all(
+        temporal.reshape(tok_count, feat_count), frame_axes, split_axis=0, concat_axis=0, tiled=True
+    )
     projected = jnp.dot(flat_temporal, w_out_full, preferred_element_type=jnp.float32)
     return projected.astype(jnp.bfloat16).reshape(1, tok_count, feat_count)
 

time: 297 us -> 314 us (1.057)
  waiting for transfers between devices: 40.8 us -> 95.6 us
  blocking collectives: 28.5 us -> 0 us
  local copies, waits for them, and re-layouts: 59.9 us -> 41.7 us
  other arithmetic: 13.1 us -> 25.6 us
  matrix products: 54.8 us -> 44.8 us
  starting transfers between devices: 10.1 us -> 15 us
    all_to_all x2 -> x3, waiting for transfers between devices: 19.7 us -> 87.5 us  [the longest x1 42.7 us: local(): lax.all_to_all(jnp.concatenate([queries, key_proj], axis=1), frame_axes,...]
    all_to_all x1 -> x0, blocking collectives: 28.5 us -> none  [local(): lax.all_to_all(temporal, frame_axes, split_axis=0, concat_axis=1, tiled=T...]
    transpose x2 -> x0, local copies, waits for them, and re-layouts: 14.5 us -> none  [local(): qk_own = qkv_all[:, tok_count:2 * tok_count].transpose(1, 0, 2).reshape(t...]
    all_gather x1, waiting for transfers between devices: 20.5 us -> 7.47 us  [local(): w_pieces = lax.all_gather(w_half, ('fsdp', 'core'), axis=0, tiled=False)]
    convert_element_type x0 -> x1, other arithmetic: none -> 12.8 us  [layer_norm(): return (normal * (1.0 + mod_scale) + mod_shift).astype(jnp.bfloat16)]
    dot_general x1 -> x2, matrix products: 40.7 us -> 28.2 us  [the longest x1 23.7 us: local(): jnp.einsum('tk,jkc->jtc', normed_all, w_full[1:], preferred_element_type=...]
    another operation x1 -> x0, local copies, waits for them, and re-layouts: 10.7 us -> none  [local(): jnp.stack([queries, key_proj]).reshape((2,) + head_shape)]
    reshape x1 -> x3, local copies, waits for them, and re-layouts: 5.42 us -> 11.3 us  [the longest x1 4.75 us: local(): qk_part[:, feat_count:].reshape(part_shape)]
  transfers between devices with their start and end apart: 5 -> 6, of which waited for: 3 -> 4; matrix products, arithmetic and copies ran while one was open for 39% -> 19% of each run, Pallas kernels for 25% -> 15%
where the time goes in v5:
time: 314 us; the launch traced here: 313 us
  waiting for transfers between devices  95.6 us (30%)
  Pallas kernels  75.2 us (24%)
  matrix products  44.8 us (14%)
  local copies, waits for them, and re-layouts  41.7 us (13%)
  other arithmetic  25.6 us (8%)
  starting transfers between devices  15 us (5%)
  between operations  15 us (5%)
    pallas_call x1, Pallas kernels, exchange_rims(): pl.pallas_call(rim_kernel, out_shape=jax.ShapeDtypeStruct((2, rows, feat)...  45.9 us
    all_to_all x1, waiting for transfers between devices, local(): lax.all_to_all(jnp.concatenate([queries, key_proj], axis=1), frame_axes,...  42.7 us
    pallas_call x1, Pallas kernels, spatial_rows(): pl.pallas_call(spatial_kernel, grid_spec=grid_spec, out_shape=jax.ShapeDt...  29.3 us
    all_to_all x1, waiting for transfers between devices, local(): lax.all_to_all(temporal.reshape(tok_count, feat_count), frame_axes, split...  25.1 us
    dot_general x1, matrix products, local(): jnp.einsum('tk,jkc->jtc', normed_all, w_full[1:], preferred_element_type=...  23.7 us
    all_to_all x1, waiting for transfers between devices, local(): lax.all_to_all(spatial, frame_axes, split_axis=0, concat_axis=0, tiled=True)  19.8 us
    convert_element_type x1, other arithmetic, layer_norm(): return (normal * (1.0 + mod_scale) + mod_shift).astype(jnp.bfloat16)  12.8 us
    dot_general x1, matrix products, local(): jnp.dot(flat_temporal, w_out_full, preferred_element_type=jnp.float32)  7.56 us
  transfers between devices with their start and end apart: 6, of which 4 were waited for; matrix products, arithmetic and copies ran while one was open for 19% of the time, Pallas kernels for 15%

profile of v5, /device:TPU:1, one launch (start us, length us, event | category | flops | bytes accessed | tf_op | source)
XLA Modules:
  0.0 312.9 jit_solution(13483401394801702427)
XLA Ops:
  11.4 45.9 %shard_map.73 = bf16[2,640,1536]{2,1,0:T(8,128)(2,1)} custom-call(bf16[640,1536]{1,0:T(8,128)(2,1)} %bitcast.38), custom_call_target="tpu_custom_call" | custom-call | bytes 157286400 | tf_op jit(solution)/shard_map/pallas_call | solution.py:172
  59.1 2.6 select_bitcast_fusion.1
  63.0 5.4 %fusion.3 = f32[1920]{0:T(1024)S(1)} fusion(f32[1920]{0:T(1024)S(1)} %broadcast_multiply_fusion, bf16[640,1536]{1,0:T(8,128)(2,1)S(1)} %get-tuple-element.10, bf16[640,1536]{1,0:T(8,128)(2,1)S(1)} %bitcast.40, bf16[640,1536]{1,0:T(8,128)(2,1)S(1)} %get-tuple-element.9), kind=kLoop, calls=%fused_computation.6 | loop fusion | flops 26540160 | bytes 5913600 | tf_op jit(solution)/shard_map/reduce_sum | solution.py:28
  68.4 12.8 %fusion.6 = bf16[1920,1536]{1,0:T(8,128)(2,1)} fusion(f32[1536]{0:T(1024)S(1)} %reduce.2, f32[1536]{0:T(1024)S(1)} %add_reduce_fusion, f32[1920]{0:T(1024)S(1)} %add_sqrt_fusion, f32[1920]{0:T(1024)S(1)} %broadcast_multiply_fusion, bf16[640,1536]{1,0:T(8,128)(2,1)S(1)} %get-tuple-element.10, bf16[640,1536]{1,0:T(8,128)(2,1)S(1)} %bitcast.41, ...), kind=kLoop, calls=%fused_computation.9 | loop fusion | flops 32440320 | bytes 11824128 | tf_op jit(solution)/shard_map/convert_element_type | solution.py:30
  81.2 7.5 %all-gather.9.cloned.1.call-done = bf16[6144,1152]{1,0:T(8,128)(2,1)} async-done(((bf16[768,1152]{1,0:T(8,128)(2,1)}), bf16[6144,1152]{1,0:T(8,128)(2,1)}) %all-gather.9.cloned.1.call-update) | async-done | bytes 14155792 | tf_op jit(solution)/shard_map/all_gather | solution.py:218
  90.3 5.7 %slice.53 = bf16[4608,1152]{1,0:T(8,128)(2,1)S(1)} slice(bf16[6144,1152]{1,0:T(8,128)(2,1)} %all-gather.9.cloned.1.call-done), slice={[1536:6144], [0:1152]} | slice | bytes 21233664 | tf_op jit(solution)/shard_map/slice | solution.py:235
  96.0 23.7 %fusion.7.k_ref.v_ref = bf16[3,1920,1152]{2,1,0:T(8,128)(2,1)} fusion(bf16[3,1536,1152]{2,1,0:T(8,128)(2,1)S(1)} %bitcast.43, bf16[1920,1536]{1,0:T(8,128)(2,1)S(1)} %bitcast.47), kind=kOutput, calls=%fused_computation.10 | convolution fusion | flops 20390952960 | bytes 29786112 | tf_op jit(solution)/shard_map/tk,jkc->jtc/dot_general | solution.py:234
  122.0 4.5 %fusion.14.q_ref = bf16[640,1536]{1,0:T(8,128)(2,1)} fusion(bf16[1536,384]{1,0:T(8,128)(2,1)S(1)} %slice_bitcast_fusion, bf16[1536,1152]{1,0:T(8,128)(2,1)S(1)} %slice.51, bf16[1920,1536]{1,0:T(8,128)(2,1)S(1)} %bitcast.47), kind=kOutput, calls=%fused_computation.21 | convolution fusion | flops 3030319104 | bytes 8650752 | tf_op jit(solution)/shard_map/dot_general | solution.py:231
  126.5 29.3 %shard_map.74 = bf16[640,1536]{1,0:T(8,128)(2,1)} custom-call(s32[30]{0:T(128)} %reshape_squeeze.3.list_ref, s32[2]{0:T(128)} %pad_add_fusion.scalar_ref, bf16[640,1536]{1,0:T(8,128)(2,1)} %fusion.14.q_ref, bf16[3,1920,1152]{2,1,0:T(8,128)(2,1)} %fusion.7.k_ref.v_ref, bf16[3,1920,1152]{2,1,0:T(8,128)(2,1)} %fusion.7.k_ref.v_ref), custom_call_target="tpu_custom_call" | custom-call | flops 3019898880 | bytes 15728640 | tf_op jit(solution)/shard_map/pallas_call | solution.py:98
  155.8 4.7 %all-to-all-start = ((bf16[8,80,1536]{2,1,0:T(8,128)(2,1)}), bf16[8,80,1536]{2,1,0:T(8,128)(2,1)S(1)}, u32[]{:S(2)}, u32[]{:S(2)}) async-start(bf16[8,80,1536]{2,1,0:T(8,128)(2,1)} %bitcast.44), calls=%async_computation | async-start | bytes 3932160 | tf_op jit(solution)/shard_map/all_to_all | solution.py:257
  165.6 19.8 %all-to-all-done = bf16[8,80,1536]{2,1,0:T(8,128)(2,1)S(1)} async-done(((bf16[8,80,1536]{2,1,0:T(8,128)(2,1)}), bf16[8,80,1536]{2,1,0:T(8,128)(2,1)S(1)}, u32[]{:S(2)}, u32[]{:S(2)}) %all-to-all-start) | async-done | bytes 1966112 | tf_op jit(solution)/shard_map/all_to_all | solution.py:257
  185.4 5.3 %all-to-all-start.1 = ((bf16[8,80,3072]{2,1,0:T(8,128)(2,1)}), bf16[8,80,3072]{2,1,0:T(8,128)(2,1)}, u32[]{:S(2)}, u32[]{:S(2)}) async-start(bf16[8,80,3072]{2,1,0:T(8,128)(2,1)} %pad_maximum_fusion.1), calls=%async_computation.1 | async-start | bytes 7864320 | tf_op jit(solution)/shard_map/all_to_all | solution.py:250
  191.4 2.8 reshape.81
  194.2 42.7 %all-to-all-done.1 = bf16[8,80,3072]{2,1,0:T(8,128)(2,1)} async-done(((bf16[8,80,3072]{2,1,0:T(8,128)(2,1)}), bf16[8,80,3072]{2,1,0:T(8,128)(2,1)}, u32[]{:S(2)}, u32[]{:S(2)}) %all-to-all-start.1) | async-done | bytes 3932192 | tf_op jit(solution)/shard_map/all_to_all | solution.py:250
  236.8 4.3 %fusion.34 = (bf16[640,1536]{1,0:T(8,128)(2,1)}, bf16[640,1536]{1,0:T(8,128)(2,1)}) fusion(bf16[640,3072]{1,0:T(8,128)(2,1)} %bitcast.15), kind=kLoop, calls=%fused_computation.52 | loop fusion | bytes 7864320 | tf_op jit(solution)/shard_map/slice | solution.py:262
  241.2 3.7 %reshape.82 = bf16[8,80,12,128]{3,2,1,0:T(8,128)(2,1)S(1)} reshape(bf16[640,1536]{1,0:T(8,128)(2,1)} %get-tuple-element.7) | data formatting | bytes 3932160 | tf_op jit(solution)/shard_map/reshape | solution.py:262
  244.9 4.8 %reshape.83 = bf16[8,80,12,128]{3,2,1,0:T(8,128)(2,1)} reshape(bf16[640,1536]{1,0:T(8,128)(2,1)} %get-tuple-element.8) | data formatting | bytes 3932160 | tf_op jit(solution)/shard_map/reshape | solution.py:263
  249.6 6.1 %fusion.20 = f32[80,12,8,8]{2,3,1,0:T(8,128)} fusion(bf16[8,80,12,128]{3,2,1,0:T(8,128)(2,1)} %reshape.83, bf16[8,80,12,128]{3,2,1,0:T(8,128)(2,1)S(1)} %reshape.82), kind=kOutput, calls=%fused_computation.25 | convolution fusion | flops 15728640 | bytes 4177920 | tf_op jit(solution)/shard_map/fphd,gphd->phfg/dot_general | solution.py:189
  255.7 3.1 %copy.29 = f32[80,12,8,8]{0,3,2,1:T(8,128)S(1)} copy(f32[80,12,8,8]{2,3,1,0:T(8,128)} %fusion.20) | data formatting | bytes 491520 | tf_op jit(solution)/shard_map/fphd,gphd->phfg/dot_general | solution.py:189
  261.8 2.9 fusion.13
  265.2 2.6 all_to_all.24
  267.7 5.1 %all-to-all-start.2 = ((bf16[8,80,1536]{2,1,0:T(8,128)(2,1)}), bf16[8,80,1536]{2,1,0:T(8,128)(2,1)}, u32[]{:S(2)}, u32[]{:S(2)}) async-start(bf16[8,80,1536]{2,1,0:T(8,128)(2,1)} %all_to_all.24), calls=%async_computation.2 | async-start | bytes 3932160 | tf_op jit(solution)/shard_map/all_to_all | solution.py:268
  272.8 25.1 %all-to-all-done.2 = bf16[8,80,1536]{2,1,0:T(8,128)(2,1)} async-done(((bf16[8,80,1536]{2,1,0:T(8,128)(2,1)}), bf16[8,80,1536]{2,1,0:T(8,128)(2,1)}, u32[]{:S(2)}, u32[]{:S(2)}) %all-to-all-start.2) | async-done | bytes 1966112 | tf_op jit(solution)/shard_map/all_to_all | solution.py:268
  297.9 7.6 %fusion.17 = bf16[1,640,1536]{2,1,0:T(8,128)(2,1)} fusion(bf16[640,1536]{1,0:T(8,128)(2,1)} %bitcast.20, bf16[1536,1536]{1,0:T(8,128)(2,1)} %all-gather.7.cloned.1.call-done), kind=kOutput, calls=%fused_computation.22 | convolution fusion | flops 3020881920 | bytes 8650752 | tf_op jit(solution)/shard_map/dot_general | solution.py:271
  (54 shorter events, 20.0 us)
Async XLA Ops:
  7.4 2.0 copy-start
  7.4 3.4 %copy-start.8 = (s32[1,5,6]{2,0,1:T(1,128)S(1)}, s32[1,5,6]{2,0,1:T(1,128)}, u32[]{:S(2)}) copy-start(s32[1,5,6]{2,0,1:T(1,128)} %param.12) | copy-start | bytes 364
  7.4 81.3 %all-gather.9.cloned.1.call-start = ((), (), s32[]{:S(2)}) async-start(), calls=%async_computation.5 | async-start | bytes 15925248 | tf_op jit(solution)/shard_map/all_gather | solution.py:218
  10.7 46.6 %copy-start.9 = (s32[1,8]{1,0:T(1,128)S(1)}, s32[1,8]{1,0:T(1,128)}, u32[]{:S(2)}) copy-start(s32[1,8]{1,0:T(1,128)} %param.13) | copy-start | bytes 100
  10.7 47.2 %copy-start.7 = (f32[1,1536]{1,0:T(1,128)S(1)}, f32[1,1536]{1,0:T(1,128)}, u32[]{:S(2)}) copy-start(f32[1,1536]{1,0:T(1,128)} %param.9) | copy-start | bytes 18436
  10.7 48.3 %copy-start.6 = (f32[1,1536]{1,0:T(1,128)S(1)}, f32[1,1536]{1,0:T(1,128)}, u32[]{:S(2)}) copy-start(f32[1,1536]{1,0:T(1,128)} %param.8) | copy-start | bytes 18436
  59.1 2.8 copy-start.2
  88.7 7.3 %slice-start = ((s8[5898240]{0:T(1024)(128)(4,1)}), s8[4194304]{0:T(1024)(128)(4,1)S(1)}, s32[]{:S(2)}) async-start(s8[5898240]{0:T(1024)(128)(4,1)} %bitcast.46), calls=%async_computation.6 | async-start | bytes 8388608
  90.2 5.7 %slice-start.1 = ((s8[5898240]{0:T(1024)(128)(4,1)}), s8[1703936]{0:T(1024)(128)(4,1)S(1)}, s32[]{:S(2)}) async-start(s8[5898240]{0:T(1024)(128)(4,1)} %bitcast.46), calls=%async_computation.7 | async-start | bytes 3407872
  155.8 4.7 %copy-start.5 = (bf16[384,1536]{1,0:T(8,128)(2,1)S(1)}, bf16[384,1536]{1,0:T(8,128)(2,1)}, u32[]{:S(2)}) copy-start(bf16[384,1536]{1,0:T(8,128)(2,1)} %param.11) | copy-start | bytes 3538948
  155.8 29.6 %all-to-all-start = ((bf16[8,80,1536]{2,1,0:T(8,128)(2,1)}), bf16[8,80,1536]{2,1,0:T(8,128)(2,1)S(1)}, u32[]{:S(2)}, u32[]{:S(2)}) async-start(bf16[8,80,1536]{2,1,0:T(8,128)(2,1)} %bitcast.44), calls=%async_computation | async-start | bytes 3932160 | tf_op jit(solution)/shard_map/all_to_all | solution.py:257
  160.4 30.2 %all-gather.5.cloned.1.call-start = ((), (), s32[]{:S(2)}) async-start(), calls=%async_computation.3 | async-start | bytes 1769472 | tf_op jit(solution)/shard_map/all_gather | solution.py:222
  161.3 2.1 copy-start.3
  185.4 51.4 %all-to-all-start.1 = ((bf16[8,80,3072]{2,1,0:T(8,128)(2,1)}), bf16[8,80,3072]{2,1,0:T(8,128)(2,1)}, u32[]{:S(2)}, u32[]{:S(2)}) async-start(bf16[8,80,3072]{2,1,0:T(8,128)(2,1)} %pad_maximum_fusion.1), calls=%async_computation.1 | async-start | bytes 7864320 | tf_op jit(solution)/shard_map/all_to_all | solution.py:250
  190.7 82.1 %all-gather.7.cloned.1.call-start = ((), (), s32[]{:S(2)}) async-start(), calls=%async_computation.4 | async-start | bytes 5898240 | tf_op jit(solution)/shard_map/all_gather | solution.py:223
  255.7 6.1 %copy-start.4 = (bf16[8,80,12,128]{3,2,1,0:T(8,128)(2,1)S(1)}, bf16[8,80,12,128]{3,2,1,0:T(8,128)(2,1)}, u32[]{:S(2)}) copy-start(bf16[8,80,12,128]{3,2,1,0:T(8,128)(2,1)} %reshape.81) | copy-start | bytes 5898244
  267.7 30.1 %all-to-all-start.2 = ((bf16[8,80,1536]{2,1,0:T(8,128)(2,1)}), bf16[8,80,1536]{2,1,0:T(8,128)(2,1)}, u32[]{:S(2)}, u32[]{:S(2)}) async-start(bf16[8,80,1536]{2,1,0:T(8,128)(2,1)} %all_to_all.24), calls=%async_computation.2 | async-start | bytes 3932160 | tf_op jit(solution)/shard_map/all_to_all | solution.py:268
  297.9 7.6 %copy-start.1 = (bf16[1536,1152]{1,0:T(8,128)(2,1)S(1)}, bf16[1536,1152]{1,0:T(8,128)(2,1)}, u32[]{:S(2)}) copy-start(bf16[1536,1152]{1,0:T(8,128)(2,1)} %param.10) | copy-start | bytes 10616836
Sparse Core Ops, SparseCore 0:
  10.9 77.7 all-gather.8
Sparse Core Ops, SparseCore 1:
  162.6 12.4 all-gather.4
  192.8 52.7 all-gather.6

commit v6 on v5

--- a/solution.py
+++ b/solution.py
@@ -110,14 +110,20 @@
 MESH_IDS = pl.DeviceIdType.MESH
 
 
-def rim_kernel(tok_ref, rim_ref, send_sem, recv_sem):
+def exchange_kernel(tok_ref, rim_ref, cross_ref, send_sem, recv_sem, cross_send, cross_recv, own_sem):
     n_piece = lax.axis_size("piece")
+    n_core = lax.axis_size("core")
+    n_frames = lax.axis_size("fy") * n_core
     piece = lax.axis_index("piece")
-    here = (lax.axis_index("fsdp"), piece, lax.axis_index("fy"), lax.axis_index("core"))
-    up = (here[0], piece - 1, here[2], here[3])
-    down = (here[0], piece + 1, here[2], here[3])
+    frame = lax.axis_index("fy") * n_core + lax.axis_index("core")
+    fsdp = lax.axis_index("fsdp")
+    here = (fsdp, piece, lax.axis_index("fy"), lax.axis_index("core"))
+    up = (fsdp, piece - 1, here[2], here[3])
+    down = (fsdp, piece + 1, here[2], here[3])
     has_up = piece > 0
     has_down = piece < n_piece - 1
+    per = tok_ref.shape[0] // n_frames
+    peers = [(frame + k) % n_frames for k in range(1, n_frames)]
     barrier = pltpu.get_barrier_semaphore()
 
     @pl.when(has_up)
@@ -128,8 +134,12 @@
     def _():
         pl.semaphore_signal(barrier, inc=1, device_id=down, device_id_type=MESH_IDS)
 
-    peers = (piece + n_piece - 1) // n_piece + (2 * n_piece - 2 - piece) // n_piece
-    pl.semaphore_wait(barrier, peers)
+    for d in peers:
+        pl.semaphore_signal(
+            barrier, inc=1, device_id=(fsdp, piece, d // n_core, d % n_core), device_id_type=MESH_IDS
+        )
+    rim_peers = (piece + n_piece - 1) // n_piece + (2 * n_piece - 2 - piece) // n_piece
+    pl.semaphore_wait(barrier, rim_peers + n_frames - 1)
 
     to_down = pltpu.make_async_remote_copy(
         src_ref=tok_ref,
@@ -156,6 +166,22 @@
     def _():
         to_up.start()
 
+    crosses = []
+    for k, d in enumerate(peers):
+        copy = pltpu.make_async_remote_copy(
+            src_ref=tok_ref.at[pl.ds(pl.multiple_of(d * per, 16), per)],
+            dst_ref=cross_ref.at[pl.ds(pl.multiple_of(frame * per, 16), per)],
+            send_sem=cross_send.at[k],
+            recv_sem=cross_recv.at[k],
+            device_id=(fsdp, piece, d // n_core, d % n_core),
+            device_id_type=MESH_IDS,
+        )
+        copy.start()
+        crosses.append(copy)
+    own_rows = pl.ds(pl.multiple_of(frame * per, 16), per)
+    own_copy = pltpu.make_async_copy(tok_ref.at[own_rows], cross_ref.at[own_rows], own_sem)
+    own_copy.start()
+
     @pl.when(has_down)
     def _():
         to_down.wait_send()
@@ -166,15 +192,28 @@
         to_up.wait_send()
         to_down.wait_recv()
 
-
-def exchange_rims(own):
+    for copy in crosses:
+        copy.wait()
+    own_copy.wait()
+
+
+def exchange_tokens(own):
     rows, feat = own.shape
     return pl.pallas_call(
-        rim_kernel,
-        out_shape=jax.ShapeDtypeStruct((2, rows, feat), own.dtype),
+        exchange_kernel,
+        out_shape=(
+            jax.ShapeDtypeStruct((2, rows, feat), own.dtype),
+            jax.ShapeDtypeStruct((rows, feat), own.dtype),
+        ),
         in_specs=[pl.BlockSpec(memory_space=pl.ANY)],
-        out_specs=pl.BlockSpec(memory_space=pl.ANY),
-        scratch_shapes=[pltpu.SemaphoreType.DMA((2,)), pltpu.SemaphoreType.DMA((2,))],
+        out_specs=(pl.BlockSpec(memory_space=pl.ANY), pl.BlockSpec(memory_space=pl.ANY)),
+        scratch_shapes=[
+            pltpu.SemaphoreType.DMA((2,)),
+            pltpu.SemaphoreType.DMA((2,)),
+            pltpu.SemaphoreType.DMA((8,)),
+            pltpu.SemaphoreType.DMA((8,)),
+            pltpu.SemaphoreType.DMA(()),
+        ],
         compiler_params=pltpu.CompilerParams(collective_id=0, has_side_effects=True),
         cost_estimate=pl.CostEstimate(flops=0, transcendentals=0, bytes_accessed=80 * rows * feat * 2),
     )(own)
@@ -208,7 +247,7 @@
     feat_count = tokens.shape[2]
     n_frames = lax.axis_size("fy") * lax.axis_size("core")
     own = tokens[0]
-    rims = exchange_rims(own)
+    rims, crossed = exchange_tokens(own)
     piece_index = lax.axis_index("piece")
     above = jnp.where(piece_index > 0, rims[0], jnp.zeros_like(own))
     below = jnp.where(piece_index < lax.axis_size("piece") - 1, rims[1], jnp.zeros_like(own))
@@ -228,17 +267,20 @@
     w_query = jnp.concatenate(
         [w_full[0], w_full[1, :, : feat_count - shard_cols]], axis=1
     )
-    queries = jnp.dot(
-        normed_all[tok_count : 2 * tok_count], w_query, preferred_element_type=jnp.float32
+    normed_cross = layer_norm(crossed, mod_scale[0], mod_shift[0])
+    w_key = jnp.concatenate(
+        [w_full[1, :, feat_count - shard_cols :], w_full[2, :, : 2 * shard_cols - feat_count]], axis=1
+    )
+    q_both = jnp.dot(
+        jnp.concatenate([normed_all[tok_count : 2 * tok_count], normed_cross], axis=0),
+        w_query,
+        preferred_element_type=jnp.float32,
     ).astype(jnp.bfloat16)
+    queries = q_both[:tok_count]
+    key_cross = jnp.dot(normed_cross, w_key, preferred_element_type=jnp.float32).astype(jnp.bfloat16)
     kv_all = jnp.einsum(
         "tk,jkc->jtc", normed_all, w_full[1:], preferred_element_type=jnp.float32
     ).astype(jnp.bfloat16)
-    key_cut = feat_count - shard_cols
-    own_kv = kv_all[:, tok_count : 2 * tok_count]
-    key_proj = jnp.concatenate(
-        [own_kv[0, :, key_cut:], own_kv[1, :, : feat_count - shard_cols + key_cut]], axis=1
-    )
     frame_index = lax.axis_index("fy") * lax.axis_size("core") + lax.axis_index("core")
     piece_index = lax.axis_index("piece")
     clip_counts = counts[0]
@@ -247,20 +289,13 @@
     first_tile = (piece_index * rows_here - 1) * TGW
     spatial = spatial_rows(queries, kv_all, neighbors[0], first_tile, count_here)
     frame_axes = ("fy", "core")
-    qk_part = lax.all_to_all(
-        jnp.concatenate([queries, key_proj], axis=1),
-        frame_axes,
-        split_axis=0,
-        concat_axis=0,
-        tiled=True,
-    )
     spatial_part = lax.all_to_all(spatial, frame_axes, split_axis=0, concat_axis=0, tiled=True)
     per_dev = tok_count // n_frames
     first_pos = piece_index * tok_count + frame_index * per_dev
     part_shape = (n_frames, per_dev, HEADS, HD)
     temporal = temporal_block(
-        qk_part[:, :feat_count].reshape(part_shape),
-        qk_part[:, feat_count:].reshape(part_shape),
+        q_both[tok_count:].reshape(part_shape),
+        key_cross.reshape(part_shape),
         spatial_part.reshape(part_shape),
         clip_counts,
         first_pos,

time: 314 us -> 260 us (0.83)
  waiting for transfers between devices: 95.6 us -> 38.2 us
  matrix products: 44.8 us -> 52.7 us
  starting transfers between devices: 15 us -> 9.41 us
    all_to_all x1 -> x0, waiting for transfers between devices: 42.7 us -> none  [local(): lax.all_to_all(jnp.concatenate([queries, key_proj], axis=1), frame_axes,...]
    all_to_all x1, waiting for transfers between devices: 19.8 us -> 0.01 us  [local(): lax.all_to_all(spatial, frame_axes, split_axis=0, concat_axis=0, tiled=True)]
    dot_general x1 -> x2, matrix products: 4.51 us -> 11.1 us  [the longest x1 6.6 us: local(): jnp.dot(jnp.concatenate([normed_all[tok_count:2 * tok_count], normed_cros...]
    all_gather x1, waiting for transfers between devices: 7.47 us -> 13.1 us  [local(): w_pieces = lax.all_gather(w_half, ('fsdp', 'core'), axis=0, tiled=False)]
    all_to_all x1 -> x0, starting transfers between devices: 5.31 us -> none  [local(): lax.all_to_all(jnp.concatenate([queries, key_proj], axis=1), frame_axes,...]
    slice x2 -> x3, local copies, waits for them, and re-layouts: 6.11 us -> 2.35 us  [the longest x1 2.17 us: local(): queries = q_both[:tok_count]]
    pallas_call x1, Pallas kernels: 45.9 us -> 49.2 us  [exchange_tokens(): pl.pallas_call(exchange_kernel, out_shape=(jax.ShapeDtypeStruct((2, rows,...]
    convert_element_type x1 -> x2, other arithmetic: 12.8 us -> 13.3 us  [layer_norm(): return (normal * (1.0 + mod_scale) + mod_shift).astype(jnp.bfloat16)]
  transfers between devices with their start and end apart: 6 -> 5, of which waited for: 4 -> 2; matrix products, arithmetic and copies ran while one was open for 19% -> 38% of each run, Pallas kernels for 15% -> 30%
where the time goes in v6:
time: 260 us
  Pallas kernels  78.3 us (30%)
  matrix products  52.7 us (20%)
  local copies, waits for them, and re-layouts  42.7 us (16%)
  waiting for transfers between devices  38.2 us (15%)
  other arithmetic  25 us (10%)
  between operations  13.3 us (5%)
  starting transfers between devices  9.41 us (4%)
    pallas_call x1, Pallas kernels, exchange_tokens(): pl.pallas_call(exchange_kernel, out_shape=(jax.ShapeDtypeStruct((2, rows,...  49.2 us
    pallas_call x1, Pallas kernels, spatial_rows(): pl.pallas_call(spatial_kernel, grid_spec=grid_spec, out_shape=jax.ShapeDt...  29.2 us
    dot_general x1, matrix products, local(): jnp.einsum('tk,jkc->jtc', normed_all, w_full[1:], preferred_element_type=...  25.2 us
    all_to_all x1, waiting for transfers between devices, local(): lax.all_to_all(temporal.reshape(tok_count, feat_count), frame_axes, split...  25 us
    convert_element_type x2, other arithmetic, layer_norm(): return (normal * (1.0 + mod_scale) + mod_shift).astype(jnp.bfloat16)  13.3 us
    all_gather x1, waiting for transfers between devices, local(): w_pieces = lax.all_gather(w_half, ('fsdp', 'core'), axis=0, tiled=False)  13.1 us
    dot_general x1, matrix products, local(): jnp.dot(flat_temporal, w_out_full, preferred_element_type=jnp.float32)  7.56 us
    dot_general x1, matrix products, local(): jnp.dot(jnp.concatenate([normed_all[tok_count:2 * tok_count], normed_cros...  6.6 us
  transfers between devices with their start and end apart: 5, of which 2 were waited for; matrix products, arithmetic and copies ran while one was open for 38% of the time, Pallas kernels for 30%

profile of v6, /device:TPU:1, one launch (start us, length us, event | category | flops | bytes accessed | tf_op | source)
XLA Modules:
  0.0 259.6 jit_solution(16155689851408637052)
XLA Ops:
  10.2 49.2 %shard_map.73 = (bf16[2,640,1536]{2,1,0:T(8,128)(2,1)}, bf16[640,1536]{1,0:T(8,128)(2,1)}) custom-call(bf16[640,1536]{1,0:T(8,128)(2,1)} %bitcast.39), custom_call_target="tpu_custom_call" | custom-call | bytes 157286400 | tf_op jit(solution)/shard_map/pallas_call | solution.py:202
  59.5 2.5 select_bitcast_fusion.1
  63.3 5.4 %fusion.3 = f32[1920]{0:T(1024)S(1)} fusion(f32[1920]{0:T(1024)S(1)} %broadcast_multiply_fusion, bf16[640,1536]{1,0:T(8,128)(2,1)S(1)} %get-tuple-element.14, bf16[640,1536]{1,0:T(8,128)(2,1)S(1)} %bitcast.41, bf16[640,1536]{1,0:T(8,128)(2,1)S(1)} %get-tuple-element.13), kind=kLoop, calls=%fused_computation.6 | loop fusion | flops 26540160 | bytes 5913600 | tf_op jit(solution)/shard_map/reduce_sum | solution.py:28
  68.7 11.2 %fusion.6 = bf16[1920,1536]{1,0:T(8,128)(2,1)S(1)} fusion(f32[1536]{0:T(1024)S(1)} %reduce.2, f32[1536]{0:T(1024)S(1)} %add_reduce_fusion, f32[1920]{0:T(1024)S(1)} %add_sqrt_fusion, f32[1920]{0:T(1024)S(1)} %broadcast_multiply_fusion, bf16[640,1536]{1,0:T(8,128)(2,1)S(1)} %get-tuple-element.14, bf16[640,1536]{1,0:T(8,128)(2,1)S(1)} %bitcast.42, ...), kind=kLoop, calls=%fused_computation.9 | loop fusion | flops 32440320 | bytes 11824128 | tf_op jit(solution)/shard_map/convert_element_type | solution.py:30
  79.9 2.5 copy-done.4
  88.7 13.1 %all-gather.9.cloned.1.call-done = bf16[6144,1152]{1,0:T(8,128)(2,1)} async-done(((bf16[768,1152]{1,0:T(8,128)(2,1)}), bf16[6144,1152]{1,0:T(8,128)(2,1)}) %all-gather.9.cloned.1.call-update) | async-done | bytes 14155792 | tf_op jit(solution)/shard_map/all_gather | solution.py:257
  101.8 4.0 %slice-done = bf16[4608,1152]{1,0:T(8,128)(2,1)S(1)} async-done(((bf16[6144,1152]{1,0:T(8,128)(2,1)}), bf16[4608,1152]{1,0:T(8,128)(2,1)S(1)}, s32[]{:S(2)}) %slice-start) | async-done | bytes 10616856 | tf_op jit(solution)/shard_map/slice | solution.py:282
  105.9 25.2 %fusion.7.k_ref.v_ref = bf16[3,1920,1152]{2,1,0:T(8,128)(2,1)} fusion(bf16[3,1536,1152]{2,1,0:T(8,128)(2,1)S(1)} %bitcast.45, bf16[1920,1536]{1,0:T(8,128)(2,1)} %copy-done.4), kind=kOutput, calls=%fused_computation.10 | convolution fusion | flops 20390952960 | bytes 29786112 | tf_op jit(solution)/shard_map/tk,jkc->jtc/dot_general | solution.py:281
  132.5 2.4 slice.48
  135.7 6.6 %convolution_convert_fusion.1 = bf16[1280,1536]{1,0:T(8,128)(2,1)S(1)} fusion(bf16[1536,384]{1,0:T(8,128)(2,1)S(1)} %slice_bitcast_fusion.2, bf16[1536,1152]{1,0:T(8,128)(2,1)S(1)} %slice.48, bf16[640,1536]{1,0:T(8,128)(2,1)S(1)} %copy-done.5, bf16[640,1536]{1,0:T(8,128)(2,1)S(1)} %slice-done.1), kind=kOutput, calls=%fused_computation.11 | convolution fusion | flops 6059065344 | bytes 12582912 | tf_op jit(solution)/shard_map/dot_general | solution.py:274
  144.5 29.2 %shard_map.74 = bf16[640,1536]{1,0:T(8,128)(2,1)} custom-call(s32[30]{0:T(128)} %reshape_squeeze.3.list_ref, s32[2]{0:T(128)} %pad_add_fusion.scalar_ref, bf16[640,1536]{1,0:T(8,128)(2,1)} %get-tuple-element.11.q_ref, bf16[3,1920,1152]{2,1,0:T(8,128)(2,1)} %fusion.7.k_ref.v_ref, bf16[3,1920,1152]{2,1,0:T(8,128)(2,1)} %fusion.7.k_ref.v_ref), custom_call_target="tpu_custom_call" | custom-call | flops 3019898880 | bytes 15728640 | tf_op jit(solution)/shard_map/pallas_call | solution.py:98
  173.6 4.5 %all-to-all-start = ((bf16[8,80,1536]{2,1,0:T(8,128)(2,1)}), bf16[8,80,1536]{2,1,0:T(8,128)(2,1)}, u32[]{:S(2)}, u32[]{:S(2)}) async-start(bf16[8,80,1536]{2,1,0:T(8,128)(2,1)} %bitcast.46), calls=%async_computation | async-start | bytes 3932160 | tf_op jit(solution)/shard_map/all_to_all | solution.py:292
  178.2 2.8 %slice_bitcast_fusion.1 = (bf16[1536,768]{1,0:T(8,128)(2,1)S(1)}, bf16[1536,768]{1,0:T(8,128)(2,1)S(1)}) fusion(bf16[4,1536,1152]{2,1,0:T(8,128)(2,1)} %bitcast.44), kind=kLoop, calls=%fused_computation.38 | loop fusion | bytes 9437184 | tf_op jit(solution)/shard_map/squeeze | solution.py:272
  181.1 4.5 %fusion.26 = bf16[640,1536]{1,0:T(8,128)(2,1)} fusion(bf16[640,1536]{1,0:T(8,128)(2,1)S(1)} %copy-done.6, bf16[1536,768]{1,0:T(8,128)(2,1)S(1)} %get-tuple-element.10, bf16[1536,768]{1,0:T(8,128)(2,1)S(1)} %get-tuple-element.9), kind=kOutput, calls=%fused_computation.35 | convolution fusion | flops 3030319104 | bytes 8650752 | tf_op jit(solution)/shard_map/dot_general | solution.py:280
  185.6 3.7 %reshape.88 = bf16[8,80,12,128]{3,2,1,0:T(8,128)(2,1)S(1)} reshape(bf16[640,1536]{1,0:T(8,128)(2,1)} %fusion.26) | data formatting | bytes 3932160 | tf_op jit(solution)/shard_map/reshape | solution.py:298
  189.3 4.7 %reshape.87 = bf16[8,80,12,128]{3,2,1,0:T(8,128)(2,1)} reshape(bf16[640,1536]{1,0:T(8,128)(2,1)} %get-tuple-element.12) | data formatting | bytes 3932160 | tf_op jit(solution)/shard_map/reshape | solution.py:297
  194.1 6.0 %fusion.31 = f32[80,12,8,8]{2,3,1,0:T(8,128)} fusion(bf16[8,80,12,128]{3,2,1,0:T(8,128)(2,1)S(1)} %reshape.88, bf16[8,80,12,128]{3,2,1,0:T(8,128)(2,1)} %reshape.87), kind=kOutput, calls=%fused_computation.40 | convolution fusion | flops 15728640 | bytes 4177920 | tf_op jit(solution)/shard_map/fphd,gphd->phfg/dot_general | solution.py:228
  200.1 3.0 %copy.31 = f32[80,12,8,8]{0,3,2,1:T(8,128)S(1)} copy(f32[80,12,8,8]{2,3,1,0:T(8,128)} %fusion.31) | data formatting | bytes 491520 | tf_op jit(solution)/shard_map/fphd,gphd->phfg/dot_general | solution.py:228
  206.0 3.7 %reshape.86 = bf16[8,80,12,128]{3,2,1,0:T(8,128)(2,1)S(1)} reshape(bf16[8,80,1536]{2,1,0:T(8,128)(2,1)} %all-to-all-done) | data formatting | bytes 3932160 | tf_op jit(solution)/shard_map/reshape | solution.py:299
  209.8 2.9 %fusion.25 = bf16[8,80,12,128]{3,0,2,1:T(8,128)(2,1)S(1)} fusion(bf16[80,12,8,8]{3,2,1,0:T(8,128)(2,1)} %copy.33, bf16[8,80,12,128]{3,2,1,0:T(8,128)(2,1)S(1)} %reshape.86, f32[8,80,12]{0,2,1:T(8,128)S(1)} %copy.34), kind=kOutput, calls=%fused_computation.33 | convolution fusion | flops 17694720 | bytes 4085760 | tf_op jit(solution)/shard_map/phfg,gphd->fphd/dot_general | solution.py:238
  213.1 2.6 all_to_all.16
  215.7 4.8 %all-to-all-start.1 = ((bf16[8,80,1536]{2,1,0:T(8,128)(2,1)}), bf16[8,80,1536]{2,1,0:T(8,128)(2,1)}, u32[]{:S(2)}, u32[]{:S(2)}) async-start(bf16[8,80,1536]{2,1,0:T(8,128)(2,1)} %all_to_all.16), calls=%async_computation.1 | async-start | bytes 3932160 | tf_op jit(solution)/shard_map/all_to_all | solution.py:303
  220.5 25.0 %all-to-all-done.1 = bf16[8,80,1536]{2,1,0:T(8,128)(2,1)} async-done(((bf16[8,80,1536]{2,1,0:T(8,128)(2,1)}), bf16[8,80,1536]{2,1,0:T(8,128)(2,1)}, u32[]{:S(2)}, u32[]{:S(2)}) %all-to-all-start.1) | async-done | bytes 1966112 | tf_op jit(solution)/shard_map/all_to_all | solution.py:303
  245.5 7.6 %fusion.29 = bf16[1,640,1536]{2,1,0:T(8,128)(2,1)} fusion(bf16[640,1536]{1,0:T(8,128)(2,1)} %bitcast.18, bf16[1536,1536]{1,0:T(8,128)(2,1)} %all-gather.7.cloned.1.call-done), kind=kOutput, calls=%fused_computation.36 | convolution fusion | flops 3020881920 | bytes 8650752 | tf_op jit(solution)/shard_map/dot_general | solution.py:306
  (57 shorter events, 19.2 us)
Async XLA Ops:
  6.5 2.2 copy-start
  6.5 82.2 %all-gather.5.cloned.1.call-start = ((), (), s32[]{:S(2)}) async-start(), calls=%async_computation.2 | async-start | bytes 1769472 | tf_op jit(solution)/shard_map/all_gather | solution.py:261
  8.6 50.8 %copy-start.8 = (f32[1,1536]{1,0:T(1,128)S(1)}, f32[1,1536]{1,0:T(1,128)}, u32[]{:S(2)}) copy-start(f32[1,1536]{1,0:T(1,128)} %param.9) | copy-start | bytes 18436
  8.6 50.8 %copy-start.7 = (f32[1,1536]{1,0:T(1,128)S(1)}, f32[1,1536]{1,0:T(1,128)}, u32[]{:S(2)}) copy-start(f32[1,1536]{1,0:T(1,128)} %param.8) | copy-start | bytes 18436
  8.7 93.2 %all-gather.9.cloned.1.call-start = ((), (), s32[]{:S(2)}) async-start(), calls=%async_computation.4 | async-start | bytes 15925248 | tf_op jit(solution)/shard_map/all_gather | solution.py:257
  10.2 210.4 %all-gather.7.cloned.1.call-start = ((), (), s32[]{:S(2)}) async-start(), calls=%async_computation.3 | async-start | bytes 5898240 | tf_op jit(solution)/shard_map/all_gather | solution.py:262
  59.5 2.7 %copy-start.2 = (bf16[1,640,1536]{2,1,0:T(8,128)(2,1)S(1)}, bf16[1,640,1536]{2,1,0:T(8,128)(2,1)}, u32[]{:S(2)}) copy-start(bf16[1,640,1536]{2,1,0:T(8,128)(2,1)} %param.7) | copy-start | bytes 5898244
  79.9 2.5 copy-start.4
  82.4 0.7 copy-start.9
  82.4 1.3 copy-start.10
  82.4 3.2 %copy-start.3 = (bf16[640,1536]{1,0:T(8,128)(2,1)S(1)}, bf16[640,1536]{1,0:T(8,128)(2,1)}, u32[]{:S(2)}) copy-start(bf16[640,1536]{1,0:T(8,128)(2,1)} %get-tuple-element.8) | copy-start | bytes 5898244
  101.8 4.0 %slice-start = ((bf16[6144,1152]{1,0:T(8,128)(2,1)}), bf16[4608,1152]{1,0:T(8,128)(2,1)S(1)}, s32[]{:S(2)}) async-start(bf16[6144,1152]{1,0:T(8,128)(2,1)} %all-gather.9.cloned.1.call-done), calls=%async_computation.5 | async-start | bytes 21233664 | tf_op jit(solution)/shard_map/slice | solution.py:282
  132.4 2.6 %slice-start.1 = ((bf16[1920,1536]{1,0:T(8,128)(2,1)}), bf16[640,1536]{1,0:T(8,128)(2,1)S(1)}, s32[]{:S(2)}) async-start(bf16[1920,1536]{1,0:T(8,128)(2,1)} %copy-done.4), calls=%async_computation.6 | async-start | bytes 3932160 | tf_op jit(solution)/shard_map/slice | solution.py:275
  132.4 3.2 %copy-start.5 = (bf16[640,1536]{1,0:T(8,128)(2,1)S(1)}, bf16[640,1536]{1,0:T(8,128)(2,1)}, u32[]{:S(2)}) copy-start(bf16[640,1536]{1,0:T(8,128)(2,1)} %fusion.21) | copy-start | bytes 5898244
  173.6 32.4 %all-to-all-start = ((bf16[8,80,1536]{2,1,0:T(8,128)(2,1)}), bf16[8,80,1536]{2,1,0:T(8,128)(2,1)}, u32[]{:S(2)}, u32[]{:S(2)}) async-start(bf16[8,80,1536]{2,1,0:T(8,128)(2,1)} %bitcast.46), calls=%async_computation | async-start | bytes 3932160 | tf_op jit(solution)/shard_map/all_to_all | solution.py:292
  178.1 3.0 %copy-start.6 = (bf16[640,1536]{1,0:T(8,128)(2,1)S(1)}, bf16[640,1536]{1,0:T(8,128)(2,1)}, u32[]{:S(2)}) copy-start(bf16[640,1536]{1,0:T(8,128)(2,1)} %fusion.21) | copy-start | bytes 5898244
  215.7 29.8 %all-to-all-start.1 = ((bf16[8,80,1536]{2,1,0:T(8,128)(2,1)}), bf16[8,80,1536]{2,1,0:T(8,128)(2,1)}, u32[]{:S(2)}, u32[]{:S(2)}) async-start(bf16[8,80,1536]{2,1,0:T(8,128)(2,1)} %all_to_all.16), calls=%async_computation.1 | async-start | bytes 3932160 | tf_op jit(solution)/shard_map/all_to_all | solution.py:303
  245.5 7.6 %copy-start.1 = (bf16[1536,1152]{1,0:T(8,128)(2,1)S(1)}, bf16[1536,1152]{1,0:T(8,128)(2,1)}, u32[]{:S(2)}) copy-start(bf16[1536,1152]{1,0:T(8,128)(2,1)} %param.10) | copy-start | bytes 10616836
Sparse Core Ops, SparseCore 0:
  9.0 15.5 all-gather.4
  26.3 75.4 all-gather.8
  103.5 52.7 all-gather.6

commit v7 on v6

--- a/solution.py
+++ b/solution.py
@@ -219,27 +219,57 @@
     )(own)
 
 
-def temporal_block(query_part, key_part, spatial_part, clip_counts, first_pos):
-    n_frames, per_dev = query_part.shape[0], query_part.shape[1]
+def temporal_kernel(scalar_ref, q_ref, k_ref, s_ref, o_ref):
     scaling = 1.0 / math.sqrt(HD)
-    position = first_pos + jnp.arange(per_dev, dtype=jnp.int32)
-    live_mask = (position[:, None] < clip_counts[None, :])[:, None, None, :]
-    scores = (
-        jnp.einsum(
-            "fphd,gphd->phfg", query_part, key_part, preferred_element_type=jnp.float32
-        )
-        * scaling
-    )
-    scores = jnp.where(live_mask, scores, -1e30)
-    row_max = jnp.max(scores, axis=-1, keepdims=True)
-    exp_terms = jnp.where(live_mask, jnp.exp(scores - row_max), 0.0)
-    denominator = jnp.sum(exp_terms, axis=-1, keepdims=True)
-    weights = exp_terms.astype(jnp.bfloat16)
-    summed = jnp.einsum(
-        "phfg,gphd->fphd", weights, spatial_part, preferred_element_type=jnp.float32
-    )
-    result = summed / jnp.transpose(denominator, (2, 0, 1, 3))
-    return result.astype(jnp.bfloat16)
+    n_frames = scalar_ref.shape[0] - 1
+    per = q_ref.shape[0] // n_frames
+    position = scalar_ref[0] + lax.broadcasted_iota(jnp.int32, (per, 1), 0)
+    live = [position < scalar_ref[1 + g] for g in range(n_frames)]
+    keys = [k_ref[g * per : (g + 1) * per, :].astype(jnp.float32) for g in range(n_frames)]
+    for f in range(n_frames):
+        query = q_ref[f * per : (f + 1) * per, :].astype(jnp.float32)
+        scores = []
+        row_max = None
+        for g in range(n_frames):
+            score = jnp.sum(query * keys[g], axis=-1, keepdims=True) * scaling
+            score = jnp.where(live[g], score, -1e30)
+            row_max = score if row_max is None else jnp.maximum(row_max, score)
+            scores.append(score)
+        denominator = None
+        summed = None
+        for g in range(n_frames):
+            exp_term = jnp.where(live[g], jnp.exp(scores[g] - row_max), 0.0)
+            denominator = exp_term if denominator is None else denominator + exp_term
+            weight = exp_term.astype(jnp.bfloat16).astype(jnp.float32)
+            term = weight * s_ref[g * per : (g + 1) * per, :].astype(jnp.float32)
+            summed = term if summed is None else summed + term
+        o_ref[f * per : (f + 1) * per, :] = (summed / denominator).astype(o_ref.dtype)
+
+
+def temporal_rows(q_src, q_block, keys, spatial_part, clip_counts, first_pos):
+    rows, feat = keys.shape
+    n_frames = clip_counts.shape[0]
+    scalars = jnp.concatenate([first_pos.reshape(1), clip_counts]).astype(jnp.int32)
+    grid_spec = pltpu.PrefetchScalarGridSpec(
+        num_scalar_prefetch=1,
+        grid=(feat // HD,),
+        in_specs=[
+            pl.BlockSpec((rows, HD), lambda h, sc: (q_block, h)),
+            pl.BlockSpec((rows, HD), lambda h, sc: (0, h)),
+            pl.BlockSpec((rows, HD), lambda h, sc: (0, h)),
+        ],
+        out_specs=pl.BlockSpec((rows, HD), lambda h, sc: (0, h)),
+    )
+    return pl.pallas_call(
+        temporal_kernel,
+        grid_spec=grid_spec,
+        out_shape=jax.ShapeDtypeStruct((rows, feat), jnp.bfloat16),
+        cost_estimate=pl.CostEstimate(
+            flops=4 * rows * n_frames * feat,
+            transcendentals=rows * n_frames * feat // HD,
+            bytes_accessed=4 * rows * feat * 2,
+        ),
+    )(scalars, q_src, keys, spatial_part)
 
 
 def local(tokens, mod_scale, mod_shift, w_qkv, w_out, neighbors, counts):
@@ -292,17 +322,8 @@
     spatial_part = lax.all_to_all(spatial, frame_axes, split_axis=0, concat_axis=0, tiled=True)
     per_dev = tok_count // n_frames
     first_pos = piece_index * tok_count + frame_index * per_dev
-    part_shape = (n_frames, per_dev, HEADS, HD)
-    temporal = temporal_block(
-        q_both[tok_count:].reshape(part_shape),
-        key_cross.reshape(part_shape),
-        spatial_part.reshape(part_shape),
-        clip_counts,
-        first_pos,
-    )
-    flat_temporal = lax.all_to_all(
-        temporal.reshape(tok_count, feat_count), frame_axes, split_axis=0, concat_axis=0, tiled=True
-    )
+    temporal = temporal_rows(q_both, 1, key_cross, spatial_part, clip_counts, first_pos)
+    flat_temporal = lax.all_to_all(temporal, frame_axes, split_axis=0, concat_axis=0, tiled=True)
     projected = jnp.dot(flat_temporal, w_out_full, preferred_element_type=jnp.float32)
     return projected.astype(jnp.bfloat16).reshape(1, tok_count, feat_count)
 

time: 260 us -> 270 us (1.038)
  Pallas kernels: 78.3 us -> 95.5 us
  local copies, waits for them, and re-layouts: 42.7 us -> 25.5 us
  waiting for transfers between devices: 38.2 us -> 54.4 us
  matrix products: 52.7 us -> 46.5 us
    pallas_call x0 -> x1, Pallas kernels: none -> 17.2 us  [temporal_rows(): pl.pallas_call(temporal_kernel, grid_spec=grid_spec, out_shape=jax.ShapeD...]
    all_to_all x1, waiting for transfers between devices: 0.01 us -> 16.9 us  [local(): lax.all_to_all(spatial, frame_axes, split_axis=0, concat_axis=0, tiled=True)]
    reshape x3 -> x0, local copies, waits for them, and re-layouts: 12.2 us -> none  [the longest x1 4.75 us: local(): q_both[tok_count:].reshape(part_shape)]
    dot_general x2 -> x0, matrix products: 8.92 us -> none  [the longest x1 5.98 us: temporal_block(): jnp.einsum('fphd,gphd->phfg', query_part, key_part, preferred_element_typ...]
    dot_general x1 -> x0, local copies, waits for them, and re-layouts: 2.98 us -> none  [temporal_block(): jnp.einsum('fphd,gphd->phfg', query_part, key_part, preferred_element_typ...]
    convert_element_type x2 -> x0, local copies, waits for them, and re-layouts: 2.74 us -> none  [the longest x1 2.32 us: temporal_block(): weights = exp_terms.astype(jnp.bfloat16)]
    dot_general x1, matrix products: 25.2 us -> 27.9 us  [local(): jnp.einsum('tk,jkc->jtc', normed_all, w_full[1:], preferred_element_type=...]
    unnamed x22 -> x40, local copies, waits for them, and re-layouts: 4.12 us -> 6.28 us
  transfers between devices with their start and end apart: 5 -> 5, of which waited for: 2 -> 3; matrix products, arithmetic and copies ran while one was open for 38% -> 30% of each run, Pallas kernels for 30% -> 35%
where the time goes in v7:
time: 270 us
  Pallas kernels  95.5 us (35%)
  waiting for transfers between devices  54.4 us (20%)
  matrix products  46.5 us (17%)
  local copies, waits for them, and re-layouts  25.5 us (9%)
  other arithmetic  25.2 us (9%)
  between operations  13.3 us (5%)
  starting transfers between devices  9.65 us (4%)
    pallas_call x1, Pallas kernels, exchange_tokens(): pl.pallas_call(exchange_kernel, out_shape=(jax.ShapeDtypeStruct((2, rows,...  49.2 us
    pallas_call x1, Pallas kernels, spatial_rows(): pl.pallas_call(spatial_kernel, grid_spec=grid_spec, out_shape=jax.ShapeDt...  29.1 us
    dot_general x1, matrix products, local(): jnp.einsum('tk,jkc->jtc', normed_all, w_full[1:], preferred_element_type=...  27.9 us
    all_to_all x1, waiting for transfers between devices, local(): lax.all_to_all(temporal, frame_axes, split_axis=0, concat_axis=0, tiled=T...  25.1 us
    pallas_call x1, Pallas kernels, temporal_rows(): pl.pallas_call(temporal_kernel, grid_spec=grid_spec, out_shape=jax.ShapeD...  17.2 us
    all_to_all x1, waiting for transfers between devices, local(): lax.all_to_all(spatial, frame_axes, split_axis=0, concat_axis=0, tiled=True)  16.9 us
    convert_element_type x2, other arithmetic, layer_norm(): return (normal * (1.0 + mod_scale) + mod_shift).astype(jnp.bfloat16)  13.3 us
    all_gather x1, waiting for transfers between devices, local(): w_pieces = lax.all_gather(w_half, ('fsdp', 'core'), axis=0, tiled=False)  12.4 us
  transfers between devices with their start and end apart: 5, of which 3 were waited for; matrix products, arithmetic and copies ran while one was open for 30% of the time, Pallas kernels for 35%

profile of v7, /device:TPU:1, one launch (start us, length us, event | category | flops | bytes accessed | tf_op | source)
XLA Modules:
  0.0 270.1 jit_solution(11572883143912580580)
XLA Ops:
  6.5 2.1 constant_dynamic-slice_fusion
  10.2 49.2 %shard_map.73 = (bf16[2,640,1536]{2,1,0:T(8,128)(2,1)}, bf16[640,1536]{1,0:T(8,128)(2,1)}) custom-call(bf16[640,1536]{1,0:T(8,128)(2,1)} %bitcast.32), custom_call_target="tpu_custom_call" | custom-call | bytes 157286400 | tf_op jit(solution)/shard_map/pallas_call | solution.py:202
  59.5 2.5 select_bitcast_fusion.1
  63.3 5.4 %fusion.2 = f32[1920]{0:T(1024)S(1)} fusion(f32[1920]{0:T(1024)S(1)} %broadcast_multiply_fusion, bf16[640,1536]{1,0:T(8,128)(2,1)S(1)} %get-tuple-element.12, bf16[640,1536]{1,0:T(8,128)(2,1)S(1)} %bitcast.34, bf16[640,1536]{1,0:T(8,128)(2,1)S(1)} %get-tuple-element.11), kind=kLoop, calls=%fused_computation.5 | loop fusion | flops 26540160 | bytes 5913600 | tf_op jit(solution)/shard_map/reduce_sum | solution.py:28
  68.7 11.2 %fusion.5 = bf16[1920,1536]{1,0:T(8,128)(2,1)S(1)} fusion(f32[1536]{0:T(1024)S(1)} %reduce.1, f32[1536]{0:T(1024)S(1)} %add_reduce_fusion, f32[1920]{0:T(1024)S(1)} %add_sqrt_fusion, f32[1920]{0:T(1024)S(1)} %broadcast_multiply_fusion, bf16[640,1536]{1,0:T(8,128)(2,1)S(1)} %get-tuple-element.12, bf16[640,1536]{1,0:T(8,128)(2,1)S(1)} %bitcast.35, ...), kind=kLoop, calls=%fused_computation.8 | loop fusion | flops 32440320 | bytes 11824128 | tf_op jit(solution)/shard_map/convert_element_type | solution.py:30
  79.9 2.4 copy-done.4
  87.3 2.1 fusion.20
  89.4 12.4 %all-gather.9.cloned.1.call-done = bf16[6144,1152]{1,0:T(8,128)(2,1)} async-done(((bf16[768,1152]{1,0:T(8,128)(2,1)}), bf16[6144,1152]{1,0:T(8,128)(2,1)}) %all-gather.9.cloned.1.call-update) | async-done | bytes 14155792 | tf_op jit(solution)/shard_map/all_gather | solution.py:287
  101.8 1.5 slice_bitcast_fusion.2
  103.4 2.4 slice.44
  106.1 6.6 %convolution_convert_fusion.1.q_ref = bf16[1280,1536]{1,0:T(8,128)(2,1)S(1)} fusion(bf16[1536,384]{1,0:T(8,128)(2,1)S(1)} %slice_bitcast_fusion.2, bf16[1536,1152]{1,0:T(8,128)(2,1)S(1)} %slice.44, bf16[640,1536]{1,0:T(8,128)(2,1)S(1)} %copy-done.7, bf16[640,1536]{1,0:T(8,128)(2,1)S(1)} %copy-done.9), kind=kOutput, calls=%fused_computation.10 | convolution fusion | flops 6059065344 | bytes 12582912 | tf_op jit(solution)/shard_map/dot_general | solution.py:304
  112.7 1.9 copy-done.5
  114.6 1.4 slice.48.q_ref
  116.1 4.9 %slice.49 = bf16[4608,1152]{1,0:T(8,128)(2,1)} slice(bf16[6144,1152]{1,0:T(8,128)(2,1)S(1)} %bitcast.39), slice={[1536:6144], [0:1152]} | slice | bytes 21233664 | tf_op jit(solution)/shard_map/slice | solution.py:312
  121.0 27.9 %fusion.6.k_ref.v_ref = bf16[3,1920,1152]{2,1,0:T(8,128)(2,1)} fusion(bf16[3,1536,1152]{2,1,0:T(8,128)(2,1)} %bitcast.40, bf16[1920,1536]{1,0:T(8,128)(2,1)S(1)} %bitcast.42), kind=kOutput, calls=%fused_computation.9 | convolution fusion | flops 20390952960 | bytes 29786112 | tf_op jit(solution)/shard_map/tk,jkc->jtc/dot_general | solution.py:311
  148.9 29.1 %shard_map.74 = bf16[640,1536]{1,0:T(8,128)(2,1)} custom-call(s32[30]{0:T(128)} %reshape_squeeze.3.list_ref, s32[2]{0:T(128)} %pad_add_fusion.1.scalar_ref, bf16[640,1536]{1,0:T(8,128)(2,1)} %slice.48.q_ref, bf16[3,1920,1152]{2,1,0:T(8,128)(2,1)} %fusion.6.k_ref.v_ref, bf16[3,1920,1152]{2,1,0:T(8,128)(2,1)} %fusion.6.k_ref.v_ref), custom_call_target="tpu_custom_call" | custom-call | flops 3019898880 | bytes 15728640 | tf_op jit(solution)/shard_map/pallas_call | solution.py:98
  178.0 4.5 %all-to-all-start = ((bf16[8,80,1536]{2,1,0:T(8,128)(2,1)}), bf16[8,80,1536]{2,1,0:T(8,128)(2,1)S(1)}, u32[]{:S(2)}, u32[]{:S(2)}) async-start(bf16[8,80,1536]{2,1,0:T(8,128)(2,1)} %bitcast.45), calls=%async_computation | async-start | bytes 3932160 | tf_op jit(solution)/shard_map/all_to_all | solution.py:322
  183.1 2.8 %slice_bitcast_fusion.1 = (bf16[1536,768]{1,0:T(8,128)(2,1)S(1)}, bf16[1536,768]{1,0:T(8,128)(2,1)S(1)}) fusion(bf16[4,1536,1152]{2,1,0:T(8,128)(2,1)} %bitcast.37), kind=kLoop, calls=%fused_computation.35 | loop fusion | bytes 9437184 | tf_op jit(solution)/shard_map/squeeze | solution.py:302
  186.1 4.5 %fusion.24.k_ref = bf16[640,1536]{1,0:T(8,128)(2,1)} fusion(bf16[640,1536]{1,0:T(8,128)(2,1)S(1)} %copy-done.8, bf16[1536,768]{1,0:T(8,128)(2,1)S(1)} %get-tuple-element.10, bf16[1536,768]{1,0:T(8,128)(2,1)S(1)} %get-tuple-element.9), kind=kOutput, calls=%fused_computation.32 | convolution fusion | flops 3030319104 | bytes 8650752 | tf_op jit(solution)/shard_map/dot_general | solution.py:310
  190.6 16.9 %all-to-all-done = bf16[8,80,1536]{2,1,0:T(8,128)(2,1)S(1)} async-done(((bf16[8,80,1536]{2,1,0:T(8,128)(2,1)}), bf16[8,80,1536]{2,1,0:T(8,128)(2,1)S(1)}, u32[]{:S(2)}, u32[]{:S(2)}) %all-to-all-start) | async-done | bytes 1966112 | tf_op jit(solution)/shard_map/all_to_all | solution.py:322
  208.7 17.2 %shard_map.75 = bf16[640,1536]{1,0:T(8,128)(2,1)} custom-call(s32[9]{0:T(128)} %pad_add_fusion.scalar_ref, bf16[1280,1536]{1,0:T(8,128)(2,1)} %copy-done.5, bf16[640,1536]{1,0:T(8,128)(2,1)} %fusion.24.k_ref, bf16[640,1536]{1,0:T(8,128)(2,1)} %bitcast.43), custom_call_target="tpu_custom_call" | custom-call | flops 31457280 | bytes 7864320 | tf_op jit(solution)/shard_map/pallas_call | solution.py:263
  225.9 5.1 %all-to-all-start.1 = ((bf16[8,80,1536]{2,1,0:T(8,128)(2,1)}), bf16[8,80,1536]{2,1,0:T(8,128)(2,1)}, u32[]{:S(2)}, u32[]{:S(2)}) async-start(bf16[8,80,1536]{2,1,0:T(8,128)(2,1)} %bitcast.44), calls=%async_computation.1 | async-start | bytes 3932160 | tf_op jit(solution)/shard_map/all_to_all | solution.py:326
  231.0 25.1 %all-to-all-done.1 = bf16[8,80,1536]{2,1,0:T(8,128)(2,1)} async-done(((bf16[8,80,1536]{2,1,0:T(8,128)(2,1)}), bf16[8,80,1536]{2,1,0:T(8,128)(2,1)}, u32[]{:S(2)}, u32[]{:S(2)}) %all-to-all-start.1) | async-done | bytes 1966112 | tf_op jit(solution)/shard_map/all_to_all | solution.py:326
  256.0 7.6 %fusion.27 = bf16[1,640,1536]{2,1,0:T(8,128)(2,1)} fusion(bf16[640,1536]{1,0:T(8,128)(2,1)} %bitcast.17, bf16[1536,1536]{1,0:T(8,128)(2,1)} %all-gather.7.cloned.1.call-done), kind=kOutput, calls=%fused_computation.33 | convolution fusion | flops 3020881920 | bytes 8650752 | tf_op jit(solution)/shard_map/dot_general | solution.py:327
  (64 shorter events, 10.1 us)
Async XLA Ops:
  6.5 2.2 copy-start
  6.5 82.9 %all-gather.5.cloned.1.call-start = ((), (), s32[]{:S(2)}) async-start(), calls=%async_computation.2 | async-start | bytes 1769472 | tf_op jit(solution)/shard_map/all_gather | solution.py:291
  8.6 50.8 %copy-start.11 = (f32[1,1536]{1,0:T(1,128)S(1)}, f32[1,1536]{1,0:T(1,128)}, u32[]{:S(2)}) copy-start(f32[1,1536]{1,0:T(1,128)} %param.9) | copy-start | bytes 18436
  8.6 50.9 %copy-start.10 = (f32[1,1536]{1,0:T(1,128)S(1)}, f32[1,1536]{1,0:T(1,128)}, u32[]{:S(2)}) copy-start(f32[1,1536]{1,0:T(1,128)} %param.8) | copy-start | bytes 18436
  8.6 93.2 %all-gather.9.cloned.1.call-start = ((), (), s32[]{:S(2)}) async-start(), calls=%async_computation.4 | async-start | bytes 15925248 | tf_op jit(solution)/shard_map/all_gather | solution.py:287
  10.1 220.8 %all-gather.7.cloned.1.call-start = ((), (), s32[]{:S(2)}) async-start(), calls=%async_computation.3 | async-start | bytes 5898240 | tf_op jit(solution)/shard_map/all_gather | solution.py:292
  59.5 2.7 %copy-start.2 = (bf16[1,640,1536]{2,1,0:T(8,128)(2,1)S(1)}, bf16[1,640,1536]{2,1,0:T(8,128)(2,1)}, u32[]{:S(2)}) copy-start(bf16[1,640,1536]{2,1,0:T(8,128)(2,1)} %param.7) | copy-start | bytes 5898244
  79.9 2.5 copy-start.4
  82.4 1.5 copy-start.12
  82.4 2.1 copy-start.13
  82.4 3.9 %copy-start.3 = (bf16[640,1536]{1,0:T(8,128)(2,1)S(1)}, bf16[640,1536]{1,0:T(8,128)(2,1)}, u32[]{:S(2)}) copy-start(bf16[640,1536]{1,0:T(8,128)(2,1)} %get-tuple-element.8) | copy-start | bytes 5898244
  101.8 4.0 %copy-start.9 = (bf16[640,1536]{1,0:T(8,128)(2,1)S(1)}, bf16[640,1536]{1,0:T(8,128)(2,1)}, u32[]{:S(2)}) copy-start(bf16[640,1536]{1,0:T(8,128)(2,1)} %slice.43) | copy-start | bytes 5898244
  103.4 2.7 %copy-start.7 = (bf16[640,1536]{1,0:T(8,128)(2,1)S(1)}, bf16[640,1536]{1,0:T(8,128)(2,1)}, u32[]{:S(2)}) copy-start(bf16[640,1536]{1,0:T(8,128)(2,1)} %fusion.20) | copy-start | bytes 5898244
  103.4 12.7 %slice-start = ((s8[14155776]{0:T(1024)(128)(4,1)}), s8[4194304]{0:T(1024)(128)(4,1)S(1)}, s32[]{:S(2)}) async-start(s8[14155776]{0:T(1024)(128)(4,1)} %bitcast.38), calls=%async_computation.5 | async-start | bytes 8388608
  106.1 10.0 %slice-start.1 = ((s8[14155776]{0:T(1024)(128)(4,1)}), s8[4194304]{0:T(1024)(128)(4,1)S(1)}, s32[]{:S(2)}) async-start(s8[14155776]{0:T(1024)(128)(4,1)} %bitcast.38), calls=%async_computation.6 | async-start | bytes 8388608
  106.1 10.0 %slice-start.2 = ((s8[14155776]{0:T(1024)(128)(4,1)}), s8[4194304]{0:T(1024)(128)(4,1)S(1)}, s32[]{:S(2)}) async-start(s8[14155776]{0:T(1024)(128)(4,1)} %bitcast.38), calls=%async_computation.7 | async-start | bytes 8388608
  106.1 10.0 %slice-start.3 = ((s8[14155776]{0:T(1024)(128)(4,1)}), s8[1572864]{0:T(1024)(128)(4,1)S(1)}, s32[]{:S(2)}) async-start(s8[14155776]{0:T(1024)(128)(4,1)} %bitcast.38), calls=%async_computation.8 | async-start | bytes 3145728
  112.7 1.9 copy-start.5
  114.6 6.4 %slice-start.4 = ((s8[5898240]{0:T(1024)(128)(4,1)}), s8[4194304]{0:T(1024)(128)(4,1)S(1)}, s32[]{:S(2)}) async-start(s8[5898240]{0:T(1024)(128)(4,1)} %bitcast.41), calls=%async_computation.9 | async-start | bytes 8388608
  116.1 4.9 %slice-start.5 = ((s8[5898240]{0:T(1024)(128)(4,1)}), s8[1703936]{0:T(1024)(128)(4,1)S(1)}, s32[]{:S(2)}) async-start(s8[5898240]{0:T(1024)(128)(4,1)} %bitcast.41), calls=%async_computation.10 | async-start | bytes 3407872
  178.0 29.4 %all-to-all-start = ((bf16[8,80,1536]{2,1,0:T(8,128)(2,1)}), bf16[8,80,1536]{2,1,0:T(8,128)(2,1)S(1)}, u32[]{:S(2)}, u32[]{:S(2)}) async-start(bf16[8,80,1536]{2,1,0:T(8,128)(2,1)} %bitcast.45), calls=%async_computation | async-start | bytes 3932160 | tf_op jit(solution)/shard_map/all_to_all | solution.py:322
  183.1 3.0 %copy-start.8 = (bf16[640,1536]{1,0:T(8,128)(2,1)S(1)}, bf16[640,1536]{1,0:T(8,128)(2,1)}, u32[]{:S(2)}) copy-start(bf16[640,1536]{1,0:T(8,128)(2,1)} %fusion.20) | copy-start | bytes 5898244
  225.9 30.1 %all-to-all-start.1 = ((bf16[8,80,1536]{2,1,0:T(8,128)(2,1)}), bf16[8,80,1536]{2,1,0:T(8,128)(2,1)}, u32[]{:S(2)}, u32[]{:S(2)}) async-start(bf16[8,80,1536]{2,1,0:T(8,128)(2,1)} %bitcast.44), calls=%async_computation.1 | async-start | bytes 3932160 | tf_op jit(solution)/shard_map/all_to_all | solution.py:326
  256.0 7.6 %copy-start.1 = (bf16[1536,1152]{1,0:T(8,128)(2,1)S(1)}, bf16[1536,1152]{1,0:T(8,128)(2,1)}, u32[]{:S(2)}) copy-start(bf16[1536,1152]{1,0:T(8,128)(2,1)} %param.10) | copy-start | bytes 10616836
  (1 other events, 1.3 us)
Sparse Core Ops, SparseCore 0:
  9.0 15.5 all-gather.4
  26.3 75.4 all-gather.8
  103.5 52.7 all-gather.6

commit v8 on v7

--- a/solution.py
+++ b/solution.py
@@ -219,34 +219,57 @@
     )(own)
 
 
-def temporal_kernel(scalar_ref, q_ref, k_ref, s_ref, o_ref):
+def temporal_weight_kernel(scalar_ref, q_ref, k_ref, w_ref):
     scaling = 1.0 / math.sqrt(HD)
     n_frames = scalar_ref.shape[0] - 1
     per = q_ref.shape[0] // n_frames
     position = scalar_ref[0] + lax.broadcasted_iota(jnp.int32, (per, 1), 0)
     live = [position < scalar_ref[1 + g] for g in range(n_frames)]
-    keys = [k_ref[g * per : (g + 1) * per, :].astype(jnp.float32) for g in range(n_frames)]
+    keys = k_ref[...].astype(jnp.float32)
+    ones = jnp.ones((HD, HD), jnp.bfloat16)
+    lane = lax.broadcasted_iota(jnp.int32, (per, HD), 1)
     for f in range(n_frames):
         query = q_ref[f * per : (f + 1) * per, :].astype(jnp.float32)
+        prod = jnp.concatenate([query] * n_frames, axis=0) * keys
+        high = prod.astype(jnp.bfloat16)
+        low = (prod - high.astype(jnp.float32)).astype(jnp.bfloat16)
+        sums = jnp.dot(high, ones, preferred_element_type=jnp.float32) + jnp.dot(
+            low, ones, preferred_element_type=jnp.float32
+        )
         scores = []
         row_max = None
         for g in range(n_frames):
-            score = jnp.sum(query * keys[g], axis=-1, keepdims=True) * scaling
-            score = jnp.where(live[g], score, -1e30)
+            score = jnp.where(live[g], sums[g * per : (g + 1) * per] * scaling, -1e30)
             row_max = score if row_max is None else jnp.maximum(row_max, score)
             scores.append(score)
         denominator = None
-        summed = None
+        packed = None
         for g in range(n_frames):
             exp_term = jnp.where(live[g], jnp.exp(scores[g] - row_max), 0.0)
             denominator = exp_term if denominator is None else denominator + exp_term
             weight = exp_term.astype(jnp.bfloat16).astype(jnp.float32)
-            term = weight * s_ref[g * per : (g + 1) * per, :].astype(jnp.float32)
+            picked = jnp.where(lane == g, weight, 0.0)
+            packed = picked if packed is None else packed + picked
+        packed = packed + jnp.where(lane == n_frames, denominator, 0.0)
+        w_ref[f * per : (f + 1) * per, :] = packed
+
+
+def temporal_sum_kernel(w_ref, s_ref, o_ref):
+    n_frames = 8
+    per = s_ref.shape[0] // n_frames
+    spatial = [s_ref[g * per : (g + 1) * per, :].astype(jnp.float32) for g in range(n_frames)]
+    for f in range(n_frames):
+        packed = w_ref[f * per : (f + 1) * per, :]
+        summed = None
+        for g in range(n_frames):
+            term = packed[:, g : g + 1] * spatial[g]
             summed = term if summed is None else summed + term
-        o_ref[f * per : (f + 1) * per, :] = (summed / denominator).astype(o_ref.dtype)
-
-
-def temporal_rows(q_src, q_block, keys, spatial_part, clip_counts, first_pos):
+        o_ref[f * per : (f + 1) * per, :] = (summed / packed[:, n_frames : n_frames + 1]).astype(
+            o_ref.dtype
+        )
+
+
+def temporal_weights(q_src, q_block, keys, clip_counts, first_pos):
     rows, feat = keys.shape
     n_frames = clip_counts.shape[0]
     scalars = jnp.concatenate([first_pos.reshape(1), clip_counts]).astype(jnp.int32)
@@ -256,20 +279,36 @@
         in_specs=[
             pl.BlockSpec((rows, HD), lambda h, sc: (q_block, h)),
             pl.BlockSpec((rows, HD), lambda h, sc: (0, h)),
-            pl.BlockSpec((rows, HD), lambda h, sc: (0, h)),
         ],
-        out_specs=pl.BlockSpec((rows, HD), lambda h, sc: (0, h)),
+        out_specs=pl.BlockSpec((None, rows, HD), lambda h, sc: (h, 0, 0)),
     )
     return pl.pallas_call(
-        temporal_kernel,
+        temporal_weight_kernel,
         grid_spec=grid_spec,
+        out_shape=jax.ShapeDtypeStruct((feat // HD, rows, HD), jnp.float32),
+        cost_estimate=pl.CostEstimate(
+            flops=4 * rows * n_frames * feat * HD,
+            transcendentals=rows * n_frames * feat,
+            bytes_accessed=2 * rows * feat * 2 + rows * feat * 4,
+        ),
+    )(scalars, q_src, keys)
+
+
+def temporal_sum(packed, spatial_part):
+    rows, feat = spatial_part.shape
+    return pl.pallas_call(
+        temporal_sum_kernel,
+        grid=(feat // HD,),
+        in_specs=[
+            pl.BlockSpec((None, rows, HD), lambda h: (h, 0, 0)),
+            pl.BlockSpec((rows, HD), lambda h: (0, h)),
+        ],
+        out_specs=pl.BlockSpec((rows, HD), lambda h: (0, h)),
         out_shape=jax.ShapeDtypeStruct((rows, feat), jnp.bfloat16),
         cost_estimate=pl.CostEstimate(
-            flops=4 * rows * n_frames * feat,
-            transcendentals=rows * n_frames * feat // HD,
-            bytes_accessed=4 * rows * feat * 2,
+            flops=2 * rows * 8 * feat, transcendentals=0, bytes_accessed=rows * feat * 8
         ),
-    )(scalars, q_src, keys, spatial_part)
+    )(packed, spatial_part)
 
 
 def local(tokens, mod_scale, mod_shift, w_qkv, w_out, neighbors, counts):
@@ -322,7 +361,8 @@
     spatial_part = lax.all_to_all(spatial, frame_axes, split_axis=0, concat_axis=0, tiled=True)
     per_dev = tok_count // n_frames
     first_pos = piece_index * tok_count + frame_index * per_dev
-    temporal = temporal_rows(q_both, 1, key_cross, spatial_part, clip_counts, first_pos)
+    packed = temporal_weights(q_both, 1, key_cross, clip_counts, first_pos)
+    temporal = temporal_sum(packed, spatial_part)
     flat_temporal = lax.all_to_all(temporal, frame_axes, split_axis=0, concat_axis=0, tiled=True)
     projected = jnp.dot(flat_temporal, w_out_full, preferred_element_type=jnp.float32)
     return projected.astype(jnp.bfloat16).reshape(1, tok_count, feat_count)

time: 270 us -> 272 us (level)
  Pallas kernels: 95.5 us -> 115 us
  waiting for transfers between devices: 54.4 us -> 36.9 us
    pallas_call x1 -> x2, Pallas kernels: 17.2 us -> 36.6 us  [the longest x1 22.4 us: temporal_weights(): pl.pallas_call(temporal_weight_kernel, grid_spec=grid_spec, out_shape=jax...]
    all_to_all x1, waiting for transfers between devices: 16.9 us -> 0.01 us  [local(): lax.all_to_all(spatial, frame_axes, split_axis=0, concat_axis=0, tiled=True)]
  transfers between devices with their start and end apart: 5 -> 5, of which waited for: 3 -> 2; matrix products, arithmetic and copies ran while one was open for 30% -> 30% of each run, Pallas kernels for 35% -> 42%
where the time goes in v8:
time: 272 us
  Pallas kernels  115 us (42%)
  matrix products  46.5 us (17%)
  waiting for transfers between devices  36.9 us (14%)
  local copies, waits for them, and re-layouts  25.5 us (9%)
  other arithmetic  25.2 us (9%)
  between operations  13.3 us (5%)
  starting transfers between devices  9.39 us (3%)
    pallas_call x1, Pallas kernels, exchange_tokens(): pl.pallas_call(exchange_kernel, out_shape=(jax.ShapeDtypeStruct((2, rows,...  49.2 us
    pallas_call x1, Pallas kernels, spatial_rows(): pl.pallas_call(spatial_kernel, grid_spec=grid_spec, out_shape=jax.ShapeDt...  29.1 us
    dot_general x1, matrix products, local(): jnp.einsum('tk,jkc->jtc', normed_all, w_full[1:], preferred_element_type=...  27.9 us
    all_to_all x1, waiting for transfers between devices, local(): lax.all_to_all(temporal, frame_axes, split_axis=0, concat_axis=0, tiled=T...  25 us
    pallas_call x1, Pallas kernels, temporal_weights(): pl.pallas_call(temporal_weight_kernel, grid_spec=grid_spec, out_shape=jax...  22.4 us
    pallas_call x1, Pallas kernels, temporal_sum(): pl.pallas_call(temporal_sum_kernel, grid=(feat // HD,), in_specs=[pl.Bloc...  14.2 us
    convert_element_type x2, other arithmetic, layer_norm(): return (normal * (1.0 + mod_scale) + mod_shift).astype(jnp.bfloat16)  13.3 us
    all_gather x1, waiting for transfers between devices, local(): w_pieces = lax.all_gather(w_half, ('fsdp', 'core'), axis=0, tiled=False)  11.8 us
  transfers between devices with their start and end apart: 5, of which 2 were waited for; matrix products, arithmetic and copies ran while one was open for 30% of the time, Pallas kernels for 42%

profile of v8, /device:TPU:1, one launch (start us, length us, event | category | flops | bytes accessed | tf_op | source)
XLA Modules:
  0.0 271.8 jit_solution(2744706921692968361)
XLA Ops:
  6.5 2.1 constant_dynamic-slice_fusion
  10.2 49.2 %shard_map.73 = (bf16[2,640,1536]{2,1,0:T(8,128)(2,1)}, bf16[640,1536]{1,0:T(8,128)(2,1)}) custom-call(bf16[640,1536]{1,0:T(8,128)(2,1)} %bitcast.32), custom_call_target="tpu_custom_call" | custom-call | bytes 157286400 | tf_op jit(solution)/shard_map/pallas_call | solution.py:202
  59.5 2.5 select_bitcast_fusion.1
  63.3 5.4 %fusion.2 = f32[1920]{0:T(1024)S(1)} fusion(f32[1920]{0:T(1024)S(1)} %broadcast_multiply_fusion, bf16[640,1536]{1,0:T(8,128)(2,1)S(1)} %get-tuple-element.12, bf16[640,1536]{1,0:T(8,128)(2,1)S(1)} %bitcast.34, bf16[640,1536]{1,0:T(8,128)(2,1)S(1)} %get-tuple-element.11), kind=kLoop, calls=%fused_computation.5 | loop fusion | flops 26540160 | bytes 5913600 | tf_op jit(solution)/shard_map/reduce_sum | solution.py:28
  68.7 11.2 %fusion.5 = bf16[1920,1536]{1,0:T(8,128)(2,1)S(1)} fusion(f32[1536]{0:T(1024)S(1)} %reduce.1, f32[1536]{0:T(1024)S(1)} %add_reduce_fusion, f32[1920]{0:T(1024)S(1)} %add_sqrt_fusion, f32[1920]{0:T(1024)S(1)} %broadcast_multiply_fusion, bf16[640,1536]{1,0:T(8,128)(2,1)S(1)} %get-tuple-element.12, bf16[640,1536]{1,0:T(8,128)(2,1)S(1)} %bitcast.35, ...), kind=kLoop, calls=%fused_computation.8 | loop fusion | flops 32440320 | bytes 11824128 | tf_op jit(solution)/shard_map/convert_element_type | solution.py:30
  79.9 2.4 copy-done.4
  88.0 2.1 fusion.20
  90.0 11.8 %all-gather.9.cloned.1.call-done = bf16[6144,1152]{1,0:T(8,128)(2,1)} async-done(((bf16[768,1152]{1,0:T(8,128)(2,1)}), bf16[6144,1152]{1,0:T(8,128)(2,1)}) %all-gather.9.cloned.1.call-update) | async-done | bytes 14155792 | tf_op jit(solution)/shard_map/all_gather | solution.py:326
  101.8 1.5 slice_bitcast_fusion.2
  103.4 2.4 slice.44
  106.1 6.6 %convolution_convert_fusion.1.q_ref = bf16[1280,1536]{1,0:T(8,128)(2,1)S(1)} fusion(bf16[1536,384]{1,0:T(8,128)(2,1)S(1)} %slice_bitcast_fusion.2, bf16[1536,1152]{1,0:T(8,128)(2,1)S(1)} %slice.44, bf16[640,1536]{1,0:T(8,128)(2,1)S(1)} %copy-done.7, bf16[640,1536]{1,0:T(8,128)(2,1)S(1)} %copy-done.6), kind=kOutput, calls=%fused_computation.10 | convolution fusion | flops 6059065344 | bytes 12582912 | tf_op jit(solution)/shard_map/dot_general | solution.py:343
  112.7 1.9 copy-done.9
  114.6 1.4 slice.48.q_ref
  116.1 4.9 %slice.49 = bf16[4608,1152]{1,0:T(8,128)(2,1)} slice(bf16[6144,1152]{1,0:T(8,128)(2,1)S(1)} %bitcast.39), slice={[1536:6144], [0:1152]} | slice | bytes 21233664 | tf_op jit(solution)/shard_map/slice | solution.py:351
  121.0 27.9 %fusion.6.k_ref.v_ref = bf16[3,1920,1152]{2,1,0:T(8,128)(2,1)} fusion(bf16[3,1536,1152]{2,1,0:T(8,128)(2,1)} %bitcast.40, bf16[1920,1536]{1,0:T(8,128)(2,1)S(1)} %bitcast.42), kind=kOutput, calls=%fused_computation.9 | convolution fusion | flops 20390952960 | bytes 29786112 | tf_op jit(solution)/shard_map/tk,jkc->jtc/dot_general | solution.py:350
  148.9 29.1 %shard_map.75 = bf16[640,1536]{1,0:T(8,128)(2,1)} custom-call(s32[30]{0:T(128)} %reshape_squeeze.3.list_ref, s32[2]{0:T(128)} %pad_add_fusion.1.scalar_ref, bf16[640,1536]{1,0:T(8,128)(2,1)} %slice.48.q_ref, bf16[3,1920,1152]{2,1,0:T(8,128)(2,1)} %fusion.6.k_ref.v_ref, bf16[3,1920,1152]{2,1,0:T(8,128)(2,1)} %fusion.6.k_ref.v_ref), custom_call_target="tpu_custom_call" | custom-call | flops 3019898880 | bytes 15728640 | tf_op jit(solution)/shard_map/pallas_call | solution.py:98
  178.0 4.5 %all-to-all-start = ((bf16[8,80,1536]{2,1,0:T(8,128)(2,1)}), bf16[8,80,1536]{2,1,0:T(8,128)(2,1)S(1)}, u32[]{:S(2)}, u32[]{:S(2)}) async-start(bf16[8,80,1536]{2,1,0:T(8,128)(2,1)} %bitcast.43), calls=%async_computation | async-start | bytes 3932160 | tf_op jit(solution)/shard_map/all_to_all | solution.py:361
  182.5 2.8 %slice_bitcast_fusion.1 = (bf16[1536,768]{1,0:T(8,128)(2,1)S(1)}, bf16[1536,768]{1,0:T(8,128)(2,1)S(1)}) fusion(bf16[4,1536,1152]{2,1,0:T(8,128)(2,1)} %bitcast.37), kind=kLoop, calls=%fused_computation.35 | loop fusion | bytes 9437184 | tf_op jit(solution)/shard_map/squeeze | solution.py:341
  185.5 4.5 %fusion.24.k_ref = bf16[640,1536]{1,0:T(8,128)(2,1)} fusion(bf16[640,1536]{1,0:T(8,128)(2,1)S(1)} %copy-done.8, bf16[1536,768]{1,0:T(8,128)(2,1)S(1)} %get-tuple-element.10, bf16[1536,768]{1,0:T(8,128)(2,1)S(1)} %get-tuple-element.9), kind=kOutput, calls=%fused_computation.32 | convolution fusion | flops 3030319104 | bytes 8650752 | tf_op jit(solution)/shard_map/dot_general | solution.py:349
  190.0 22.4 %shard_map.74.w_ref = f32[12,640,128]{2,1,0:T(8,128)} custom-call(s32[9]{0:T(128)} %pad_add_fusion.scalar_ref, bf16[1280,1536]{1,0:T(8,128)(2,1)} %copy-done.9, bf16[640,1536]{1,0:T(8,128)(2,1)} %fusion.24.k_ref), custom_call_target="tpu_custom_call" | custom-call | flops 4026531840 | bytes 7864320 | tf_op jit(solution)/shard_map/pallas_call | solution.py:285
  213.6 14.2 %shard_map.76 = bf16[640,1536]{1,0:T(8,128)(2,1)} custom-call(f32[12,640,128]{2,1,0:T(8,128)} %shard_map.74.w_ref, bf16[640,1536]{1,0:T(8,128)(2,1)} %bitcast.44), custom_call_target="tpu_custom_call" | custom-call | flops 15728640 | bytes 7864320 | tf_op jit(solution)/shard_map/pallas_call | solution.py:299
  227.8 4.8 %all-to-all-start.1 = ((bf16[8,80,1536]{2,1,0:T(8,128)(2,1)}), bf16[8,80,1536]{2,1,0:T(8,128)(2,1)}, u32[]{:S(2)}, u32[]{:S(2)}) async-start(bf16[8,80,1536]{2,1,0:T(8,128)(2,1)} %bitcast.45), calls=%async_computation.1 | async-start | bytes 3932160 | tf_op jit(solution)/shard_map/all_to_all | solution.py:366
  232.6 25.0 %all-to-all-done.1 = bf16[8,80,1536]{2,1,0:T(8,128)(2,1)} async-done(((bf16[8,80,1536]{2,1,0:T(8,128)(2,1)}), bf16[8,80,1536]{2,1,0:T(8,128)(2,1)}, u32[]{:S(2)}, u32[]{:S(2)}) %all-to-all-start.1) | async-done | bytes 1966112 | tf_op jit(solution)/shard_map/all_to_all | solution.py:366
  257.7 7.6 %fusion.27 = bf16[1,640,1536]{2,1,0:T(8,128)(2,1)} fusion(bf16[640,1536]{1,0:T(8,128)(2,1)} %bitcast.17, bf16[1536,1536]{1,0:T(8,128)(2,1)} %all-gather.7.cloned.1.call-done), kind=kOutput, calls=%fused_computation.33 | convolution fusion | flops 3020881920 | bytes 8650752 | tf_op jit(solution)/shard_map/dot_general | solution.py:367
  (65 shorter events, 10.1 us)
Async XLA Ops:
  6.5 2.2 copy-start
  6.5 83.5 %all-gather.5.cloned.1.call-start = ((), (), s32[]{:S(2)}) async-start(), calls=%async_computation.2 | async-start | bytes 1769472 | tf_op jit(solution)/shard_map/all_gather | solution.py:330
  8.6 50.8 %copy-start.11 = (f32[1,1536]{1,0:T(1,128)S(1)}, f32[1,1536]{1,0:T(1,128)}, u32[]{:S(2)}) copy-start(f32[1,1536]{1,0:T(1,128)} %param.9) | copy-start | bytes 18436
  8.6 50.9 %copy-start.10 = (f32[1,1536]{1,0:T(1,128)S(1)}, f32[1,1536]{1,0:T(1,128)}, u32[]{:S(2)}) copy-start(f32[1,1536]{1,0:T(1,128)} %param.8) | copy-start | bytes 18436
  8.6 93.2 %all-gather.9.cloned.1.call-start = ((), (), s32[]{:S(2)}) async-start(), calls=%async_computation.4 | async-start | bytes 15925248 | tf_op jit(solution)/shard_map/all_gather | solution.py:326
  10.1 222.5 %all-gather.7.cloned.1.call-start = ((), (), s32[]{:S(2)}) async-start(), calls=%async_computation.3 | async-start | bytes 5898240 | tf_op jit(solution)/shard_map/all_gather | solution.py:331
  59.5 2.7 %copy-start.2 = (bf16[1,640,1536]{2,1,0:T(8,128)(2,1)S(1)}, bf16[1,640,1536]{2,1,0:T(8,128)(2,1)}, u32[]{:S(2)}) copy-start(bf16[1,640,1536]{2,1,0:T(8,128)(2,1)} %param.7) | copy-start | bytes 5898244
  79.9 2.5 copy-start.4
  82.4 1.5 copy-start.12
  82.4 2.1 copy-start.13
  82.4 4.6 %copy-start.3 = (bf16[640,1536]{1,0:T(8,128)(2,1)S(1)}, bf16[640,1536]{1,0:T(8,128)(2,1)}, u32[]{:S(2)}) copy-start(bf16[640,1536]{1,0:T(8,128)(2,1)} %get-tuple-element.8) | copy-start | bytes 5898244
  101.8 4.0 %copy-start.7 = (bf16[640,1536]{1,0:T(8,128)(2,1)S(1)}, bf16[640,1536]{1,0:T(8,128)(2,1)}, u32[]{:S(2)}) copy-start(bf16[640,1536]{1,0:T(8,128)(2,1)} %fusion.20) | copy-start | bytes 5898244
  103.4 2.7 copy-start.6
  103.4 12.7 %slice-start = ((s8[14155776]{0:T(1024)(128)(4,1)}), s8[4194304]{0:T(1024)(128)(4,1)S(1)}, s32[]{:S(2)}) async-start(s8[14155776]{0:T(1024)(128)(4,1)} %bitcast.38), calls=%async_computation.5 | async-start | bytes 8388608
  106.1 10.0 %slice-start.1 = ((s8[14155776]{0:T(1024)(128)(4,1)}), s8[4194304]{0:T(1024)(128)(4,1)S(1)}, s32[]{:S(2)}) async-start(s8[14155776]{0:T(1024)(128)(4,1)} %bitcast.38), calls=%async_computation.6 | async-start | bytes 8388608
  106.1 10.0 %slice-start.2 = ((s8[14155776]{0:T(1024)(128)(4,1)}), s8[4194304]{0:T(1024)(128)(4,1)S(1)}, s32[]{:S(2)}) async-start(s8[14155776]{0:T(1024)(128)(4,1)} %bitcast.38), calls=%async_computation.7 | async-start | bytes 8388608
  106.1 10.0 %slice-start.3 = ((s8[14155776]{0:T(1024)(128)(4,1)}), s8[1572864]{0:T(1024)(128)(4,1)S(1)}, s32[]{:S(2)}) async-start(s8[14155776]{0:T(1024)(128)(4,1)} %bitcast.38), calls=%async_computation.8 | async-start | bytes 3145728
  112.7 1.9 copy-start.9
  114.6 6.4 %slice-start.4 = ((s8[5898240]{0:T(1024)(128)(4,1)}), s8[4194304]{0:T(1024)(128)(4,1)S(1)}, s32[]{:S(2)}) async-start(s8[5898240]{0:T(1024)(128)(4,1)} %bitcast.41), calls=%async_computation.9 | async-start | bytes 8388608
  116.1 4.9 %slice-start.5 = ((s8[5898240]{0:T(1024)(128)(4,1)}), s8[1703936]{0:T(1024)(128)(4,1)S(1)}, s32[]{:S(2)}) async-start(s8[5898240]{0:T(1024)(128)(4,1)} %bitcast.41), calls=%async_computation.10 | async-start | bytes 3407872
  178.0 34.3 %all-to-all-start = ((bf16[8,80,1536]{2,1,0:T(8,128)(2,1)}), bf16[8,80,1536]{2,1,0:T(8,128)(2,1)S(1)}, u32[]{:S(2)}, u32[]{:S(2)}) async-start(bf16[8,80,1536]{2,1,0:T(8,128)(2,1)} %bitcast.43), calls=%async_computation | async-start | bytes 3932160 | tf_op jit(solution)/shard_map/all_to_all | solution.py:361
  182.5 3.0 %copy-start.8 = (bf16[640,1536]{1,0:T(8,128)(2,1)S(1)}, bf16[640,1536]{1,0:T(8,128)(2,1)}, u32[]{:S(2)}) copy-start(bf16[640,1536]{1,0:T(8,128)(2,1)} %fusion.20) | copy-start | bytes 5898244
  227.8 29.8 %all-to-all-start.1 = ((bf16[8,80,1536]{2,1,0:T(8,128)(2,1)}), bf16[8,80,1536]{2,1,0:T(8,128)(2,1)}, u32[]{:S(2)}, u32[]{:S(2)}) async-start(bf16[8,80,1536]{2,1,0:T(8,128)(2,1)} %bitcast.45), calls=%async_computation.1 | async-start | bytes 3932160 | tf_op jit(solution)/shard_map/all_to_all | solution.py:366
  257.7 7.6 %copy-start.1 = (bf16[1536,1152]{1,0:T(8,128)(2,1)S(1)}, bf16[1536,1152]{1,0:T(8,128)(2,1)}, u32[]{:S(2)}) copy-start(bf16[1536,1152]{1,0:T(8,128)(2,1)} %param.10) | copy-start | bytes 10616836
  (1 other events, 1.3 us)
Sparse Core Ops, SparseCore 0:
  9.0 15.5 all-gather.4
  26.3 75.4 all-gather.8
  103.5 52.7 all-gather.6

commit v9 on v6

--- a/solution.py
+++ b/solution.py
@@ -38,7 +38,7 @@
     for t in range(local_tiles):
         query = q_ref[t * TILE : (t + 1) * TILE, :]
         parts = []
-        row_max = None
+        block_max = None
         for n in range(NBR):
             tile_id = list_ref[t * NBR + n]
             start = pl.multiple_of((tile_id - first_tile) * TILE, TILE)
@@ -52,20 +52,20 @@
             key_pos = tile_id * TILE + lax.broadcasted_iota(jnp.int32, scores.shape, 1)
             live = key_pos < count_here
             scores = jnp.where(live, scores, -1e30)
-            part_max = jnp.max(scores, axis=-1, keepdims=True)
-            row_max = part_max if row_max is None else jnp.maximum(row_max, part_max)
+            block_max = scores if block_max is None else jnp.maximum(block_max, scores)
             parts.append((scores, live, start))
-        denominator = None
+        row_max = jnp.max(block_max, axis=-1, keepdims=True)
+        exp_total = None
         summed = None
         for scores, live, start in parts:
             exp_terms = jnp.where(live, jnp.exp(scores - row_max), 0.0)
-            part_sum = jnp.sum(exp_terms, axis=-1, keepdims=True)
             value = v_ref[pl.ds(start, TILE), :]
             part_out = jnp.dot(
                 exp_terms.astype(jnp.bfloat16), value, preferred_element_type=jnp.float32
             )
-            denominator = part_sum if denominator is None else denominator + part_sum
+            exp_total = exp_terms if exp_total is None else exp_total + exp_terms
             summed = part_out if summed is None else summed + part_out
+        denominator = jnp.sum(exp_total, axis=-1, keepdims=True)
         o_ref[t * TILE : (t + 1) * TILE, :] = (summed / denominator).astype(o_ref.dtype)
 
 

time: 260 us -> 261 us (level)
  no operation moved by 1% of the time
where the time goes in v9:
time: 261 us; the launch traced here: 260 us
  Pallas kernels  79 us (30%)
  matrix products  52.7 us (20%)
  local copies, waits for them, and re-layouts  42.7 us (16%)
  waiting for transfers between devices  38.2 us (15%)
  other arithmetic  25 us (10%)
  between operations  13.3 us (5%)
  starting transfers between devices  9.42 us (4%)
    pallas_call x1, Pallas kernels, exchange_tokens(): pl.pallas_call(exchange_kernel, out_shape=(jax.ShapeDtypeStruct((2, rows,...  49.2 us
    pallas_call x1, Pallas kernels, spatial_rows(): pl.pallas_call(spatial_kernel, grid_spec=grid_spec, out_shape=jax.ShapeDt...  29.8 us
    dot_general x1, matrix products, local(): jnp.einsum('tk,jkc->jtc', normed_all, w_full[1:], preferred_element_type=...  25.2 us
    all_to_all x1, waiting for transfers between devices, local(): lax.all_to_all(temporal.reshape(tok_count, feat_count), frame_axes, split...  25 us
    convert_element_type x2, other arithmetic, layer_norm(): return (normal * (1.0 + mod_scale) + mod_shift).astype(jnp.bfloat16)  13.3 us
    all_gather x1, waiting for transfers between devices, local(): w_pieces = lax.all_gather(w_half, ('fsdp', 'core'), axis=0, tiled=False)  13.1 us
    dot_general x1, matrix products, local(): jnp.dot(flat_temporal, w_out_full, preferred_element_type=jnp.float32)  7.56 us
    dot_general x1, matrix products, local(): jnp.dot(jnp.concatenate([normed_all[tok_count:2 * tok_count], normed_cros...  6.6 us
  transfers between devices with their start and end apart: 5, of which 2 were waited for; matrix products, arithmetic and copies ran while one was open for 38% of the time, Pallas kernels for 30%

profile of v9, /device:TPU:1, one launch (start us, length us, event | category | flops | bytes accessed | tf_op | source)
XLA Modules:
  0.0 260.3 jit_solution(16659574083157727910)
XLA Ops:
  10.2 49.2 %shard_map.73 = (bf16[2,640,1536]{2,1,0:T(8,128)(2,1)}, bf16[640,1536]{1,0:T(8,128)(2,1)}) custom-call(bf16[640,1536]{1,0:T(8,128)(2,1)} %bitcast.39), custom_call_target="tpu_custom_call" | custom-call | bytes 157286400 | tf_op jit(solution)/shard_map/pallas_call | solution.py:202
  59.5 2.5 select_bitcast_fusion.1
  63.3 5.4 %fusion.3 = f32[1920]{0:T(1024)S(1)} fusion(f32[1920]{0:T(1024)S(1)} %broadcast_multiply_fusion, bf16[640,1536]{1,0:T(8,128)(2,1)S(1)} %get-tuple-element.14, bf16[640,1536]{1,0:T(8,128)(2,1)S(1)} %bitcast.41, bf16[640,1536]{1,0:T(8,128)(2,1)S(1)} %get-tuple-element.13), kind=kLoop, calls=%fused_computation.6 | loop fusion | flops 26540160 | bytes 5913600 | tf_op jit(solution)/shard_map/reduce_sum | solution.py:28
  68.7 11.2 %fusion.6 = bf16[1920,1536]{1,0:T(8,128)(2,1)S(1)} fusion(f32[1536]{0:T(1024)S(1)} %reduce.2, f32[1536]{0:T(1024)S(1)} %add_reduce_fusion, f32[1920]{0:T(1024)S(1)} %add_sqrt_fusion, f32[1920]{0:T(1024)S(1)} %broadcast_multiply_fusion, bf16[640,1536]{1,0:T(8,128)(2,1)S(1)} %get-tuple-element.14, bf16[640,1536]{1,0:T(8,128)(2,1)S(1)} %bitcast.42, ...), kind=kLoop, calls=%fused_computation.9 | loop fusion | flops 32440320 | bytes 11824128 | tf_op jit(solution)/shard_map/convert_element_type | solution.py:30
  79.9 2.5 copy-done.4
  88.7 13.1 %all-gather.9.cloned.1.call-done = bf16[6144,1152]{1,0:T(8,128)(2,1)} async-done(((bf16[768,1152]{1,0:T(8,128)(2,1)}), bf16[6144,1152]{1,0:T(8,128)(2,1)}) %all-gather.9.cloned.1.call-update) | async-done | bytes 14155792 | tf_op jit(solution)/shard_map/all_gather | solution.py:257
  101.8 4.0 %slice-done = bf16[4608,1152]{1,0:T(8,128)(2,1)S(1)} async-done(((bf16[6144,1152]{1,0:T(8,128)(2,1)}), bf16[4608,1152]{1,0:T(8,128)(2,1)S(1)}, s32[]{:S(2)}) %slice-start) | async-done | bytes 10616856 | tf_op jit(solution)/shard_map/slice | solution.py:282
  105.9 25.2 %fusion.7.k_ref.v_ref = bf16[3,1920,1152]{2,1,0:T(8,128)(2,1)} fusion(bf16[3,1536,1152]{2,1,0:T(8,128)(2,1)S(1)} %bitcast.45, bf16[1920,1536]{1,0:T(8,128)(2,1)} %copy-done.4), kind=kOutput, calls=%fused_computation.10 | convolution fusion | flops 20390952960 | bytes 29786112 | tf_op jit(solution)/shard_map/tk,jkc->jtc/dot_general | solution.py:281
  132.5 2.4 slice.48
  135.7 6.6 %convolution_convert_fusion.1 = bf16[1280,1536]{1,0:T(8,128)(2,1)S(1)} fusion(bf16[1536,384]{1,0:T(8,128)(2,1)S(1)} %slice_bitcast_fusion.2, bf16[1536,1152]{1,0:T(8,128)(2,1)S(1)} %slice.48, bf16[640,1536]{1,0:T(8,128)(2,1)S(1)} %copy-done.5, bf16[640,1536]{1,0:T(8,128)(2,1)S(1)} %slice-done.1), kind=kOutput, calls=%fused_computation.11 | convolution fusion | flops 6059065344 | bytes 12582912 | tf_op jit(solution)/shard_map/dot_general | solution.py:274
  144.5 29.8 %shard_map.74 = bf16[640,1536]{1,0:T(8,128)(2,1)} custom-call(s32[30]{0:T(128)} %reshape_squeeze.3.list_ref, s32[2]{0:T(128)} %pad_add_fusion.scalar_ref, bf16[640,1536]{1,0:T(8,128)(2,1)} %get-tuple-element.11.q_ref, bf16[3,1920,1152]{2,1,0:T(8,128)(2,1)} %fusion.7.k_ref.v_ref, bf16[3,1920,1152]{2,1,0:T(8,128)(2,1)} %fusion.7.k_ref.v_ref), custom_call_target="tpu_custom_call" | custom-call | flops 3019898880 | bytes 15728640 | tf_op jit(solution)/shard_map/pallas_call | solution.py:98
  174.3 4.5 %all-to-all-start = ((bf16[8,80,1536]{2,1,0:T(8,128)(2,1)}), bf16[8,80,1536]{2,1,0:T(8,128)(2,1)}, u32[]{:S(2)}, u32[]{:S(2)}) async-start(bf16[8,80,1536]{2,1,0:T(8,128)(2,1)} %bitcast.46), calls=%async_computation | async-start | bytes 3932160 | tf_op jit(solution)/shard_map/all_to_all | solution.py:292
  178.8 2.8 %slice_bitcast_fusion.1 = (bf16[1536,768]{1,0:T(8,128)(2,1)S(1)}, bf16[1536,768]{1,0:T(8,128)(2,1)S(1)}) fusion(bf16[4,1536,1152]{2,1,0:T(8,128)(2,1)} %bitcast.44), kind=kLoop, calls=%fused_computation.38 | loop fusion | bytes 9437184 | tf_op jit(solution)/shard_map/squeeze | solution.py:272
  181.8 4.5 %fusion.26 = bf16[640,1536]{1,0:T(8,128)(2,1)} fusion(bf16[640,1536]{1,0:T(8,128)(2,1)S(1)} %copy-done.6, bf16[1536,768]{1,0:T(8,128)(2,1)S(1)} %get-tuple-element.10, bf16[1536,768]{1,0:T(8,128)(2,1)S(1)} %get-tuple-element.9), kind=kOutput, calls=%fused_computation.35 | convolution fusion | flops 3030319104 | bytes 8650752 | tf_op jit(solution)/shard_map/dot_general | solution.py:280
  186.3 3.7 %reshape.88 = bf16[8,80,12,128]{3,2,1,0:T(8,128)(2,1)S(1)} reshape(bf16[640,1536]{1,0:T(8,128)(2,1)} %fusion.26) | data formatting | bytes 3932160 | tf_op jit(solution)/shard_map/reshape | solution.py:298
  190.0 4.7 %reshape.87 = bf16[8,80,12,128]{3,2,1,0:T(8,128)(2,1)} reshape(bf16[640,1536]{1,0:T(8,128)(2,1)} %get-tuple-element.12) | data formatting | bytes 3932160 | tf_op jit(solution)/shard_map/reshape | solution.py:297
  194.8 6.0 %fusion.31 = f32[80,12,8,8]{2,3,1,0:T(8,128)} fusion(bf16[8,80,12,128]{3,2,1,0:T(8,128)(2,1)S(1)} %reshape.88, bf16[8,80,12,128]{3,2,1,0:T(8,128)(2,1)} %reshape.87), kind=kOutput, calls=%fused_computation.40 | convolution fusion | flops 15728640 | bytes 4177920 | tf_op jit(solution)/shard_map/fphd,gphd->phfg/dot_general | solution.py:228
  200.8 3.0 %copy.31 = f32[80,12,8,8]{0,3,2,1:T(8,128)S(1)} copy(f32[80,12,8,8]{2,3,1,0:T(8,128)} %fusion.31) | data formatting | bytes 491520 | tf_op jit(solution)/shard_map/fphd,gphd->phfg/dot_general | solution.py:228
  206.7 3.7 %reshape.86 = bf16[8,80,12,128]{3,2,1,0:T(8,128)(2,1)S(1)} reshape(bf16[8,80,1536]{2,1,0:T(8,128)(2,1)} %all-to-all-done) | data formatting | bytes 3932160 | tf_op jit(solution)/shard_map/reshape | solution.py:299
  210.4 2.9 %fusion.25 = bf16[8,80,12,128]{3,0,2,1:T(8,128)(2,1)S(1)} fusion(bf16[80,12,8,8]{3,2,1,0:T(8,128)(2,1)} %copy.33, bf16[8,80,12,128]{3,2,1,0:T(8,128)(2,1)S(1)} %reshape.86, f32[8,80,12]{0,2,1:T(8,128)S(1)} %copy.34), kind=kOutput, calls=%fused_computation.33 | convolution fusion | flops 17694720 | bytes 4085760 | tf_op jit(solution)/shard_map/phfg,gphd->fphd/dot_general | solution.py:238
  213.8 2.6 all_to_all.16
  216.4 4.8 %all-to-all-start.1 = ((bf16[8,80,1536]{2,1,0:T(8,128)(2,1)}), bf16[8,80,1536]{2,1,0:T(8,128)(2,1)}, u32[]{:S(2)}, u32[]{:S(2)}) async-start(bf16[8,80,1536]{2,1,0:T(8,128)(2,1)} %all_to_all.16), calls=%async_computation.1 | async-start | bytes 3932160 | tf_op jit(solution)/shard_map/all_to_all | solution.py:303
  221.2 25.0 %all-to-all-done.1 = bf16[8,80,1536]{2,1,0:T(8,128)(2,1)} async-done(((bf16[8,80,1536]{2,1,0:T(8,128)(2,1)}), bf16[8,80,1536]{2,1,0:T(8,128)(2,1)}, u32[]{:S(2)}, u32[]{:S(2)}) %all-to-all-start.1) | async-done | bytes 1966112 | tf_op jit(solution)/shard_map/all_to_all | solution.py:303
  246.2 7.6 %fusion.29 = bf16[1,640,1536]{2,1,0:T(8,128)(2,1)} fusion(bf16[640,1536]{1,0:T(8,128)(2,1)} %bitcast.18, bf16[1536,1536]{1,0:T(8,128)(2,1)} %all-gather.7.cloned.1.call-done), kind=kOutput, calls=%fused_computation.36 | convolution fusion | flops 3020881920 | bytes 8650752 | tf_op jit(solution)/shard_map/dot_general | solution.py:306
  (57 shorter events, 19.2 us)
Async XLA Ops:
  6.5 2.2 copy-start
  6.5 82.2 %all-gather.5.cloned.1.call-start = ((), (), s32[]{:S(2)}) async-start(), calls=%async_computation.2 | async-start | bytes 1769472 | tf_op jit(solution)/shard_map/all_gather | solution.py:261
  8.6 50.8 %copy-start.8 = (f32[1,1536]{1,0:T(1,128)S(1)}, f32[1,1536]{1,0:T(1,128)}, u32[]{:S(2)}) copy-start(f32[1,1536]{1,0:T(1,128)} %param.9) | copy-start | bytes 18436
  8.6 50.8 %copy-start.7 = (f32[1,1536]{1,0:T(1,128)S(1)}, f32[1,1536]{1,0:T(1,128)}, u32[]{:S(2)}) copy-start(f32[1,1536]{1,0:T(1,128)} %param.8) | copy-start | bytes 18436
  8.7 93.2 %all-gather.9.cloned.1.call-start = ((), (), s32[]{:S(2)}) async-start(), calls=%async_computation.4 | async-start | bytes 15925248 | tf_op jit(solution)/shard_map/all_gather | solution.py:257
  10.2 211.1 %all-gather.7.cloned.1.call-start = ((), (), s32[]{:S(2)}) async-start(), calls=%async_computation.3 | async-start | bytes 5898240 | tf_op jit(solution)/shard_map/all_gather | solution.py:262
  59.5 2.7 %copy-start.2 = (bf16[1,640,1536]{2,1,0:T(8,128)(2,1)S(1)}, bf16[1,640,1536]{2,1,0:T(8,128)(2,1)}, u32[]{:S(2)}) copy-start(bf16[1,640,1536]{2,1,0:T(8,128)(2,1)} %param.7) | copy-start | bytes 5898244
  79.9 2.5 copy-start.4
  82.4 0.7 copy-start.9
  82.4 1.3 copy-start.10
  82.4 3.2 %copy-start.3 = (bf16[640,1536]{1,0:T(8,128)(2,1)S(1)}, bf16[640,1536]{1,0:T(8,128)(2,1)}, u32[]{:S(2)}) copy-start(bf16[640,1536]{1,0:T(8,128)(2,1)} %get-tuple-element.8) | copy-start | bytes 5898244
  101.8 4.0 %slice-start = ((bf16[6144,1152]{1,0:T(8,128)(2,1)}), bf16[4608,1152]{1,0:T(8,128)(2,1)S(1)}, s32[]{:S(2)}) async-start(bf16[6144,1152]{1,0:T(8,128)(2,1)} %all-gather.9.cloned.1.call-done), calls=%async_computation.5 | async-start | bytes 21233664 | tf_op jit(solution)/shard_map/slice | solution.py:282
  132.4 2.6 %slice-start.1 = ((bf16[1920,1536]{1,0:T(8,128)(2,1)}), bf16[640,1536]{1,0:T(8,128)(2,1)S(1)}, s32[]{:S(2)}) async-start(bf16[1920,1536]{1,0:T(8,128)(2,1)} %copy-done.4), calls=%async_computation.6 | async-start | bytes 3932160 | tf_op jit(solution)/shard_map/slice | solution.py:275
  132.4 3.2 %copy-start.5 = (bf16[640,1536]{1,0:T(8,128)(2,1)S(1)}, bf16[640,1536]{1,0:T(8,128)(2,1)}, u32[]{:S(2)}) copy-start(bf16[640,1536]{1,0:T(8,128)(2,1)} %fusion.21) | copy-start | bytes 5898244
  174.3 32.4 %all-to-all-start = ((bf16[8,80,1536]{2,1,0:T(8,128)(2,1)}), bf16[8,80,1536]{2,1,0:T(8,128)(2,1)}, u32[]{:S(2)}, u32[]{:S(2)}) async-start(bf16[8,80,1536]{2,1,0:T(8,128)(2,1)} %bitcast.46), calls=%async_computation | async-start | bytes 3932160 | tf_op jit(solution)/shard_map/all_to_all | solution.py:292
  178.8 3.0 %copy-start.6 = (bf16[640,1536]{1,0:T(8,128)(2,1)S(1)}, bf16[640,1536]{1,0:T(8,128)(2,1)}, u32[]{:S(2)}) copy-start(bf16[640,1536]{1,0:T(8,128)(2,1)} %fusion.21) | copy-start | bytes 5898244
  216.4 29.8 %all-to-all-start.1 = ((bf16[8,80,1536]{2,1,0:T(8,128)(2,1)}), bf16[8,80,1536]{2,1,0:T(8,128)(2,1)}, u32[]{:S(2)}, u32[]{:S(2)}) async-start(bf16[8,80,1536]{2,1,0:T(8,128)(2,1)} %all_to_all.16), calls=%async_computation.1 | async-start | bytes 3932160 | tf_op jit(solution)/shard_map/all_to_all | solution.py:303
  246.2 7.6 %copy-start.1 = (bf16[1536,1152]{1,0:T(8,128)(2,1)S(1)}, bf16[1536,1152]{1,0:T(8,128)(2,1)}, u32[]{:S(2)}) copy-start(bf16[1536,1152]{1,0:T(8,128)(2,1)} %param.10) | copy-start | bytes 10616836
Sparse Core Ops, SparseCore 0:
  9.0 15.5 all-gather.4
  26.3 75.4 all-gather.8
  103.5 52.7 all-gather.6

commit v10 on v9

--- a/solution.py
+++ b/solution.py
@@ -49,16 +49,15 @@
                 )
                 * scaling
             )
-            key_pos = tile_id * TILE + lax.broadcasted_iota(jnp.int32, scores.shape, 1)
-            live = key_pos < count_here
-            scores = jnp.where(live, scores, -1e30)
+            key_pos = tile_id * TILE + lax.broadcasted_iota(jnp.int32, (1, TILE), 1)
+            scores = scores + jnp.where(key_pos < count_here, 0.0, -1e30)
             block_max = scores if block_max is None else jnp.maximum(block_max, scores)
-            parts.append((scores, live, start))
+            parts.append((scores, start))
         row_max = jnp.max(block_max, axis=-1, keepdims=True)
         exp_total = None
         summed = None
-        for scores, live, start in parts:
-            exp_terms = jnp.where(live, jnp.exp(scores - row_max), 0.0)
+        for scores, start in parts:
+            exp_terms = jnp.exp(scores - row_max)
             value = v_ref[pl.ds(start, TILE), :]
             part_out = jnp.dot(
                 exp_terms.astype(jnp.bfloat16), value, preferred_element_type=jnp.float32

time: 261 us -> 260 us (level)
  no operation moved by 1% of the time
where the time goes in v10:
time: 260 us
  Pallas kernels  78.4 us (30%)
  matrix products  52.7 us (20%)
  local copies, waits for them, and re-layouts  42.7 us (16%)
  waiting for transfers between devices  38.2 us (15%)
  other arithmetic  25 us (10%)
  between operations  13.3 us (5%)
  starting transfers between devices  9.4 us (4%)
    pallas_call x1, Pallas kernels, exchange_tokens(): pl.pallas_call(exchange_kernel, out_shape=(jax.ShapeDtypeStruct((2, rows,...  49.2 us
    pallas_call x1, Pallas kernels, spatial_rows(): pl.pallas_call(spatial_kernel, grid_spec=grid_spec, out_shape=jax.ShapeDt...  29.2 us
    dot_general x1, matrix products, local(): jnp.einsum('tk,jkc->jtc', normed_all, w_full[1:], preferred_element_type=...  25.2 us
    all_to_all x1, waiting for transfers between devices, local(): lax.all_to_all(temporal.reshape(tok_count, feat_count), frame_axes, split...  25 us
    convert_element_type x2, other arithmetic, layer_norm(): return (normal * (1.0 + mod_scale) + mod_shift).astype(jnp.bfloat16)  13.3 us
    all_gather x1, waiting for transfers between devices, local(): w_pieces = lax.all_gather(w_half, ('fsdp', 'core'), axis=0, tiled=False)  13.1 us
    dot_general x1, matrix products, local(): jnp.dot(flat_temporal, w_out_full, preferred_element_type=jnp.float32)  7.56 us
    dot_general x1, matrix products, local(): jnp.dot(jnp.concatenate([normed_all[tok_count:2 * tok_count], normed_cros...  6.6 us
  transfers between devices with their start and end apart: 5, of which 2 were waited for; matrix products, arithmetic and copies ran while one was open for 38% of the time, Pallas kernels for 30%

profile of v10, /device:TPU:1, one launch (start us, length us, event | category | flops | bytes accessed | tf_op | source)
XLA Modules:
  0.0 259.7 jit_solution(13840498898432429808)
XLA Ops:
  10.2 49.2 %shard_map.73 = (bf16[2,640,1536]{2,1,0:T(8,128)(2,1)}, bf16[640,1536]{1,0:T(8,128)(2,1)}) custom-call(bf16[640,1536]{1,0:T(8,128)(2,1)} %bitcast.39), custom_call_target="tpu_custom_call" | custom-call | bytes 157286400 | tf_op jit(solution)/shard_map/pallas_call | solution.py:201
  59.5 2.5 select_bitcast_fusion.1
  63.3 5.4 %fusion.3 = f32[1920]{0:T(1024)S(1)} fusion(f32[1920]{0:T(1024)S(1)} %broadcast_multiply_fusion, bf16[640,1536]{1,0:T(8,128)(2,1)S(1)} %get-tuple-element.14, bf16[640,1536]{1,0:T(8,128)(2,1)S(1)} %bitcast.41, bf16[640,1536]{1,0:T(8,128)(2,1)S(1)} %get-tuple-element.13), kind=kLoop, calls=%fused_computation.6 | loop fusion | flops 26540160 | bytes 5913600 | tf_op jit(solution)/shard_map/reduce_sum | solution.py:28
  68.7 11.2 %fusion.6 = bf16[1920,1536]{1,0:T(8,128)(2,1)S(1)} fusion(f32[1536]{0:T(1024)S(1)} %reduce.2, f32[1536]{0:T(1024)S(1)} %add_reduce_fusion, f32[1920]{0:T(1024)S(1)} %add_sqrt_fusion, f32[1920]{0:T(1024)S(1)} %broadcast_multiply_fusion, bf16[640,1536]{1,0:T(8,128)(2,1)S(1)} %get-tuple-element.14, bf16[640,1536]{1,0:T(8,128)(2,1)S(1)} %bitcast.42, ...), kind=kLoop, calls=%fused_computation.9 | loop fusion | flops 32440320 | bytes 11824128 | tf_op jit(solution)/shard_map/convert_element_type | solution.py:30
  79.9 2.5 copy-done.4
  88.7 13.1 %all-gather.9.cloned.1.call-done = bf16[6144,1152]{1,0:T(8,128)(2,1)} async-done(((bf16[768,1152]{1,0:T(8,128)(2,1)}), bf16[6144,1152]{1,0:T(8,128)(2,1)}) %all-gather.9.cloned.1.call-update) | async-done | bytes 14155792 | tf_op jit(solution)/shard_map/all_gather | solution.py:256
  101.8 4.0 %slice-done = bf16[4608,1152]{1,0:T(8,128)(2,1)S(1)} async-done(((bf16[6144,1152]{1,0:T(8,128)(2,1)}), bf16[4608,1152]{1,0:T(8,128)(2,1)S(1)}, s32[]{:S(2)}) %slice-start) | async-done | bytes 10616856 | tf_op jit(solution)/shard_map/slice | solution.py:281
  105.9 25.2 %fusion.7.k_ref.v_ref = bf16[3,1920,1152]{2,1,0:T(8,128)(2,1)} fusion(bf16[3,1536,1152]{2,1,0:T(8,128)(2,1)S(1)} %bitcast.45, bf16[1920,1536]{1,0:T(8,128)(2,1)} %copy-done.4), kind=kOutput, calls=%fused_computation.10 | convolution fusion | flops 20390952960 | bytes 29786112 | tf_op jit(solution)/shard_map/tk,jkc->jtc/dot_general | solution.py:280
  132.5 2.4 slice.48
  135.7 6.6 %convolution_convert_fusion.1 = bf16[1280,1536]{1,0:T(8,128)(2,1)S(1)} fusion(bf16[1536,384]{1,0:T(8,128)(2,1)S(1)} %slice_bitcast_fusion.2, bf16[1536,1152]{1,0:T(8,128)(2,1)S(1)} %slice.48, bf16[640,1536]{1,0:T(8,128)(2,1)S(1)} %copy-done.5, bf16[640,1536]{1,0:T(8,128)(2,1)S(1)} %slice-done.1), kind=kOutput, calls=%fused_computation.11 | convolution fusion | flops 6059065344 | bytes 12582912 | tf_op jit(solution)/shard_map/dot_general | solution.py:273
  144.5 29.2 %shard_map.74 = bf16[640,1536]{1,0:T(8,128)(2,1)} custom-call(s32[30]{0:T(128)} %reshape_squeeze.3.list_ref, s32[2]{0:T(128)} %pad_add_fusion.scalar_ref, bf16[640,1536]{1,0:T(8,128)(2,1)} %get-tuple-element.11.q_ref, bf16[3,1920,1152]{2,1,0:T(8,128)(2,1)} %fusion.7.k_ref.v_ref, bf16[3,1920,1152]{2,1,0:T(8,128)(2,1)} %fusion.7.k_ref.v_ref), custom_call_target="tpu_custom_call" | custom-call | flops 3019898880 | bytes 15728640 | tf_op jit(solution)/shard_map/pallas_call | solution.py:97
  173.7 4.5 %all-to-all-start = ((bf16[8,80,1536]{2,1,0:T(8,128)(2,1)}), bf16[8,80,1536]{2,1,0:T(8,128)(2,1)}, u32[]{:S(2)}, u32[]{:S(2)}) async-start(bf16[8,80,1536]{2,1,0:T(8,128)(2,1)} %bitcast.46), calls=%async_computation | async-start | bytes 3932160 | tf_op jit(solution)/shard_map/all_to_all | solution.py:291
  178.2 2.8 %slice_bitcast_fusion.1 = (bf16[1536,768]{1,0:T(8,128)(2,1)S(1)}, bf16[1536,768]{1,0:T(8,128)(2,1)S(1)}) fusion(bf16[4,1536,1152]{2,1,0:T(8,128)(2,1)} %bitcast.44), kind=kLoop, calls=%fused_computation.38 | loop fusion | bytes 9437184 | tf_op jit(solution)/shard_map/squeeze | solution.py:271
  181.2 4.5 %fusion.26 = bf16[640,1536]{1,0:T(8,128)(2,1)} fusion(bf16[640,1536]{1,0:T(8,128)(2,1)S(1)} %copy-done.6, bf16[1536,768]{1,0:T(8,128)(2,1)S(1)} %get-tuple-element.10, bf16[1536,768]{1,0:T(8,128)(2,1)S(1)} %get-tuple-element.9), kind=kOutput, calls=%fused_computation.35 | convolution fusion | flops 3030319104 | bytes 8650752 | tf_op jit(solution)/shard_map/dot_general | solution.py:279
  185.6 3.7 %reshape.88 = bf16[8,80,12,128]{3,2,1,0:T(8,128)(2,1)S(1)} reshape(bf16[640,1536]{1,0:T(8,128)(2,1)} %fusion.26) | data formatting | bytes 3932160 | tf_op jit(solution)/shard_map/reshape | solution.py:297
  189.4 4.7 %reshape.87 = bf16[8,80,12,128]{3,2,1,0:T(8,128)(2,1)} reshape(bf16[640,1536]{1,0:T(8,128)(2,1)} %get-tuple-element.12) | data formatting | bytes 3932160 | tf_op jit(solution)/shard_map/reshape | solution.py:296
  194.1 6.0 %fusion.31 = f32[80,12,8,8]{2,3,1,0:T(8,128)} fusion(bf16[8,80,12,128]{3,2,1,0:T(8,128)(2,1)S(1)} %reshape.88, bf16[8,80,12,128]{3,2,1,0:T(8,128)(2,1)} %reshape.87), kind=kOutput, calls=%fused_computation.40 | convolution fusion | flops 15728640 | bytes 4177920 | tf_op jit(solution)/shard_map/fphd,gphd->phfg/dot_general | solution.py:227
  200.1 3.0 %copy.31 = f32[80,12,8,8]{0,3,2,1:T(8,128)S(1)} copy(f32[80,12,8,8]{2,3,1,0:T(8,128)} %fusion.31) | data formatting | bytes 491520 | tf_op jit(solution)/shard_map/fphd,gphd->phfg/dot_general | solution.py:227
  206.0 3.7 %reshape.86 = bf16[8,80,12,128]{3,2,1,0:T(8,128)(2,1)S(1)} reshape(bf16[8,80,1536]{2,1,0:T(8,128)(2,1)} %all-to-all-done) | data formatting | bytes 3932160 | tf_op jit(solution)/shard_map/reshape | solution.py:298
  209.8 2.9 %fusion.25 = bf16[8,80,12,128]{3,0,2,1:T(8,128)(2,1)S(1)} fusion(bf16[80,12,8,8]{3,2,1,0:T(8,128)(2,1)} %copy.33, bf16[8,80,12,128]{3,2,1,0:T(8,128)(2,1)S(1)} %reshape.86, f32[8,80,12]{0,2,1:T(8,128)S(1)} %copy.34), kind=kOutput, calls=%fused_computation.33 | convolution fusion | flops 17694720 | bytes 4085760 | tf_op jit(solution)/shard_map/phfg,gphd->fphd/dot_general | solution.py:237
  213.2 2.6 all_to_all.16
  215.8 4.8 %all-to-all-start.1 = ((bf16[8,80,1536]{2,1,0:T(8,128)(2,1)}), bf16[8,80,1536]{2,1,0:T(8,128)(2,1)}, u32[]{:S(2)}, u32[]{:S(2)}) async-start(bf16[8,80,1536]{2,1,0:T(8,128)(2,1)} %all_to_all.16), calls=%async_computation.1 | async-start | bytes 3932160 | tf_op jit(solution)/shard_map/all_to_all | solution.py:302
  220.5 25.0 %all-to-all-done.1 = bf16[8,80,1536]{2,1,0:T(8,128)(2,1)} async-done(((bf16[8,80,1536]{2,1,0:T(8,128)(2,1)}), bf16[8,80,1536]{2,1,0:T(8,128)(2,1)}, u32[]{:S(2)}, u32[]{:S(2)}) %all-to-all-start.1) | async-done | bytes 1966112 | tf_op jit(solution)/shard_map/all_to_all | solution.py:302
  245.6 7.6 %fusion.29 = bf16[1,640,1536]{2,1,0:T(8,128)(2,1)} fusion(bf16[640,1536]{1,0:T(8,128)(2,1)} %bitcast.18, bf16[1536,1536]{1,0:T(8,128)(2,1)} %all-gather.7.cloned.1.call-done), kind=kOutput, calls=%fused_computation.36 | convolution fusion | flops 3020881920 | bytes 8650752 | tf_op jit(solution)/shard_map/dot_general | solution.py:305
  (57 shorter events, 19.2 us)
Async XLA Ops:
  6.5 2.2 copy-start
  6.5 82.2 %all-gather.5.cloned.1.call-start = ((), (), s32[]{:S(2)}) async-start(), calls=%async_computation.2 | async-start | bytes 1769472 | tf_op jit(solution)/shard_map/all_gather | solution.py:260
  8.6 50.8 %copy-start.8 = (f32[1,1536]{1,0:T(1,128)S(1)}, f32[1,1536]{1,0:T(1,128)}, u32[]{:S(2)}) copy-start(f32[1,1536]{1,0:T(1,128)} %param.9) | copy-start | bytes 18436
  8.6 50.8 %copy-start.7 = (f32[1,1536]{1,0:T(1,128)S(1)}, f32[1,1536]{1,0:T(1,128)}, u32[]{:S(2)}) copy-start(f32[1,1536]{1,0:T(1,128)} %param.8) | copy-start | bytes 18436
  8.7 93.2 %all-gather.9.cloned.1.call-start = ((), (), s32[]{:S(2)}) async-start(), calls=%async_computation.4 | async-start | bytes 15925248 | tf_op jit(solution)/shard_map/all_gather | solution.py:256
  10.2 210.4 %all-gather.7.cloned.1.call-start = ((), (), s32[]{:S(2)}) async-start(), calls=%async_computation.3 | async-start | bytes 5898240 | tf_op jit(solution)/shard_map/all_gather | solution.py:261
  59.5 2.7 %copy-start.2 = (bf16[1,640,1536]{2,1,0:T(8,128)(2,1)S(1)}, bf16[1,640,1536]{2,1,0:T(8,128)(2,1)}, u32[]{:S(2)}) copy-start(bf16[1,640,1536]{2,1,0:T(8,128)(2,1)} %param.7) | copy-start | bytes 5898244
  79.9 2.5 copy-start.4
  82.4 0.7 copy-start.9
  82.4 1.3 copy-start.10
  82.4 3.2 %copy-start.3 = (bf16[640,1536]{1,0:T(8,128)(2,1)S(1)}, bf16[640,1536]{1,0:T(8,128)(2,1)}, u32[]{:S(2)}) copy-start(bf16[640,1536]{1,0:T(8,128)(2,1)} %get-tuple-element.8) | copy-start | bytes 5898244
  101.8 4.0 %slice-start = ((bf16[6144,1152]{1,0:T(8,128)(2,1)}), bf16[4608,1152]{1,0:T(8,128)(2,1)S(1)}, s32[]{:S(2)}) async-start(bf16[6144,1152]{1,0:T(8,128)(2,1)} %all-gather.9.cloned.1.call-done), calls=%async_computation.5 | async-start | bytes 21233664 | tf_op jit(solution)/shard_map/slice | solution.py:281
  132.4 2.6 %slice-start.1 = ((bf16[1920,1536]{1,0:T(8,128)(2,1)}), bf16[640,1536]{1,0:T(8,128)(2,1)S(1)}, s32[]{:S(2)}) async-start(bf16[1920,1536]{1,0:T(8,128)(2,1)} %copy-done.4), calls=%async_computation.6 | async-start | bytes 3932160 | tf_op jit(solution)/shard_map/slice | solution.py:274
  132.4 3.2 %copy-start.5 = (bf16[640,1536]{1,0:T(8,128)(2,1)S(1)}, bf16[640,1536]{1,0:T(8,128)(2,1)}, u32[]{:S(2)}) copy-start(bf16[640,1536]{1,0:T(8,128)(2,1)} %fusion.21) | copy-start | bytes 5898244
  173.7 32.4 %all-to-all-start = ((bf16[8,80,1536]{2,1,0:T(8,128)(2,1)}), bf16[8,80,1536]{2,1,0:T(8,128)(2,1)}, u32[]{:S(2)}, u32[]{:S(2)}) async-start(bf16[8,80,1536]{2,1,0:T(8,128)(2,1)} %bitcast.46), calls=%async_computation | async-start | bytes 3932160 | tf_op jit(solution)/shard_map/all_to_all | solution.py:291
  178.2 3.0 %copy-start.6 = (bf16[640,1536]{1,0:T(8,128)(2,1)S(1)}, bf16[640,1536]{1,0:T(8,128)(2,1)}, u32[]{:S(2)}) copy-start(bf16[640,1536]{1,0:T(8,128)(2,1)} %fusion.21) | copy-start | bytes 5898244
  215.8 29.8 %all-to-all-start.1 = ((bf16[8,80,1536]{2,1,0:T(8,128)(2,1)}), bf16[8,80,1536]{2,1,0:T(8,128)(2,1)}, u32[]{:S(2)}, u32[]{:S(2)}) async-start(bf16[8,80,1536]{2,1,0:T(8,128)(2,1)} %all_to_all.16), calls=%async_computation.1 | async-start | bytes 3932160 | tf_op jit(solution)/shard_map/all_to_all | solution.py:302
  245.6 7.6 %copy-start.1 = (bf16[1536,1152]{1,0:T(8,128)(2,1)S(1)}, bf16[1536,1152]{1,0:T(8,128)(2,1)}, u32[]{:S(2)}) copy-start(bf16[1536,1152]{1,0:T(8,128)(2,1)} %param.10) | copy-start | bytes 10616836
Sparse Core Ops, SparseCore 0:
  9.0 15.5 all-gather.4
  26.3 75.4 all-gather.8
  103.5 52.7 all-gather.6

commit v11 on v10

--- a/solution.py
+++ b/solution.py
@@ -35,14 +35,15 @@
     first_tile = scalar_ref[0]
     count_here = scalar_ref[1]
     local_tiles = q_ref.shape[0] // TILE
-    for t in range(local_tiles):
-        query = q_ref[t * TILE : (t + 1) * TILE, :]
+    for t, c in [(t, c) for c in range(q_ref.shape[1] // HD) for t in range(local_tiles)]:
+        cols = slice(c * HD, (c + 1) * HD)
+        query = q_ref[t * TILE : (t + 1) * TILE, cols]
         parts = []
         block_max = None
         for n in range(NBR):
             tile_id = list_ref[t * NBR + n]
             start = pl.multiple_of((tile_id - first_tile) * TILE, TILE)
-            key = k_ref[pl.ds(start, TILE), :]
+            key = k_ref[pl.ds(start, TILE), cols]
             scores = (
                 lax.dot_general(
                     query, key, (((1,), (1,)), ((), ())), preferred_element_type=jnp.float32
@@ -58,40 +59,38 @@
         summed = None
         for scores, start in parts:
             exp_terms = jnp.exp(scores - row_max)
-            value = v_ref[pl.ds(start, TILE), :]
+            value = v_ref[pl.ds(start, TILE), cols]
             part_out = jnp.dot(
                 exp_terms.astype(jnp.bfloat16), value, preferred_element_type=jnp.float32
             )
             exp_total = exp_terms if exp_total is None else exp_total + exp_terms
             summed = part_out if summed is None else summed + part_out
         denominator = jnp.sum(exp_total, axis=-1, keepdims=True)
-        o_ref[t * TILE : (t + 1) * TILE, :] = (summed / denominator).astype(o_ref.dtype)
+        o_ref[t * TILE : (t + 1) * TILE, cols] = (summed / denominator).astype(o_ref.dtype)
 
 
 def spatial_rows(queries, kv_all, tile_list, first_tile, count_here):
     buffer_rows = kv_all.shape[1]
     rows, feat = queries.shape
-    per_shard = kv_all.shape[2] // HD
     scalars = jnp.stack([first_tile, count_here]).astype(jnp.int32)
+    width = 3 * HD
+    per_shard = kv_all.shape[2] // width
+    k0 = feat // width
     grid_spec = pltpu.PrefetchScalarGridSpec(
         num_scalar_prefetch=2,
-        grid=(HEADS,),
+        grid=(feat // width,),
         in_specs=[
-            pl.BlockSpec((rows, HD), lambda h, lst, sc: (0, h)),
+            pl.BlockSpec((rows, width), lambda g, lst, sc: (0, g)),
             pl.BlockSpec(
-                (None, buffer_rows, HD),
-                lambda h, lst, sc: ((HEADS + h) // per_shard - 1, 0, (HEADS + h) % per_shard),
+                (None, buffer_rows, width),
+                lambda g, lst, sc: ((k0 + g) // per_shard - 1, 0, (k0 + g) % per_shard),
             ),
             pl.BlockSpec(
-                (None, buffer_rows, HD),
-                lambda h, lst, sc: (
-                    (2 * HEADS + h) // per_shard - 1,
-                    0,
-                    (2 * HEADS + h) % per_shard,
-                ),
+                (None, buffer_rows, width),
+                lambda g, lst, sc: ((2 * k0 + g) // per_shard - 1, 0, (2 * k0 + g) % per_shard),
             ),
         ],
-        out_specs=pl.BlockSpec((rows, HD), lambda h, lst, sc: (0, h)),
+        out_specs=pl.BlockSpec((rows, width), lambda g, lst, sc: (0, g)),
     )
     flops = 4 * rows * NBR * TILE * feat
     return pl.pallas_call(

time: 260 us -> 259 us (level)
  transfers between devices with their start and end apart: 5 -> 5, of which waited for: 2 -> 2; matrix products, arithmetic and copies ran while one was open for 38% -> 39% of each run, Pallas kernels for 30% -> 30%
where the time goes in v11:
time: 259 us; the launch traced here: 258 us
  Pallas kernels  76.5 us (30%)
  matrix products  52.7 us (20%)
  local copies, waits for them, and re-layouts  42.7 us (16%)
  waiting for transfers between devices  38.2 us (15%)
  other arithmetic  25 us (10%)
  between operations  13.3 us (5%)
  starting transfers between devices  9.44 us (4%)
    pallas_call x1, Pallas kernels, exchange_tokens(): pl.pallas_call(exchange_kernel, out_shape=(jax.ShapeDtypeStruct((2, rows,...  49.2 us
    pallas_call x1, Pallas kernels, spatial_rows(): pl.pallas_call(spatial_kernel, grid_spec=grid_spec, out_shape=jax.ShapeDt...  27.3 us
    dot_general x1, matrix products, local(): jnp.einsum('tk,jkc->jtc', normed_all, w_full[1:], preferred_element_type=...  25.2 us
    all_to_all x1, waiting for transfers between devices, local(): lax.all_to_all(temporal.reshape(tok_count, feat_count), frame_axes, split...  25 us
    convert_element_type x2, other arithmetic, layer_norm(): return (normal * (1.0 + mod_scale) + mod_shift).astype(jnp.bfloat16)  13.3 us
    all_gather x1, waiting for transfers between devices, local(): w_pieces = lax.all_gather(w_half, ('fsdp', 'core'), axis=0, tiled=False)  13.1 us
    dot_general x1, matrix products, local(): jnp.dot(flat_temporal, w_out_full, preferred_element_type=jnp.float32)  7.56 us
    dot_general x1, matrix products, local(): jnp.dot(jnp.concatenate([normed_all[tok_count:2 * tok_count], normed_cros...  6.6 us
  transfers between devices with their start and end apart: 5, of which 2 were waited for; matrix products, arithmetic and copies ran while one was open for 39% of the time, Pallas kernels for 30%

profile of v11, /device:TPU:1, one launch (start us, length us, event | category | flops | bytes accessed | tf_op | source)
XLA Modules:
  0.0 257.8 jit_solution(7594396042853720597)
XLA Ops:
  10.2 49.2 %shard_map.73 = (bf16[2,640,1536]{2,1,0:T(8,128)(2,1)}, bf16[640,1536]{1,0:T(8,128)(2,1)}) custom-call(bf16[640,1536]{1,0:T(8,128)(2,1)} %bitcast.39), custom_call_target="tpu_custom_call" | custom-call | bytes 157286400 | tf_op jit(solution)/shard_map/pallas_call | solution.py:200
  59.5 2.5 select_bitcast_fusion.1
  63.3 5.4 %fusion.3 = f32[1920]{0:T(1024)S(1)} fusion(f32[1920]{0:T(1024)S(1)} %broadcast_multiply_fusion, bf16[640,1536]{1,0:T(8,128)(2,1)S(1)} %get-tuple-element.14, bf16[640,1536]{1,0:T(8,128)(2,1)S(1)} %bitcast.41, bf16[640,1536]{1,0:T(8,128)(2,1)S(1)} %get-tuple-element.13), kind=kLoop, calls=%fused_computation.6 | loop fusion | flops 26540160 | bytes 5913600 | tf_op jit(solution)/shard_map/reduce_sum | solution.py:28
  68.7 11.2 %fusion.6 = bf16[1920,1536]{1,0:T(8,128)(2,1)S(1)} fusion(f32[1536]{0:T(1024)S(1)} %reduce.2, f32[1536]{0:T(1024)S(1)} %add_reduce_fusion, f32[1920]{0:T(1024)S(1)} %add_sqrt_fusion, f32[1920]{0:T(1024)S(1)} %broadcast_multiply_fusion, bf16[640,1536]{1,0:T(8,128)(2,1)S(1)} %get-tuple-element.14, bf16[640,1536]{1,0:T(8,128)(2,1)S(1)} %bitcast.42, ...), kind=kLoop, calls=%fused_computation.9 | loop fusion | flops 32440320 | bytes 11824128 | tf_op jit(solution)/shard_map/convert_element_type | solution.py:30
  79.9 2.5 copy-done.4
  88.7 13.1 %all-gather.9.cloned.1.call-done = bf16[6144,1152]{1,0:T(8,128)(2,1)} async-done(((bf16[768,1152]{1,0:T(8,128)(2,1)}), bf16[6144,1152]{1,0:T(8,128)(2,1)}) %all-gather.9.cloned.1.call-update) | async-done | bytes 14155792 | tf_op jit(solution)/shard_map/all_gather | solution.py:255
  101.8 4.0 %slice-done = bf16[4608,1152]{1,0:T(8,128)(2,1)S(1)} async-done(((bf16[6144,1152]{1,0:T(8,128)(2,1)}), bf16[4608,1152]{1,0:T(8,128)(2,1)S(1)}, s32[]{:S(2)}) %slice-start) | async-done | bytes 10616856 | tf_op jit(solution)/shard_map/slice | solution.py:280
  105.9 25.2 %fusion.7.k_ref.v_ref = bf16[3,1920,1152]{2,1,0:T(8,128)(2,1)} fusion(bf16[3,1536,1152]{2,1,0:T(8,128)(2,1)S(1)} %bitcast.45, bf16[1920,1536]{1,0:T(8,128)(2,1)} %copy-done.4), kind=kOutput, calls=%fused_computation.10 | convolution fusion | flops 20390952960 | bytes 29786112 | tf_op jit(solution)/shard_map/tk,jkc->jtc/dot_general | solution.py:279
  132.5 2.4 slice.48
  135.7 6.6 %convolution_convert_fusion.1 = bf16[1280,1536]{1,0:T(8,128)(2,1)S(1)} fusion(bf16[1536,384]{1,0:T(8,128)(2,1)S(1)} %slice_bitcast_fusion.2, bf16[1536,1152]{1,0:T(8,128)(2,1)S(1)} %slice.48, bf16[640,1536]{1,0:T(8,128)(2,1)S(1)} %copy-done.5, bf16[640,1536]{1,0:T(8,128)(2,1)S(1)} %slice-done.1), kind=kOutput, calls=%fused_computation.11 | convolution fusion | flops 6059065344 | bytes 12582912 | tf_op jit(solution)/shard_map/dot_general | solution.py:272
  144.5 27.3 %shard_map.74 = bf16[640,1536]{1,0:T(8,128)(2,1)} custom-call(s32[30]{0:T(128)} %reshape_squeeze.3.list_ref, s32[2]{0:T(128)} %pad_add_fusion.scalar_ref, bf16[640,1536]{1,0:T(8,128)(2,1)} %get-tuple-element.11.q_ref, bf16[3,1920,1152]{2,1,0:T(8,128)(2,1)} %fusion.7.k_ref.v_ref, bf16[3,1920,1152]{2,1,0:T(8,128)(2,1)} %fusion.7.k_ref.v_ref), custom_call_target="tpu_custom_call" | custom-call | flops 3019898880 | bytes 15728640 | tf_op jit(solution)/shard_map/pallas_call | solution.py:96
  171.8 4.5 %all-to-all-start = ((bf16[8,80,1536]{2,1,0:T(8,128)(2,1)}), bf16[8,80,1536]{2,1,0:T(8,128)(2,1)}, u32[]{:S(2)}, u32[]{:S(2)}) async-start(bf16[8,80,1536]{2,1,0:T(8,128)(2,1)} %bitcast.46), calls=%async_computation | async-start | bytes 3932160 | tf_op jit(solution)/shard_map/all_to_all | solution.py:290
  176.3 2.8 %slice_bitcast_fusion.1 = (bf16[1536,768]{1,0:T(8,128)(2,1)S(1)}, bf16[1536,768]{1,0:T(8,128)(2,1)S(1)}) fusion(bf16[4,1536,1152]{2,1,0:T(8,128)(2,1)} %bitcast.44), kind=kLoop, calls=%fused_computation.38 | loop fusion | bytes 9437184 | tf_op jit(solution)/shard_map/squeeze | solution.py:270
  179.3 4.5 %fusion.26 = bf16[640,1536]{1,0:T(8,128)(2,1)} fusion(bf16[640,1536]{1,0:T(8,128)(2,1)S(1)} %copy-done.6, bf16[1536,768]{1,0:T(8,128)(2,1)S(1)} %get-tuple-element.10, bf16[1536,768]{1,0:T(8,128)(2,1)S(1)} %get-tuple-element.9), kind=kOutput, calls=%fused_computation.35 | convolution fusion | flops 3030319104 | bytes 8650752 | tf_op jit(solution)/shard_map/dot_general | solution.py:278
  183.8 3.7 %reshape.88 = bf16[8,80,12,128]{3,2,1,0:T(8,128)(2,1)S(1)} reshape(bf16[640,1536]{1,0:T(8,128)(2,1)} %fusion.26) | data formatting | bytes 3932160 | tf_op jit(solution)/shard_map/reshape | solution.py:296
  187.5 4.7 %reshape.87 = bf16[8,80,12,128]{3,2,1,0:T(8,128)(2,1)} reshape(bf16[640,1536]{1,0:T(8,128)(2,1)} %get-tuple-element.12) | data formatting | bytes 3932160 | tf_op jit(solution)/shard_map/reshape | solution.py:295
  192.3 6.0 %fusion.31 = f32[80,12,8,8]{2,3,1,0:T(8,128)} fusion(bf16[8,80,12,128]{3,2,1,0:T(8,128)(2,1)S(1)} %reshape.88, bf16[8,80,12,128]{3,2,1,0:T(8,128)(2,1)} %reshape.87), kind=kOutput, calls=%fused_computation.40 | convolution fusion | flops 15728640 | bytes 4177920 | tf_op jit(solution)/shard_map/fphd,gphd->phfg/dot_general | solution.py:226
  198.3 3.0 %copy.31 = f32[80,12,8,8]{0,3,2,1:T(8,128)S(1)} copy(f32[80,12,8,8]{2,3,1,0:T(8,128)} %fusion.31) | data formatting | bytes 491520 | tf_op jit(solution)/shard_map/fphd,gphd->phfg/dot_general | solution.py:226
  204.2 3.7 %reshape.86 = bf16[8,80,12,128]{3,2,1,0:T(8,128)(2,1)S(1)} reshape(bf16[8,80,1536]{2,1,0:T(8,128)(2,1)} %all-to-all-done) | data formatting | bytes 3932160 | tf_op jit(solution)/shard_map/reshape | solution.py:297
  207.9 2.9 %fusion.25 = bf16[8,80,12,128]{3,0,2,1:T(8,128)(2,1)S(1)} fusion(bf16[80,12,8,8]{3,2,1,0:T(8,128)(2,1)} %copy.33, bf16[8,80,12,128]{3,2,1,0:T(8,128)(2,1)S(1)} %reshape.86, f32[8,80,12]{0,2,1:T(8,128)S(1)} %copy.34), kind=kOutput, calls=%fused_computation.33 | convolution fusion | flops 17694720 | bytes 4085760 | tf_op jit(solution)/shard_map/phfg,gphd->fphd/dot_general | solution.py:236
  211.3 2.6 %all_to_all.16 = bf16[8,80,1536]{2,1,0:T(8,128)(2,1)} reshape(bf16[8,80,12,128]{3,2,1,0:T(8,128)(2,1)S(1)} %copy.35) | data formatting | bytes 3932160 | tf_op jit(solution)/shard_map/all_to_all | solution.py:301
  213.9 4.8 %all-to-all-start.1 = ((bf16[8,80,1536]{2,1,0:T(8,128)(2,1)}), bf16[8,80,1536]{2,1,0:T(8,128)(2,1)}, u32[]{:S(2)}, u32[]{:S(2)}) async-start(bf16[8,80,1536]{2,1,0:T(8,128)(2,1)} %all_to_all.16), calls=%async_computation.1 | async-start | bytes 3932160 | tf_op jit(solution)/shard_map/all_to_all | solution.py:301
  218.7 25.0 %all-to-all-done.1 = bf16[8,80,1536]{2,1,0:T(8,128)(2,1)} async-done(((bf16[8,80,1536]{2,1,0:T(8,128)(2,1)}), bf16[8,80,1536]{2,1,0:T(8,128)(2,1)}, u32[]{:S(2)}, u32[]{:S(2)}) %all-to-all-start.1) | async-done | bytes 1966112 | tf_op jit(solution)/shard_map/all_to_all | solution.py:301
  243.7 7.6 %fusion.29 = bf16[1,640,1536]{2,1,0:T(8,128)(2,1)} fusion(bf16[640,1536]{1,0:T(8,128)(2,1)} %bitcast.18, bf16[1536,1536]{1,0:T(8,128)(2,1)} %all-gather.7.cloned.1.call-done), kind=kOutput, calls=%fused_computation.36 | convolution fusion | flops 3020881920 | bytes 8650752 | tf_op jit(solution)/shard_map/dot_general | solution.py:304
  (57 shorter events, 19.2 us)
Async XLA Ops:
  6.5 2.2 copy-start
  6.5 82.2 %all-gather.5.cloned.1.call-start = ((), (), s32[]{:S(2)}) async-start(), calls=%async_computation.2 | async-start | bytes 1769472 | tf_op jit(solution)/shard_map/all_gather | solution.py:259
  8.6 50.8 %copy-start.8 = (f32[1,1536]{1,0:T(1,128)S(1)}, f32[1,1536]{1,0:T(1,128)}, u32[]{:S(2)}) copy-start(f32[1,1536]{1,0:T(1,128)} %param.9) | copy-start | bytes 18436
  8.6 50.8 %copy-start.7 = (f32[1,1536]{1,0:T(1,128)S(1)}, f32[1,1536]{1,0:T(1,128)}, u32[]{:S(2)}) copy-start(f32[1,1536]{1,0:T(1,128)} %param.8) | copy-start | bytes 18436
  8.7 93.2 %all-gather.9.cloned.1.call-start = ((), (), s32[]{:S(2)}) async-start(), calls=%async_computation.4 | async-start | bytes 15925248 | tf_op jit(solution)/shard_map/all_gather | solution.py:255
  10.2 208.6 %all-gather.7.cloned.1.call-start = ((), (), s32[]{:S(2)}) async-start(), calls=%async_computation.3 | async-start | bytes 5898240 | tf_op jit(solution)/shard_map/all_gather | solution.py:260
  59.5 2.7 %copy-start.2 = (bf16[1,640,1536]{2,1,0:T(8,128)(2,1)S(1)}, bf16[1,640,1536]{2,1,0:T(8,128)(2,1)}, u32[]{:S(2)}) copy-start(bf16[1,640,1536]{2,1,0:T(8,128)(2,1)} %param.7) | copy-start | bytes 5898244
  79.9 2.5 copy-start.4
  82.4 0.7 copy-start.9
  82.4 1.3 copy-start.10
  82.4 3.2 %copy-start.3 = (bf16[640,1536]{1,0:T(8,128)(2,1)S(1)}, bf16[640,1536]{1,0:T(8,128)(2,1)}, u32[]{:S(2)}) copy-start(bf16[640,1536]{1,0:T(8,128)(2,1)} %get-tuple-element.8) | copy-start | bytes 5898244
  101.8 4.0 %slice-start = ((bf16[6144,1152]{1,0:T(8,128)(2,1)}), bf16[4608,1152]{1,0:T(8,128)(2,1)S(1)}, s32[]{:S(2)}) async-start(bf16[6144,1152]{1,0:T(8,128)(2,1)} %all-gather.9.cloned.1.call-done), calls=%async_computation.5 | async-start | bytes 21233664 | tf_op jit(solution)/shard_map/slice | solution.py:280
  132.4 2.6 %slice-start.1 = ((bf16[1920,1536]{1,0:T(8,128)(2,1)}), bf16[640,1536]{1,0:T(8,128)(2,1)S(1)}, s32[]{:S(2)}) async-start(bf16[1920,1536]{1,0:T(8,128)(2,1)} %copy-done.4), calls=%async_computation.6 | async-start | bytes 3932160 | tf_op jit(solution)/shard_map/slice | solution.py:273
  132.4 3.2 %copy-start.5 = (bf16[640,1536]{1,0:T(8,128)(2,1)S(1)}, bf16[640,1536]{1,0:T(8,128)(2,1)}, u32[]{:S(2)}) copy-start(bf16[640,1536]{1,0:T(8,128)(2,1)} %fusion.21) | copy-start | bytes 5898244
  171.8 32.4 %all-to-all-start = ((bf16[8,80,1536]{2,1,0:T(8,128)(2,1)}), bf16[8,80,1536]{2,1,0:T(8,128)(2,1)}, u32[]{:S(2)}, u32[]{:S(2)}) async-start(bf16[8,80,1536]{2,1,0:T(8,128)(2,1)} %bitcast.46), calls=%async_computation | async-start | bytes 3932160 | tf_op jit(solution)/shard_map/all_to_all | solution.py:290
  176.3 3.0 %copy-start.6 = (bf16[640,1536]{1,0:T(8,128)(2,1)S(1)}, bf16[640,1536]{1,0:T(8,128)(2,1)}, u32[]{:S(2)}) copy-start(bf16[640,1536]{1,0:T(8,128)(2,1)} %fusion.21) | copy-start | bytes 5898244
  213.9 29.9 %all-to-all-start.1 = ((bf16[8,80,1536]{2,1,0:T(8,128)(2,1)}), bf16[8,80,1536]{2,1,0:T(8,128)(2,1)}, u32[]{:S(2)}, u32[]{:S(2)}) async-start(bf16[8,80,1536]{2,1,0:T(8,128)(2,1)} %all_to_all.16), calls=%async_computation.1 | async-start | bytes 3932160 | tf_op jit(solution)/shard_map/all_to_all | solution.py:301
  243.7 7.6 %copy-start.1 = (bf16[1536,1152]{1,0:T(8,128)(2,1)S(1)}, bf16[1536,1152]{1,0:T(8,128)(2,1)}, u32[]{:S(2)}) copy-start(bf16[1536,1152]{1,0:T(8,128)(2,1)} %param.10) | copy-start | bytes 10616836
Sparse Core Ops, SparseCore 0:
  9.0 15.5 all-gather.4
  26.3 75.4 all-gather.8
  103.5 52.7 all-gather.6

commit v12 on v11

--- a/solution.py
+++ b/solution.py
@@ -254,6 +254,7 @@
     w_half = lax.dynamic_slice_in_dim(w_qkv, core * half_rows, half_rows, axis=0)
     w_pieces = lax.all_gather(w_half, ("fsdp", "core"), axis=0, tiled=False)
     w_full = w_pieces.reshape(lax.axis_size("fsdp"), w_qkv.shape[0], w_qkv.shape[1])
+    w_out, w_full = lax.optimization_barrier((w_out, w_full))
     out_rows = w_out.shape[0] // 2
     w_out_half = lax.dynamic_slice_in_dim(w_out, core * out_rows, out_rows, axis=0)
     w_out_half = lax.all_gather(w_out_half, "core", axis=0, tiled=True)

time: 259 us -> 258 us (level)
  blocking collectives: 0 us -> 30.1 us
  waiting for transfers between devices: 38.2 us -> 8.79 us
  matrix products: 52.7 us -> 58.4 us
  starting transfers between devices: 9.44 us -> 4.67 us
    all_to_all x0 -> x1, blocking collectives: none -> 30.1 us  [local(): lax.all_to_all(temporal.reshape(tok_count, feat_count), frame_axes, split...]
    all_to_all x1 -> x0, waiting for transfers between devices: 25 us -> none  [local(): lax.all_to_all(temporal.reshape(tok_count, feat_count), frame_axes, split...]
    all_gather x1, waiting for transfers between devices: 13.1 us -> 0.01 us  [local(): w_pieces = lax.all_gather(w_half, ('fsdp', 'core'), axis=0, tiled=False)]
    all_gather x1, waiting for transfers between devices: 0.01 us -> 8.74 us  [local(): w_out_half = lax.all_gather(w_out_half, 'core', axis=0, tiled=True)]
    slice x3 -> x0, local copies, waits for them, and re-layouts: 6.44 us -> none  [the longest x2 4.02 us: local(): w_full[1:]]
    all_to_all x1 -> x0, starting transfers between devices: 4.81 us -> none  [local(): lax.all_to_all(temporal.reshape(tok_count, feat_count), frame_axes, split...]
    squeeze x0 -> x1, local copies, waits for them, and re-layouts: none -> 4.13 us  [local(): w_full[0]]
    dot_general x1, matrix products: 25.2 us -> 28.4 us  [local(): jnp.einsum('tk,jkc->jtc', normed_all, w_full[1:], preferred_element_type=...]
  transfers between devices with their start and end apart: 5 -> 4, of which waited for: 2 -> 1; matrix products, arithmetic and copies ran while one was open for 39% -> 30% of each run, Pallas kernels for 30% -> 30%
where the time goes in v12:
time: 258 us; the launch traced here: 257 us
  Pallas kernels  76.8 us (30%)
  matrix products  58.4 us (23%)
  local copies, waits for them, and re-layouts  40.3 us (16%)
  blocking collectives  30.1 us (12%)
  other arithmetic  25 us (10%)
  between operations  13.3 us (5%)
  waiting for transfers between devices  8.79 us (3%)
  starting transfers between devices  4.67 us (2%)
    pallas_call x1, Pallas kernels, exchange_tokens(): pl.pallas_call(exchange_kernel, out_shape=(jax.ShapeDtypeStruct((2, rows,...  49.2 us
    all_to_all x1, blocking collectives, local(): lax.all_to_all(temporal.reshape(tok_count, feat_count), frame_axes, split...  30.1 us
    dot_general x1, matrix products, local(): jnp.einsum('tk,jkc->jtc', normed_all, w_full[1:], preferred_element_type=...  28.4 us
    pallas_call x1, Pallas kernels, spatial_rows(): pl.pallas_call(spatial_kernel, grid_spec=grid_spec, out_shape=jax.ShapeDt...  27.6 us
    convert_element_type x2, other arithmetic, layer_norm(): return (normal * (1.0 + mod_scale) + mod_shift).astype(jnp.bfloat16)  13.3 us
    dot_general x1, matrix products, local(): jnp.dot(jnp.concatenate([normed_all[tok_count:2 * tok_count], normed_cros...  9.07 us
    all_gather x1, waiting for transfers between devices, local(): w_out_half = lax.all_gather(w_out_half, 'core', axis=0, tiled=True)  8.74 us
    dot_general x1, matrix products, local(): jnp.dot(flat_temporal, w_out_full, preferred_element_type=jnp.float32)  7.56 us
  transfers between devices with their start and end apart: 4, of which 1 were waited for; matrix products, arithmetic and copies ran while one was open for 30% of the time, Pallas kernels for 30%

profile of v12, /device:TPU:1, one launch (start us, length us, event | category | flops | bytes accessed | tf_op | source)
XLA Modules:
  0.0 257.4 jit_solution(5326501339722049525)
XLA Ops:
  10.0 49.2 %shard_map.73 = (bf16[2,640,1536]{2,1,0:T(8,128)(2,1)}, bf16[640,1536]{1,0:T(8,128)(2,1)}) custom-call(bf16[640,1536]{1,0:T(8,128)(2,1)} %bitcast.43), custom_call_target="tpu_custom_call" | custom-call | bytes 157286400 | tf_op jit(solution)/shard_map/pallas_call | solution.py:200
  59.3 2.6 select_bitcast_fusion.1
  63.1 5.4 %fusion.3 = f32[1920]{0:T(1024)S(1)} fusion(f32[1920]{0:T(1024)S(1)} %broadcast_multiply_fusion, bf16[640,1536]{1,0:T(8,128)(2,1)S(1)} %get-tuple-element.18, bf16[640,1536]{1,0:T(8,128)(2,1)S(1)} %bitcast.45, bf16[640,1536]{1,0:T(8,128)(2,1)S(1)} %get-tuple-element.17), kind=kLoop, calls=%fused_computation.6 | loop fusion | flops 26540160 | bytes 5913600 | tf_op jit(solution)/shard_map/reduce_sum | solution.py:28
  68.5 11.2 %fusion.6 = bf16[1920,1536]{1,0:T(8,128)(2,1)S(1)} fusion(f32[1536]{0:T(1024)S(1)} %reduce.2, f32[1536]{0:T(1024)S(1)} %add_reduce_fusion, f32[1920]{0:T(1024)S(1)} %add_sqrt_fusion, f32[1920]{0:T(1024)S(1)} %broadcast_multiply_fusion, bf16[640,1536]{1,0:T(8,128)(2,1)S(1)} %get-tuple-element.18, bf16[640,1536]{1,0:T(8,128)(2,1)S(1)} %bitcast.46, ...), kind=kLoop, calls=%fused_computation.9 | loop fusion | flops 32440320 | bytes 11824128 | tf_op jit(solution)/shard_map/convert_element_type | solution.py:30
  79.7 2.5 copy-done.4
  88.5 28.4 %fusion.7.k_ref.v_ref = bf16[3,1920,1152]{2,1,0:T(8,128)(2,1)} fusion(bf16[4,1536,1152]{2,1,0:T(8,128)(2,1)} %bitcast.48, bf16[1920,1536]{1,0:T(8,128)(2,1)} %copy-done.4), kind=kOutput, calls=%fused_computation.10 | convolution fusion | flops 20390952960 | bytes 33325056 | tf_op jit(solution)/shard_map/tk,jkc->jtc/dot_general | solution.py:280
  117.9 4.1 %slice_bitcast_fusion = bf16[1536,1152]{1,0:T(8,128)(2,1)} fusion(bf16[4,1536,1152]{2,1,0:T(8,128)(2,1)} %bitcast.49), kind=kLoop, calls=%fused_computation.34 | loop fusion | bytes 7077888 | tf_op jit(solution)/shard_map/squeeze | solution.py:267
  122.0 8.7 %all-gather.5.cloned.1.call-done = bf16[384,1536]{1,0:T(8,128)(2,1)} async-done(((bf16[192,1536]{1,0:T(8,128)(2,1)}), bf16[384,1536]{1,0:T(8,128)(2,1)}) %all-gather.5.cloned.1.call-update) | async-done | bytes 1179664 | tf_op jit(solution)/shard_map/all_gather | solution.py:260
  132.2 9.1 %convolution_convert_fusion.1 = bf16[1280,1536]{1,0:T(8,128)(2,1)S(1)} fusion(bf16[1536,384]{1,0:T(8,128)(2,1)S(1)} %slice_bitcast_fusion.3, bf16[1536,1152]{1,0:T(8,128)(2,1)} %slice_bitcast_fusion, bf16[640,1536]{1,0:T(8,128)(2,1)} %fusion.21, bf16[640,1536]{1,0:T(8,128)(2,1)S(1)} %slice-done), kind=kOutput, calls=%fused_computation.11 | convolution fusion | flops 6059065344 | bytes 12582912 | tf_op jit(solution)/shard_map/dot_general | solution.py:273
  141.3 2.2 fusion.45
  143.5 27.6 %shard_map.74 = bf16[640,1536]{1,0:T(8,128)(2,1)} custom-call(s32[30]{0:T(128)} %reshape_squeeze.3.list_ref, s32[2]{0:T(128)} %pad_add_fusion.scalar_ref, bf16[640,1536]{1,0:T(8,128)(2,1)} %get-tuple-element.15.q_ref, bf16[3,1920,1152]{2,1,0:T(8,128)(2,1)} %fusion.7.k_ref.v_ref, bf16[3,1920,1152]{2,1,0:T(8,128)(2,1)} %fusion.7.k_ref.v_ref), custom_call_target="tpu_custom_call" | custom-call | flops 3019898880 | bytes 15728640 | tf_op jit(solution)/shard_map/pallas_call | solution.py:96
  171.0 4.6 %all-to-all-start = ((bf16[8,80,1536]{2,1,0:T(8,128)(2,1)}), bf16[8,80,1536]{2,1,0:T(8,128)(2,1)}, u32[]{:S(2)}, u32[]{:S(2)}) async-start(bf16[8,80,1536]{2,1,0:T(8,128)(2,1)} %bitcast.47), calls=%async_computation | async-start | bytes 3932160 | tf_op jit(solution)/shard_map/all_to_all | solution.py:291
  175.6 2.8 %slice_bitcast_fusion.2 = (bf16[1536,768]{1,0:T(8,128)(2,1)S(1)}, bf16[1536,768]{1,0:T(8,128)(2,1)S(1)}) fusion(bf16[4,1536,1152]{2,1,0:T(8,128)(2,1)} %bitcast.51), kind=kLoop, calls=%fused_computation.39 | loop fusion | bytes 9437184 | tf_op jit(solution)/shard_map/squeeze | solution.py:271
  178.6 4.5 %fusion.26 = bf16[640,1536]{1,0:T(8,128)(2,1)} fusion(bf16[640,1536]{1,0:T(8,128)(2,1)S(1)} %copy-done.5, bf16[1536,768]{1,0:T(8,128)(2,1)S(1)} %get-tuple-element.14, bf16[1536,768]{1,0:T(8,128)(2,1)S(1)} %get-tuple-element.13), kind=kOutput, calls=%fused_computation.36 | convolution fusion | flops 3030319104 | bytes 8650752 | tf_op jit(solution)/shard_map/dot_general | solution.py:279
  183.1 3.7 %reshape.85 = bf16[8,80,12,128]{3,2,1,0:T(8,128)(2,1)S(1)} reshape(bf16[640,1536]{1,0:T(8,128)(2,1)} %fusion.26) | data formatting | bytes 3932160 | tf_op jit(solution)/shard_map/reshape | solution.py:297
  186.8 4.8 %reshape.84 = bf16[8,80,12,128]{3,2,1,0:T(8,128)(2,1)} reshape(bf16[640,1536]{1,0:T(8,128)(2,1)} %get-tuple-element.16) | data formatting | bytes 3932160 | tf_op jit(solution)/shard_map/reshape | solution.py:296
  191.6 6.0 %fusion.31 = f32[80,12,8,8]{2,3,1,0:T(8,128)} fusion(bf16[8,80,12,128]{3,2,1,0:T(8,128)(2,1)S(1)} %reshape.85, bf16[8,80,12,128]{3,2,1,0:T(8,128)(2,1)} %reshape.84), kind=kOutput, calls=%fused_computation.41 | convolution fusion | flops 15728640 | bytes 4177920 | tf_op jit(solution)/shard_map/fphd,gphd->phfg/dot_general | solution.py:226
  197.5 3.0 %copy.31 = f32[80,12,8,8]{0,3,2,1:T(8,128)S(1)} copy(f32[80,12,8,8]{2,3,1,0:T(8,128)} %fusion.31) | data formatting | bytes 491520 | tf_op jit(solution)/shard_map/fphd,gphd->phfg/dot_general | solution.py:226
  200.8 2.3 copy.33
  203.5 3.7 %reshape.83 = bf16[8,80,12,128]{3,2,1,0:T(8,128)(2,1)S(1)} reshape(bf16[8,80,1536]{2,1,0:T(8,128)(2,1)} %all-to-all-done) | data formatting | bytes 3932160 | tf_op jit(solution)/shard_map/reshape | solution.py:298
  207.2 2.9 %fusion.25 = bf16[8,80,12,128]{3,0,2,1:T(8,128)(2,1)S(1)} fusion(bf16[80,12,8,8]{3,2,1,0:T(8,128)(2,1)} %copy.33, bf16[8,80,12,128]{3,2,1,0:T(8,128)(2,1)S(1)} %reshape.83, f32[8,80,12]{0,2,1:T(8,128)S(1)} %copy.34), kind=kOutput, calls=%fused_computation.33 | convolution fusion | flops 17694720 | bytes 4085760 | tf_op jit(solution)/shard_map/phfg,gphd->fphd/dot_general | solution.py:236
  210.6 2.6 %all_to_all.16 = bf16[8,80,1536]{2,1,0:T(8,128)(2,1)} reshape(bf16[8,80,12,128]{3,2,1,0:T(8,128)(2,1)S(1)} %copy.35) | data formatting | bytes 3932160 | tf_op jit(solution)/shard_map/all_to_all | solution.py:302
  213.2 30.1 %all_to_all.21 = bf16[8,80,1536]{2,1,0:T(8,128)(2,1)} all-to-all(bf16[8,80,1536]{2,1,0:T(8,128)(2,1)} %all_to_all.16), channel_id=1, replica_groups=mesh['fsdp'=4,'piece'=4,'fy'=4,'core'=2] {'fy','core'}, dimensions={0} | all-to-all | bytes 3932160 | tf_op jit(solution)/shard_map/all_to_all | solution.py:302
  243.3 7.6 %fusion.29 = bf16[1,640,1536]{2,1,0:T(8,128)(2,1)} fusion(bf16[640,1536]{1,0:T(8,128)(2,1)} %bitcast.52, bf16[1536,1536]{1,0:T(8,128)(2,1)} %all-gather.7.cloned.1.call-done), kind=kOutput, calls=%fused_computation.37 | convolution fusion | flops 3020881920 | bytes 8650752 | tf_op jit(solution)/shard_map/dot_general | solution.py:305
  (54 shorter events, 14.6 us)
Async XLA Ops:
  6.5 2.0 copy-start
  6.5 52.6 %copy-start.8 = (f32[1,1536]{1,0:T(1,128)S(1)}, f32[1,1536]{1,0:T(1,128)}, u32[]{:S(2)}) copy-start(f32[1,1536]{1,0:T(1,128)} %param.9) | copy-start | bytes 18436
  6.5 52.7 %copy-start.7 = (f32[1,1536]{1,0:T(1,128)S(1)}, f32[1,1536]{1,0:T(1,128)}, u32[]{:S(2)}) copy-start(f32[1,1536]{1,0:T(1,128)} %param.8) | copy-start | bytes 18436
  6.5 82.0 %all-gather.9.cloned.1.call-start = ((), (), s32[]{:S(2)}) async-start(), calls=%async_computation.4 | async-start | bytes 15925248 | tf_op jit(solution)/shard_map/all_gather | solution.py:255
  9.9 120.8 %all-gather.5.cloned.1.call-start = ((), (), s32[]{:S(2)}) async-start(), calls=%async_computation.2 | async-start | bytes 1769472 | tf_op jit(solution)/shard_map/all_gather | solution.py:260
  59.3 2.8 %copy-start.2 = (bf16[1,640,1536]{2,1,0:T(8,128)(2,1)S(1)}, bf16[1,640,1536]{2,1,0:T(8,128)(2,1)}, u32[]{:S(2)}) copy-start(bf16[1,640,1536]{2,1,0:T(8,128)(2,1)} %param.7) | copy-start | bytes 5898244
  79.7 2.5 copy-start.4
  82.2 0.7 copy-start.9
  82.2 1.3 copy-start.10
  82.2 3.2 %copy-start.3 = (bf16[640,1536]{1,0:T(8,128)(2,1)S(1)}, bf16[640,1536]{1,0:T(8,128)(2,1)}, u32[]{:S(2)}) copy-start(bf16[640,1536]{1,0:T(8,128)(2,1)} %get-tuple-element.10) | copy-start | bytes 5898244
  88.5 28.4 %copy-start.6 = (bf16[384,1536]{1,0:T(8,128)(2,1)S(1)}, bf16[384,1536]{1,0:T(8,128)(2,1)}, u32[]{:S(2)}) copy-start(bf16[384,1536]{1,0:T(8,128)(2,1)} %param.11) | copy-start | bytes 3538948
  117.8 14.4 %slice-start = ((bf16[1920,1536]{1,0:T(8,128)(2,1)}), bf16[640,1536]{1,0:T(8,128)(2,1)S(1)}, s32[]{:S(2)}) async-start(bf16[1920,1536]{1,0:T(8,128)(2,1)} %copy-done.4), calls=%async_computation.5 | async-start | bytes 3932160 | tf_op jit(solution)/shard_map/slice | solution.py:274
  117.8 125.5 %all-gather.7.cloned.1.call-start = ((), (), s32[]{:S(2)}) async-start(), calls=%async_computation.3 | async-start | bytes 5898240 | tf_op jit(solution)/shard_map/all_gather | solution.py:261
  171.0 32.4 %all-to-all-start = ((bf16[8,80,1536]{2,1,0:T(8,128)(2,1)}), bf16[8,80,1536]{2,1,0:T(8,128)(2,1)}, u32[]{:S(2)}, u32[]{:S(2)}) async-start(bf16[8,80,1536]{2,1,0:T(8,128)(2,1)} %bitcast.47), calls=%async_computation | async-start | bytes 3932160 | tf_op jit(solution)/shard_map/all_to_all | solution.py:291
  175.6 3.0 %copy-start.5 = (bf16[640,1536]{1,0:T(8,128)(2,1)S(1)}, bf16[640,1536]{1,0:T(8,128)(2,1)}, u32[]{:S(2)}) copy-start(bf16[640,1536]{1,0:T(8,128)(2,1)} %fusion.21) | copy-start | bytes 5898244
  243.3 7.6 %copy-start.1 = (bf16[1536,1152]{1,0:T(8,128)(2,1)S(1)}, bf16[1536,1152]{1,0:T(8,128)(2,1)}, u32[]{:S(2)}) copy-start(bf16[1536,1152]{1,0:T(8,128)(2,1)} %param.10) | copy-start | bytes 10616836
Sparse Core Ops, SparseCore 0:
  10.0 77.7 all-gather.8
  117.9 12.7 all-gather.4
  132.4 53.7 all-gather.6

commit v13 on v11

--- a/solution.py
+++ b/solution.py
@@ -254,10 +254,6 @@
     w_half = lax.dynamic_slice_in_dim(w_qkv, core * half_rows, half_rows, axis=0)
     w_pieces = lax.all_gather(w_half, ("fsdp", "core"), axis=0, tiled=False)
     w_full = w_pieces.reshape(lax.axis_size("fsdp"), w_qkv.shape[0], w_qkv.shape[1])
-    out_rows = w_out.shape[0] // 2
-    w_out_half = lax.dynamic_slice_in_dim(w_out, core * out_rows, out_rows, axis=0)
-    w_out_half = lax.all_gather(w_out_half, "core", axis=0, tiled=True)
-    w_out_full = lax.all_gather(w_out_half, "fsdp", axis=0, tiled=True)
     normed_all = layer_norm(
         jnp.concatenate([above, own, below], axis=0), mod_scale[0], mod_shift[0]
     )
@@ -286,6 +282,11 @@
     rows_here = tok_count // (TGW * TILE)
     first_tile = (piece_index * rows_here - 1) * TGW
     spatial = spatial_rows(queries, kv_all, neighbors[0], first_tile, count_here)
+    w_out, spatial = lax.optimization_barrier((w_out, spatial))
+    out_rows = w_out.shape[0] // 2
+    w_out_half = lax.dynamic_slice_in_dim(w_out, core * out_rows, out_rows, axis=0)
+    w_out_half = lax.all_gather(w_out_half, "core", axis=0, tiled=True)
+    w_out_full = lax.all_gather(w_out_half, "fsdp", axis=0, tiled=True)
     frame_axes = ("fy", "core")
     spatial_part = lax.all_to_all(spatial, frame_axes, split_axis=0, concat_axis=0, tiled=True)
     per_dev = tok_count // n_frames

time: 259 us -> 263 us (1.015)
  blocking collectives: 0 us -> 30 us
  waiting for transfers between devices: 38.2 us -> 13 us
  starting transfers between devices: 9.44 us -> 4.68 us
  matrix products: 52.7 us -> 55.5 us
    all_to_all x0 -> x1, blocking collectives: none -> 30 us  [local(): lax.all_to_all(temporal.reshape(tok_count, feat_count), frame_axes, split...]
    all_to_all x1 -> x0, waiting for transfers between devices: 25 us -> none  [local(): lax.all_to_all(temporal.reshape(tok_count, feat_count), frame_axes, split...]
    all_gather x1, waiting for transfers between devices: 13.1 us -> 0.01 us  [local(): w_pieces = lax.all_gather(w_half, ('fsdp', 'core'), axis=0, tiled=False)]
    all_gather x1, waiting for transfers between devices: 0.01 us -> 12.9 us  [local(): w_out_half = lax.all_gather(w_out_half, 'core', axis=0, tiled=True)]
    all_to_all x1 -> x0, starting transfers between devices: 4.81 us -> none  [local(): lax.all_to_all(temporal.reshape(tok_count, feat_count), frame_axes, split...]
    dot_general x1, matrix products: 25.2 us -> 27.9 us  [local(): jnp.einsum('tk,jkc->jtc', normed_all, w_full[1:], preferred_element_type=...]
  transfers between devices with their start and end apart: 5 -> 4, of which waited for: 2 -> 1; matrix products, arithmetic and copies ran while one was open for 39% -> 24% of each run, Pallas kernels for 30% -> 19%
where the time goes in v13:
time: 263 us
  Pallas kernels  76.6 us (29%)
  matrix products  55.5 us (21%)
  local copies, waits for them, and re-layouts  44.7 us (17%)
  blocking collectives  30 us (11%)
  other arithmetic  25 us (10%)
  between operations  13.4 us (5%)
  waiting for transfers between devices  13 us (5%)
  starting transfers between devices  4.68 us (2%)
    pallas_call x1, Pallas kernels, exchange_tokens(): pl.pallas_call(exchange_kernel, out_shape=(jax.ShapeDtypeStruct((2, rows,...  49.2 us
    all_to_all x1, blocking collectives, local(): lax.all_to_all(temporal.reshape(tok_count, feat_count), frame_axes, split...  30 us
    dot_general x1, matrix products, local(): jnp.einsum('tk,jkc->jtc', normed_all, w_full[1:], preferred_element_type=...  27.9 us
    pallas_call x1, Pallas kernels, spatial_rows(): pl.pallas_call(spatial_kernel, grid_spec=grid_spec, out_shape=jax.ShapeDt...  27.4 us
    convert_element_type x2, other arithmetic, layer_norm(): return (normal * (1.0 + mod_scale) + mod_shift).astype(jnp.bfloat16)  13.3 us
    all_gather x1, waiting for transfers between devices, local(): w_out_half = lax.all_gather(w_out_half, 'core', axis=0, tiled=True)  12.9 us
    dot_general x1, matrix products, local(): jnp.dot(flat_temporal, w_out_full, preferred_element_type=jnp.float32)  7.56 us
    dot_general x1, matrix products, local(): jnp.dot(jnp.concatenate([normed_all[tok_count:2 * tok_count], normed_cros...  6.6 us
  transfers between devices with their start and end apart: 4, of which 1 were waited for; matrix products, arithmetic and copies ran while one was open for 24% of the time, Pallas kernels for 19%

profile of v13, /device:TPU:1, one launch (start us, length us, event | category | flops | bytes accessed | tf_op | source)
XLA Modules:
  0.0 262.9 jit_solution(4015059826688117151)
XLA Ops:
  10.0 49.2 %shard_map.73 = (bf16[2,640,1536]{2,1,0:T(8,128)(2,1)}, bf16[640,1536]{1,0:T(8,128)(2,1)}) custom-call(bf16[640,1536]{1,0:T(8,128)(2,1)} %bitcast.39), custom_call_target="tpu_custom_call" | custom-call | bytes 157286400 | tf_op jit(solution)/shard_map/pallas_call | solution.py:200
  59.3 2.6 select_bitcast_fusion.1
  63.1 5.4 %fusion.3 = f32[1920]{0:T(1024)S(1)} fusion(f32[1920]{0:T(1024)S(1)} %broadcast_multiply_fusion, bf16[640,1536]{1,0:T(8,128)(2,1)S(1)} %get-tuple-element.18, bf16[640,1536]{1,0:T(8,128)(2,1)S(1)} %bitcast.41, bf16[640,1536]{1,0:T(8,128)(2,1)S(1)} %get-tuple-element.17), kind=kLoop, calls=%fused_computation.6 | loop fusion | flops 26540160 | bytes 5913600 | tf_op jit(solution)/shard_map/reduce_sum | solution.py:28
  68.6 11.2 %fusion.6 = bf16[1920,1536]{1,0:T(8,128)(2,1)S(1)} fusion(f32[1536]{0:T(1024)S(1)} %reduce.2, f32[1536]{0:T(1024)S(1)} %add_reduce_fusion, f32[1920]{0:T(1024)S(1)} %add_sqrt_fusion, f32[1920]{0:T(1024)S(1)} %broadcast_multiply_fusion, bf16[640,1536]{1,0:T(8,128)(2,1)S(1)} %get-tuple-element.18, bf16[640,1536]{1,0:T(8,128)(2,1)S(1)} %bitcast.42, ...), kind=kLoop, calls=%fused_computation.9 | loop fusion | flops 32440320 | bytes 11824128 | tf_op jit(solution)/shard_map/convert_element_type | solution.py:30
  79.8 2.5 copy-done.4
  90.9 2.4 slice.48
  93.6 6.6 %convolution_convert_fusion.1 = bf16[1280,1536]{1,0:T(8,128)(2,1)S(1)} fusion(bf16[1536,384]{1,0:T(8,128)(2,1)S(1)} %slice_bitcast_fusion.2, bf16[1536,1152]{1,0:T(8,128)(2,1)S(1)} %slice.48, bf16[640,1536]{1,0:T(8,128)(2,1)S(1)} %copy-done.5, bf16[640,1536]{1,0:T(8,128)(2,1)S(1)} %copy-done.7), kind=kOutput, calls=%fused_computation.11 | convolution fusion | flops 6059065344 | bytes 12582912 | tf_op jit(solution)/shard_map/dot_general | solution.py:268
  102.5 4.6 %slice.51 = bf16[4608,1152]{1,0:T(8,128)(2,1)} slice(bf16[6144,1152]{1,0:T(8,128)(2,1)S(1)} %bitcast.46), slice={[1536:6144], [0:1152]} | slice | bytes 21233664 | tf_op jit(solution)/shard_map/slice | solution.py:276
  107.1 27.9 %fusion.7.k_ref.v_ref = bf16[3,1920,1152]{2,1,0:T(8,128)(2,1)} fusion(bf16[3,1536,1152]{2,1,0:T(8,128)(2,1)} %bitcast.47, bf16[1920,1536]{1,0:T(8,128)(2,1)S(1)} %bitcast.49), kind=kOutput, calls=%fused_computation.10 | convolution fusion | flops 20390952960 | bytes 29786112 | tf_op jit(solution)/shard_map/tk,jkc->jtc/dot_general | solution.py:275
  135.0 27.4 %shard_map.74 = bf16[640,1536]{1,0:T(8,128)(2,1)} custom-call(s32[30]{0:T(128)} %reshape_squeeze.3.list_ref, s32[2]{0:T(128)} %pad_add_fusion.scalar_ref, bf16[640,1536]{1,0:T(8,128)(2,1)} %get-tuple-element.15.q_ref, bf16[3,1920,1152]{2,1,0:T(8,128)(2,1)} %fusion.7.k_ref.v_ref, bf16[3,1920,1152]{2,1,0:T(8,128)(2,1)} %fusion.7.k_ref.v_ref), custom_call_target="tpu_custom_call" | custom-call | flops 3019898880 | bytes 15728640 | tf_op jit(solution)/shard_map/pallas_call | solution.py:96
  163.4 12.9 %all-gather.5.cloned.1.call-done = bf16[384,1536]{1,0:T(8,128)(2,1)} async-done(((bf16[192,1536]{1,0:T(8,128)(2,1)}), bf16[384,1536]{1,0:T(8,128)(2,1)}) %all-gather.5.cloned.1.call-update) | async-done | bytes 1179664 | tf_op jit(solution)/shard_map/all_gather | solution.py:288
  176.4 4.6 %all-to-all-start = ((bf16[8,80,1536]{2,1,0:T(8,128)(2,1)}), bf16[8,80,1536]{2,1,0:T(8,128)(2,1)}, u32[]{:S(2)}, u32[]{:S(2)}) async-start(bf16[8,80,1536]{2,1,0:T(8,128)(2,1)} %bitcast.50), calls=%async_computation | async-start | bytes 3932160 | tf_op jit(solution)/shard_map/all_to_all | solution.py:291
  181.0 2.8 %slice_bitcast_fusion.1 = (bf16[1536,768]{1,0:T(8,128)(2,1)S(1)}, bf16[1536,768]{1,0:T(8,128)(2,1)S(1)}) fusion(bf16[4,1536,1152]{2,1,0:T(8,128)(2,1)} %bitcast.44), kind=kLoop, calls=%fused_computation.38 | loop fusion | bytes 9437184 | tf_op jit(solution)/shard_map/squeeze | solution.py:266
  184.0 4.5 %fusion.26 = bf16[640,1536]{1,0:T(8,128)(2,1)} fusion(bf16[640,1536]{1,0:T(8,128)(2,1)S(1)} %copy-done.6, bf16[1536,768]{1,0:T(8,128)(2,1)S(1)} %get-tuple-element.14, bf16[1536,768]{1,0:T(8,128)(2,1)S(1)} %get-tuple-element.13), kind=kOutput, calls=%fused_computation.35 | convolution fusion | flops 3030319104 | bytes 8650752 | tf_op jit(solution)/shard_map/dot_general | solution.py:274
  188.5 3.8 %reshape.88 = bf16[8,80,12,128]{3,2,1,0:T(8,128)(2,1)S(1)} reshape(bf16[640,1536]{1,0:T(8,128)(2,1)} %fusion.26) | data formatting | bytes 3932160 | tf_op jit(solution)/shard_map/reshape | solution.py:297
  192.3 4.8 %reshape.87 = bf16[8,80,12,128]{3,2,1,0:T(8,128)(2,1)} reshape(bf16[640,1536]{1,0:T(8,128)(2,1)} %get-tuple-element.16) | data formatting | bytes 3932160 | tf_op jit(solution)/shard_map/reshape | solution.py:296
  197.1 6.0 %fusion.31 = f32[80,12,8,8]{2,3,1,0:T(8,128)} fusion(bf16[8,80,12,128]{3,2,1,0:T(8,128)(2,1)S(1)} %reshape.88, bf16[8,80,12,128]{3,2,1,0:T(8,128)(2,1)} %reshape.87), kind=kOutput, calls=%fused_computation.40 | convolution fusion | flops 15728640 | bytes 4177920 | tf_op jit(solution)/shard_map/fphd,gphd->phfg/dot_general | solution.py:226
  203.1 3.0 %copy.31 = f32[80,12,8,8]{0,3,2,1:T(8,128)S(1)} copy(f32[80,12,8,8]{2,3,1,0:T(8,128)} %fusion.31) | data formatting | bytes 491520 | tf_op jit(solution)/shard_map/fphd,gphd->phfg/dot_general | solution.py:226
  206.4 2.3 copy.33
  209.0 3.7 %reshape.86 = bf16[8,80,12,128]{3,2,1,0:T(8,128)(2,1)S(1)} reshape(bf16[8,80,1536]{2,1,0:T(8,128)(2,1)} %all-to-all-done) | data formatting | bytes 3932160 | tf_op jit(solution)/shard_map/reshape | solution.py:298
  212.8 3.0 %fusion.25 = bf16[8,80,12,128]{3,0,2,1:T(8,128)(2,1)S(1)} fusion(bf16[80,12,8,8]{3,2,1,0:T(8,128)(2,1)} %copy.33, bf16[8,80,12,128]{3,2,1,0:T(8,128)(2,1)S(1)} %reshape.86, f32[8,80,12]{0,2,1:T(8,128)S(1)} %copy.34), kind=kOutput, calls=%fused_computation.33 | convolution fusion | flops 17694720 | bytes 4085760 | tf_op jit(solution)/shard_map/phfg,gphd->fphd/dot_general | solution.py:236
  216.2 2.6 all_to_all.16
  218.8 30.0 %all_to_all.21 = bf16[8,80,1536]{2,1,0:T(8,128)(2,1)} all-to-all(bf16[8,80,1536]{2,1,0:T(8,128)(2,1)} %all_to_all.16), channel_id=1, replica_groups=mesh['fsdp'=4,'piece'=4,'fy'=4,'core'=2] {'fy','core'}, dimensions={0} | all-to-all | bytes 3932160 | tf_op jit(solution)/shard_map/all_to_all | solution.py:302
  248.8 7.6 %fusion.29 = bf16[1,640,1536]{2,1,0:T(8,128)(2,1)} fusion(bf16[640,1536]{1,0:T(8,128)(2,1)} %bitcast.51, bf16[1536,1536]{1,0:T(8,128)(2,1)} %all-gather.7.cloned.1.call-done), kind=kOutput, calls=%fused_computation.36 | convolution fusion | flops 3020881920 | bytes 8650752 | tf_op jit(solution)/shard_map/dot_general | solution.py:305
  (72 shorter events, 18.1 us)
Async XLA Ops:
  6.5 2.0 copy-start
  6.5 52.7 %copy-start.10 = (f32[1,1536]{1,0:T(1,128)S(1)}, f32[1,1536]{1,0:T(1,128)}, u32[]{:S(2)}) copy-start(f32[1,1536]{1,0:T(1,128)} %param.9) | copy-start | bytes 18436
  6.5 52.7 %copy-start.9 = (f32[1,1536]{1,0:T(1,128)S(1)}, f32[1,1536]{1,0:T(1,128)}, u32[]{:S(2)}) copy-start(f32[1,1536]{1,0:T(1,128)} %param.8) | copy-start | bytes 18436
  6.5 82.8 %all-gather.9.cloned.1.call-start = ((), (), s32[]{:S(2)}) async-start(), calls=%async_computation.4 | async-start | bytes 15925248 | tf_op jit(solution)/shard_map/all_gather | solution.py:255
  10.0 166.3 %all-gather.5.cloned.1.call-start = ((), (), s32[]{:S(2)}) async-start(), calls=%async_computation.2 | async-start | bytes 1769472 | tf_op jit(solution)/shard_map/all_gather | solution.py:288
  59.3 2.8 %copy-start.2 = (bf16[1,640,1536]{2,1,0:T(8,128)(2,1)S(1)}, bf16[1,640,1536]{2,1,0:T(8,128)(2,1)}, u32[]{:S(2)}) copy-start(bf16[1,640,1536]{2,1,0:T(8,128)(2,1)} %param.7) | copy-start | bytes 5898244
  79.8 2.5 copy-start.4
  82.3 1.4 copy-start.11
  82.3 2.1 copy-start.12
  82.3 4.0 %copy-start.3 = (bf16[640,1536]{1,0:T(8,128)(2,1)S(1)}, bf16[640,1536]{1,0:T(8,128)(2,1)}, u32[]{:S(2)}) copy-start(bf16[640,1536]{1,0:T(8,128)(2,1)} %get-tuple-element.10) | copy-start | bytes 5898244
  89.3 4.0 %copy-start.7 = (bf16[640,1536]{1,0:T(8,128)(2,1)S(1)}, bf16[640,1536]{1,0:T(8,128)(2,1)}, u32[]{:S(2)}) copy-start(bf16[640,1536]{1,0:T(8,128)(2,1)} %slice.47) | copy-start | bytes 5898244
  90.9 2.7 %copy-start.5 = (bf16[640,1536]{1,0:T(8,128)(2,1)S(1)}, bf16[640,1536]{1,0:T(8,128)(2,1)}, u32[]{:S(2)}) copy-start(bf16[640,1536]{1,0:T(8,128)(2,1)} %fusion.21) | copy-start | bytes 5898244
  90.9 11.6 %slice-start = ((s8[14155776]{0:T(1024)(128)(4,1)}), s8[4194304]{0:T(1024)(128)(4,1)S(1)}, s32[]{:S(2)}) async-start(s8[14155776]{0:T(1024)(128)(4,1)} %bitcast.45), calls=%async_computation.5 | async-start | bytes 8388608
  93.6 8.9 %slice-start.1 = ((s8[14155776]{0:T(1024)(128)(4,1)}), s8[4194304]{0:T(1024)(128)(4,1)S(1)}, s32[]{:S(2)}) async-start(s8[14155776]{0:T(1024)(128)(4,1)} %bitcast.45), calls=%async_computation.6 | async-start | bytes 8388608
  93.6 8.9 %slice-start.2 = ((s8[14155776]{0:T(1024)(128)(4,1)}), s8[4194304]{0:T(1024)(128)(4,1)S(1)}, s32[]{:S(2)}) async-start(s8[14155776]{0:T(1024)(128)(4,1)} %bitcast.45), calls=%async_computation.7 | async-start | bytes 8388608
  93.6 8.9 %slice-start.3 = ((s8[14155776]{0:T(1024)(128)(4,1)}), s8[1572864]{0:T(1024)(128)(4,1)S(1)}, s32[]{:S(2)}) async-start(s8[14155776]{0:T(1024)(128)(4,1)} %bitcast.45), calls=%async_computation.8 | async-start | bytes 3145728
  100.2 6.9 %slice-start.4 = ((s8[5898240]{0:T(1024)(128)(4,1)}), s8[4194304]{0:T(1024)(128)(4,1)S(1)}, s32[]{:S(2)}) async-start(s8[5898240]{0:T(1024)(128)(4,1)} %bitcast.48), calls=%async_computation.9 | async-start | bytes 8388608
  102.5 4.6 %slice-start.5 = ((s8[5898240]{0:T(1024)(128)(4,1)}), s8[1703936]{0:T(1024)(128)(4,1)S(1)}, s32[]{:S(2)}) async-start(s8[5898240]{0:T(1024)(128)(4,1)} %bitcast.48), calls=%async_computation.10 | async-start | bytes 3407872
  135.0 27.5 %copy-start.8 = (bf16[384,1536]{1,0:T(8,128)(2,1)S(1)}, bf16[384,1536]{1,0:T(8,128)(2,1)}, u32[]{:S(2)}) copy-start(bf16[384,1536]{1,0:T(8,128)(2,1)} %param.11) | copy-start | bytes 3538948
  163.4 85.5 %all-gather.7.cloned.1.call-start = ((), (), s32[]{:S(2)}) async-start(), calls=%async_computation.3 | async-start | bytes 5898240 | tf_op jit(solution)/shard_map/all_gather | solution.py:289
  176.4 32.6 %all-to-all-start = ((bf16[8,80,1536]{2,1,0:T(8,128)(2,1)}), bf16[8,80,1536]{2,1,0:T(8,128)(2,1)}, u32[]{:S(2)}, u32[]{:S(2)}) async-start(bf16[8,80,1536]{2,1,0:T(8,128)(2,1)} %bitcast.50), calls=%async_computation | async-start | bytes 3932160 | tf_op jit(solution)/shard_map/all_to_all | solution.py:291
  181.0 3.0 %copy-start.6 = (bf16[640,1536]{1,0:T(8,128)(2,1)S(1)}, bf16[640,1536]{1,0:T(8,128)(2,1)}, u32[]{:S(2)}) copy-start(bf16[640,1536]{1,0:T(8,128)(2,1)} %fusion.21) | copy-start | bytes 5898244
  248.8 7.6 %copy-start.1 = (bf16[1536,1152]{1,0:T(8,128)(2,1)S(1)}, bf16[1536,1152]{1,0:T(8,128)(2,1)}, u32[]{:S(2)}) copy-start(bf16[1536,1152]{1,0:T(8,128)(2,1)} %param.10) | copy-start | bytes 10616836
Sparse Core Ops, SparseCore 0:
  10.1 77.8 all-gather.8
  163.5 12.7 all-gather.4
  178.0 53.7 all-gather.6

commit v14 on v12

--- a/solution.py
+++ b/solution.py
@@ -255,10 +255,7 @@
     w_pieces = lax.all_gather(w_half, ("fsdp", "core"), axis=0, tiled=False)
     w_full = w_pieces.reshape(lax.axis_size("fsdp"), w_qkv.shape[0], w_qkv.shape[1])
     w_out, w_full = lax.optimization_barrier((w_out, w_full))
-    out_rows = w_out.shape[0] // 2
-    w_out_half = lax.dynamic_slice_in_dim(w_out, core * out_rows, out_rows, axis=0)
-    w_out_half = lax.all_gather(w_out_half, "core", axis=0, tiled=True)
-    w_out_full = lax.all_gather(w_out_half, "fsdp", axis=0, tiled=True)
+    w_out_full = lax.all_gather(w_out, "fsdp", axis=0, tiled=True)
     normed_all = layer_norm(
         jnp.concatenate([above, own, below], axis=0), mod_scale[0], mod_shift[0]
     )

time: 258 us -> 249 us (0.965)
  waiting for transfers between devices: 8.79 us -> 0.04 us
    all_gather x2 -> x1, waiting for transfers between devices: 8.74 us -> 0.01 us  [local(): w_out_full = lax.all_gather(w_out, 'fsdp', axis=0, tiled=True)]
  transfers between devices with their start and end apart: 4 -> 3, of which waited for: 1 -> 0; matrix products, arithmetic and copies ran while one was open for 30% -> 29% of each run, Pallas kernels for 30% -> 31%
where the time goes in v14:
time: 249 us; the launch traced here: 248 us
  Pallas kernels  76.6 us (31%)
  matrix products  58 us (23%)
  local copies, waits for them, and re-layouts  40 us (16%)
  blocking collectives  30.1 us (12%)
  other arithmetic  25 us (10%)
  between operations  13.6 us (5%)
  starting transfers between devices  5.04 us (2%)
    pallas_call x1, Pallas kernels, exchange_tokens(): pl.pallas_call(exchange_kernel, out_shape=(jax.ShapeDtypeStruct((2, rows,...  49.2 us
    all_to_all x1, blocking collectives, local(): lax.all_to_all(temporal.reshape(tok_count, feat_count), frame_axes, split...  30.1 us
    dot_general x1, matrix products, local(): jnp.einsum('tk,jkc->jtc', normed_all, w_full[1:], preferred_element_type=...  28.1 us
    pallas_call x1, Pallas kernels, spatial_rows(): pl.pallas_call(spatial_kernel, grid_spec=grid_spec, out_shape=jax.ShapeDt...  27.4 us
    convert_element_type x2, other arithmetic, layer_norm(): return (normal * (1.0 + mod_scale) + mod_shift).astype(jnp.bfloat16)  13.3 us
    dot_general x1, matrix products, local(): jnp.dot(jnp.concatenate([normed_all[tok_count:2 * tok_count], normed_cros...  8.85 us
    dot_general x1, matrix products, local(): jnp.dot(flat_temporal, w_out_full, preferred_element_type=jnp.float32)  7.56 us
    reduce_sum x2, other arithmetic, layer_norm(): spread = jnp.mean((values_f32 - center) ** 2, axis=-1, keepdims=True)  6.05 us
  transfers between devices with their start and end apart: 3, of which 0 were waited for; matrix products, arithmetic and copies ran while one was open for 29% of the time, Pallas kernels for 31%

profile of v14, /device:TPU:1, one launch (start us, length us, event | category | flops | bytes accessed | tf_op | source)
XLA Modules:
  0.0 248.3 jit_solution(14028742563280140526)
XLA Ops:
  10.0 49.2 %shard_map.73 = (bf16[2,640,1536]{2,1,0:T(8,128)(2,1)}, bf16[640,1536]{1,0:T(8,128)(2,1)}) custom-call(bf16[640,1536]{1,0:T(8,128)(2,1)} %bitcast.43), custom_call_target="tpu_custom_call" | custom-call | bytes 157286400 | tf_op jit(solution)/shard_map/pallas_call | solution.py:200
  59.3 2.6 %select_bitcast_fusion.1 = (bf16[640,1536]{1,0:T(8,128)(2,1)S(1)}, bf16[640,1536]{1,0:T(8,128)(2,1)S(1)}) fusion(bf16[2,640,1536]{2,1,0:T(8,128)(2,1)} %get-tuple-element.9, pred[]{:T(512)S(6)} %gt.3, pred[]{:T(512)S(6)} %lt.30), kind=kLoop, calls=%fused_computation.45 | loop fusion | flops 1966080 | bytes 7864322 | tf_op jit(solution)/shard_map/jit(_where)/select_n | solution.py:250
  63.1 5.4 %fusion.3 = f32[1920]{0:T(1024)S(1)} fusion(f32[1920]{0:T(1024)S(1)} %broadcast_multiply_fusion, bf16[640,1536]{1,0:T(8,128)(2,1)S(1)} %get-tuple-element.18, bf16[640,1536]{1,0:T(8,128)(2,1)S(1)} %bitcast.45, bf16[640,1536]{1,0:T(8,128)(2,1)S(1)} %get-tuple-element.17), kind=kLoop, calls=%fused_computation.6 | loop fusion | flops 26540160 | bytes 5913600 | tf_op jit(solution)/shard_map/reduce_sum | solution.py:28
  68.5 11.2 %fusion.6 = bf16[1920,1536]{1,0:T(8,128)(2,1)S(1)} fusion(f32[1536]{0:T(1024)S(1)} %reduce.2, f32[1536]{0:T(1024)S(1)} %add_reduce_fusion, f32[1920]{0:T(1024)S(1)} %add_sqrt_fusion, f32[1920]{0:T(1024)S(1)} %broadcast_multiply_fusion, bf16[640,1536]{1,0:T(8,128)(2,1)S(1)} %get-tuple-element.18, bf16[640,1536]{1,0:T(8,128)(2,1)S(1)} %bitcast.46, ...), kind=kLoop, calls=%fused_computation.9 | loop fusion | flops 32440320 | bytes 11824128 | tf_op jit(solution)/shard_map/convert_element_type | solution.py:30
  79.7 2.5 copy-done.4
  86.5 2.1 fusion.21
  88.6 4.1 %slice_bitcast_fusion = bf16[1536,1152]{1,0:T(8,128)(2,1)} fusion(bf16[4,1536,1152]{2,1,0:T(8,128)(2,1)} %bitcast.48), kind=kLoop, calls=%fused_computation.34 | loop fusion | bytes 7077888 | tf_op jit(solution)/shard_map/squeeze | solution.py:264
  93.2 28.1 %fusion.7.k_ref.v_ref = bf16[3,1920,1152]{2,1,0:T(8,128)(2,1)} fusion(bf16[4,1536,1152]{2,1,0:T(8,128)(2,1)} %bitcast.49, bf16[1920,1536]{1,0:T(8,128)(2,1)S(1)} %copy-done.5), kind=kOutput, calls=%fused_computation.10 | convolution fusion | flops 20390952960 | bytes 33325056 | tf_op jit(solution)/shard_map/tk,jkc->jtc/dot_general | solution.py:277
  122.7 8.9 %convolution_convert_fusion.1 = bf16[1280,1536]{1,0:T(8,128)(2,1)S(1)} fusion(bf16[1536,384]{1,0:T(8,128)(2,1)S(1)} %slice_bitcast_fusion.3, bf16[1536,1152]{1,0:T(8,128)(2,1)} %slice_bitcast_fusion, bf16[640,1536]{1,0:T(8,128)(2,1)} %fusion.21, bf16[640,1536]{1,0:T(8,128)(2,1)S(1)} %slice-done), kind=kOutput, calls=%fused_computation.11 | convolution fusion | flops 6059065344 | bytes 12582912 | tf_op jit(solution)/shard_map/dot_general | solution.py:270
  131.6 2.2 fusion.45
  133.8 27.4 %shard_map.74 = bf16[640,1536]{1,0:T(8,128)(2,1)} custom-call(s32[30]{0:T(128)} %reshape_squeeze.3.list_ref, s32[2]{0:T(128)} %pad_add_fusion.scalar_ref, bf16[640,1536]{1,0:T(8,128)(2,1)} %get-tuple-element.15.q_ref, bf16[3,1920,1152]{2,1,0:T(8,128)(2,1)} %fusion.7.k_ref.v_ref, bf16[3,1920,1152]{2,1,0:T(8,128)(2,1)} %fusion.7.k_ref.v_ref), custom_call_target="tpu_custom_call" | custom-call | flops 3019898880 | bytes 15728640 | tf_op jit(solution)/shard_map/pallas_call | solution.py:96
  161.2 5.0 %all-to-all-start = ((bf16[8,80,1536]{2,1,0:T(8,128)(2,1)}), bf16[8,80,1536]{2,1,0:T(8,128)(2,1)}, u32[]{:S(2)}, u32[]{:S(2)}) async-start(bf16[8,80,1536]{2,1,0:T(8,128)(2,1)} %bitcast.47), calls=%async_computation | async-start | bytes 3932160 | tf_op jit(solution)/shard_map/all_to_all | solution.py:288
  166.2 2.8 %slice_bitcast_fusion.2 = (bf16[1536,768]{1,0:T(8,128)(2,1)S(1)}, bf16[1536,768]{1,0:T(8,128)(2,1)S(1)}) fusion(bf16[4,1536,1152]{2,1,0:T(8,128)(2,1)} %bitcast.51), kind=kLoop, calls=%fused_computation.39 | loop fusion | bytes 9437184 | tf_op jit(solution)/shard_map/squeeze | solution.py:268
  169.2 4.5 %fusion.26 = bf16[640,1536]{1,0:T(8,128)(2,1)} fusion(bf16[640,1536]{1,0:T(8,128)(2,1)S(1)} %copy-done.6, bf16[1536,768]{1,0:T(8,128)(2,1)S(1)} %get-tuple-element.14, bf16[1536,768]{1,0:T(8,128)(2,1)S(1)} %get-tuple-element.13), kind=kOutput, calls=%fused_computation.36 | convolution fusion | flops 3030319104 | bytes 8650752 | tf_op jit(solution)/shard_map/dot_general | solution.py:276
  173.7 3.7 %reshape.85 = bf16[8,80,12,128]{3,2,1,0:T(8,128)(2,1)S(1)} reshape(bf16[640,1536]{1,0:T(8,128)(2,1)} %fusion.26) | data formatting | bytes 3932160 | tf_op jit(solution)/shard_map/reshape | solution.py:294
  177.4 4.8 %reshape.84 = bf16[8,80,12,128]{3,2,1,0:T(8,128)(2,1)} reshape(bf16[640,1536]{1,0:T(8,128)(2,1)} %get-tuple-element.16) | data formatting | bytes 3932160 | tf_op jit(solution)/shard_map/reshape | solution.py:293
  182.2 6.0 %fusion.31 = f32[80,12,8,8]{2,3,1,0:T(8,128)} fusion(bf16[8,80,12,128]{3,2,1,0:T(8,128)(2,1)S(1)} %reshape.85, bf16[8,80,12,128]{3,2,1,0:T(8,128)(2,1)} %reshape.84), kind=kOutput, calls=%fused_computation.41 | convolution fusion | flops 15728640 | bytes 4177920 | tf_op jit(solution)/shard_map/fphd,gphd->phfg/dot_general | solution.py:226
  188.2 3.0 %copy.31 = f32[80,12,8,8]{0,3,2,1:T(8,128)S(1)} copy(f32[80,12,8,8]{2,3,1,0:T(8,128)} %fusion.31) | data formatting | bytes 491520 | tf_op jit(solution)/shard_map/fphd,gphd->phfg/dot_general | solution.py:226
  191.4 2.3 copy.33
  194.1 3.7 %reshape.83 = bf16[8,80,12,128]{3,2,1,0:T(8,128)(2,1)S(1)} reshape(bf16[8,80,1536]{2,1,0:T(8,128)(2,1)} %all-to-all-done) | data formatting | bytes 3932160 | tf_op jit(solution)/shard_map/reshape | solution.py:295
  197.8 2.9 %fusion.25 = bf16[8,80,12,128]{3,0,2,1:T(8,128)(2,1)S(1)} fusion(bf16[80,12,8,8]{3,2,1,0:T(8,128)(2,1)} %copy.33, bf16[8,80,12,128]{3,2,1,0:T(8,128)(2,1)S(1)} %reshape.83, f32[8,80,12]{0,2,1:T(8,128)S(1)} %copy.34), kind=kOutput, calls=%fused_computation.33 | convolution fusion | flops 17694720 | bytes 4085760 | tf_op jit(solution)/shard_map/phfg,gphd->fphd/dot_general | solution.py:236
  201.2 2.6 %all_to_all.16 = bf16[8,80,1536]{2,1,0:T(8,128)(2,1)} reshape(bf16[8,80,12,128]{3,2,1,0:T(8,128)(2,1)S(1)} %copy.35) | data formatting | bytes 3932160 | tf_op jit(solution)/shard_map/all_to_all | solution.py:299
  203.8 30.1 %all_to_all.21 = bf16[8,80,1536]{2,1,0:T(8,128)(2,1)} all-to-all(bf16[8,80,1536]{2,1,0:T(8,128)(2,1)} %all_to_all.16), channel_id=1, replica_groups=mesh['fsdp'=4,'piece'=4,'fy'=4,'core'=2] {'fy','core'}, dimensions={0} | all-to-all | bytes 3932160 | tf_op jit(solution)/shard_map/all_to_all | solution.py:299
  233.9 7.6 %fusion.29 = bf16[1,640,1536]{2,1,0:T(8,128)(2,1)} fusion(bf16[640,1536]{1,0:T(8,128)(2,1)} %bitcast.52, bf16[1536,1536]{1,0:T(8,128)(2,1)} %all-gather.4.cloned.1.call-done), kind=kOutput, calls=%fused_computation.37 | convolution fusion | flops 3020881920 | bytes 8650752 | tf_op jit(solution)/shard_map/dot_general | solution.py:302
  (50 shorter events, 12.1 us)
Async XLA Ops:
  6.5 2.0 copy-start
  6.5 52.6 %copy-start.8 = (f32[1,1536]{1,0:T(1,128)S(1)}, f32[1,1536]{1,0:T(1,128)}, u32[]{:S(2)}) copy-start(f32[1,1536]{1,0:T(1,128)} %param.9) | copy-start | bytes 18436
  6.5 52.7 %copy-start.7 = (f32[1,1536]{1,0:T(1,128)S(1)}, f32[1,1536]{1,0:T(1,128)}, u32[]{:S(2)}) copy-start(f32[1,1536]{1,0:T(1,128)} %param.8) | copy-start | bytes 18436
  6.5 82.0 %all-gather.6.cloned.1.call-start = ((), (), s32[]{:S(2)}) async-start(), calls=%async_computation.3 | async-start | bytes 15925248 | tf_op jit(solution)/shard_map/all_gather | solution.py:255
  9.9 224.0 %all-gather.4.cloned.1.call-start = ((), (), s32[]{:S(2)}) async-start(), calls=%async_computation.2 | async-start | bytes 5898240 | tf_op jit(solution)/shard_map/all_gather | solution.py:258
  59.3 2.8 %copy-start.2 = (bf16[1,640,1536]{2,1,0:T(8,128)(2,1)S(1)}, bf16[1,640,1536]{2,1,0:T(8,128)(2,1)}, u32[]{:S(2)}) copy-start(bf16[1,640,1536]{2,1,0:T(8,128)(2,1)} %param.7) | copy-start | bytes 5898244
  79.7 2.5 copy-start.4
  82.2 0.7 copy-start.9
  82.2 1.4 copy-start.10
  82.2 3.3 %copy-start.3 = (bf16[640,1536]{1,0:T(8,128)(2,1)S(1)}, bf16[640,1536]{1,0:T(8,128)(2,1)}, u32[]{:S(2)}) copy-start(bf16[640,1536]{1,0:T(8,128)(2,1)} %get-tuple-element.10) | copy-start | bytes 5898244
  88.6 4.6 %copy-start.5 = (bf16[1920,1536]{1,0:T(8,128)(2,1)S(1)}, bf16[1920,1536]{1,0:T(8,128)(2,1)}, u32[]{:S(2)}) copy-start(bf16[1920,1536]{1,0:T(8,128)(2,1)} %copy-done.4) | copy-start | bytes 17694724
  93.2 29.6 %slice-start = ((bf16[1920,1536]{1,0:T(8,128)(2,1)}), bf16[640,1536]{1,0:T(8,128)(2,1)S(1)}, s32[]{:S(2)}) async-start(bf16[1920,1536]{1,0:T(8,128)(2,1)} %copy-done.4), calls=%async_computation.4 | async-start | bytes 3932160 | tf_op jit(solution)/shard_map/slice | solution.py:271
  161.2 32.9 %all-to-all-start = ((bf16[8,80,1536]{2,1,0:T(8,128)(2,1)}), bf16[8,80,1536]{2,1,0:T(8,128)(2,1)}, u32[]{:S(2)}, u32[]{:S(2)}) async-start(bf16[8,80,1536]{2,1,0:T(8,128)(2,1)} %bitcast.47), calls=%async_computation | async-start | bytes 3932160 | tf_op jit(solution)/shard_map/all_to_all | solution.py:288
  166.2 3.0 %copy-start.6 = (bf16[640,1536]{1,0:T(8,128)(2,1)S(1)}, bf16[640,1536]{1,0:T(8,128)(2,1)}, u32[]{:S(2)}) copy-start(bf16[640,1536]{1,0:T(8,128)(2,1)} %fusion.21) | copy-start | bytes 5898244
  233.9 7.6 %copy-start.1 = (bf16[1536,1152]{1,0:T(8,128)(2,1)S(1)}, bf16[1536,1152]{1,0:T(8,128)(2,1)}, u32[]{:S(2)}) copy-start(bf16[1536,1152]{1,0:T(8,128)(2,1)} %param.10) | copy-start | bytes 10616836
Sparse Core Ops, SparseCore 0:
  10.0 77.7 all-gather.5
  121.5 53.2 all-gather.3

commit v15 on v14

--- a/solution.py
+++ b/solution.py
@@ -240,6 +240,57 @@
     return result.astype(jnp.bfloat16)
 
 
+def swap_kernel(x_ref, y_ref, cross_send, cross_recv, own_sem):
+    n_core = lax.axis_size("core")
+    n_frames = lax.axis_size("fy") * n_core
+    piece = lax.axis_index("piece")
+    frame = lax.axis_index("fy") * n_core + lax.axis_index("core")
+    fsdp = lax.axis_index("fsdp")
+    per = x_ref.shape[0] // n_frames
+    peers = [(frame + k) % n_frames for k in range(1, n_frames)]
+    barrier = pltpu.get_barrier_semaphore()
+    for d in peers:
+        pl.semaphore_signal(
+            barrier, inc=1, device_id=(fsdp, piece, d // n_core, d % n_core), device_id_type=MESH_IDS
+        )
+    pl.semaphore_wait(barrier, n_frames - 1)
+    crosses = []
+    for k, d in enumerate(peers):
+        copy = pltpu.make_async_remote_copy(
+            src_ref=x_ref.at[pl.ds(pl.multiple_of(d * per, 16), per)],
+            dst_ref=y_ref.at[pl.ds(pl.multiple_of(frame * per, 16), per)],
+            send_sem=cross_send.at[k],
+            recv_sem=cross_recv.at[k],
+            device_id=(fsdp, piece, d // n_core, d % n_core),
+            device_id_type=MESH_IDS,
+        )
+        copy.start()
+        crosses.append(copy)
+    own_rows = pl.ds(pl.multiple_of(frame * per, 16), per)
+    own_copy = pltpu.make_async_copy(x_ref.at[own_rows], y_ref.at[own_rows], own_sem)
+    own_copy.start()
+    for copy in crosses:
+        copy.wait()
+    own_copy.wait()
+
+
+def swap_frames(x):
+    rows, feat = x.shape
+    return pl.pallas_call(
+        swap_kernel,
+        out_shape=jax.ShapeDtypeStruct((rows, feat), x.dtype),
+        in_specs=[pl.BlockSpec(memory_space=pl.ANY)],
+        out_specs=pl.BlockSpec(memory_space=pl.ANY),
+        scratch_shapes=[
+            pltpu.SemaphoreType.DMA((8,)),
+            pltpu.SemaphoreType.DMA((8,)),
+            pltpu.SemaphoreType.DMA(()),
+        ],
+        compiler_params=pltpu.CompilerParams(collective_id=1, has_side_effects=True),
+        cost_estimate=pl.CostEstimate(flops=0, transcendentals=0, bytes_accessed=2 * rows * feat * 2),
+    )(x)
+
+
 def local(tokens, mod_scale, mod_shift, w_qkv, w_out, neighbors, counts):
     tok_count = tokens.shape[1]
     feat_count = tokens.shape[2]
@@ -296,9 +347,7 @@
         clip_counts,
         first_pos,
     )
-    flat_temporal = lax.all_to_all(
-        temporal.reshape(tok_count, feat_count), frame_axes, split_axis=0, concat_axis=0, tiled=True
-    )
+    flat_temporal = swap_frames(temporal.reshape(tok_count, feat_count))
     projected = jnp.dot(flat_temporal, w_out_full, preferred_element_type=jnp.float32)
     return projected.astype(jnp.bfloat16).reshape(1, tok_count, feat_count)
 

time: 249 us -> 242 us (0.972)
  blocking collectives: 30.1 us -> 0 us
  Pallas kernels: 76.6 us -> 103 us
    all_to_all x1 -> x0, blocking collectives: 30.1 us -> none  [local(): lax.all_to_all(temporal.reshape(tok_count, feat_count), frame_axes, split...]
    pallas_call x0 -> x1, Pallas kernels: none -> 26.6 us  [swap_frames(): pl.pallas_call(swap_kernel, out_shape=jax.ShapeDtypeStruct((rows, feat),...]
    all_to_all x1 -> x0, local copies, waits for them, and re-layouts: 2.59 us -> none  [local(): lax.all_to_all(temporal.reshape(tok_count, feat_count), frame_axes, split...]
    unnamed x22 -> x25, local copies, waits for them, and re-layouts: 5.91 us -> 7.34 us
  transfers between devices with their start and end apart: 3 -> 3, of which waited for: 0 -> 0; matrix products, arithmetic and copies ran while one was open for 29% -> 38% of each run, Pallas kernels for 31% -> 43%
where the time goes in v15:
time: 242 us; the launch traced here: 241 us
  Pallas kernels  103 us (43%)
  matrix products  56.1 us (23%)
  local copies, waits for them, and re-layouts  38.4 us (16%)
  other arithmetic  25 us (10%)
  between operations  13.6 us (6%)
  starting transfers between devices  5.14 us (2%)
    pallas_call x1, Pallas kernels, exchange_tokens(): pl.pallas_call(exchange_kernel, out_shape=(jax.ShapeDtypeStruct((2, rows,...  49.2 us
    dot_general x1, matrix products, local(): jnp.einsum('tk,jkc->jtc', normed_all, w_full[1:], preferred_element_type=...  28.5 us
    pallas_call x1, Pallas kernels, spatial_rows(): pl.pallas_call(spatial_kernel, grid_spec=grid_spec, out_shape=jax.ShapeDt...  27.4 us
    pallas_call x1, Pallas kernels, swap_frames(): pl.pallas_call(swap_kernel, out_shape=jax.ShapeDtypeStruct((rows, feat),...  26.6 us
    convert_element_type x2, other arithmetic, layer_norm(): return (normal * (1.0 + mod_scale) + mod_shift).astype(jnp.bfloat16)  13.3 us
    dot_general x1, matrix products, local(): jnp.dot(flat_temporal, w_out_full, preferred_element_type=jnp.float32)  7.56 us
    unnamed x25, local copies, waits for them, and re-layouts  7.34 us
    dot_general x1, matrix products, local(): jnp.dot(jnp.concatenate([normed_all[tok_count:2 * tok_count], normed_cros...  6.6 us
  transfers between devices with their start and end apart: 3, of which 0 were waited for; matrix products, arithmetic and copies ran while one was open for 38% of the time, Pallas kernels for 43%

profile of v15, /device:TPU:1, one launch (start us, length us, event | category | flops | bytes accessed | tf_op | source)
XLA Modules:
  0.0 241.3 jit_solution(10137702883483791471)
XLA Ops:
  6.6 2.0 copy-done
  10.0 49.2 %shard_map.73 = (bf16[2,640,1536]{2,1,0:T(8,128)(2,1)}, bf16[640,1536]{1,0:T(8,128)(2,1)}) custom-call(bf16[640,1536]{1,0:T(8,128)(2,1)} %bitcast.47), custom_call_target="tpu_custom_call" | custom-call | bytes 157286400 | tf_op jit(solution)/shard_map/pallas_call | solution.py:200
  59.3 2.6 %select_bitcast_fusion.1 = (bf16[640,1536]{1,0:T(8,128)(2,1)S(1)}, bf16[640,1536]{1,0:T(8,128)(2,1)S(1)}) fusion(bf16[2,640,1536]{2,1,0:T(8,128)(2,1)} %get-tuple-element.9, pred[]{:T(512)S(6)} %gt.3, pred[]{:T(512)S(6)} %lt.30), kind=kLoop, calls=%fused_computation.46 | loop fusion | flops 1966080 | bytes 7864322 | tf_op jit(solution)/shard_map/jit(_where)/select_n | solution.py:301
  63.1 5.4 %fusion.3 = f32[1920]{0:T(1024)S(1)} fusion(f32[1920]{0:T(1024)S(1)} %broadcast_multiply_fusion, bf16[640,1536]{1,0:T(8,128)(2,1)S(1)} %get-tuple-element.18, bf16[640,1536]{1,0:T(8,128)(2,1)S(1)} %bitcast.49, bf16[640,1536]{1,0:T(8,128)(2,1)S(1)} %get-tuple-element.17), kind=kLoop, calls=%fused_computation.6 | loop fusion | flops 26540160 | bytes 5913600 | tf_op jit(solution)/shard_map/reduce_sum | solution.py:28
  68.5 11.2 %fusion.6 = bf16[1920,1536]{1,0:T(8,128)(2,1)S(1)} fusion(f32[1536]{0:T(1024)S(1)} %reduce.2, f32[1536]{0:T(1024)S(1)} %add_reduce_fusion, f32[1920]{0:T(1024)S(1)} %add_sqrt_fusion, f32[1920]{0:T(1024)S(1)} %broadcast_multiply_fusion, bf16[640,1536]{1,0:T(8,128)(2,1)S(1)} %get-tuple-element.18, bf16[640,1536]{1,0:T(8,128)(2,1)S(1)} %bitcast.50, ...), kind=kLoop, calls=%fused_computation.9 | loop fusion | flops 32440320 | bytes 11824128 | tf_op jit(solution)/shard_map/convert_element_type | solution.py:30
  79.7 2.5 %copy-done.4 = bf16[1920,1536]{1,0:T(8,128)(2,1)} copy-done((bf16[1920,1536]{1,0:T(8,128)(2,1)}, bf16[1920,1536]{1,0:T(8,128)(2,1)S(1)}, u32[]{:S(2)}) %copy-start.4) | copy-done | bytes 5898264
  87.2 2.1 fusion.21
  90.6 2.4 %slice_bitcast_fusion = bf16[1536,1152]{1,0:T(8,128)(2,1)S(1)} fusion(bf16[4,1536,1152]{2,1,0:T(8,128)(2,1)} %bitcast.55), kind=kLoop, calls=%fused_computation.34 | loop fusion | bytes 7077888 | tf_op jit(solution)/shard_map/squeeze | solution.py:315
  93.8 6.6 %convolution_convert_fusion.1 = bf16[1280,1536]{1,0:T(8,128)(2,1)S(1)} fusion(bf16[1536,384]{1,0:T(8,128)(2,1)S(1)} %slice_bitcast_fusion.3, bf16[1536,1152]{1,0:T(8,128)(2,1)S(1)} %slice_bitcast_fusion, bf16[640,1536]{1,0:T(8,128)(2,1)S(1)} %copy-done.6, bf16[640,1536]{1,0:T(8,128)(2,1)S(1)} %copy-done.5), kind=kOutput, calls=%fused_computation.11 | convolution fusion | flops 6059065344 | bytes 12582912 | tf_op jit(solution)/shard_map/dot_general | solution.py:321
  100.4 2.1 fusion.45
  102.6 28.5 %fusion.7.k_ref.v_ref = bf16[3,1920,1152]{2,1,0:T(8,128)(2,1)} fusion(bf16[4,1536,1152]{2,1,0:T(8,128)(2,1)} %bitcast.56, bf16[1920,1536]{1,0:T(8,128)(2,1)} %copy-done.4), kind=kOutput, calls=%fused_computation.10 | convolution fusion | flops 20390952960 | bytes 33325056 | tf_op jit(solution)/shard_map/tk,jkc->jtc/dot_general | solution.py:328
  131.1 27.4 %shard_map.74 = bf16[640,1536]{1,0:T(8,128)(2,1)} custom-call(s32[30]{0:T(128)} %reshape_squeeze.3.list_ref, s32[2]{0:T(128)} %pad_add_fusion.scalar_ref, bf16[640,1536]{1,0:T(8,128)(2,1)} %get-tuple-element.15.q_ref, bf16[3,1920,1152]{2,1,0:T(8,128)(2,1)} %fusion.7.k_ref.v_ref, bf16[3,1920,1152]{2,1,0:T(8,128)(2,1)} %fusion.7.k_ref.v_ref), custom_call_target="tpu_custom_call" | custom-call | flops 3019898880 | bytes 15728640 | tf_op jit(solution)/shard_map/pallas_call | solution.py:96
  158.4 5.1 %all-to-all-start = ((bf16[8,80,1536]{2,1,0:T(8,128)(2,1)}), bf16[8,80,1536]{2,1,0:T(8,128)(2,1)}, u32[]{:S(2)}, u32[]{:S(2)}) async-start(bf16[8,80,1536]{2,1,0:T(8,128)(2,1)} %bitcast.52), calls=%async_computation | async-start | bytes 3932160 | tf_op jit(solution)/shard_map/all_to_all | solution.py:339
  163.5 2.8 %slice_bitcast_fusion.2 = (bf16[1536,768]{1,0:T(8,128)(2,1)S(1)}, bf16[1536,768]{1,0:T(8,128)(2,1)S(1)}) fusion(bf16[4,1536,1152]{2,1,0:T(8,128)(2,1)} %bitcast.57), kind=kLoop, calls=%fused_computation.39 | loop fusion | bytes 9437184 | tf_op jit(solution)/shard_map/squeeze | solution.py:319
  166.5 4.5 %fusion.26 = bf16[640,1536]{1,0:T(8,128)(2,1)} fusion(bf16[640,1536]{1,0:T(8,128)(2,1)S(1)} %copy-done.7, bf16[1536,768]{1,0:T(8,128)(2,1)S(1)} %get-tuple-element.14, bf16[1536,768]{1,0:T(8,128)(2,1)S(1)} %get-tuple-element.13), kind=kOutput, calls=%fused_computation.36 | convolution fusion | flops 3030319104 | bytes 8650752 | tf_op jit(solution)/shard_map/dot_general | solution.py:327
  171.0 3.7 %reshape.84 = bf16[8,80,12,128]{3,2,1,0:T(8,128)(2,1)S(1)} reshape(bf16[640,1536]{1,0:T(8,128)(2,1)} %fusion.26) | data formatting | bytes 3932160 | tf_op jit(solution)/shard_map/reshape | solution.py:345
  174.7 4.8 %reshape.83 = bf16[8,80,12,128]{3,2,1,0:T(8,128)(2,1)} reshape(bf16[640,1536]{1,0:T(8,128)(2,1)} %get-tuple-element.16) | data formatting | bytes 3932160 | tf_op jit(solution)/shard_map/reshape | solution.py:344
  179.5 6.0 %fusion.31 = f32[80,12,8,8]{2,3,1,0:T(8,128)} fusion(bf16[8,80,12,128]{3,2,1,0:T(8,128)(2,1)S(1)} %reshape.84, bf16[8,80,12,128]{3,2,1,0:T(8,128)(2,1)} %reshape.83), kind=kOutput, calls=%fused_computation.42 | convolution fusion | flops 15728640 | bytes 4177920 | tf_op jit(solution)/shard_map/fphd,gphd->phfg/dot_general | solution.py:226
  185.5 3.0 %copy.32 = f32[80,12,8,8]{0,3,2,1:T(8,128)S(1)} copy(f32[80,12,8,8]{2,3,1,0:T(8,128)} %fusion.31) | data formatting | bytes 491520 | tf_op jit(solution)/shard_map/fphd,gphd->phfg/dot_general | solution.py:226
  188.7 2.3 copy.34
  191.4 3.7 %reshape.82 = bf16[8,80,12,128]{3,2,1,0:T(8,128)(2,1)S(1)} reshape(bf16[8,80,1536]{2,1,0:T(8,128)(2,1)} %all-to-all-done) | data formatting | bytes 3932160 | tf_op jit(solution)/shard_map/reshape | solution.py:346
  195.1 2.9 %fusion.25 = bf16[8,80,12,128]{3,0,2,1:T(8,128)(2,1)S(1)} fusion(bf16[80,12,8,8]{3,2,1,0:T(8,128)(2,1)} %copy.34, bf16[8,80,12,128]{3,2,1,0:T(8,128)(2,1)S(1)} %reshape.82, f32[8,80,12]{0,2,1:T(8,128)S(1)} %copy.35), kind=kOutput, calls=%fused_computation.33 | convolution fusion | flops 17694720 | bytes 4085760 | tf_op jit(solution)/shard_map/phfg,gphd->fphd/dot_general | solution.py:236
  200.3 26.6 %shard_map.75 = bf16[640,1536]{1,0:T(8,128)(2,1)} custom-call(bf16[640,1536]{1,0:T(8,128)(2,1)} %bitcast.53), custom_call_target="tpu_custom_call" | custom-call | bytes 3932160 | tf_op jit(solution)/shard_map/pallas_call | solution.py:279
  226.9 7.6 %fusion.29 = bf16[1,640,1536]{2,1,0:T(8,128)(2,1)} fusion(bf16[640,1536]{1,0:T(8,128)(2,1)} %shard_map.75, bf16[1536,1536]{1,0:T(8,128)(2,1)} %all-gather.4.cloned.1.call-done), kind=kOutput, calls=%fused_computation.37 | convolution fusion | flops 3020881920 | bytes 8650752 | tf_op jit(solution)/shard_map/dot_general | solution.py:351
  (51 shorter events, 12.9 us)
Async XLA Ops:
  6.5 2.0 copy-start
  6.5 52.6 %copy-start.9 = (f32[1,1536]{1,0:T(1,128)S(1)}, f32[1,1536]{1,0:T(1,128)}, u32[]{:S(2)}) copy-start(f32[1,1536]{1,0:T(1,128)} %param.9) | copy-start | bytes 18436
  6.5 52.7 %copy-start.8 = (f32[1,1536]{1,0:T(1,128)S(1)}, f32[1,1536]{1,0:T(1,128)}, u32[]{:S(2)}) copy-start(f32[1,1536]{1,0:T(1,128)} %param.8) | copy-start | bytes 18436
  6.5 82.7 %all-gather.6.cloned.1.call-start = ((), (), s32[]{:S(2)}) async-start(), calls=%async_computation.2 | async-start | bytes 15925248 | tf_op jit(solution)/shard_map/all_gather | solution.py:306
  9.9 217.0 %all-gather.4.cloned.1.call-start = ((), (), s32[]{:S(2)}) async-start(), calls=%async_computation.1 | async-start | bytes 5898240 | tf_op jit(solution)/shard_map/all_gather | solution.py:309
  59.3 2.8 %copy-start.2 = (bf16[1,640,1536]{2,1,0:T(8,128)(2,1)S(1)}, bf16[1,640,1536]{2,1,0:T(8,128)(2,1)}, u32[]{:S(2)}) copy-start(bf16[1,640,1536]{2,1,0:T(8,128)(2,1)} %param.7) | copy-start | bytes 5898244
  79.7 2.5 %copy-start.4 = (bf16[1920,1536]{1,0:T(8,128)(2,1)}, bf16[1920,1536]{1,0:T(8,128)(2,1)S(1)}, u32[]{:S(2)}) copy-start(bf16[1920,1536]{1,0:T(8,128)(2,1)S(1)} %fusion.6) | copy-start | bytes 17694724
  82.2 1.4 copy-start.10
  82.2 2.1 copy-start.11
  82.2 3.9 %copy-start.3 = (bf16[640,1536]{1,0:T(8,128)(2,1)S(1)}, bf16[640,1536]{1,0:T(8,128)(2,1)}, u32[]{:S(2)}) copy-start(bf16[640,1536]{1,0:T(8,128)(2,1)} %get-tuple-element.10) | copy-start | bytes 5898244
  90.6 2.6 %copy-start.5 = (bf16[640,1536]{1,0:T(8,128)(2,1)S(1)}, bf16[640,1536]{1,0:T(8,128)(2,1)}, u32[]{:S(2)}) copy-start(bf16[640,1536]{1,0:T(8,128)(2,1)} %slice.40) | copy-start | bytes 5898244
  90.6 3.2 %copy-start.6 = (bf16[640,1536]{1,0:T(8,128)(2,1)S(1)}, bf16[640,1536]{1,0:T(8,128)(2,1)}, u32[]{:S(2)}) copy-start(bf16[640,1536]{1,0:T(8,128)(2,1)} %fusion.21) | copy-start | bytes 5898244
  158.4 33.0 %all-to-all-start = ((bf16[8,80,1536]{2,1,0:T(8,128)(2,1)}), bf16[8,80,1536]{2,1,0:T(8,128)(2,1)}, u32[]{:S(2)}, u32[]{:S(2)}) async-start(bf16[8,80,1536]{2,1,0:T(8,128)(2,1)} %bitcast.52), calls=%async_computation | async-start | bytes 3932160 | tf_op jit(solution)/shard_map/all_to_all | solution.py:339
  163.5 3.0 %copy-start.7 = (bf16[640,1536]{1,0:T(8,128)(2,1)S(1)}, bf16[640,1536]{1,0:T(8,128)(2,1)}, u32[]{:S(2)}) copy-start(bf16[640,1536]{1,0:T(8,128)(2,1)} %fusion.21) | copy-start | bytes 5898244
  226.9 7.6 %copy-start.1 = (bf16[1536,1152]{1,0:T(8,128)(2,1)S(1)}, bf16[1536,1152]{1,0:T(8,128)(2,1)}, u32[]{:S(2)}) copy-start(bf16[1536,1152]{1,0:T(8,128)(2,1)} %param.10) | copy-start | bytes 10616836
Sparse Core Ops, SparseCore 0:
  10.0 77.7 all-gather.5
  102.7 53.2 all-gather.3

commit v16 on v15

--- a/solution.py
+++ b/solution.py
@@ -301,9 +301,11 @@
     above = jnp.where(piece_index > 0, rims[0], jnp.zeros_like(own))
     below = jnp.where(piece_index < lax.axis_size("piece") - 1, rims[1], jnp.zeros_like(own))
     core = lax.axis_index("core")
-    half_rows = w_qkv.shape[0] // 2
-    w_half = lax.dynamic_slice_in_dim(w_qkv, core * half_rows, half_rows, axis=0)
-    w_pieces = lax.all_gather(w_half, ("fsdp", "core"), axis=0, tiled=False)
+    n_share = lax.axis_size("fy") * lax.axis_size("core")
+    share = lax.axis_index("fy") * lax.axis_size("core") + core
+    share_rows = w_qkv.shape[0] // n_share
+    w_half = lax.dynamic_slice_in_dim(w_qkv, share * share_rows, share_rows, axis=0)
+    w_pieces = lax.all_gather(w_half, ("fsdp", "fy", "core"), axis=0, tiled=False)
     w_full = w_pieces.reshape(lax.axis_size("fsdp"), w_qkv.shape[0], w_qkv.shape[1])
     w_out, w_full = lax.optimization_barrier((w_out, w_full))
     w_out_full = lax.all_gather(w_out, "fsdp", axis=0, tiled=True)

time: 242 us -> 243 us (level)
    unnamed x25 -> x21, local copies, waits for them, and re-layouts: 7.34 us -> 7.55 us
  transfers between devices with their start and end apart: 3 -> 3, of which waited for: 0 -> 0; matrix products, arithmetic and copies ran while one was open for 38% -> 39% of each run, Pallas kernels for 43% -> 43%
where the time goes in v16:
time: 243 us; the launch traced here: 242 us
  Pallas kernels  103 us (42%)
  matrix products  56.1 us (23%)
  local copies, waits for them, and re-layouts  38 us (16%)
  other arithmetic  26.4 us (11%)
  between operations  13.6 us (6%)
  starting transfers between devices  5.12 us (2%)
    pallas_call x1, Pallas kernels, exchange_tokens(): pl.pallas_call(exchange_kernel, out_shape=(jax.ShapeDtypeStruct((2, rows,...  49.2 us
    dot_general x1, matrix products, local(): jnp.einsum('tk,jkc->jtc', normed_all, w_full[1:], preferred_element_type=...  28.5 us
    pallas_call x1, Pallas kernels, spatial_rows(): pl.pallas_call(spatial_kernel, grid_spec=grid_spec, out_shape=jax.ShapeDt...  27.4 us
    pallas_call x1, Pallas kernels, swap_frames(): pl.pallas_call(swap_kernel, out_shape=jax.ShapeDtypeStruct((rows, feat),...  26.6 us
    convert_element_type x2, other arithmetic, layer_norm(): return (normal * (1.0 + mod_scale) + mod_shift).astype(jnp.bfloat16)  13.3 us
    dot_general x1, matrix products, local(): jnp.dot(flat_temporal, w_out_full, preferred_element_type=jnp.float32)  7.56 us
    unnamed x21, local copies, waits for them, and re-layouts  7.55 us
    dot_general x1, matrix products, local(): jnp.dot(jnp.concatenate([normed_all[tok_count:2 * tok_count], normed_cros...  6.61 us
  transfers between devices with their start and end apart: 3, of which 0 were waited for; matrix products, arithmetic and copies ran while one was open for 39% of the time, Pallas kernels for 43%

profile of v16, /device:TPU:1, one launch (start us, length us, event | category | flops | bytes accessed | tf_op | source)
XLA Modules:
  0.0 242.4 jit_solution(12718051414261387030)
XLA Ops:
  6.5 2.0 copy-done
  9.4 49.2 %shard_map.73 = (bf16[2,640,1536]{2,1,0:T(8,128)(2,1)}, bf16[640,1536]{1,0:T(8,128)(2,1)}) custom-call(bf16[640,1536]{1,0:T(8,128)(2,1)} %bitcast.47), custom_call_target="tpu_custom_call" | custom-call | bytes 157286400 | tf_op jit(solution)/shard_map/pallas_call | solution.py:200
  60.1 2.6 %select_bitcast_fusion.1 = (bf16[640,1536]{1,0:T(8,128)(2,1)S(1)}, bf16[640,1536]{1,0:T(8,128)(2,1)S(1)}) fusion(bf16[2,640,1536]{2,1,0:T(8,128)(2,1)} %get-tuple-element.9, pred[]{:T(512)S(6)} %gt.3, pred[]{:T(512)S(6)} %lt.30), kind=kLoop, calls=%fused_computation.46 | loop fusion | flops 1966080 | bytes 7864322 | tf_op jit(solution)/shard_map/jit(_where)/select_n | solution.py:301
  64.1 5.4 %fusion.3 = f32[1920]{0:T(1024)S(1)} fusion(f32[1920]{0:T(1024)S(1)} %broadcast_multiply_fusion, bf16[640,1536]{1,0:T(8,128)(2,1)S(1)} %get-tuple-element.18, bf16[640,1536]{1,0:T(8,128)(2,1)S(1)} %bitcast.49, bf16[640,1536]{1,0:T(8,128)(2,1)S(1)} %get-tuple-element.17), kind=kLoop, calls=%fused_computation.6 | loop fusion | flops 26540160 | bytes 5913600 | tf_op jit(solution)/shard_map/reduce_sum | solution.py:28
  69.5 11.2 %fusion.6 = bf16[1920,1536]{1,0:T(8,128)(2,1)S(1)} fusion(f32[1536]{0:T(1024)S(1)} %reduce.2, f32[1536]{0:T(1024)S(1)} %add_reduce_fusion, f32[1920]{0:T(1024)S(1)} %add_sqrt_fusion, f32[1920]{0:T(1024)S(1)} %broadcast_multiply_fusion, bf16[640,1536]{1,0:T(8,128)(2,1)S(1)} %get-tuple-element.18, bf16[640,1536]{1,0:T(8,128)(2,1)S(1)} %bitcast.50, ...), kind=kLoop, calls=%fused_computation.9 | loop fusion | flops 32440320 | bytes 11824128 | tf_op jit(solution)/shard_map/convert_element_type | solution.py:30
  80.8 2.5 %copy-done.4 = bf16[1920,1536]{1,0:T(8,128)(2,1)} copy-done((bf16[1920,1536]{1,0:T(8,128)(2,1)}, bf16[1920,1536]{1,0:T(8,128)(2,1)S(1)}, u32[]{:S(2)}) %copy-start.4) | copy-done | bytes 5898264
  88.2 2.1 fusion.21
  91.7 2.4 slice_bitcast_fusion
  94.9 6.6 %convolution_convert_fusion.1 = bf16[1280,1536]{1,0:T(8,128)(2,1)S(1)} fusion(bf16[1536,384]{1,0:T(8,128)(2,1)S(1)} %slice_bitcast_fusion.3, bf16[1536,1152]{1,0:T(8,128)(2,1)S(1)} %slice_bitcast_fusion, bf16[640,1536]{1,0:T(8,128)(2,1)S(1)} %copy-done.6, bf16[640,1536]{1,0:T(8,128)(2,1)S(1)} %copy-done.5), kind=kOutput, calls=%fused_computation.11 | convolution fusion | flops 6059065344 | bytes 12582912 | tf_op jit(solution)/shard_map/dot_general | solution.py:323
  101.5 2.1 fusion.45
  103.6 28.5 %fusion.7.k_ref.v_ref = bf16[3,1920,1152]{2,1,0:T(8,128)(2,1)} fusion(bf16[4,1536,1152]{2,1,0:T(8,128)(2,1)} %bitcast.56, bf16[1920,1536]{1,0:T(8,128)(2,1)} %copy-done.4), kind=kOutput, calls=%fused_computation.10 | convolution fusion | flops 20390952960 | bytes 33325056 | tf_op jit(solution)/shard_map/tk,jkc->jtc/dot_general | solution.py:330
  132.1 27.4 %shard_map.74 = bf16[640,1536]{1,0:T(8,128)(2,1)} custom-call(s32[30]{0:T(128)} %reshape_squeeze.3.list_ref, s32[2]{0:T(128)} %pad_add_fusion.scalar_ref, bf16[640,1536]{1,0:T(8,128)(2,1)} %get-tuple-element.15.q_ref, bf16[3,1920,1152]{2,1,0:T(8,128)(2,1)} %fusion.7.k_ref.v_ref, bf16[3,1920,1152]{2,1,0:T(8,128)(2,1)} %fusion.7.k_ref.v_ref), custom_call_target="tpu_custom_call" | custom-call | flops 3019898880 | bytes 15728640 | tf_op jit(solution)/shard_map/pallas_call | solution.py:96
  159.5 5.1 %all-to-all-start = ((bf16[8,80,1536]{2,1,0:T(8,128)(2,1)}), bf16[8,80,1536]{2,1,0:T(8,128)(2,1)}, u32[]{:S(2)}, u32[]{:S(2)}) async-start(bf16[8,80,1536]{2,1,0:T(8,128)(2,1)} %bitcast.52), calls=%async_computation | async-start | bytes 3932160 | tf_op jit(solution)/shard_map/all_to_all | solution.py:341
  164.5 2.8 %slice_bitcast_fusion.2 = (bf16[1536,768]{1,0:T(8,128)(2,1)S(1)}, bf16[1536,768]{1,0:T(8,128)(2,1)S(1)}) fusion(bf16[4,1536,1152]{2,1,0:T(8,128)(2,1)} %bitcast.57), kind=kLoop, calls=%fused_computation.39 | loop fusion | bytes 9437184 | tf_op jit(solution)/shard_map/squeeze | solution.py:321
  167.5 4.5 %fusion.26 = bf16[640,1536]{1,0:T(8,128)(2,1)} fusion(bf16[640,1536]{1,0:T(8,128)(2,1)S(1)} %copy-done.7, bf16[1536,768]{1,0:T(8,128)(2,1)S(1)} %get-tuple-element.14, bf16[1536,768]{1,0:T(8,128)(2,1)S(1)} %get-tuple-element.13), kind=kOutput, calls=%fused_computation.36 | convolution fusion | flops 3030319104 | bytes 8650752 | tf_op jit(solution)/shard_map/dot_general | solution.py:329
  172.0 3.7 %reshape.84 = bf16[8,80,12,128]{3,2,1,0:T(8,128)(2,1)S(1)} reshape(bf16[640,1536]{1,0:T(8,128)(2,1)} %fusion.26) | data formatting | bytes 3932160 | tf_op jit(solution)/shard_map/reshape | solution.py:347
  175.7 4.8 %reshape.83 = bf16[8,80,12,128]{3,2,1,0:T(8,128)(2,1)} reshape(bf16[640,1536]{1,0:T(8,128)(2,1)} %get-tuple-element.16) | data formatting | bytes 3932160 | tf_op jit(solution)/shard_map/reshape | solution.py:346
  180.5 6.0 %fusion.31 = f32[80,12,8,8]{2,3,1,0:T(8,128)} fusion(bf16[8,80,12,128]{3,2,1,0:T(8,128)(2,1)S(1)} %reshape.84, bf16[8,80,12,128]{3,2,1,0:T(8,128)(2,1)} %reshape.83), kind=kOutput, calls=%fused_computation.42 | convolution fusion | flops 15728640 | bytes 4177920 | tf_op jit(solution)/shard_map/fphd,gphd->phfg/dot_general | solution.py:226
  186.5 3.0 %copy.32 = f32[80,12,8,8]{0,3,2,1:T(8,128)S(1)} copy(f32[80,12,8,8]{2,3,1,0:T(8,128)} %fusion.31) | data formatting | bytes 491520 | tf_op jit(solution)/shard_map/fphd,gphd->phfg/dot_general | solution.py:226
  189.8 2.3 copy.34
  192.4 3.7 %reshape.82 = bf16[8,80,12,128]{3,2,1,0:T(8,128)(2,1)S(1)} reshape(bf16[8,80,1536]{2,1,0:T(8,128)(2,1)} %all-to-all-done) | data formatting | bytes 3932160 | tf_op jit(solution)/shard_map/reshape | solution.py:348
  196.2 2.9 %fusion.25 = bf16[8,80,12,128]{3,0,2,1:T(8,128)(2,1)S(1)} fusion(bf16[80,12,8,8]{3,2,1,0:T(8,128)(2,1)} %copy.34, bf16[8,80,12,128]{3,2,1,0:T(8,128)(2,1)S(1)} %reshape.82, f32[8,80,12]{0,2,1:T(8,128)S(1)} %copy.35), kind=kOutput, calls=%fused_computation.33 | convolution fusion | flops 17694720 | bytes 4085760 | tf_op jit(solution)/shard_map/phfg,gphd->fphd/dot_general | solution.py:236
  201.3 26.6 %shard_map.75 = bf16[640,1536]{1,0:T(8,128)(2,1)} custom-call(bf16[640,1536]{1,0:T(8,128)(2,1)} %bitcast.53), custom_call_target="tpu_custom_call" | custom-call | bytes 3932160 | tf_op jit(solution)/shard_map/pallas_call | solution.py:279
  228.0 7.6 %fusion.29 = bf16[1,640,1536]{2,1,0:T(8,128)(2,1)} fusion(bf16[640,1536]{1,0:T(8,128)(2,1)} %shard_map.75, bf16[1536,1536]{1,0:T(8,128)(2,1)} %all-gather.4.cloned.1.call-done), kind=kOutput, calls=%fused_computation.37 | convolution fusion | flops 3020881920 | bytes 8650752 | tf_op jit(solution)/shard_map/dot_general | solution.py:353
  (47 shorter events, 13.9 us)
Async XLA Ops:
  6.5 2.0 copy-start
  6.5 83.7 %all-gather.6.cloned.1.call-start = ((), (), s32[]{:S(2)}) async-start(), calls=%async_computation.2 | async-start | bytes 14598144 | tf_op jit(solution)/shard_map/all_gather | solution.py:308
  9.4 218.6 %all-gather.4.cloned.1.call-start = ((), (), s32[]{:S(2)}) async-start(), calls=%async_computation.1 | async-start | bytes 5898240 | tf_op jit(solution)/shard_map/all_gather | solution.py:311
  60.1 3.0 %copy-start.2 = (bf16[1,640,1536]{2,1,0:T(8,128)(2,1)S(1)}, bf16[1,640,1536]{2,1,0:T(8,128)(2,1)}, u32[]{:S(2)}) copy-start(bf16[1,640,1536]{2,1,0:T(8,128)(2,1)} %param.7) | copy-start | bytes 5898244
  80.8 2.5 %copy-start.4 = (bf16[1920,1536]{1,0:T(8,128)(2,1)}, bf16[1920,1536]{1,0:T(8,128)(2,1)S(1)}, u32[]{:S(2)}) copy-start(bf16[1920,1536]{1,0:T(8,128)(2,1)S(1)} %fusion.6) | copy-start | bytes 17694724
  83.2 1.4 copy-start.8
  83.2 2.1 copy-start.9
  83.2 3.9 %copy-start.3 = (bf16[640,1536]{1,0:T(8,128)(2,1)S(1)}, bf16[640,1536]{1,0:T(8,128)(2,1)}, u32[]{:S(2)}) copy-start(bf16[640,1536]{1,0:T(8,128)(2,1)} %get-tuple-element.10) | copy-start | bytes 5898244
  91.7 2.6 %copy-start.5 = (bf16[640,1536]{1,0:T(8,128)(2,1)S(1)}, bf16[640,1536]{1,0:T(8,128)(2,1)}, u32[]{:S(2)}) copy-start(bf16[640,1536]{1,0:T(8,128)(2,1)} %slice.40) | copy-start | bytes 5898244
  91.7 3.2 %copy-start.6 = (bf16[640,1536]{1,0:T(8,128)(2,1)S(1)}, bf16[640,1536]{1,0:T(8,128)(2,1)}, u32[]{:S(2)}) copy-start(bf16[640,1536]{1,0:T(8,128)(2,1)} %fusion.21) | copy-start | bytes 5898244
  159.5 32.9 %all-to-all-start = ((bf16[8,80,1536]{2,1,0:T(8,128)(2,1)}), bf16[8,80,1536]{2,1,0:T(8,128)(2,1)}, u32[]{:S(2)}, u32[]{:S(2)}) async-start(bf16[8,80,1536]{2,1,0:T(8,128)(2,1)} %bitcast.52), calls=%async_computation | async-start | bytes 3932160 | tf_op jit(solution)/shard_map/all_to_all | solution.py:341
  164.5 3.0 %copy-start.7 = (bf16[640,1536]{1,0:T(8,128)(2,1)S(1)}, bf16[640,1536]{1,0:T(8,128)(2,1)}, u32[]{:S(2)}) copy-start(bf16[640,1536]{1,0:T(8,128)(2,1)} %fusion.21) | copy-start | bytes 5898244
  227.9 7.6 %copy-start.1 = (bf16[1536,1152]{1,0:T(8,128)(2,1)S(1)}, bf16[1536,1152]{1,0:T(8,128)(2,1)}, u32[]{:S(2)}) copy-start(bf16[1536,1152]{1,0:T(8,128)(2,1)} %param.10) | copy-start | bytes 10616836
Sparse Core Ops, SparseCore 0:
  9.6 75.4 all-gather.5
  103.7 53.2 all-gather.3

commit v17 on v15

--- a/solution.py
+++ b/solution.py
@@ -303,10 +303,26 @@
     core = lax.axis_index("core")
     half_rows = w_qkv.shape[0] // 2
     w_half = lax.dynamic_slice_in_dim(w_qkv, core * half_rows, half_rows, axis=0)
-    w_pieces = lax.all_gather(w_half, ("fsdp", "core"), axis=0, tiled=False)
-    w_full = w_pieces.reshape(lax.axis_size("fsdp"), w_qkv.shape[0], w_qkv.shape[1])
+    n_fsdp = lax.axis_size("fsdp")
+    fsdp_index = lax.axis_index("fsdp")
+    back = (fsdp_index - jnp.arange(n_fsdp, dtype=jnp.int32)) % n_fsdp
+
+    def gather_fsdp(block):
+        ring = [block] + [
+            lax.ppermute(block, "fsdp", [(d, (d + k) % n_fsdp) for d in range(n_fsdp)])
+            for k in range(1, n_fsdp)
+        ]
+        return jnp.take(jnp.stack(ring), back, axis=0)
+
+    mine = gather_fsdp(w_half)
+    other = lax.ppermute(mine, "core", [(0, 1), (1, 0)])
+    w_full = jnp.where(
+        core == 0,
+        jnp.concatenate([mine, other], axis=1),
+        jnp.concatenate([other, mine], axis=1),
+    )
     w_out, w_full = lax.optimization_barrier((w_out, w_full))
-    w_out_full = lax.all_gather(w_out, "fsdp", axis=0, tiled=True)
+    w_out_full = gather_fsdp(w_out).reshape(n_fsdp * w_out.shape[0], w_out.shape[1])
     normed_all = layer_norm(
         jnp.concatenate([above, own, below], axis=0), mod_scale[0], mod_shift[0]
     )

time: 242 us -> 380 us (1.57); the launches traced: 241 us -> 375 us
  waiting for transfers between devices: 0.06 us -> 89 us
  other arithmetic: 25 us -> 58.3 us
  local copies, waits for them, and re-layouts: 38.4 us -> 55.3 us
  between operations: 13.6 us -> 0.47 us
  starting transfers between devices: 5.14 us -> 12.7 us
    ppermute x0 -> x7, waiting for transfers between devices: none -> 78.7 us  [the longest x6 78.7 us: gather_fsdp(): lax.ppermute(block, 'fsdp', [(d, (d + k) % n_fsdp) for d in range(n_fsdp)])]
    select_n x0 -> x4, other arithmetic: none -> 23.2 us  [the longest x3 11.7 us: gather_fsdp(): return jnp.take(jnp.stack(ring), back, axis=0)]
    gather x0 -> x3, local copies, waits for them, and re-layouts: none -> 22.9 us  [gather_fsdp(): return jnp.take(jnp.stack(ring), back, axis=0)]
    all_to_all x1, waiting for transfers between devices: 0.01 us -> 10.2 us  [local(): lax.all_to_all(spatial, frame_axes, split_axis=0, concat_axis=0, tiled=True)]
    another operation x0 -> x2, other arithmetic: none -> 10.1 us  [gather_fsdp(): return jnp.take(jnp.stack(ring), back, axis=0)]
    ppermute x0 -> x7, starting transfers between devices: none -> 7.74 us  [the longest x6 6.9 us: gather_fsdp(): lax.ppermute(block, 'fsdp', [(d, (d + k) % n_fsdp) for d in range(n_fsdp)])]
  transfers between devices with their start and end apart: 3 -> 8, of which waited for: 0 -> 3; matrix products, arithmetic and copies ran while one was open for 38% -> 21% of each run, Pallas kernels for 43% -> 20%
where the time goes in v17:
time: 380 us; the launch traced here: 375 us
  Pallas kernels  102 us (27%)
  waiting for transfers between devices  89 us (23%)
  other arithmetic  58.3 us (15%)
  matrix products  57.7 us (15%)
  local copies, waits for them, and re-layouts  55.3 us (15%)
  starting transfers between devices  12.7 us (3%)
    ppermute x6, waiting for transfers between devices, gather_fsdp(): lax.ppermute(block, 'fsdp', [(d, (d + k) % n_fsdp) for d in range(n_fsdp)])  78.7 us
    pallas_call x1, Pallas kernels, exchange_tokens(): pl.pallas_call(exchange_kernel, out_shape=(jax.ShapeDtypeStruct((2, rows,...  48.1 us
    pallas_call x1, Pallas kernels, spatial_rows(): pl.pallas_call(spatial_kernel, grid_spec=grid_spec, out_shape=jax.ShapeDt...  27.5 us
    pallas_call x1, Pallas kernels, swap_frames(): pl.pallas_call(swap_kernel, out_shape=jax.ShapeDtypeStruct((rows, feat),...  26.3 us
    dot_general x1, matrix products, local(): jnp.einsum('tk,jkc->jtc', normed_all, w_full[1:], preferred_element_type=...  25.4 us
    gather x3, local copies, waits for them, and re-layouts, gather_fsdp(): return jnp.take(jnp.stack(ring), back, axis=0)  22.9 us
    convert_element_type x2, other arithmetic, layer_norm(): return (normal * (1.0 + mod_scale) + mod_shift).astype(jnp.bfloat16)  13.3 us
    select_n x3, other arithmetic, gather_fsdp(): return jnp.take(jnp.stack(ring), back, axis=0)  11.7 us
  transfers between devices with their start and end apart: 8, of which 3 were waited for; matrix products, arithmetic and copies ran while one was open for 21% of the time, Pallas kernels for 20%

profile of v17, /device:TPU:1, one launch (start us, length us, event | category | flops | bytes accessed | tf_op | source)
XLA Modules:
  0.0 375.3 jit_solution(17409660291949247447)
XLA Ops:
  3.3 4.6 %collective-permute-start.2 = (bf16[768,1152]{1,0:T(8,128)(2,1)}, bf16[768,1152]{1,0:T(8,128)(2,1)}, u32[]{:S(2)}, u32[]{:S(2)}) collective-permute-start(bf16[768,1152]{1,0:T(8,128)(2,1)} %constant_dynamic-slice_fusion), channel_id=1, source_target_pairs={{0,96},{32,0},{64,32},{96,64},{1,97},{33,1},{65,33},{97,65},{2,98}... | collective-permute-start | bytes 5308424 | tf_op jit(solution)/shard_map/ppermute | solution.py:312
  8.8 74.5 %collective-permute-done.2 = bf16[768,1152]{1,0:T(8,128)(2,1)} collective-permute-done((bf16[768,1152]{1,0:T(8,128)(2,1)}, bf16[768,1152]{1,0:T(8,128)(2,1)}, u32[]{:S(2)}, u32[]{:S(2)}) %collective-permute-start.2) | collective-permute-done | bytes 1769504 | tf_op jit(solution)/shard_map/ppermute | solution.py:312
  83.3 4.3 %collective-permute-done = bf16[768,1152]{1,0:T(8,128)(2,1)} collective-permute-done((bf16[768,1152]{1,0:T(8,128)(2,1)}, bf16[768,1152]{1,0:T(8,128)(2,1)}, u32[]{:S(2)}, u32[]{:S(2)}) %collective-permute-start) | collective-permute-done | bytes 1769504 | tf_op jit(solution)/shard_map/ppermute | solution.py:312
  87.6 6.1 %pad_maximum_fusion = bf16[4,768,1152]{2,1,0:T(8,128)(2,1)} fusion(bf16[1,768,1152]{2,1,0:T(8,128)(2,1)} %bitcast.8, bf16[1,768,1152]{2,1,0:T(8,128)(2,1)} %bitcast.7, bf16[1,768,1152]{2,1,0:T(8,128)(2,1)} %bitcast.6, bf16[1,768,1152]{2,1,0:T(8,128)(2,1)S(1)} %fusion.55), kind=kLoop, calls=%fused_computation.15 | loop fusion | flops 10616832 | bytes 14155776 | tf_op jit(solution)/shard_map/stack | solution.py:315
  93.6 7.3 %gather_fusion = bf16[4,768,1152]{2,1,0:T(8,128)(2,1)} fusion(bf16[4,768,1152]{2,1,0:T(8,128)(2,1)} %pad_maximum_fusion, s32[1024]{0:T(1024)S(1)} %pad_clamp_fusion), kind=kCustom, calls=%fused_computation | custom fusion | bytes 14155792 | tf_op jit(solution)/shard_map/jit(_take)/gather | solution.py:315
  100.9 10.3 %copy.28 = bf16[4,768,1152]{1,2,0:T(8,128)(2,1)} copy(bf16[4,768,1152]{2,1,0:T(8,128)(2,1)} %gather_fusion) | data formatting | bytes 14155776 | tf_op jit(solution)/shard_map/jit(_take)/gather | solution.py:315
  111.3 6.7 %broadcast_select_fusion = bf16[4,768,1152]{1,2,0:T(8,128)(2,1)} fusion(bf16[4,768,1152]{1,2,0:T(8,128)(2,1)} %copy.28, pred[4]{0:T(512)(128)(4,1)S(1)} %compare_and_fusion), kind=kLoop, calls=%fused_computation.16 | loop fusion | flops 3538944 | bytes 14155780 | tf_op jit(solution)/shard_map/jit(_take)/select_n | solution.py:315
  118.8 48.1 %shard_map.73 = (bf16[2,640,1536]{2,1,0:T(8,128)(2,1)}, bf16[640,1536]{1,0:T(8,128)(2,1)}) custom-call(bf16[640,1536]{1,0:T(8,128)(2,1)} %bitcast.56), custom_call_target="tpu_custom_call" | custom-call | bytes 157286400 | tf_op jit(solution)/shard_map/pallas_call | solution.py:200
  170.8 5.4 %fusion.3 = f32[1920]{0:T(1024)S(1)} fusion(f32[1920]{0:T(1024)S(1)} %broadcast_multiply_fusion, bf16[640,1536]{1,0:T(8,128)(2,1)S(1)} %get-tuple-element.18, bf16[640,1536]{1,0:T(8,128)(2,1)S(1)} %bitcast.58, bf16[640,1536]{1,0:T(8,128)(2,1)S(1)} %get-tuple-element.17), kind=kLoop, calls=%fused_computation.9 | loop fusion | flops 26540160 | bytes 5913600 | tf_op jit(solution)/shard_map/reduce_sum | solution.py:28
  176.2 11.2 %fusion.6 = bf16[1920,1536]{1,0:T(8,128)(2,1)S(1)} fusion(f32[1536]{0:T(1024)S(1)} %reduce.2, f32[1536]{0:T(1024)S(1)} %add_reduce_fusion, f32[1920]{0:T(1024)S(1)} %add_sqrt_fusion, f32[1920]{0:T(1024)S(1)} %broadcast_multiply_fusion, bf16[640,1536]{1,0:T(8,128)(2,1)S(1)} %get-tuple-element.18, bf16[640,1536]{1,0:T(8,128)(2,1)S(1)} %bitcast.59, ...), kind=kLoop, calls=%fused_computation.12 | loop fusion | flops 32440320 | bytes 11824128 | tf_op jit(solution)/shard_map/convert_element_type | solution.py:30
  196.4 11.6 %maximum_select_fusion = bf16[4,1536,1152]{1,2,0:T(8,128)(2,1)S(1)} fusion(bf16[4,768,1152]{1,2,0:T(8,128)(2,1)} %collective-permute-done.3, bf16[4,768,1152]{1,2,0:T(8,128)(2,1)} %broadcast_select_fusion, pred[]{:T(512)S(6)} %eq.5), kind=kLoop, calls=%fused_computation.5 | loop fusion | flops 63700992 | bytes 28311552 | tf_op jit(solution)/shard_map/jit(_where)/select_n | solution.py:319
  210.8 25.4 %fusion.7.k_ref.v_ref = bf16[3,1920,1152]{2,1,0:T(8,128)(2,1)} fusion(bf16[4,1536,1152]{1,2,0:T(8,128)(2,1)S(1)} %maximum_select_fusion, bf16[1920,1536]{1,0:T(8,128)(2,1)} %copy-done.4), kind=kOutput, calls=%fused_computation.13 | convolution fusion | flops 20390952960 | bytes 33325056 | tf_op jit(solution)/shard_map/tk,jkc->jtc/dot_general | solution.py:344
  237.8 7.6 %fusion.26 = bf16[640,1536]{1,0:T(8,128)(2,1)} fusion(bf16[640,1536]{1,0:T(8,128)(2,1)} %fusion.21, bf16[1536,768]{0,1:T(8,128)(2,1)} %get-tuple-element.14, bf16[1536,768]{0,1:T(8,128)(2,1)} %get-tuple-element.13), kind=kOutput, calls=%fused_computation.43 | convolution fusion | flops 3030319104 | bytes 8650752 | tf_op jit(solution)/shard_map/dot_general | solution.py:343
  245.4 6.9 %convolution_convert_fusion.1 = bf16[1280,1536]{1,0:T(8,128)(2,1)S(1)} fusion(bf16[1536,384]{0,1:T(8,128)(2,1)S(1)} %slice_bitcast_fusion.3, bf16[1536,1152]{0,1:T(8,128)(2,1)S(1)} %slice_bitcast_fusion, bf16[640,1536]{1,0:T(8,128)(2,1)S(1)} %copy-done.5, bf16[640,1536]{1,0:T(8,128)(2,1)S(1)} %slice-done), kind=kOutput, calls=%fused_computation.14 | convolution fusion | flops 6059065344 | bytes 12582912 | tf_op jit(solution)/shard_map/dot_general | solution.py:337
  258.3 4.7 %reshape.136 = bf16[8,80,12,128]{3,2,1,0:T(8,128)(2,1)} reshape(bf16[640,1536]{1,0:T(8,128)(2,1)} %get-tuple-element.16) | data formatting | bytes 3932160 | tf_op jit(solution)/shard_map/reshape | solution.py:360
  263.0 6.1 %fusion.31 = f32[80,12,8,8]{2,3,1,0:T(8,128)} fusion(bf16[8,80,12,128]{3,2,1,0:T(8,128)(2,1)S(1)} %reshape.137, bf16[8,80,12,128]{3,2,1,0:T(8,128)(2,1)} %reshape.136), kind=kOutput, calls=%fused_computation.49 | convolution fusion | flops 15728640 | bytes 4177920 | tf_op jit(solution)/shard_map/fphd,gphd->phfg/dot_general | solution.py:226
  274.7 27.5 %shard_map.74 = bf16[640,1536]{1,0:T(8,128)(2,1)} custom-call(s32[30]{0:T(128)} %reshape_squeeze.3.list_ref, s32[2]{0:T(128)} %pad_add_fusion.scalar_ref, bf16[640,1536]{1,0:T(8,128)(2,1)} %get-tuple-element.15.q_ref, bf16[3,1920,1152]{2,1,0:T(8,128)(2,1)} %fusion.7.k_ref.v_ref, bf16[3,1920,1152]{2,1,0:T(8,128)(2,1)} %fusion.7.k_ref.v_ref), custom_call_target="tpu_custom_call" | custom-call | flops 3019898880 | bytes 15728640 | tf_op jit(solution)/shard_map/pallas_call | solution.py:96
  302.3 4.9 %all-to-all-start = ((bf16[8,80,1536]{2,1,0:T(8,128)(2,1)}), bf16[8,80,1536]{2,1,0:T(8,128)(2,1)S(1)}, u32[]{:S(2)}, u32[]{:S(2)}) async-start(bf16[8,80,1536]{2,1,0:T(8,128)(2,1)} %bitcast.61), calls=%async_computation | async-start | bytes 3932160 | tf_op jit(solution)/shard_map/all_to_all | solution.py:355
  311.6 5.3 %gather_fusion.1 = bf16[4,384,1536]{2,1,0:T(8,128)(2,1)} fusion(bf16[4,384,1536]{2,1,0:T(8,128)(2,1)} %pad_maximum_fusion.2, s32[1024]{0:T(1024)S(1)} %pad_clamp_fusion), kind=kCustom, calls=%fused_computation.1 | custom fusion | bytes 9437200 | tf_op jit(solution)/shard_map/jit(_take)/gather | solution.py:315
  317.0 5.0 %bitcast_select_fusion = bf16[1536,1536]{1,0:T(8,128)(2,1)} fusion(bf16[4,384,1536]{2,1,0:T(8,128)(2,1)} %gather_fusion.1, pred[1536]{0:T(1024)(128)(4,1)S(1)} %broadcast_in_dim.61), kind=kLoop, calls=%fused_computation.29 | loop fusion | flops 2359296 | bytes 9438720 | tf_op jit(solution)/shard_map/jit(_take)/select_n | solution.py:315
  321.9 10.2 %all-to-all-done = bf16[8,80,1536]{2,1,0:T(8,128)(2,1)S(1)} async-done(((bf16[8,80,1536]{2,1,0:T(8,128)(2,1)}), bf16[8,80,1536]{2,1,0:T(8,128)(2,1)S(1)}, u32[]{:S(2)}, u32[]{:S(2)}) %all-to-all-start) | async-done | bytes 1966112 | tf_op jit(solution)/shard_map/all_to_all | solution.py:355
  334.9 4.1 %fusion.25 = bf16[8,80,12,128]{3,0,2,1:T(8,128)(2,1)S(1)} fusion(bf16[80,12,8,8]{3,2,1,0:T(8,128)(2,1)} %copy.34, bf16[8,80,12,128]{3,2,1,0:T(8,128)(2,1)} %reshape.135, f32[8,80,12]{0,2,1:T(8,128)S(1)} %copy.35), kind=kOutput, calls=%fused_computation.40 | convolution fusion | flops 17694720 | bytes 4085760 | tf_op jit(solution)/shard_map/phfg,gphd->fphd/dot_general | solution.py:236
  341.2 26.3 %shard_map.75 = bf16[640,1536]{1,0:T(8,128)(2,1)} custom-call(bf16[640,1536]{1,0:T(8,128)(2,1)} %bitcast.62), custom_call_target="tpu_custom_call" | custom-call | bytes 3932160 | tf_op jit(solution)/shard_map/pallas_call | solution.py:279
  367.5 7.6 %fusion.29 = bf16[1,640,1536]{2,1,0:T(8,128)(2,1)} fusion(bf16[640,1536]{1,0:T(8,128)(2,1)} %shard_map.75, bf16[1536,1536]{1,0:T(8,128)(2,1)} %bitcast_select_fusion), kind=kOutput, calls=%fused_computation.44 | convolution fusion | flops 3020881920 | bytes 8650752 | tf_op jit(solution)/shard_map/dot_general | solution.py:367
  (70 shorter events, 43.2 us)
Async XLA Ops:
  0.0 2.0 copy-start
  3.3 80.0 %collective-permute-start.2 = (bf16[768,1152]{1,0:T(8,128)(2,1)}, bf16[768,1152]{1,0:T(8,128)(2,1)}, u32[]{:S(2)}, u32[]{:S(2)}) collective-permute-start(bf16[768,1152]{1,0:T(8,128)(2,1)} %constant_dynamic-slice_fusion), channel_id=1, source_target_pairs={{0,96},{32,0},{64,32},{96,64},{1,97},{33,1},{65,33},{97,65},{2,98}... | collective-permute-start | bytes 5308424 | tf_op jit(solution)/shard_map/ppermute | solution.py:312
  7.9 75.4 %collective-permute-start.1 = (bf16[768,1152]{1,0:T(8,128)(2,1)}, bf16[768,1152]{1,0:T(8,128)(2,1)}, u32[]{:S(2)}, u32[]{:S(2)}) collective-permute-start(bf16[768,1152]{1,0:T(8,128)(2,1)} %constant_dynamic-slice_fusion), channel_id=1, source_target_pairs={{0,64},{32,96},{64,0},{96,32},{1,65},{33,97},{65,1},{97,33},{2,66}... | collective-permute-start | bytes 5308424 | tf_op jit(solution)/shard_map/ppermute | solution.py:312
  7.9 79.6 %collective-permute-start = (bf16[768,1152]{1,0:T(8,128)(2,1)}, bf16[768,1152]{1,0:T(8,128)(2,1)}, u32[]{:S(2)}, u32[]{:S(2)}) collective-permute-start(bf16[768,1152]{1,0:T(8,128)(2,1)} %constant_dynamic-slice_fusion), channel_id=1, source_target_pairs={{0,32},{32,64},{64,96},{96,0},{1,33},{33,65},{65,97},{97,1},{2,34}... | collective-permute-start | bytes 5308424 | tf_op jit(solution)/shard_map/ppermute | solution.py:312
  111.3 55.7 %copy-start.7 = (f32[1,1536]{1,0:T(1,128)S(1)}, f32[1,1536]{1,0:T(1,128)}, u32[]{:S(2)}) copy-start(f32[1,1536]{1,0:T(1,128)} %param.9) | copy-start | bytes 18436
  111.3 55.7 %copy-start.6 = (f32[1,1536]{1,0:T(1,128)S(1)}, f32[1,1536]{1,0:T(1,128)}, u32[]{:S(2)}) copy-start(f32[1,1536]{1,0:T(1,128)} %param.8) | copy-start | bytes 18436
  118.0 78.4 %collective-permute-start.3 = (bf16[4,768,1152]{1,2,0:T(8,128)(2,1)}, bf16[4,768,1152]{1,2,0:T(8,128)(2,1)}, u32[]{:S(2)}, u32[]{:S(2)}) collective-permute-start(bf16[4,768,1152]{1,2,0:T(8,128)(2,1)} %broadcast_select_fusion), channel_id=1, source_target_pairs={{0,1},{1,0},{2,3},{3,2},{4,5},{5,4},{6,7},{7,6},{8,9},{9,8},{10,11... | collective-permute-start | bytes 21233672 | tf_op jit(solution)/shard_map/ppermute | solution.py:318
  167.0 2.7 copy-start.2
  187.4 2.5 copy-start.4
  189.9 0.7 copy-start.8
  189.9 1.5 copy-start.9
  190.0 3.3 copy-start.3
  236.2 71.4 %collective-permute-start.6 = (bf16[384,1536]{1,0:T(8,128)(2,1)}, bf16[384,1536]{1,0:T(8,128)(2,1)}, u32[]{:S(2)}, u32[]{:S(2)}) collective-permute-start(bf16[384,1536]{1,0:T(8,128)(2,1)} %param.11), channel_id=1, source_target_pairs={{0,96},{32,0},{64,32},{96,64},{1,97},{33,1},{65,33},{97,65},{2,98}... | collective-permute-start | bytes 3538952 | tf_op jit(solution)/shard_map/ppermute | solution.py:312
  236.9 70.6 %collective-permute-start.5 = (bf16[384,1536]{1,0:T(8,128)(2,1)}, bf16[384,1536]{1,0:T(8,128)(2,1)}, u32[]{:S(2)}, u32[]{:S(2)}) collective-permute-start(bf16[384,1536]{1,0:T(8,128)(2,1)} %param.11), channel_id=1, source_target_pairs={{0,64},{32,96},{64,0},{96,32},{1,65},{33,97},{65,1},{97,33},{2,66}... | collective-permute-start | bytes 3538952 | tf_op jit(solution)/shard_map/ppermute | solution.py:312
  237.0 70.6 %collective-permute-start.4 = (bf16[384,1536]{1,0:T(8,128)(2,1)}, bf16[384,1536]{1,0:T(8,128)(2,1)}, u32[]{:S(2)}, u32[]{:S(2)}) collective-permute-start(bf16[384,1536]{1,0:T(8,128)(2,1)} %param.11), channel_id=1, source_target_pairs={{0,32},{32,64},{64,96},{96,0},{1,33},{33,65},{65,97},{97,1},{2,34}... | collective-permute-start | bytes 3538952 | tf_op jit(solution)/shard_map/ppermute | solution.py:312
  237.8 7.6 %slice-start = ((bf16[1920,1536]{1,0:T(8,128)(2,1)}), bf16[640,1536]{1,0:T(8,128)(2,1)S(1)}, s32[]{:S(2)}) async-start(bf16[1920,1536]{1,0:T(8,128)(2,1)} %copy-done.4), calls=%async_computation.1 | async-start | bytes 3932160 | tf_op jit(solution)/shard_map/slice | solution.py:338
  237.8 7.6 %copy-start.5 = (bf16[640,1536]{1,0:T(8,128)(2,1)S(1)}, bf16[640,1536]{1,0:T(8,128)(2,1)}, u32[]{:S(2)}) copy-start(bf16[640,1536]{1,0:T(8,128)(2,1)} %fusion.21) | copy-start | bytes 5898244
  302.3 29.9 %all-to-all-start = ((bf16[8,80,1536]{2,1,0:T(8,128)(2,1)}), bf16[8,80,1536]{2,1,0:T(8,128)(2,1)S(1)}, u32[]{:S(2)}, u32[]{:S(2)}) async-start(bf16[8,80,1536]{2,1,0:T(8,128)(2,1)} %bitcast.61), calls=%async_computation | async-start | bytes 3932160 | tf_op jit(solution)/shard_map/all_to_all | solution.py:355
  367.5 7.6 %copy-start.1 = (bf16[1536,1152]{1,0:T(8,128)(2,1)S(1)}, bf16[1536,1152]{1,0:T(8,128)(2,1)}, u32[]{:S(2)}) copy-start(bf16[1536,1152]{1,0:T(8,128)(2,1)} %param.10) | copy-start | bytes 10616836

commit v18 on v15

--- a/solution.py
+++ b/solution.py
@@ -291,6 +291,78 @@
     )(x)
 
 
+def swap_project_kernel(x_ref, w_ref, o_ref, recv, cross_send, cross_recv, own_sem):
+    n_core = lax.axis_size("core")
+    n_frames = lax.axis_size("fy") * n_core
+    piece = lax.axis_index("piece")
+    frame = lax.axis_index("fy") * n_core + lax.axis_index("core")
+    fsdp = lax.axis_index("fsdp")
+    per = x_ref.shape[0] // n_frames
+    peers = [(frame + k) % n_frames for k in range(1, n_frames)]
+    sources = [(frame + n_frames - k) % n_frames for k in range(1, n_frames)]
+    barrier = pltpu.get_barrier_semaphore()
+    for d in peers:
+        pl.semaphore_signal(
+            barrier, inc=1, device_id=(fsdp, piece, d // n_core, d % n_core), device_id_type=MESH_IDS
+        )
+    pl.semaphore_wait(barrier, n_frames - 1)
+    crosses = []
+    for k, d in enumerate(peers):
+        copy = pltpu.make_async_remote_copy(
+            src_ref=x_ref.at[pl.ds(pl.multiple_of(d * per, 16), per)],
+            dst_ref=recv.at[pl.ds(pl.multiple_of(frame * per, 16), per)],
+            send_sem=cross_send.at[k],
+            recv_sem=cross_recv.at[k],
+            device_id=(fsdp, piece, d // n_core, d % n_core),
+            device_id_type=MESH_IDS,
+        )
+        copy.start()
+        crosses.append(copy)
+    own_rows = pl.ds(pl.multiple_of(frame * per, 16), per)
+    own_copy = pltpu.make_async_copy(x_ref.at[own_rows], recv.at[own_rows], own_sem)
+    own_copy.start()
+    own_copy.wait()
+    o_ref[own_rows, :] = jnp.dot(
+        recv[own_rows, :], w_ref[...], preferred_element_type=jnp.float32
+    ).astype(o_ref.dtype)
+    for k, src in enumerate(sources):
+        rows = pl.ds(pl.multiple_of(src * per, 16), per)
+        incoming = pltpu.make_async_remote_copy(
+            src_ref=x_ref.at[rows],
+            dst_ref=recv.at[rows],
+            send_sem=cross_send.at[k],
+            recv_sem=cross_recv.at[k],
+            device_id=(fsdp, piece, src // n_core, src % n_core),
+            device_id_type=MESH_IDS,
+        )
+        incoming.wait_recv()
+        o_ref[rows, :] = jnp.dot(
+            recv[rows, :], w_ref[...], preferred_element_type=jnp.float32
+        ).astype(o_ref.dtype)
+    for copy in crosses:
+        copy.wait_send()
+
+
+def swap_project(x, w):
+    rows, feat = x.shape
+    return pl.pallas_call(
+        swap_project_kernel,
+        out_shape=jax.ShapeDtypeStruct((rows, w.shape[1]), x.dtype),
+        in_specs=[pl.BlockSpec(memory_space=pl.ANY), pl.BlockSpec(memory_space=pltpu.VMEM)],
+        out_specs=pl.BlockSpec(memory_space=pltpu.VMEM),
+        scratch_shapes=[
+            pltpu.VMEM((rows, feat), x.dtype),
+            pltpu.SemaphoreType.DMA((8,)),
+            pltpu.SemaphoreType.DMA((8,)),
+            pltpu.SemaphoreType.DMA(()),
+        ],
+        compiler_params=pltpu.CompilerParams(collective_id=1, has_side_effects=True),
+        cost_estimate=pl.CostEstimate(
+            flops=2 * rows * feat * w.shape[1], transcendentals=0, bytes_accessed=2 * rows * feat * 2
+        ),
+    )(x, w)
+
+
 def local(tokens, mod_scale, mod_shift, w_qkv, w_out, neighbors, counts):
     tok_count = tokens.shape[1]
     feat_count = tokens.shape[2]
@@ -347,9 +419,8 @@
         clip_counts,
         first_pos,
     )
-    flat_temporal = swap_frames(temporal.reshape(tok_count, feat_count))
-    projected = jnp.dot(flat_temporal, w_out_full, preferred_element_type=jnp.float32)
-    return projected.astype(jnp.bfloat16).reshape(1, tok_count, feat_count)
+    projected = swap_project(temporal.reshape(tok_count, feat_count), w_out_full)
+    return projected.reshape(1, tok_count, feat_count)
 
 
 def solution(mesh):

time: 242 us -> 244 us (level)
  matrix products: 56.1 us -> 48.8 us
  Pallas kernels: 103 us -> 110 us
  local copies, waits for them, and re-layouts: 38.4 us -> 41.3 us
    dot_general x1 -> x0, matrix products: 7.56 us -> none  [local(): jnp.dot(flat_temporal, w_out_full, preferred_element_type=jnp.float32)]
    pallas_call x1, Pallas kernels: 26.6 us -> 33.5 us  [swap_project(): pl.pallas_call(swap_project_kernel, out_shape=jax.ShapeDtypeStruct((rows,...]
    unnamed x25 -> x26, local copies, waits for them, and re-layouts: 7.34 us -> 10.3 us
  transfers between devices with their start and end apart: 3 -> 3, of which waited for: 0 -> 0; matrix products, arithmetic and copies ran while one was open for 38% -> 38% of each run, Pallas kernels for 43% -> 31%
where the time goes in v18:
time: 244 us
  Pallas kernels  110 us (45%)
  matrix products  48.8 us (20%)
  local copies, waits for them, and re-layouts  41.3 us (17%)
  other arithmetic  25 us (10%)
  between operations  13.6 us (6%)
  starting transfers between devices  5.14 us (2%)
    pallas_call x1, Pallas kernels, exchange_tokens(): pl.pallas_call(exchange_kernel, out_shape=(jax.ShapeDtypeStruct((2, rows,...  49.2 us
    pallas_call x1, Pallas kernels, swap_project(): pl.pallas_call(swap_project_kernel, out_shape=jax.ShapeDtypeStruct((rows,...  33.5 us
    dot_general x1, matrix products, local(): jnp.einsum('tk,jkc->jtc', normed_all, w_full[1:], preferred_element_type=...  28.5 us
    pallas_call x1, Pallas kernels, spatial_rows(): pl.pallas_call(spatial_kernel, grid_spec=grid_spec, out_shape=jax.ShapeDt...  27.4 us
    convert_element_type x2, other arithmetic, layer_norm(): return (normal * (1.0 + mod_scale) + mod_shift).astype(jnp.bfloat16)  13.3 us
    unnamed x26, local copies, waits for them, and re-layouts  10.3 us
    dot_general x1, matrix products, local(): jnp.dot(jnp.concatenate([normed_all[tok_count:2 * tok_count], normed_cros...  6.6 us
    reduce_sum x2, other arithmetic, layer_norm(): spread = jnp.mean((values_f32 - center) ** 2, axis=-1, keepdims=True)  6.05 us
  transfers between devices with their start and end apart: 3, of which 0 were waited for; matrix products, arithmetic and copies ran while one was open for 38% of the time, Pallas kernels for 31%

profile of v18, /device:TPU:1, one launch (start us, length us, event | category | flops | bytes accessed | tf_op | source)
XLA Modules:
  0.0 243.9 jit_solution(7818734004322616768)
XLA Ops:
  6.6 2.0 copy-done
  10.0 49.2 %shard_map.73 = (bf16[2,640,1536]{2,1,0:T(8,128)(2,1)}, bf16[640,1536]{1,0:T(8,128)(2,1)}) custom-call(bf16[640,1536]{1,0:T(8,128)(2,1)} %bitcast.44), custom_call_target="tpu_custom_call" | custom-call | bytes 157286400 | tf_op jit(solution)/shard_map/pallas_call | solution.py:200
  59.3 2.6 %select_bitcast_fusion.1 = (bf16[640,1536]{1,0:T(8,128)(2,1)S(1)}, bf16[640,1536]{1,0:T(8,128)(2,1)S(1)}) fusion(bf16[2,640,1536]{2,1,0:T(8,128)(2,1)} %get-tuple-element.9, pred[]{:T(512)S(6)} %gt.3, pred[]{:T(512)S(6)} %lt.30), kind=kLoop, calls=%fused_computation.44 | loop fusion | flops 1966080 | bytes 7864322 | tf_op jit(solution)/shard_map/jit(_where)/select_n | solution.py:373
  63.1 5.4 %fusion.3 = f32[1920]{0:T(1024)S(1)} fusion(f32[1920]{0:T(1024)S(1)} %broadcast_multiply_fusion, bf16[640,1536]{1,0:T(8,128)(2,1)S(1)} %get-tuple-element.18, bf16[640,1536]{1,0:T(8,128)(2,1)S(1)} %bitcast.46, bf16[640,1536]{1,0:T(8,128)(2,1)S(1)} %get-tuple-element.17), kind=kLoop, calls=%fused_computation.6 | loop fusion | flops 26540160 | bytes 5913600 | tf_op jit(solution)/shard_map/reduce_sum | solution.py:28
  68.5 11.2 %fusion.6 = bf16[1920,1536]{1,0:T(8,128)(2,1)S(1)} fusion(f32[1536]{0:T(1024)S(1)} %reduce.2, f32[1536]{0:T(1024)S(1)} %add_reduce_fusion, f32[1920]{0:T(1024)S(1)} %add_sqrt_fusion, f32[1920]{0:T(1024)S(1)} %broadcast_multiply_fusion, bf16[640,1536]{1,0:T(8,128)(2,1)S(1)} %get-tuple-element.18, bf16[640,1536]{1,0:T(8,128)(2,1)S(1)} %bitcast.47, ...), kind=kLoop, calls=%fused_computation.9 | loop fusion | flops 32440320 | bytes 11824128 | tf_op jit(solution)/shard_map/convert_element_type | solution.py:30
  79.7 2.5 %copy-done.4 = bf16[1920,1536]{1,0:T(8,128)(2,1)} copy-done((bf16[1920,1536]{1,0:T(8,128)(2,1)}, bf16[1920,1536]{1,0:T(8,128)(2,1)S(1)}, u32[]{:S(2)}) %copy-start.4) | copy-done | bytes 5898264
  87.2 2.1 fusion.21
  90.6 2.4 slice_bitcast_fusion
  93.8 6.6 %convolution_convert_fusion.1 = bf16[1280,1536]{1,0:T(8,128)(2,1)S(1)} fusion(bf16[1536,384]{1,0:T(8,128)(2,1)S(1)} %slice_bitcast_fusion.3, bf16[1536,1152]{1,0:T(8,128)(2,1)S(1)} %slice_bitcast_fusion, bf16[640,1536]{1,0:T(8,128)(2,1)S(1)} %copy-done.6, bf16[640,1536]{1,0:T(8,128)(2,1)S(1)} %copy-done.5), kind=kOutput, calls=%fused_computation.11 | convolution fusion | flops 6059065344 | bytes 12582912 | tf_op jit(solution)/shard_map/dot_general | solution.py:393
  100.4 2.1 fusion.44
  102.6 28.5 %fusion.7.k_ref.v_ref = bf16[3,1920,1152]{2,1,0:T(8,128)(2,1)} fusion(bf16[4,1536,1152]{2,1,0:T(8,128)(2,1)} %bitcast.52, bf16[1920,1536]{1,0:T(8,128)(2,1)} %copy-done.4), kind=kOutput, calls=%fused_computation.10 | convolution fusion | flops 20390952960 | bytes 33325056 | tf_op jit(solution)/shard_map/tk,jkc->jtc/dot_general | solution.py:400
  131.1 27.4 %shard_map.74 = bf16[640,1536]{1,0:T(8,128)(2,1)} custom-call(s32[30]{0:T(128)} %reshape_squeeze.3.list_ref, s32[2]{0:T(128)} %pad_add_fusion.scalar_ref, bf16[640,1536]{1,0:T(8,128)(2,1)} %get-tuple-element.15.q_ref, bf16[3,1920,1152]{2,1,0:T(8,128)(2,1)} %fusion.7.k_ref.v_ref, bf16[3,1920,1152]{2,1,0:T(8,128)(2,1)} %fusion.7.k_ref.v_ref), custom_call_target="tpu_custom_call" | custom-call | flops 3019898880 | bytes 15728640 | tf_op jit(solution)/shard_map/pallas_call | solution.py:96
  158.4 5.1 %all-to-all-start = ((bf16[8,80,1536]{2,1,0:T(8,128)(2,1)}), bf16[8,80,1536]{2,1,0:T(8,128)(2,1)}, u32[]{:S(2)}, u32[]{:S(2)}) async-start(bf16[8,80,1536]{2,1,0:T(8,128)(2,1)} %bitcast.49), calls=%async_computation | async-start | bytes 3932160 | tf_op jit(solution)/shard_map/all_to_all | solution.py:411
  163.5 2.8 %slice_bitcast_fusion.2 = (bf16[1536,768]{1,0:T(8,128)(2,1)S(1)}, bf16[1536,768]{1,0:T(8,128)(2,1)S(1)}) fusion(bf16[4,1536,1152]{2,1,0:T(8,128)(2,1)} %bitcast.53), kind=kLoop, calls=%fused_computation.37 | loop fusion | bytes 9437184 | tf_op jit(solution)/shard_map/squeeze | solution.py:391
  166.5 4.5 %fusion.26 = bf16[640,1536]{1,0:T(8,128)(2,1)} fusion(bf16[640,1536]{1,0:T(8,128)(2,1)S(1)} %copy-done.7, bf16[1536,768]{1,0:T(8,128)(2,1)S(1)} %get-tuple-element.14, bf16[1536,768]{1,0:T(8,128)(2,1)S(1)} %get-tuple-element.13), kind=kOutput, calls=%fused_computation.35 | convolution fusion | flops 3030319104 | bytes 8650752 | tf_op jit(solution)/shard_map/dot_general | solution.py:399
  171.0 3.7 %reshape.84 = bf16[8,80,12,128]{3,2,1,0:T(8,128)(2,1)S(1)} reshape(bf16[640,1536]{1,0:T(8,128)(2,1)} %fusion.26) | data formatting | bytes 3932160 | tf_op jit(solution)/shard_map/reshape | solution.py:417
  174.7 4.8 %reshape.83 = bf16[8,80,12,128]{3,2,1,0:T(8,128)(2,1)} reshape(bf16[640,1536]{1,0:T(8,128)(2,1)} %get-tuple-element.16) | data formatting | bytes 3932160 | tf_op jit(solution)/shard_map/reshape | solution.py:416
  179.5 6.0 %fusion.30 = f32[80,12,8,8]{2,3,1,0:T(8,128)} fusion(bf16[8,80,12,128]{3,2,1,0:T(8,128)(2,1)S(1)} %reshape.84, bf16[8,80,12,128]{3,2,1,0:T(8,128)(2,1)} %reshape.83), kind=kOutput, calls=%fused_computation.40 | convolution fusion | flops 15728640 | bytes 4177920 | tf_op jit(solution)/shard_map/fphd,gphd->phfg/dot_general | solution.py:226
  185.5 3.0 %copy.32 = f32[80,12,8,8]{0,3,2,1:T(8,128)S(1)} copy(f32[80,12,8,8]{2,3,1,0:T(8,128)} %fusion.30) | data formatting | bytes 491520 | tf_op jit(solution)/shard_map/fphd,gphd->phfg/dot_general | solution.py:226
  188.7 2.3 copy.34
  191.4 3.7 %reshape.82 = bf16[8,80,12,128]{3,2,1,0:T(8,128)(2,1)S(1)} reshape(bf16[8,80,1536]{2,1,0:T(8,128)(2,1)} %all-to-all-done) | data formatting | bytes 3932160 | tf_op jit(solution)/shard_map/reshape | solution.py:418
  195.1 3.2 %fusion.25 = bf16[8,80,12,128]{3,0,2,1:T(8,128)(2,1)S(1)} fusion(bf16[80,12,8,8]{3,2,1,0:T(8,128)(2,1)} %copy.34, bf16[8,80,12,128]{3,2,1,0:T(8,128)(2,1)S(1)} %reshape.82, f32[8,80,12]{0,2,1:T(8,128)S(1)} %copy.35), kind=kOutput, calls=%fused_computation.33 | convolution fusion | flops 17694720 | bytes 4085760 | tf_op jit(solution)/shard_map/phfg,gphd->fphd/dot_general | solution.py:236
  200.6 33.5 %shard_map.75 = bf16[640,1536]{1,0:T(8,128)(2,1)} custom-call(bf16[640,1536]{1,0:T(8,128)(2,1)} %bitcast.54, bf16[1536,1536]{1,0:T(8,128)(2,1)} %all-gather.4.cloned.1.call-done.w_ref), custom_call_target="tpu_custom_call" | custom-call | flops 3019898880 | bytes 3932160 | tf_op jit(solution)/shard_map/pallas_call | solution.py:348
  234.1 2.9 %copy.48 = bf16[1,640,1536]{2,1,0:T(8,128)(2,1)} copy(bf16[1,640,1536]{2,1,0:T(8,128)(2,1)} %bitcast.55) | data formatting | bytes 3932160
  (51 shorter events, 12.8 us)
Async XLA Ops:
  6.5 2.0 copy-start
  6.5 52.6 %copy-start.9 = (f32[1,1536]{1,0:T(1,128)S(1)}, f32[1,1536]{1,0:T(1,128)}, u32[]{:S(2)}) copy-start(f32[1,1536]{1,0:T(1,128)} %param.9) | copy-start | bytes 18436
  6.5 52.7 %copy-start.8 = (f32[1,1536]{1,0:T(1,128)S(1)}, f32[1,1536]{1,0:T(1,128)}, u32[]{:S(2)}) copy-start(f32[1,1536]{1,0:T(1,128)} %param.8) | copy-start | bytes 18436
  6.5 82.7 %all-gather.6.cloned.1.call-start = ((), (), s32[]{:S(2)}) async-start(), calls=%async_computation.2 | async-start | bytes 15925248 | tf_op jit(solution)/shard_map/all_gather | solution.py:378
  9.9 190.6 %all-gather.4.cloned.1.call-start = ((), (), s32[]{:S(2)}) async-start(), calls=%async_computation.1 | async-start | bytes 5898240 | tf_op jit(solution)/shard_map/all_gather | solution.py:381
  59.3 2.8 %copy-start.2 = (bf16[1,640,1536]{2,1,0:T(8,128)(2,1)S(1)}, bf16[1,640,1536]{2,1,0:T(8,128)(2,1)}, u32[]{:S(2)}) copy-start(bf16[1,640,1536]{2,1,0:T(8,128)(2,1)} %param.7) | copy-start | bytes 5898244
  79.7 2.5 %copy-start.4 = (bf16[1920,1536]{1,0:T(8,128)(2,1)}, bf16[1920,1536]{1,0:T(8,128)(2,1)S(1)}, u32[]{:S(2)}) copy-start(bf16[1920,1536]{1,0:T(8,128)(2,1)S(1)} %fusion.6) | copy-start | bytes 17694724
  82.2 1.4 copy-start.10
  82.2 2.1 copy-start.11
  82.2 3.9 %copy-start.3 = (bf16[640,1536]{1,0:T(8,128)(2,1)S(1)}, bf16[640,1536]{1,0:T(8,128)(2,1)}, u32[]{:S(2)}) copy-start(bf16[640,1536]{1,0:T(8,128)(2,1)} %get-tuple-element.10) | copy-start | bytes 5898244
  90.6 2.6 %copy-start.5 = (bf16[640,1536]{1,0:T(8,128)(2,1)S(1)}, bf16[640,1536]{1,0:T(8,128)(2,1)}, u32[]{:S(2)}) copy-start(bf16[640,1536]{1,0:T(8,128)(2,1)} %slice.40) | copy-start | bytes 5898244
  90.6 3.2 %copy-start.6 = (bf16[640,1536]{1,0:T(8,128)(2,1)S(1)}, bf16[640,1536]{1,0:T(8,128)(2,1)}, u32[]{:S(2)}) copy-start(bf16[640,1536]{1,0:T(8,128)(2,1)} %fusion.21) | copy-start | bytes 5898244
  158.4 33.0 %all-to-all-start = ((bf16[8,80,1536]{2,1,0:T(8,128)(2,1)}), bf16[8,80,1536]{2,1,0:T(8,128)(2,1)}, u32[]{:S(2)}, u32[]{:S(2)}) async-start(bf16[8,80,1536]{2,1,0:T(8,128)(2,1)} %bitcast.49), calls=%async_computation | async-start | bytes 3932160 | tf_op jit(solution)/shard_map/all_to_all | solution.py:411
  163.5 3.0 %copy-start.7 = (bf16[640,1536]{1,0:T(8,128)(2,1)S(1)}, bf16[640,1536]{1,0:T(8,128)(2,1)}, u32[]{:S(2)}) copy-start(bf16[640,1536]{1,0:T(8,128)(2,1)} %fusion.21) | copy-start | bytes 5898244
  200.6 36.5 %copy-start.1 = (bf16[1536,1152]{1,0:T(8,128)(2,1)S(1)}, bf16[1536,1152]{1,0:T(8,128)(2,1)}, u32[]{:S(2)}) copy-start(bf16[1536,1152]{1,0:T(8,128)(2,1)} %param.10) | copy-start | bytes 10616836
Sparse Core Ops, SparseCore 0:
  10.0 77.7 all-gather.5
  102.7 53.2 all-gather.3

commit v19 on v15

--- a/solution.py
+++ b/solution.py
@@ -255,7 +255,8 @@
         )
     pl.semaphore_wait(barrier, n_frames - 1)
     crosses = []
-    for k, d in enumerate(peers):
+    for k in (3, 2, 4, 1, 5, 0, 6):
+        d = peers[k]
         copy = pltpu.make_async_remote_copy(
             src_ref=x_ref.at[pl.ds(pl.multiple_of(d * per, 16), per)],
             dst_ref=y_ref.at[pl.ds(pl.multiple_of(frame * per, 16), per)],

time: 242 us -> 242 us (level)
  no operation moved by 1% of the time
where the time goes in v19:
time: 242 us; the launch traced here: 241 us
  Pallas kernels  103 us (43%)
  matrix products  56.1 us (23%)
  local copies, waits for them, and re-layouts  38.4 us (16%)
  other arithmetic  25 us (10%)
  between operations  13.6 us (6%)
  starting transfers between devices  5.14 us (2%)
    pallas_call x1, Pallas kernels, exchange_tokens(): pl.pallas_call(exchange_kernel, out_shape=(jax.ShapeDtypeStruct((2, rows,...  49.2 us
    dot_general x1, matrix products, local(): jnp.einsum('tk,jkc->jtc', normed_all, w_full[1:], preferred_element_type=...  28.5 us
    pallas_call x1, Pallas kernels, spatial_rows(): pl.pallas_call(spatial_kernel, grid_spec=grid_spec, out_shape=jax.ShapeDt...  27.4 us
    pallas_call x1, Pallas kernels, swap_frames(): pl.pallas_call(swap_kernel, out_shape=jax.ShapeDtypeStruct((rows, feat),...  26.3 us
    convert_element_type x2, other arithmetic, layer_norm(): return (normal * (1.0 + mod_scale) + mod_shift).astype(jnp.bfloat16)  13.3 us
    dot_general x1, matrix products, local(): jnp.dot(flat_temporal, w_out_full, preferred_element_type=jnp.float32)  7.56 us
    unnamed x25, local copies, waits for them, and re-layouts  7.34 us
    dot_general x1, matrix products, local(): jnp.dot(jnp.concatenate([normed_all[tok_count:2 * tok_count], normed_cros...  6.6 us
  transfers between devices with their start and end apart: 3, of which 0 were waited for; matrix products, arithmetic and copies ran while one was open for 38% of the time, Pallas kernels for 43%

profile of v19, /device:TPU:1, one launch (start us, length us, event | category | flops | bytes accessed | tf_op | source)
XLA Modules:
  0.0 241.1 jit_solution(2426114175057582573)
XLA Ops:
  6.6 2.0 copy-done
  10.0 49.2 %shard_map.73 = (bf16[2,640,1536]{2,1,0:T(8,128)(2,1)}, bf16[640,1536]{1,0:T(8,128)(2,1)}) custom-call(bf16[640,1536]{1,0:T(8,128)(2,1)} %bitcast.47), custom_call_target="tpu_custom_call" | custom-call | bytes 157286400 | tf_op jit(solution)/shard_map/pallas_call | solution.py:200
  59.3 2.6 %select_bitcast_fusion.1 = (bf16[640,1536]{1,0:T(8,128)(2,1)S(1)}, bf16[640,1536]{1,0:T(8,128)(2,1)S(1)}) fusion(bf16[2,640,1536]{2,1,0:T(8,128)(2,1)} %get-tuple-element.9, pred[]{:T(512)S(6)} %gt.3, pred[]{:T(512)S(6)} %lt.30), kind=kLoop, calls=%fused_computation.46 | loop fusion | flops 1966080 | bytes 7864322 | tf_op jit(solution)/shard_map/jit(_where)/select_n | solution.py:302
  63.1 5.4 %fusion.3 = f32[1920]{0:T(1024)S(1)} fusion(f32[1920]{0:T(1024)S(1)} %broadcast_multiply_fusion, bf16[640,1536]{1,0:T(8,128)(2,1)S(1)} %get-tuple-element.18, bf16[640,1536]{1,0:T(8,128)(2,1)S(1)} %bitcast.49, bf16[640,1536]{1,0:T(8,128)(2,1)S(1)} %get-tuple-element.17), kind=kLoop, calls=%fused_computation.6 | loop fusion | flops 26540160 | bytes 5913600 | tf_op jit(solution)/shard_map/reduce_sum | solution.py:28
  68.5 11.2 %fusion.6 = bf16[1920,1536]{1,0:T(8,128)(2,1)S(1)} fusion(f32[1536]{0:T(1024)S(1)} %reduce.2, f32[1536]{0:T(1024)S(1)} %add_reduce_fusion, f32[1920]{0:T(1024)S(1)} %add_sqrt_fusion, f32[1920]{0:T(1024)S(1)} %broadcast_multiply_fusion, bf16[640,1536]{1,0:T(8,128)(2,1)S(1)} %get-tuple-element.18, bf16[640,1536]{1,0:T(8,128)(2,1)S(1)} %bitcast.50, ...), kind=kLoop, calls=%fused_computation.9 | loop fusion | flops 32440320 | bytes 11824128 | tf_op jit(solution)/shard_map/convert_element_type | solution.py:30
  79.7 2.5 %copy-done.4 = bf16[1920,1536]{1,0:T(8,128)(2,1)} copy-done((bf16[1920,1536]{1,0:T(8,128)(2,1)}, bf16[1920,1536]{1,0:T(8,128)(2,1)S(1)}, u32[]{:S(2)}) %copy-start.4) | copy-done | bytes 5898264
  87.2 2.1 fusion.21
  90.6 2.4 %slice_bitcast_fusion = bf16[1536,1152]{1,0:T(8,128)(2,1)S(1)} fusion(bf16[4,1536,1152]{2,1,0:T(8,128)(2,1)} %bitcast.55), kind=kLoop, calls=%fused_computation.34 | loop fusion | bytes 7077888 | tf_op jit(solution)/shard_map/squeeze | solution.py:316
  93.8 6.6 %convolution_convert_fusion.1 = bf16[1280,1536]{1,0:T(8,128)(2,1)S(1)} fusion(bf16[1536,384]{1,0:T(8,128)(2,1)S(1)} %slice_bitcast_fusion.3, bf16[1536,1152]{1,0:T(8,128)(2,1)S(1)} %slice_bitcast_fusion, bf16[640,1536]{1,0:T(8,128)(2,1)S(1)} %copy-done.6, bf16[640,1536]{1,0:T(8,128)(2,1)S(1)} %copy-done.5), kind=kOutput, calls=%fused_computation.11 | convolution fusion | flops 6059065344 | bytes 12582912 | tf_op jit(solution)/shard_map/dot_general | solution.py:322
  100.4 2.1 fusion.45
  102.6 28.5 %fusion.7.k_ref.v_ref = bf16[3,1920,1152]{2,1,0:T(8,128)(2,1)} fusion(bf16[4,1536,1152]{2,1,0:T(8,128)(2,1)} %bitcast.56, bf16[1920,1536]{1,0:T(8,128)(2,1)} %copy-done.4), kind=kOutput, calls=%fused_computation.10 | convolution fusion | flops 20390952960 | bytes 33325056 | tf_op jit(solution)/shard_map/tk,jkc->jtc/dot_general | solution.py:329
  131.1 27.4 %shard_map.74 = bf16[640,1536]{1,0:T(8,128)(2,1)} custom-call(s32[30]{0:T(128)} %reshape_squeeze.3.list_ref, s32[2]{0:T(128)} %pad_add_fusion.scalar_ref, bf16[640,1536]{1,0:T(8,128)(2,1)} %get-tuple-element.15.q_ref, bf16[3,1920,1152]{2,1,0:T(8,128)(2,1)} %fusion.7.k_ref.v_ref, bf16[3,1920,1152]{2,1,0:T(8,128)(2,1)} %fusion.7.k_ref.v_ref), custom_call_target="tpu_custom_call" | custom-call | flops 3019898880 | bytes 15728640 | tf_op jit(solution)/shard_map/pallas_call | solution.py:96
  158.4 5.1 %all-to-all-start = ((bf16[8,80,1536]{2,1,0:T(8,128)(2,1)}), bf16[8,80,1536]{2,1,0:T(8,128)(2,1)}, u32[]{:S(2)}, u32[]{:S(2)}) async-start(bf16[8,80,1536]{2,1,0:T(8,128)(2,1)} %bitcast.52), calls=%async_computation | async-start | bytes 3932160 | tf_op jit(solution)/shard_map/all_to_all | solution.py:340
  163.5 2.8 %slice_bitcast_fusion.2 = (bf16[1536,768]{1,0:T(8,128)(2,1)S(1)}, bf16[1536,768]{1,0:T(8,128)(2,1)S(1)}) fusion(bf16[4,1536,1152]{2,1,0:T(8,128)(2,1)} %bitcast.57), kind=kLoop, calls=%fused_computation.39 | loop fusion | bytes 9437184 | tf_op jit(solution)/shard_map/squeeze | solution.py:320
  166.5 4.5 %fusion.26 = bf16[640,1536]{1,0:T(8,128)(2,1)} fusion(bf16[640,1536]{1,0:T(8,128)(2,1)S(1)} %copy-done.7, bf16[1536,768]{1,0:T(8,128)(2,1)S(1)} %get-tuple-element.14, bf16[1536,768]{1,0:T(8,128)(2,1)S(1)} %get-tuple-element.13), kind=kOutput, calls=%fused_computation.36 | convolution fusion | flops 3030319104 | bytes 8650752 | tf_op jit(solution)/shard_map/dot_general | solution.py:328
  171.0 3.7 %reshape.84 = bf16[8,80,12,128]{3,2,1,0:T(8,128)(2,1)S(1)} reshape(bf16[640,1536]{1,0:T(8,128)(2,1)} %fusion.26) | data formatting | bytes 3932160 | tf_op jit(solution)/shard_map/reshape | solution.py:346
  174.7 4.8 %reshape.83 = bf16[8,80,12,128]{3,2,1,0:T(8,128)(2,1)} reshape(bf16[640,1536]{1,0:T(8,128)(2,1)} %get-tuple-element.16) | data formatting | bytes 3932160 | tf_op jit(solution)/shard_map/reshape | solution.py:345
  179.5 6.0 %fusion.31 = f32[80,12,8,8]{2,3,1,0:T(8,128)} fusion(bf16[8,80,12,128]{3,2,1,0:T(8,128)(2,1)S(1)} %reshape.84, bf16[8,80,12,128]{3,2,1,0:T(8,128)(2,1)} %reshape.83), kind=kOutput, calls=%fused_computation.42 | convolution fusion | flops 15728640 | bytes 4177920 | tf_op jit(solution)/shard_map/fphd,gphd->phfg/dot_general | solution.py:226
  185.5 3.0 %copy.32 = f32[80,12,8,8]{0,3,2,1:T(8,128)S(1)} copy(f32[80,12,8,8]{2,3,1,0:T(8,128)} %fusion.31) | data formatting | bytes 491520 | tf_op jit(solution)/shard_map/fphd,gphd->phfg/dot_general | solution.py:226
  188.7 2.3 copy.34
  191.4 3.7 %reshape.82 = bf16[8,80,12,128]{3,2,1,0:T(8,128)(2,1)S(1)} reshape(bf16[8,80,1536]{2,1,0:T(8,128)(2,1)} %all-to-all-done) | data formatting | bytes 3932160 | tf_op jit(solution)/shard_map/reshape | solution.py:347
  195.1 2.9 %fusion.25 = bf16[8,80,12,128]{3,0,2,1:T(8,128)(2,1)S(1)} fusion(bf16[80,12,8,8]{3,2,1,0:T(8,128)(2,1)} %copy.34, bf16[8,80,12,128]{3,2,1,0:T(8,128)(2,1)S(1)} %reshape.82, f32[8,80,12]{0,2,1:T(8,128)S(1)} %copy.35), kind=kOutput, calls=%fused_computation.33 | convolution fusion | flops 17694720 | bytes 4085760 | tf_op jit(solution)/shard_map/phfg,gphd->fphd/dot_general | solution.py:236
  200.3 26.3 %shard_map.75 = bf16[640,1536]{1,0:T(8,128)(2,1)} custom-call(bf16[640,1536]{1,0:T(8,128)(2,1)} %bitcast.53), custom_call_target="tpu_custom_call" | custom-call | bytes 3932160 | tf_op jit(solution)/shard_map/pallas_call | solution.py:280
  226.6 7.6 %fusion.29 = bf16[1,640,1536]{2,1,0:T(8,128)(2,1)} fusion(bf16[640,1536]{1,0:T(8,128)(2,1)} %shard_map.75, bf16[1536,1536]{1,0:T(8,128)(2,1)} %all-gather.4.cloned.1.call-done), kind=kOutput, calls=%fused_computation.37 | convolution fusion | flops 3020881920 | bytes 8650752 | tf_op jit(solution)/shard_map/dot_general | solution.py:352
  (51 shorter events, 12.9 us)
Async XLA Ops:
  6.5 2.0 copy-start
  6.5 52.6 %copy-start.9 = (f32[1,1536]{1,0:T(1,128)S(1)}, f32[1,1536]{1,0:T(1,128)}, u32[]{:S(2)}) copy-start(f32[1,1536]{1,0:T(1,128)} %param.9) | copy-start | bytes 18436
  6.5 52.7 %copy-start.8 = (f32[1,1536]{1,0:T(1,128)S(1)}, f32[1,1536]{1,0:T(1,128)}, u32[]{:S(2)}) copy-start(f32[1,1536]{1,0:T(1,128)} %param.8) | copy-start | bytes 18436
  6.5 82.7 %all-gather.6.cloned.1.call-start = ((), (), s32[]{:S(2)}) async-start(), calls=%async_computation.2 | async-start | bytes 15925248 | tf_op jit(solution)/shard_map/all_gather | solution.py:307
  9.9 216.7 %all-gather.4.cloned.1.call-start = ((), (), s32[]{:S(2)}) async-start(), calls=%async_computation.1 | async-start | bytes 5898240 | tf_op jit(solution)/shard_map/all_gather | solution.py:310
  59.3 2.8 %copy-start.2 = (bf16[1,640,1536]{2,1,0:T(8,128)(2,1)S(1)}, bf16[1,640,1536]{2,1,0:T(8,128)(2,1)}, u32[]{:S(2)}) copy-start(bf16[1,640,1536]{2,1,0:T(8,128)(2,1)} %param.7) | copy-start | bytes 5898244
  79.7 2.5 %copy-start.4 = (bf16[1920,1536]{1,0:T(8,128)(2,1)}, bf16[1920,1536]{1,0:T(8,128)(2,1)S(1)}, u32[]{:S(2)}) copy-start(bf16[1920,1536]{1,0:T(8,128)(2,1)S(1)} %fusion.6) | copy-start | bytes 17694724
  82.2 1.4 copy-start.10
  82.2 2.1 copy-start.11
  82.2 3.9 %copy-start.3 = (bf16[640,1536]{1,0:T(8,128)(2,1)S(1)}, bf16[640,1536]{1,0:T(8,128)(2,1)}, u32[]{:S(2)}) copy-start(bf16[640,1536]{1,0:T(8,128)(2,1)} %get-tuple-element.10) | copy-start | bytes 5898244
  90.6 2.6 %copy-start.5 = (bf16[640,1536]{1,0:T(8,128)(2,1)S(1)}, bf16[640,1536]{1,0:T(8,128)(2,1)}, u32[]{:S(2)}) copy-start(bf16[640,1536]{1,0:T(8,128)(2,1)} %slice.40) | copy-start | bytes 5898244
  90.6 3.2 %copy-start.6 = (bf16[640,1536]{1,0:T(8,128)(2,1)S(1)}, bf16[640,1536]{1,0:T(8,128)(2,1)}, u32[]{:S(2)}) copy-start(bf16[640,1536]{1,0:T(8,128)(2,1)} %fusion.21) | copy-start | bytes 5898244
  158.4 33.0 %all-to-all-start = ((bf16[8,80,1536]{2,1,0:T(8,128)(2,1)}), bf16[8,80,1536]{2,1,0:T(8,128)(2,1)}, u32[]{:S(2)}, u32[]{:S(2)}) async-start(bf16[8,80,1536]{2,1,0:T(8,128)(2,1)} %bitcast.52), calls=%async_computation | async-start | bytes 3932160 | tf_op jit(solution)/shard_map/all_to_all | solution.py:340
  163.5 3.0 %copy-start.7 = (bf16[640,1536]{1,0:T(8,128)(2,1)S(1)}, bf16[640,1536]{1,0:T(8,128)(2,1)}, u32[]{:S(2)}) copy-start(bf16[640,1536]{1,0:T(8,128)(2,1)} %fusion.21) | copy-start | bytes 5898244
  226.6 7.6 %copy-start.1 = (bf16[1536,1152]{1,0:T(8,128)(2,1)S(1)}, bf16[1536,1152]{1,0:T(8,128)(2,1)}, u32[]{:S(2)}) copy-start(bf16[1536,1152]{1,0:T(8,128)(2,1)} %param.10) | copy-start | bytes 10616836
Sparse Core Ops, SparseCore 0:
  10.0 77.7 all-gather.5
  102.7 53.2 all-gather.3

commit v20 on v15

--- a/solution.py
+++ b/solution.py
@@ -318,12 +318,12 @@
     w_key = jnp.concatenate(
         [w_full[1, :, feat_count - shard_cols :], w_full[2, :, : 2 * shard_cols - feat_count]], axis=1
     )
-    q_both = jnp.dot(
-        jnp.concatenate([normed_all[tok_count : 2 * tok_count], normed_cross], axis=0),
-        w_query,
-        preferred_element_type=jnp.float32,
+    queries = jnp.dot(
+        normed_all[tok_count : 2 * tok_count], w_query, preferred_element_type=jnp.float32
     ).astype(jnp.bfloat16)
-    queries = q_both[:tok_count]
+    query_cross = jnp.dot(normed_cross, w_query, preferred_element_type=jnp.float32).astype(
+        jnp.bfloat16
+    )
     key_cross = jnp.dot(normed_cross, w_key, preferred_element_type=jnp.float32).astype(jnp.bfloat16)
     kv_all = jnp.einsum(
         "tk,jkc->jtc", normed_all, w_full[1:], preferred_element_type=jnp.float32
@@ -341,7 +341,7 @@
     first_pos = piece_index * tok_count + frame_index * per_dev
     part_shape = (n_frames, per_dev, HEADS, HD)
     temporal = temporal_block(
-        q_both[tok_count:].reshape(part_shape),
+        query_cross.reshape(part_shape),
         key_cross.reshape(part_shape),
         spatial_part.reshape(part_shape),
         clip_counts,

time: 242 us -> 248 us (1.025)
  matrix products: 56.1 us -> 64.4 us
  local copies, waits for them, and re-layouts: 38.4 us -> 33.8 us
    dot_general x1 -> x2, matrix products: 6.6 us -> 14.8 us  [the longest x1 7.51 us: local(): jnp.dot(normed_cross, w_query, preferred_element_type=jnp.float32)]
    slice x2 -> x0, local copies, waits for them, and re-layouts: 3.53 us -> none  [the longest x1 2.12 us: local(): queries = q_both[:tok_count]]
    unnamed x25 -> x29, local copies, waits for them, and re-layouts: 7.34 us -> 5.25 us
    convert_element_type x2 -> x1, other arithmetic: 13.3 us -> 12.8 us  [layer_norm(): return (normal * (1.0 + mod_scale) + mod_shift).astype(jnp.bfloat16)]
  transfers between devices with their start and end apart: 3 -> 3, of which waited for: 0 -> 0; matrix products, arithmetic and copies ran while one was open for 38% -> 46% of each run, Pallas kernels for 43% -> 42%
where the time goes in v20:
time: 248 us
  Pallas kernels  103 us (42%)
  matrix products  64.4 us (26%)
  local copies, waits for them, and re-layouts  33.8 us (14%)
  other arithmetic  27.4 us (11%)
  between operations  13.6 us (5%)
  starting transfers between devices  5.13 us (2%)
    pallas_call x1, Pallas kernels, exchange_tokens(): pl.pallas_call(exchange_kernel, out_shape=(jax.ShapeDtypeStruct((2, rows,...  49.2 us
    dot_general x1, matrix products, local(): jnp.einsum('tk,jkc->jtc', normed_all, w_full[1:], preferred_element_type=...  28.3 us
    pallas_call x1, Pallas kernels, spatial_rows(): pl.pallas_call(spatial_kernel, grid_spec=grid_spec, out_shape=jax.ShapeDt...  27.4 us
    pallas_call x1, Pallas kernels, swap_frames(): pl.pallas_call(swap_kernel, out_shape=jax.ShapeDtypeStruct((rows, feat),...  26.6 us
    convert_element_type x1, other arithmetic, layer_norm(): return (normal * (1.0 + mod_scale) + mod_shift).astype(jnp.bfloat16)  12.8 us
    reduce_sum x2, other arithmetic, layer_norm(): spread = jnp.mean((values_f32 - center) ** 2, axis=-1, keepdims=True)  7.59 us
    dot_general x1, matrix products, local(): jnp.dot(flat_temporal, w_out_full, preferred_element_type=jnp.float32)  7.56 us
    dot_general x1, matrix products, local(): jnp.dot(normed_cross, w_query, preferred_element_type=jnp.float32)  7.51 us
  transfers between devices with their start and end apart: 3, of which 0 were waited for; matrix products, arithmetic and copies ran while one was open for 46% of the time, Pallas kernels for 42%

profile of v20, /device:TPU:1, one launch (start us, length us, event | category | flops | bytes accessed | tf_op | source)
XLA Modules:
  0.0 247.5 jit_solution(14417189863354497189)
XLA Ops:
  6.6 2.0 copy-done
  10.0 49.2 %shard_map.73 = (bf16[2,640,1536]{2,1,0:T(8,128)(2,1)}, bf16[640,1536]{1,0:T(8,128)(2,1)}) custom-call(bf16[640,1536]{1,0:T(8,128)(2,1)} %bitcast.46), custom_call_target="tpu_custom_call" | custom-call | bytes 157286400 | tf_op jit(solution)/shard_map/pallas_call | solution.py:200
  63.3 1.9 convert_reduce_fusion.1
  65.9 2.2 fusion.15
  71.4 5.4 %fusion.3 = f32[1920]{0:T(1024)S(1)} fusion(f32[1920]{0:T(1024)S(1)} %broadcast_multiply_fusion, bf16[640,1536]{1,0:T(8,128)(2,1)S(1)} %get-tuple-element.16, bf16[640,1536]{1,0:T(8,128)(2,1)S(1)} %bitcast.48, bf16[640,1536]{1,0:T(8,128)(2,1)S(1)} %get-tuple-element.15), kind=kLoop, calls=%fused_computation.6 | loop fusion | flops 26540160 | bytes 5913600 | tf_op jit(solution)/shard_map/reduce_sum | solution.py:28
  76.8 12.8 %fusion.6 = bf16[1920,1536]{1,0:T(8,128)(2,1)} fusion(f32[1536]{0:T(1024)S(1)} %reduce.2, f32[1536]{0:T(1024)S(1)} %add_reduce_fusion, f32[1920]{0:T(1024)S(1)} %add_sqrt_fusion, f32[1920]{0:T(1024)S(1)} %broadcast_multiply_fusion, bf16[640,1536]{1,0:T(8,128)(2,1)S(1)} %get-tuple-element.16, bf16[640,1536]{1,0:T(8,128)(2,1)S(1)} %bitcast.49, ...), kind=kLoop, calls=%fused_computation.9 | loop fusion | flops 32440320 | bytes 11824128 | tf_op jit(solution)/shard_map/convert_element_type | solution.py:30
  89.7 28.3 %fusion.7.k_ref.v_ref = bf16[3,1920,1152]{2,1,0:T(8,128)(2,1)} fusion(bf16[4,1536,1152]{2,1,0:T(8,128)(2,1)} %bitcast.53, bf16[1920,1536]{1,0:T(8,128)(2,1)} %fusion.6), kind=kOutput, calls=%fused_computation.10 | convolution fusion | flops 20390952960 | bytes 33325056 | tf_op jit(solution)/shard_map/tk,jkc->jtc/dot_general | solution.py:328
  119.4 2.7 %slice_bitcast_fusion = bf16[1536,1152]{1,0:T(8,128)(2,1)S(1)} fusion(bf16[4,1536,1152]{2,1,0:T(8,128)(2,1)} %bitcast.55), kind=kLoop, calls=%fused_computation.28 | loop fusion | bytes 7077888 | tf_op jit(solution)/shard_map/squeeze | solution.py:315
  122.1 7.3 %convolution_convert_fusion.3.q_ref = bf16[640,1536]{1,0:T(8,128)(2,1)} fusion(bf16[1536,384]{1,0:T(8,128)(2,1)S(1)} %slice_bitcast_fusion.3, bf16[1536,1152]{1,0:T(8,128)(2,1)S(1)} %slice_bitcast_fusion, bf16[1920,1536]{1,0:T(8,128)(2,1)} %fusion.6), kind=kOutput, calls=%fused_computation.31 | convolution fusion | flops 3030319104 | bytes 8650752 | tf_op jit(solution)/shard_map/dot_general | solution.py:321
  129.4 27.4 %shard_map.74 = bf16[640,1536]{1,0:T(8,128)(2,1)} custom-call(s32[30]{0:T(128)} %reshape_squeeze.3.list_ref, s32[2]{0:T(128)} %pad_add_fusion.scalar_ref, bf16[640,1536]{1,0:T(8,128)(2,1)} %convolution_convert_fusion.3.q_ref, bf16[3,1920,1152]{2,1,0:T(8,128)(2,1)} %fusion.7.k_ref.v_ref, bf16[3,1920,1152]{2,1,0:T(8,128)(2,1)} %fusion.7.k_ref.v_ref), custom_call_target="tpu_custom_call" | custom-call | flops 3019898880 | bytes 15728640 | tf_op jit(solution)/shard_map/pallas_call | solution.py:96
  156.8 5.1 %all-to-all-start = ((bf16[8,80,1536]{2,1,0:T(8,128)(2,1)}), bf16[8,80,1536]{2,1,0:T(8,128)(2,1)}, u32[]{:S(2)}, u32[]{:S(2)}) async-start(bf16[8,80,1536]{2,1,0:T(8,128)(2,1)} %bitcast.51), calls=%async_computation | async-start | bytes 3932160 | tf_op jit(solution)/shard_map/all_to_all | solution.py:339
  161.9 2.8 %slice_bitcast_fusion.2 = (bf16[1536,768]{1,0:T(8,128)(2,1)S(1)}, bf16[1536,768]{1,0:T(8,128)(2,1)S(1)}) fusion(bf16[4,1536,1152]{2,1,0:T(8,128)(2,1)} %bitcast.56), kind=kLoop, calls=%fused_computation.35 | loop fusion | bytes 9437184 | tf_op jit(solution)/shard_map/squeeze | solution.py:319
  164.9 4.6 %fusion.20 = bf16[640,1536]{1,0:T(8,128)(2,1)} fusion(bf16[1536,768]{1,0:T(8,128)(2,1)S(1)} %get-tuple-element.14, bf16[1536,768]{1,0:T(8,128)(2,1)S(1)} %get-tuple-element.13, bf16[640,1536]{1,0:T(8,128)(2,1)S(1)} %copy-done.3, f32[1536]{0:T(1024)S(1)} %reduce.2, f32[1536]{0:T(1024)S(1)} %add_reduce_fusion, f32[640]{0:T(1024)S(1)} %copy-done.10, ...), kind=kOutput, calls=%fused_computation.32 | convolution fusion | flops 3036217344 | bytes 8668160 | tf_op jit(solution)/shard_map/dot_general | solution.py:327
  169.5 3.7 %reshape.84 = bf16[8,80,12,128]{3,2,1,0:T(8,128)(2,1)S(1)} reshape(bf16[640,1536]{1,0:T(8,128)(2,1)} %fusion.20) | data formatting | bytes 3932160 | tf_op jit(solution)/shard_map/reshape | solution.py:345
  173.2 7.5 %convolution_convert_fusion.2 = bf16[640,1536]{1,0:T(8,128)(2,1)} fusion(bf16[1536,384]{1,0:T(8,128)(2,1)} %copy-done.6, bf16[1536,1152]{1,0:T(8,128)(2,1)} %copy-done.5, bf16[640,1536]{1,0:T(8,128)(2,1)} %get-tuple-element.11, f32[1536]{0:T(1024)S(1)} %reduce.2, f32[1536]{0:T(1024)S(1)} %add_reduce_fusion, f32[640]{0:T(1024)S(1)} %copy-done.10, ...), kind=kOutput, calls=%fused_computation.30 | convolution fusion | flops 3036217344 | bytes 8668160 | tf_op jit(solution)/shard_map/dot_general | solution.py:324
  180.7 4.7 %reshape.83 = bf16[8,80,12,128]{3,2,1,0:T(8,128)(2,1)} reshape(bf16[640,1536]{1,0:T(8,128)(2,1)} %convolution_convert_fusion.2) | data formatting | bytes 3932160 | tf_op jit(solution)/shard_map/reshape | solution.py:344
  185.5 6.0 %fusion.26 = f32[80,12,8,8]{2,3,1,0:T(8,128)} fusion(bf16[8,80,12,128]{3,2,1,0:T(8,128)(2,1)S(1)} %reshape.84, bf16[8,80,12,128]{3,2,1,0:T(8,128)(2,1)} %reshape.83), kind=kOutput, calls=%fused_computation.39 | convolution fusion | flops 15728640 | bytes 4177920 | tf_op jit(solution)/shard_map/fphd,gphd->phfg/dot_general | solution.py:226
  191.4 3.0 %copy.32 = f32[80,12,8,8]{0,3,2,1:T(8,128)S(1)} copy(f32[80,12,8,8]{2,3,1,0:T(8,128)} %fusion.26) | data formatting | bytes 491520 | tf_op jit(solution)/shard_map/fphd,gphd->phfg/dot_general | solution.py:226
  194.7 2.3 copy.34
  197.4 3.7 %reshape.82 = bf16[8,80,12,128]{3,2,1,0:T(8,128)(2,1)S(1)} reshape(bf16[8,80,1536]{2,1,0:T(8,128)(2,1)} %all-to-all-done) | data formatting | bytes 3932160 | tf_op jit(solution)/shard_map/reshape | solution.py:346
  201.1 3.2 %fusion.19 = bf16[8,80,12,128]{3,0,2,1:T(8,128)(2,1)S(1)} fusion(bf16[80,12,8,8]{3,2,1,0:T(8,128)(2,1)} %copy.34, bf16[8,80,12,128]{3,2,1,0:T(8,128)(2,1)S(1)} %reshape.82, f32[8,80,12]{0,2,1:T(8,128)S(1)} %copy.35), kind=kOutput, calls=%fused_computation.27 | convolution fusion | flops 17694720 | bytes 4085760 | tf_op jit(solution)/shard_map/phfg,gphd->fphd/dot_general | solution.py:236
  204.7 1.8 copy.46
  206.5 26.6 %shard_map.75 = bf16[640,1536]{1,0:T(8,128)(2,1)} custom-call(bf16[640,1536]{1,0:T(8,128)(2,1)} %bitcast.52), custom_call_target="tpu_custom_call" | custom-call | bytes 3932160 | tf_op jit(solution)/shard_map/pallas_call | solution.py:279
  233.1 7.6 %fusion.23 = bf16[1,640,1536]{2,1,0:T(8,128)(2,1)} fusion(bf16[640,1536]{1,0:T(8,128)(2,1)} %shard_map.75, bf16[1536,1536]{1,0:T(8,128)(2,1)} %all-gather.4.cloned.1.call-done), kind=kOutput, calls=%fused_computation.33 | convolution fusion | flops 3020881920 | bytes 8650752 | tf_op jit(solution)/shard_map/dot_general | solution.py:351
  (53 shorter events, 12.1 us)
Async XLA Ops:
  6.5 2.0 copy-start
  6.5 52.6 %copy-start.11 = (s32[1,5,6]{2,0,1:T(1,128)S(1)}, s32[1,5,6]{2,0,1:T(1,128)}, u32[]{:S(2)}) copy-start(s32[1,5,6]{2,0,1:T(1,128)} %param.12) | copy-start | bytes 364
  6.5 53.3 %copy-start.9 = (f32[1,1536]{1,0:T(1,128)S(1)}, f32[1,1536]{1,0:T(1,128)}, u32[]{:S(2)}) copy-start(f32[1,1536]{1,0:T(1,128)} %param.9) | copy-start | bytes 18436
  6.5 83.1 %all-gather.6.cloned.1.call-start = ((), (), s32[]{:S(2)}) async-start(), calls=%async_computation.2 | async-start | bytes 15925248 | tf_op jit(solution)/shard_map/all_gather | solution.py:306
  9.9 55.4 %copy-start.13 = (s32[1,8]{1,0:T(1,128)S(1)}, s32[1,8]{1,0:T(1,128)}, u32[]{:S(2)}) copy-start(s32[1,8]{1,0:T(1,128)} %param.13) | copy-start | bytes 100
  9.9 223.2 %all-gather.4.cloned.1.call-start = ((), (), s32[]{:S(2)}) async-start(), calls=%async_computation.1 | async-start | bytes 5898240 | tf_op jit(solution)/shard_map/all_gather | solution.py:309
  61.2 7.5 %copy-start.4 = (bf16[2,640,1536]{2,1,0:T(8,128)(2,1)S(1)}, bf16[2,640,1536]{2,1,0:T(8,128)(2,1)}, u32[]{:S(2)}) copy-start(bf16[2,640,1536]{2,1,0:T(8,128)(2,1)} %get-tuple-element.9) | copy-start | bytes 11796484
  65.9 2.8 %copy-start.7 = (f32[640]{0:T(1024)}, f32[640]{0:T(1024)S(1)}, u32[]{:S(2)}) copy-start(f32[640]{0:T(1024)S(1)} %broadcast_multiply_fusion.1) | copy-start | bytes 7684
  68.7 1.6 copy-start.2
  119.4 2.7 %copy-start.6 = (bf16[1536,384]{1,0:T(8,128)(2,1)}, bf16[1536,384]{1,0:T(8,128)(2,1)S(1)}, u32[]{:S(2)}) copy-start(bf16[1536,384]{1,0:T(8,128)(2,1)S(1)} %slice_bitcast_fusion.3) | copy-start | bytes 3538948
  122.1 7.3 %copy-start.5 = (bf16[1536,1152]{1,0:T(8,128)(2,1)}, bf16[1536,1152]{1,0:T(8,128)(2,1)S(1)}, u32[]{:S(2)}) copy-start(bf16[1536,1152]{1,0:T(8,128)(2,1)S(1)} %slice_bitcast_fusion) | copy-start | bytes 10616836
  156.8 40.6 %all-to-all-start = ((bf16[8,80,1536]{2,1,0:T(8,128)(2,1)}), bf16[8,80,1536]{2,1,0:T(8,128)(2,1)}, u32[]{:S(2)}, u32[]{:S(2)}) async-start(bf16[8,80,1536]{2,1,0:T(8,128)(2,1)} %bitcast.51), calls=%async_computation | async-start | bytes 3932160 | tf_op jit(solution)/shard_map/all_to_all | solution.py:339
  161.9 3.0 %copy-start.3 = (bf16[640,1536]{1,0:T(8,128)(2,1)S(1)}, bf16[640,1536]{1,0:T(8,128)(2,1)}, u32[]{:S(2)}) copy-start(bf16[640,1536]{1,0:T(8,128)(2,1)} %get-tuple-element.11) | copy-start | bytes 5898244
  161.9 3.0 %copy-start.8 = (f32[640]{0:T(1024)S(1)}, f32[640]{0:T(1024)}, u32[]{:S(2)}) copy-start(f32[640]{0:T(1024)} %copy-done.7) | copy-start | bytes 7684
  161.9 3.0 %copy-start.10 = (f32[640]{0:T(1024)S(1)}, f32[640]{0:T(1024)}, u32[]{:S(2)}) copy-start(f32[640]{0:T(1024)} %add_sqrt_fusion.1) | copy-start | bytes 7684
  191.4 3.0 %copy-start.12 = (pred[80,8]{0,1:T(8,128)(4,1)S(1)}, pred[80,8]{0,1:T(8,128)(4,1)}, u32[]{:S(2)}) copy-start(pred[80,8]{0,1:T(8,128)(4,1)} %broadcast_compare_fusion) | copy-start | bytes 1924
  233.1 7.6 %copy-start.1 = (bf16[1536,1152]{1,0:T(8,128)(2,1)S(1)}, bf16[1536,1152]{1,0:T(8,128)(2,1)}, u32[]{:S(2)}) copy-start(bf16[1536,1152]{1,0:T(8,128)(2,1)} %param.10) | copy-start | bytes 10616836
Sparse Core Ops, SparseCore 0:
  10.0 77.7 all-gather.5
  89.8 53.2 all-gather.3
